TPU v7x, 128 devices: a whole 4x4x4 slice. The times are simulated.
128 devices in a mesh: member: 8 (over y, core), mesh: 16 (over x, z).
Axes of the slice: x: 4, y: 4, z: 4, core: 2. Of those that a mesh axis runs over, the one named last changes fastest.
Arguments:
- hidden_embedding: bfloat16 [16, 8192, 512], P('member', 'mesh'), may hold values from -6 to 6
- decoder_matrix: bfloat16 [512, 96], replicated, may hold values from -0.25 to 0.25
- baseline_field: float32 [96, 8192], P(None, 'mesh'), may hold values from -6 to 6
- truth_field: float32 [96, 8192], P(None, 'mesh'), may hold values from -6 to 6
- cell_surface_share: float32 [8192], P('mesh'), may hold values from 0.3 to 3
- node_order: int32 [16, 512], P('mesh'), may hold values from 0 to 511, each once within a row
- query: bfloat16 [16, 8192, 512], P('member', 'mesh'), may hold values from -6 to 6
- key_rows: bfloat16 [16, 8192, 512], P('member', 'mesh'), may hold values from -6 to 6
- value_rows: bfloat16 [16, 8192, 512], P('member', 'mesh'), may hold values from -6 to 6
- row_lse: float32 [16, 8, 8192], P('member', None, 'mesh'), may hold values from 6.5 to 8.5
- kv_owner: int32 [16, 16], replicated, may hold values from 0 to 15, each once within a row
- kv_local: int32 [16, 16], replicated, may hold values from 0 to 3
Outputs:
- grad_query: float32 [16, 8192, 512], P('member', 'mesh')
- grad_key: float32 [16, 8192, 512], P('member', 'mesh')
- grad_value: float32 [16, 8192, 512], P('member', 'mesh')
Inputs may be any that keep to these rules, and one draw needn't show every extreme that they name: `kv_owner`: each row names every shard once. `node_order`: each row holds every number of 0 to 511 once.
All inputs are finite; a program needn't handle non-finite values.
Results may differ from a plain program's by a relative error of at most 0.0068.
Values may be sent and summed in bfloat16 or wider, within the bound.
No kernel may reach another device: no remote copies, remote signals or barrier semaphores. Data moves between devices by JAX's collectives and lax.ppermute only.
A program may use at most 128 MiB of HBM per device.

v0:
```python
import jax
import jax.numpy as jnp
from jax import lax
from jax.sharding import Mesh
from jax.sharding import PartitionSpec as P

KB = 128
MEMBER = ("member_0", "member_1")


LOSS_SCALE = 4096.0
FAIR_EPS = 0.05
NORM_EPS = 1e-06


def cut_along(x, dim, length):
    dims = x.shape
    tiles = x.reshape(*dims[:dim], length, dims[dim] // length, *dims[dim + 1 :])
    return jnp.moveaxis(tiles, dim, 0)


def in_order(tiles, dim):
    tiles = jnp.moveaxis(tiles, 0, dim)
    dims = tiles.shape
    return tiles.reshape(*dims[:dim], dims[dim] * dims[dim + 1], *dims[dim + 2 :])


def moved_by_axis(tiles, axes, sequence):
    inside = tiles.shape[1:]
    filled = tiles.reshape(*(lax.axis_size(a) for a in axes), *inside)
    for k in sequence:
        filled = lax.all_to_all(filled, axes[k], k, k, tiled=True)
    return filled.reshape(-1, *inside)


def exchange_by_axis(x, axes, sequence, split_dim, concat_dim):
    tiles = cut_along(x, split_dim, lax.axis_size(axes))
    return in_order(moved_by_axis(tiles, axes, sequence), concat_dim)


def piece_ends(length, count):
    turn = length // count
    if turn >= 8:
        turn -= turn % 8
    return [turn * k for k in range(1, count)]


def cut_exchange(x, axis, pieces, split_dim, concat_dim):
    tiles = cut_along(x, split_dim, lax.axis_size(axis))
    cut = max(range(1, max(2, tiles.ndim - 1)), key=lambda d: tiles.shape[d])
    done = []
    for section in jnp.split(tiles, piece_ends(tiles.shape[cut], pieces), axis=cut):
        if section.size:
            done.append(lax.all_to_all(section, axis, split_axis=0, concat_axis=0, tiled=True))
    return in_order(jnp.concatenate(done, axis=cut), concat_dim)


def unit_scaled_lines(differences):
    return differences / jnp.sqrt(
        jnp.sum(differences * differences, axis=-2, keepdims=True) + NORM_EPS
    )


def outlook_derivative(shard_lines, entire_collection, truth_field, cell_surface_share):
    realization_list = entire_collection.shape[0]
    polarity_unit = unit_scaled_lines(shard_lines - truth_field[None])
    differences = shard_lines[:, None] - entire_collection[None]
    couple_total = jnp.sum(unit_scaled_lines(differences), axis=1)
    weight = LOSS_SCALE * cell_surface_share[None, None, :]
    return weight * (
        polarity_unit / realization_list
        - (1.0 - FAIR_EPS) / (realization_list * (realization_list - 1)) * couple_total
    )


def shards(
    hidden_embedding,
    decoder_matrix,
    baseline_field,
    truth_field,
    cell_surface_share,
    node_order,
    query,
    key_rows,
    value_rows,
    row_lse,
    kv_owner,
    kv_local,
):
    member_count = hidden_embedding.shape[0]
    node_count = hidden_embedding.shape[1]
    model_width = hidden_embedding.shape[2]
    realization_outlook = baseline_field[None] + jnp.einsum(
        "mou,ut->mto", hidden_embedding, decoder_matrix, preferred_element_type=jnp.float32
    )
    groups = lax.axis_size(MEMBER)
    member_index = lax.axis_index(MEMBER)
    entire_collection = exchange_by_axis(realization_outlook, MEMBER, (1, 0), 2, 0)
    node_span = node_count // groups
    offset = member_index * node_span
    observation_term = lax.dynamic_slice_in_dim(truth_field, offset, node_span, 1)
    area_factor = lax.dynamic_slice_in_dim(cell_surface_share, offset, node_span, 0)
    loss_derivative = outlook_derivative(
        entire_collection, entire_collection, observation_term, area_factor
    ).astype(jnp.bfloat16)
    estimate_derivative = exchange_by_axis(loss_derivative, MEMBER, (1, 0), 0, 2)
    head_count = row_lse.shape[1]
    head_dim = model_width // head_count
    score_scale = head_dim ** (-0.5)
    split_shape = (member_count, head_count, head_dim, node_count)
    permuter = (node_order[0][:, None] == jnp.arange(node_count, dtype=jnp.int32)[None, :]).astype(
        jnp.bfloat16
    )
    grad_columns = jnp.einsum(
        "mcg,tg->mct", estimate_derivative, permuter, preferred_element_type=jnp.float32
    ).astype(jnp.bfloat16)
    grad_heads = (
        jnp.einsum("wc,mct->mwt", decoder_matrix, grad_columns, preferred_element_type=jnp.float32)
        .astype(jnp.bfloat16)
        .reshape(split_shape)
    )
    saved_heads = (
        jnp.einsum("mgw,tg->mwt", hidden_embedding, permuter, preferred_element_type=jnp.float32)
        .astype(jnp.bfloat16)
        .reshape(split_shape)
    )
    row_delta = jnp.sum(grad_heads.astype(jnp.float32) * saved_heads.astype(jnp.float32), axis=2)
    query_heads = jnp.swapaxes(query, 1, 2).reshape(split_shape)
    mesh_index = lax.axis_index("mesh")
    block_rows = KB
    block_count = node_count // block_rows
    paired = jnp.swapaxes(jnp.stack([key_rows, value_rows], axis=1), 2, 3).reshape(
        member_count, 2, head_count, head_dim, block_count, block_rows
    )
    wanted = (kv_owner == mesh_index)[:, :, None] & (
        kv_local[:, :, None] == jnp.arange(block_count, dtype=jnp.int32)[None, None, :]
    )
    select = jnp.sum(wanted.astype(jnp.float32), axis=1).astype(jnp.bfloat16)
    outgoing = jnp.einsum(
        "sl,mahdlk->smahdk", select, paired, preferred_element_type=jnp.float32
    ).astype(jnp.bfloat16)
    incoming = cut_exchange(outgoing, "mesh", 2, 0, 0)

    def one_block(query_sum, tile_pair):
        key_tile = tile_pair[:, 0]
        value_tile = tile_pair[:, 1]
        scores = (
            jnp.einsum("mhdr,mhdk->mhrk", query_heads, key_tile, preferred_element_type=jnp.float32)
            * score_scale
        )
        probability = jnp.exp(scores - row_lse[:, :, :, None])
        dprobs = jnp.einsum(
            "mhdr,mhdk->mhrk", grad_heads, value_tile, preferred_element_type=jnp.float32
        )
        dscores = (probability * (dprobs - row_delta[:, :, :, None])).astype(jnp.bfloat16)
        query_grad = (
            score_scale
            * jnp.einsum("mhrk,mhdk->mhdr", dscores, key_tile, preferred_element_type=jnp.float32)
        ).astype(jnp.bfloat16)
        key_grad = (
            score_scale
            * jnp.einsum(
                "mhrk,mhdr->mhdk", dscores, query_heads, preferred_element_type=jnp.float32
            )
        ).astype(jnp.bfloat16)
        value_grad = jnp.einsum(
            "mhrk,mhdr->mhdk",
            probability.astype(jnp.bfloat16),
            grad_heads,
            preferred_element_type=jnp.float32,
        ).astype(jnp.bfloat16)
        return (
            query_sum + query_grad.astype(jnp.float32),
            jnp.stack([key_grad, value_grad], axis=1),
        )

    query_sum, returned = lax.scan(one_block, jnp.zeros(split_shape, jnp.float32), incoming)
    arrived = cut_exchange(returned, "mesh", 2, 0, 0)
    block_grads = jnp.einsum(
        "sl,smahdk->mahdlk", select, arrived, preferred_element_type=jnp.float32
    )
    block_grads = jnp.swapaxes(block_grads.reshape(member_count, 2, model_width, node_count), 2, 3)
    grad_query = jnp.swapaxes(query_sum.reshape(member_count, model_width, node_count), 1, 2)
    return (grad_query, block_grads[:, 0], block_grads[:, 1])


def solution(mesh):
    finer = Mesh(mesh.devices.reshape(4, 2, mesh.shape["mesh"]), ("member_0", "member_1", "mesh"))
    in_specs = (
        P(MEMBER, "mesh", None),
        P(),
        P(None, "mesh"),
        P(None, "mesh"),
        P("mesh"),
        P("mesh", None),
        P(MEMBER, "mesh", None),
        P(MEMBER, "mesh", None),
        P(MEMBER, "mesh", None),
        P(MEMBER, None, "mesh"),
        P(),
        P(),
    )
    out_specs = (P(MEMBER, "mesh", None), P(MEMBER, "mesh", None), P(MEMBER, "mesh", None))
    return jax.shard_map(
        shards, mesh=finer, in_specs=in_specs, out_specs=out_specs, check_vma=False
    )
```

profile of v0, /device:TPU:2, one launch (start us, length us, event | category | flops | bytes accessed | tf_op | source)
XLA Modules:
  0.0 452.0 jit_solution(4851500701383454047)
XLA Ops:
  0.7 1.2 copy-done
  1.9 1.4 fusion.22
  3.5 4.2 all_to_all.40
  8.5 4.5 all-to-all-start.3
  14.7 2.7 maximum_bitcast_fusion.6
  17.5 4.2 copy.75
  21.6 4.0 reshape.79
  25.7 5.9 %convert_bitcast_fusion = bf16[16,1,2,2,8,64,128]{6,0,5,4,3,2,1:T(8,128)(2,1)} fusion(bf16[2,2,8,64,4,128]{5,4,3,2,1,0:T(4,128)(2,1)} %reshape.79, bf16[16,4]{0,1:T(4,128)(2,1)S(1)} %convert_reduce_fusion), kind=kOutput, calls=%fused_computation.30 | convolution fusion | flops 37748736 | bytes 10485888 | tf_op jit(solution)/shard_map/sl,mahdlk->smahdk/dot_general | solution.py:139
  31.8 2.2 fusion.16
  34.1 2.6 fusion.15
  37.0 3.9 all_to_all.41
  41.7 4.8 %all-to-all-start.5 = ((bf16[4,2,2,96,64]{3,4,2,1,0:T(8,128)(2,1)}), bf16[4,2,2,96,64]{3,4,2,1,0:T(8,128)(2,1)S(1)}, u32[]{:S(2)}, u32[]{:S(2)}) async-start(bf16[4,2,2,96,64]{3,4,2,1,0:T(8,128)(2,1)} %copy.84), calls=%async_computation.5 | async-start | bytes 524288 | tf_op jit(solution)/shard_map/all_to_all | solution.py:32
  46.5 5.6 %fusion.39 = (bf16[16,1,2,2,8,32,128]{6,0,5,4,3,2,1:T(8,128)(2,1)S(1)}, bf16[16,1,2,2,8,32,128]{6,0,5,4,3,2,1:T(8,128)(2,1)}) fusion(bf16[16,1,2,2,8,64,128]{6,0,5,4,3,2,1:T(8,128)(2,1)} %convert_bitcast_fusion), kind=kLoop, calls=%fused_computation.65 | loop fusion | bytes 16777216 | tf_op jit(solution)/shard_map/split | solution.py:52
  52.1 3.0 copy.76
  55.1 8.3 %all-to-all-start = ((bf16[16,1,2,2,8,32,128]{6,5,4,3,2,1,0:T(8,128)(2,1)}), bf16[16,1,2,2,8,32,128]{6,5,4,3,2,1,0:T(8,128)(2,1)}, u32[]{:S(2)}, u32[]{:S(2)}) async-start(bf16[16,1,2,2,8,32,128]{6,5,4,3,2,1,0:T(8,128)(2,1)} %copy.76), calls=%async_computation | async-start | bytes 8388608 | tf_op jit(solution)/shard_map/all_to_all | solution.py:54
  63.4 5.2 %copy.77 = bf16[16,1,2,2,8,32,128]{6,5,4,3,2,1,0:T(8,128)(2,1)} copy(bf16[16,1,2,2,8,32,128]{6,0,5,4,3,2,1:T(8,128)(2,1)} %get-tuple-element.146) | data formatting | bytes 8388608 | tf_op jit(solution)/shard_map/split | solution.py:52
  68.7 49.0 %all-to-all-done = bf16[16,1,2,2,8,32,128]{6,5,4,3,2,1,0:T(8,128)(2,1)} async-done(((bf16[16,1,2,2,8,32,128]{6,5,4,3,2,1,0:T(8,128)(2,1)}), bf16[16,1,2,2,8,32,128]{6,5,4,3,2,1,0:T(8,128)(2,1)}, u32[]{:S(2)}, u32[]{:S(2)}) %all-to-all-start) | async-done | bytes 4194336 | tf_op jit(solution)/shard_map/all_to_all | solution.py:54
  117.7 19.2 %all-to-all-start.1 = ((bf16[16,1,2,2,8,32,128]{6,5,4,3,2,1,0:T(8,128)(2,1)}), bf16[16,1,2,2,8,32,128]{6,5,4,3,2,1,0:T(8,128)(2,1)}, u32[]{:S(2)}, u32[]{:S(2)}) async-start(bf16[16,1,2,2,8,32,128]{6,5,4,3,2,1,0:T(8,128)(2,1)} %copy.77), calls=%async_computation.1 | async-start | bytes 8388608 | tf_op jit(solution)/shard_map/all_to_all | solution.py:54
  138.2 1.7 convolution_convert_fusion.1
  141.0 45.4 %all-to-all-done.1 = bf16[16,1,2,2,8,32,128]{6,5,4,3,2,1,0:T(8,128)(2,1)} async-done(((bf16[16,1,2,2,8,32,128]{6,5,4,3,2,1,0:T(8,128)(2,1)}), bf16[16,1,2,2,8,32,128]{6,5,4,3,2,1,0:T(8,128)(2,1)}, u32[]{:S(2)}, u32[]{:S(2)}) %all-to-all-start.1) | async-done | bytes 4194336 | tf_op jit(solution)/shard_map/all_to_all | solution.py:54
  186.4 9.8 %maximum_bitcast_fusion.1 = bf16[16,2,2,8,64,128]{5,4,3,2,1,0:T(8,128)(2,1)} fusion(bf16[16,1,2,2,8,32,128]{6,5,4,3,2,1,0:T(8,128)(2,1)} %all-to-all-done.1, bf16[16,1,2,2,8,32,128]{6,5,4,3,2,1,0:T(8,128)(2,1)} %all-to-all-done), kind=kLoop, calls=%fused_computation.25 | loop fusion | flops 16777216 | bytes 16777216 | tf_op jit(solution)/shard_map/reshape | solution.py:25
  196.2 115.6 %while.13 = (s32[]{:T(128)}, f32[2,8,64,512]{3,2,1,0:T(8,128)}, bf16[16,2,2,8,64,128]{5,4,3,2,1,0:T(8,128)(2,1)}, bf16[16,2,2,8,64,128]{5,4,3,2,1,0:T(8,128)(2,1...) while((s32[]{:T(128)}, f32[2,8,64,512]{3,2,1,0:T(8,128)}, ...), condition=%wide.region_6.7_spmd.clone, body=%wide.region_5.6_spmd.clone.sunk | while | flops 682754048 | bytes 47546548 | solution.py:177
  196.2 1.1 copy_bitcast_fusion.2
  199.0 1.3 multiply_convert_fusion.4
  203.4 1.1 copy_bitcast_fusion.2
  206.2 1.3 multiply_convert_fusion.4
  210.6 1.1 copy_bitcast_fusion.2
  213.5 1.3 multiply_convert_fusion.4
  217.9 1.1 copy_bitcast_fusion.2
  220.7 1.3 multiply_convert_fusion.4
  225.1 1.1 copy_bitcast_fusion.2
  227.9 1.3 multiply_convert_fusion.4
  232.3 1.1 copy_bitcast_fusion.2
  235.1 1.3 multiply_convert_fusion.4
  239.5 1.1 copy_bitcast_fusion.2
  242.4 1.3 multiply_convert_fusion.4
  246.8 1.1 copy_bitcast_fusion.2
  249.6 1.3 multiply_convert_fusion.4
  254.0 1.1 copy_bitcast_fusion.2
  256.8 1.3 multiply_convert_fusion.4
  261.2 1.1 copy_bitcast_fusion.2
  264.0 1.3 multiply_convert_fusion.4
  268.4 1.1 copy_bitcast_fusion.2
  271.3 1.3 multiply_convert_fusion.4
  275.7 1.1 copy_bitcast_fusion.2
  278.5 1.3 multiply_convert_fusion.4
  282.9 1.1 copy_bitcast_fusion.2
  285.7 1.3 multiply_convert_fusion.4
  290.1 1.1 copy_bitcast_fusion.2
  292.9 1.3 multiply_convert_fusion.4
  297.3 1.1 copy_bitcast_fusion.2
  300.2 1.3 multiply_convert_fusion.4
  307.4 1.3 multiply_convert_fusion.4
  311.8 5.8 %fusion.38 = (bf16[16,1,2,2,8,32,128]{6,5,4,3,2,1,0:T(8,128)(2,1)S(1)}, bf16[16,1,2,2,8,32,128]{6,5,4,3,2,1,0:T(8,128)(2,1)}) fusion(bf16[16,1,2,2,8,64,128]{6,5,4,3,2,1,0:T(8,128)(2,1)} %bitcast.131), kind=kLoop, calls=%fused_computation.64 | loop fusion | bytes 16777216 | tf_op jit(solution)/shard_map/split | solution.py:52
  317.6 53.3 %all_to_all.42 = bf16[16,1,2,2,8,32,128]{6,5,4,3,2,1,0:T(8,128)(2,1)} all-to-all(bf16[16,1,2,2,8,32,128]{6,5,4,3,2,1,0:T(8,128)(2,1)S(1)} %get-tuple-element.143), channel_id=1, replica_groups=mesh['member_0'=4,'member_1'=2,'mesh'=16] {'mesh'}, dimensions={0} | all-to-all | bytes 8388608 | tf_op jit(solution)/shard_map/all_to_all | solution.py:54
  371.0 6.7 %all-to-all-start.7 = ((bf16[16,1,2,2,8,32,128]{6,5,4,3,2,1,0:T(8,128)(2,1)}), bf16[16,1,2,2,8,32,128]{6,5,4,3,2,1,0:T(8,128)(2,1)}, u32[]{:S(2)}, u32[]{:S(2)}) async-start(bf16[16,1,2,2,8,32,128]{6,5,4,3,2,1,0:T(8,128)(2,1)} %get-tuple-element.144), calls=%async_computation.7 | async-start | bytes 8388608 | tf_op jit(solution)/shard_map/all_to_all | solution.py:54
  377.7 1.8 copy.93
  379.5 9.0 %copy.90 = bf16[16,1,2,2,8,32,128]{6,0,5,4,3,2,1:T(8,128)(2,1)} copy(bf16[16,1,2,2,8,32,128]{6,5,4,3,2,1,0:T(8,128)(2,1)} %all_to_all.42) | data formatting | bytes 8388608 | tf_op jit(solution)/shard_map/all_to_all | solution.py:54
  388.5 37.9 %all-to-all-done.7 = bf16[16,1,2,2,8,32,128]{6,5,4,3,2,1,0:T(8,128)(2,1)} async-done(((bf16[16,1,2,2,8,32,128]{6,5,4,3,2,1,0:T(8,128)(2,1)}), bf16[16,1,2,2,8,32,128]{6,5,4,3,2,1,0:T(8,128)(2,1)}, u32[]{:S(2)}, u32[]{:S(2)}) %all-to-all-start.7) | async-done | bytes 4194336 | tf_op jit(solution)/shard_map/all_to_all | solution.py:54
  426.4 7.2 %copy.91 = bf16[16,1,2,2,8,32,128]{6,0,5,4,3,2,1:T(8,128)(2,1)S(1)} copy(bf16[16,1,2,2,8,32,128]{6,5,4,3,2,1,0:T(8,128)(2,1)} %all-to-all-done.7) | data formatting | bytes 8388608 | tf_op jit(solution)/shard_map/all_to_all | solution.py:54
  433.6 2.9 fusion.20
  436.5 5.5 %reshape.91 = f32[2,2,512,512]{3,2,1,0:T(8,128)} reshape(f32[2,2,8,64,4,128]{5,4,3,2,1,0:T(4,128)} %fusion.20) | data formatting | bytes 8388608 | tf_op jit(solution)/shard_map/reshape | solution.py:182
  441.9 5.3 %copy.92 = f32[2,2,512,512]{2,3,0,1:T(8,128)} copy(f32[2,2,512,512]{3,2,1,0:T(8,128)} %reshape.91) | data formatting | bytes 8388608 | tf_op jit(solution)/shard_map/reshape | solution.py:182
  447.2 4.8 %slice_bitcast_fusion.5 = (f32[2,512,512]{2,1,0:T(8,128)}, f32[2,512,512]{2,1,0:T(8,128)}) fusion(f32[2,2,512,512]{3,2,0,1:T(8,128)} %bitcast.130), kind=kLoop, calls=%fused_computation.32 | loop fusion | bytes 8388608 | tf_op jit(solution)/shard_map/squeeze | solution.py:184
  (188 shorter events, 84.9 us)
Async XLA Ops:
  0.6 1.2 copy-start
  0.6 14.1 %copy-start.8 = (bf16[2,512,512]{2,1,0:T(8,128)(2,1)S(1)}, bf16[2,512,512]{2,1,0:T(8,128)(2,1)}, u32[]{:S(2)}) copy-start(bf16[2,512,512]{2,1,0:T(8,128)(2,1)} %param.22) | copy-start | bytes 3145732
  8.5 23.0 %all-to-all-start.3 = ((f32[4,2,2,96,64]{3,4,2,1,0:T(8,128)}), f32[4,2,2,96,64]{3,4,2,1,0:T(8,128)S(1)}, u32[]{:S(2)}, u32[]{:S(2)}) async-start(f32[4,2,2,96,64]{3,4,2,1,0:T(8,128)} %copy.81), calls=%async_computation.3 | async-start | bytes 1048576 | tf_op jit(solution)/shard_map/all_to_all | solution.py:32
  17.5 8.1 %copy-start.10 = (s32[16,16]{1,0:T(8,128)S(1)}, s32[16,16]{1,0:T(8,128)}, u32[]{:S(2)}) copy-start(s32[16,16]{1,0:T(8,128)} %param.24) | copy-start | bytes 3076
  17.5 8.1 %copy-start.11 = (s32[16,16]{1,0:T(8,128)S(1)}, s32[16,16]{1,0:T(8,128)}, u32[]{:S(2)}) copy-start(s32[16,16]{1,0:T(8,128)} %param.25) | copy-start | bytes 3076
  41.7 13.5 %all-to-all-start.5 = ((bf16[4,2,2,96,64]{3,4,2,1,0:T(8,128)(2,1)}), bf16[4,2,2,96,64]{3,4,2,1,0:T(8,128)(2,1)S(1)}, u32[]{:S(2)}, u32[]{:S(2)}) async-start(bf16[4,2,2,96,64]{3,4,2,1,0:T(8,128)(2,1)} %copy.84), calls=%async_computation.5 | async-start | bytes 524288 | tf_op jit(solution)/shard_map/all_to_all | solution.py:32
  55.1 62.6 %all-to-all-start = ((bf16[16,1,2,2,8,32,128]{6,5,4,3,2,1,0:T(8,128)(2,1)}), bf16[16,1,2,2,8,32,128]{6,5,4,3,2,1,0:T(8,128)(2,1)}, u32[]{:S(2)}, u32[]{:S(2)}) async-start(bf16[16,1,2,2,8,32,128]{6,5,4,3,2,1,0:T(8,128)(2,1)} %copy.76), calls=%async_computation | async-start | bytes 8388608 | tf_op jit(solution)/shard_map/all_to_all | solution.py:54
  68.7 68.3 %copy-start.7 = (bf16[2,512,512]{2,1,0:T(8,128)(2,1)S(1)}, bf16[2,512,512]{2,1,0:T(8,128)(2,1)}, u32[]{:S(2)}) copy-start(bf16[2,512,512]{2,1,0:T(8,128)(2,1)} %param.20) | copy-start | bytes 3145732
  68.7 69.6 %copy-start.9 = (bf16[512,96]{0,1:T(8,128)(2,1)S(1)}, bf16[512,96]{0,1:T(8,128)(2,1)}, u32[]{:S(2)}) copy-start(bf16[512,96]{0,1:T(8,128)(2,1)} %param.15) | copy-start | bytes 294916
  68.7 69.6 %copy-start.12 = (s32[1,512]{1,0:T(1,128)S(1)}, s32[1,512]{1,0:T(1,128)}, u32[]{:S(2)}) copy-start(s32[1,512]{1,0:T(1,128)} %param.19) | copy-start | bytes 6148
  117.7 68.7 %all-to-all-start.1 = ((bf16[16,1,2,2,8,32,128]{6,5,4,3,2,1,0:T(8,128)(2,1)}), bf16[16,1,2,2,8,32,128]{6,5,4,3,2,1,0:T(8,128)(2,1)}, u32[]{:S(2)}, u32[]{:S(2)}) async-start(bf16[16,1,2,2,8,32,128]{6,5,4,3,2,1,0:T(8,128)(2,1)} %copy.77), calls=%async_computation.1 | async-start | bytes 8388608 | tf_op jit(solution)/shard_map/all_to_all | solution.py:54
  140.9 55.2 %copy-start.6 = (f32[2,8,512]{2,1,0:T(8,128)S(1)}, f32[2,8,512]{2,1,0:T(8,128)}, u32[]{:S(2)}) copy-start(f32[2,8,512]{2,1,0:T(8,128)} %param.23) | copy-start | bytes 98308
  199.0 2.1 copy-start.2
  201.9 1.5 copy-start.3
  206.2 2.1 copy-start.2
  209.1 1.5 copy-start.3
  213.4 2.1 copy-start.2
  216.4 1.5 copy-start.3
  220.7 2.1 copy-start.2
  223.6 1.5 copy-start.3
  227.9 2.1 copy-start.2
  230.8 1.5 copy-start.3
  235.1 2.1 copy-start.2
  238.0 1.5 copy-start.3
  242.3 2.1 copy-start.2
  245.3 1.5 copy-start.3
  249.6 2.1 copy-start.2
  252.5 1.5 copy-start.3
  256.8 2.1 copy-start.2
  259.7 1.5 copy-start.3
  264.0 2.1 copy-start.2
  266.9 1.5 copy-start.3
  271.2 2.1 copy-start.2
  274.2 1.5 copy-start.3
  278.5 2.1 copy-start.2
  281.4 1.5 copy-start.3
  285.7 2.1 copy-start.2
  288.6 1.5 copy-start.3
  292.9 2.1 copy-start.2
  295.8 1.5 copy-start.3
  300.1 2.1 copy-start.2
  303.1 1.5 copy-start.3
  307.4 2.1 copy-start.2
  310.3 1.5 copy-start.3
  371.0 6.7 %copy-start.4 = (f32[2,8,64,512]{3,2,1,0:T(8,128)S(1)}, f32[2,8,64,512]{3,2,1,0:T(8,128)}, u32[]{:S(2)}) copy-start(f32[2,8,64,512]{3,2,1,0:T(8,128)} %get-tuple-element.46) | copy-start | bytes 6291460
  371.0 55.4 %all-to-all-start.7 = ((bf16[16,1,2,2,8,32,128]{6,5,4,3,2,1,0:T(8,128)(2,1)}), bf16[16,1,2,2,8,32,128]{6,5,4,3,2,1,0:T(8,128)(2,1)}, u32[]{:S(2)}, u32[]{:S(2)}) async-start(bf16[16,1,2,2,8,32,128]{6,5,4,3,2,1,0:T(8,128)(2,1)} %get-tuple-element.144), calls=%async_computation.7 | async-start | bytes 8388608 | tf_op jit(solution)/shard_map/all_to_all | solution.py:54
  426.4 7.2 %copy-start.5 = (bf16[16,1,2,2,8,32,128]{6,0,5,4,3,2,1:T(8,128)(2,1)S(1)}, bf16[16,1,2,2,8,32,128]{6,0,5,4,3,2,1:T(8,128)(2,1)}, u32[]{:S(2)}) copy-start(bf16[16,1,2,2,8,32,128]{6,0,5,4,3,2,1:T(8,128)(2,1)} %copy.90) | copy-start | bytes 12582916
  447.2 4.8 %copy-start.1 = (bf16[2,512,512]{2,1,0:T(8,128)(2,1)S(1)}, bf16[2,512,512]{2,1,0:T(8,128)(2,1)}, u32[]{:S(2)}) copy-start(bf16[2,512,512]{2,1,0:T(8,128)(2,1)} %param.14) | copy-start | bytes 3145732
where the time goes:
time: 455 us; the launch traced here: 452 us
  waiting for transfers between devices  132 us (29%)
  local copies, waits for them, and re-layouts  93.1 us (20%)
  matrix products  86.4 us (19%)
  blocking collectives  61.4 us (13%)
  starting transfers between devices  43.6 us (10%)
  other arithmetic  33.4 us (7%)
    all_to_all x3, waiting for transfers between devices, cut_exchange(): lax.all_to_all(section, axis, split_axis=0, concat_axis=0, tiled=True)  132 us
    all_to_all x1, blocking collectives, cut_exchange(): lax.all_to_all(section, axis, split_axis=0, concat_axis=0, tiled=True)  53.3 us
    all_to_all x3, starting transfers between devices, cut_exchange(): lax.all_to_all(section, axis, split_axis=0, concat_axis=0, tiled=True)  34.3 us
    dot_general x16, matrix products, one_block(): jnp.einsum('mhdr,mhdk->mhrk', grad_heads, value_tile, preferred_element_t...  20 us
    split x4, local copies, waits for them, and re-layouts, cut_exchange(): jnp.split(tiles, piece_ends(tiles.shape[cut], pieces), axis=cut)  19.7 us
    squeeze x16, local copies, waits for them, and re-layouts, shards(): lax.scan(one_block, jnp.zeros(split_shape, jnp.float32), incoming)  17.2 us
    all_to_all x2, local copies, waits for them, and re-layouts, cut_exchange(): lax.all_to_all(section, axis, split_axis=0, concat_axis=0, tiled=True)  16.2 us
    dot_general x16, matrix products, one_block(): jnp.einsum('mhrk,mhdr->mhdk', probability.astype(jnp.bfloat16), grad_head...  15.4 us
  transfers between devices with their start and end apart: 5, of which 3 were waited for; matrix products, arithmetic and copies ran while one was open for 10% of the time, Pallas kernels for 0%

commit v1 on v0

v1 whole, which is shorter than its diff:
```python
import math

import jax
import jax.numpy as jnp
from jax import lax
from jax.experimental import pallas as pl
from jax.experimental.pallas import tpu as pltpu
from jax.sharding import Mesh
from jax.sharding import PartitionSpec as P

KB = 128
SIDE = 4
MEMBER = ("y", "core")
LOSS_SCALE = 4096.0
FAIR_EPS = 0.05
NORM_EPS = 1e-06
LOG2E = math.log2(math.e)
F32 = jnp.float32
BF16 = jnp.bfloat16


def cut_along(x, dim, length):
    dims = x.shape
    tiles = x.reshape(*dims[:dim], length, dims[dim] // length, *dims[dim + 1 :])
    return jnp.moveaxis(tiles, dim, 0)


def in_order(tiles, dim):
    tiles = jnp.moveaxis(tiles, 0, dim)
    dims = tiles.shape
    return tiles.reshape(*dims[:dim], dims[dim] * dims[dim + 1], *dims[dim + 2 :])


def moved_by_axis(tiles, axes, sequence):
    inside = tiles.shape[1:]
    filled = tiles.reshape(*(lax.axis_size(a) for a in axes), *inside)
    for k in sequence:
        filled = lax.all_to_all(filled, axes[k], k, k, tiled=True)
    return filled.reshape(-1, *inside)


def exchange_by_axis(x, axes, sequence, split_dim, concat_dim):
    tiles = cut_along(x, split_dim, lax.axis_size(axes))
    return in_order(moved_by_axis(tiles, axes, sequence), concat_dim)


def unit_scaled_lines(differences):
    return differences / jnp.sqrt(
        jnp.sum(differences * differences, axis=-2, keepdims=True) + NORM_EPS
    )


def outlook_derivative(forecasts, truth_field, cell_surface_share):
    count = forecasts.shape[0]
    polarity_unit = unit_scaled_lines(forecasts - truth_field[None])
    differences = forecasts[:, None] - forecasts[None]
    couple_total = jnp.sum(unit_scaled_lines(differences), axis=1)
    weight = LOSS_SCALE * cell_surface_share[None, None, :]
    return weight * (
        polarity_unit / count - (1.0 - FAIR_EPS) / (count * (count - 1)) * couple_total
    )


def fetched(x, axis, distance):
    return lax.ppermute(x, axis, [(i, (i - distance) % SIDE) for i in range(SIDE)])


def delivered(x, axis, distance):
    return lax.ppermute(x, axis, [(i, (i + distance) % SIDE) for i in range(SIDE)])


def tile_kernel(table, *refs):
    kv = refs[0:4]
    queries = refs[4:8]
    grads = refs[8:12]
    stats = refs[12:16]
    decoder = refs[16]
    dkv = refs[17:21]
    dq = refs[21:25]
    q_stack, g_stack, stat_rows, dk_acc, dv_acc, dq_acc = refs[25:]
    rows = queries[0].shape[0]
    head_dim = 64
    score_scale = head_dim ** (-0.5)
    lane = lax.broadcasted_iota(jnp.int32, (rows, 2 * head_dim), 1)
    first = lane < head_dim
    nt = (((1,), (1,)), ((), ()))
    for t in range(SIDE):
        q = queries[t][...]
        g = lax.dot_general(grads[t][...], decoder[...], nt, preferred_element_type=F32)
        q = q.astype(F32)
        q_stack[t, :rows] = jnp.where(first, q, 0.0).astype(BF16)
        q_stack[t, rows:] = jnp.where(first, 0.0, q).astype(BF16)
        g_stack[t, :rows] = jnp.where(first, g, 0.0).astype(BF16)
        g_stack[t, rows:] = jnp.where(first, 0.0, g).astype(BF16)
        stat_rows[t] = stats[t][0]
    dk_acc[...] = jnp.zeros_like(dk_acc)
    dv_acc[...] = jnp.zeros_like(dv_acc)

    def one_query_block(t, carry):
        q = q_stack[t]
        g = g_stack[t]
        lse = stat_rows[t, 0:1, :] * LOG2E
        delta = stat_rows[t, 1:2, :]
        dq_acc[...] = jnp.zeros_like(dq_acc)
        for pair in ((0, 1), (2, 3)):
            starts = [pl.multiple_of(table[t * SIDE + a] * KB, KB) for a in pair]
            k = jnp.concatenate([kv[a][0, pl.ds(s, KB), :] for a, s in zip(pair, starts)], axis=0)
            v = jnp.concatenate([kv[a][1, pl.ds(s, KB), :] for a, s in zip(pair, starts)], axis=0)
            scores = lax.dot_general(k, q, nt, preferred_element_type=F32)
            p = jnp.exp2(scores * (score_scale * LOG2E) - lse)
            dp = lax.dot_general(v, g, nt, preferred_element_type=F32)
            ds = (p * (dp - delta)).astype(BF16)
            dv = jnp.dot(p.astype(BF16), g, preferred_element_type=F32)
            dk = jnp.dot(ds, q, preferred_element_type=F32)
            for n, (a, s) in enumerate(zip(pair, starts)):
                dv_acc[a, pl.ds(s, KB), :] += dv[n * KB : (n + 1) * KB]
                dk_acc[a, pl.ds(s, KB), :] += dk[n * KB : (n + 1) * KB]
            kt = k.T
            dq_acc[:head_dim] += jnp.dot(kt[:head_dim], ds[:, :rows], preferred_element_type=F32)
            dq_acc[head_dim:] += jnp.dot(kt[head_dim:], ds[:, rows:], preferred_element_type=F32)
        stat_dq = dq_acc[...].T * score_scale
        for n in range(SIDE):

            @pl.when(t == n)
            def _():
                dq[n][...] = stat_dq.astype(dq[n].dtype)

        return carry

    lax.fori_loop(0, SIDE, one_query_block, 0)
    for a in range(SIDE):
        dkv[a][0] = (dk_acc[a] * score_scale).astype(dkv[a].dtype)
        dkv[a][1] = dv_acc[a].astype(dkv[a].dtype)


def attention_tiles(table, kv, queries, grads, stats, decoder_matrix):
    _, rows, width = kv[0].shape
    channels = grads[0].shape[1]
    pairs = width // 128
    kv_spec = pl.BlockSpec((2, rows, 128), lambda h, tab: (0, 0, h))
    q_spec = pl.BlockSpec((rows, 128), lambda h, tab: (0, h))
    g_spec = pl.BlockSpec((rows, channels), lambda h, tab: (0, 0))
    s_spec = pl.BlockSpec((1, 2, 2 * rows), lambda h, tab: (h, 0, 0))
    d_spec = pl.BlockSpec((128, channels), lambda h, tab: (h, 0))
    kinds = [F32, BF16, BF16, BF16]
    out = pl.pallas_call(
        tile_kernel,
        out_shape=[jax.ShapeDtypeStruct((2, rows, width), d) for d in kinds]
        + [jax.ShapeDtypeStruct((rows, width), d) for d in kinds],
        grid_spec=pltpu.PrefetchScalarGridSpec(
            num_scalar_prefetch=1,
            grid=(pairs,),
            in_specs=[kv_spec] * 4 + [q_spec] * 4 + [g_spec] * 4 + [s_spec] * 4 + [d_spec],
            out_specs=[kv_spec] * 4 + [q_spec] * 4,
            scratch_shapes=[
                pltpu.VMEM((SIDE, 2 * rows, 128), BF16),
                pltpu.VMEM((SIDE, 2 * rows, 128), BF16),
                pltpu.VMEM((SIDE, 2, 2 * rows), F32),
                pltpu.VMEM((SIDE, rows, 128), F32),
                pltpu.VMEM((SIDE, rows, 128), F32),
                pltpu.VMEM((128, rows), F32),
            ],
        ),
        compiler_params=pltpu.CompilerParams(
            dimension_semantics=("arbitrary",), vmem_limit_bytes=48 * 1024 * 1024
        ),
        name="attention_tiles",
    )(table, *kv, *queries, *grads, *stats, decoder_matrix)
    return out[:4], out[4:]


def shards(
    hidden_embedding,
    decoder_matrix,
    baseline_field,
    truth_field,
    cell_surface_share,
    node_order,
    query,
    key_rows,
    value_rows,
    row_lse,
    kv_owner,
    kv_local,
):
    members, nodes, width = hidden_embedding.shape
    heads = row_lse.shape[1]
    pairs = heads // 2
    x_at = lax.axis_index("x")
    z_at = lax.axis_index("z")
    around = jnp.arange(SIDE, dtype=jnp.int32)
    axes = (("x", "z"), ("z", "x"))

    shard_ids = jnp.arange(kv_owner.shape[0], dtype=jnp.int32)
    where = jnp.sum(
        jnp.where(kv_owner[:, :, None] == shard_ids[None, None, :], kv_local[:, :, None], 0), axis=1
    )
    tables = []
    for key_axis, query_axis in axes:
        if key_axis == "x":
            s_ids = x_at * SIDE + (z_at + around) % SIDE
            o_ids = ((x_at + around) % SIDE) * SIDE + z_at
        else:
            s_ids = ((x_at + around) % SIDE) * SIDE + z_at
            o_ids = x_at * SIDE + (z_at + around) % SIDE
        tables.append(where[s_ids][:, o_ids].reshape(-1))

    kv, queries = [], []
    for m, (key_axis, query_axis) in enumerate(axes):
        own = jnp.stack([key_rows[m], value_rows[m]])
        kv.append([own] + [fetched(own, key_axis, d) for d in (1, 2, 3)])
        own = query[m]
        queries.append([own] + [fetched(own, query_axis, d) for d in (1, 2, 3)])

    forecast = baseline_field[None] + jnp.einsum(
        "mou,ut->mto", hidden_embedding, decoder_matrix, preferred_element_type=F32
    )
    groups = lax.axis_size(MEMBER)
    member_index = lax.axis_index(MEMBER)
    everyone = exchange_by_axis(forecast, MEMBER, (1, 0), 2, 0)
    span = nodes // groups
    offset = member_index * span
    observed = lax.dynamic_slice_in_dim(truth_field, offset, span, 1)
    area = lax.dynamic_slice_in_dim(cell_surface_share, offset, span, 0)
    derivative = outlook_derivative(everyone, observed, area).astype(BF16)
    grad_forecast = exchange_by_axis(derivative, MEMBER, (1, 0), 0, 2)

    permuter = (node_order[0][:, None] == jnp.arange(nodes, dtype=jnp.int32)[None, :]).astype(BF16)
    grad_rows = jnp.einsum(
        "mcg,tg->mtc", grad_forecast, permuter, preferred_element_type=F32
    ).astype(BF16)
    grad_latent = jnp.einsum(
        "wc,mtc->mwt", decoder_matrix, grad_rows, preferred_element_type=F32
    ).astype(BF16)
    saved = jnp.einsum("mgw,tg->mwt", hidden_embedding, permuter, preferred_element_type=F32).astype(
        BF16
    )
    split = (members, heads, width // heads, nodes)
    delta = jnp.sum(
        grad_latent.astype(F32).reshape(split) * saved.astype(F32).reshape(split), axis=2
    )
    stats = jnp.stack(
        [row_lse.reshape(members, pairs, 2 * nodes), delta.reshape(members, pairs, 2 * nodes)], axis=2
    )

    key_parts, query_parts = [], []
    for m, (key_axis, query_axis) in enumerate(axes):
        own_g, own_s = grad_rows[m], stats[m]
        grads = [own_g] + [fetched(own_g, query_axis, d) for d in (1, 2, 3)]
        stat = [own_s] + [fetched(own_s, query_axis, d) for d in (1, 2, 3)]
        dkv, dq = attention_tiles(tables[m], kv[m], queries[m], grads, stat, decoder_matrix)
        back = dkv[0]
        for d in (1, 2, 3):
            back = back + delivered(dkv[d], key_axis, d).astype(F32)
        key_parts.append(back)
        back = dq[0]
        for d in (1, 2, 3):
            back = back + delivered(dq[d], query_axis, d).astype(F32)
        query_parts.append(back)
    grad_query = jnp.stack(query_parts)
    grad_key = jnp.stack([k[0] for k in key_parts])
    grad_value = jnp.stack([k[1] for k in key_parts])
    return grad_query, grad_key, grad_value


def solution(mesh):
    finer = Mesh(mesh.devices.reshape(4, 2, SIDE, SIDE), ("y", "core", "x", "z"))
    plane = ("x", "z")
    in_specs = (
        P(MEMBER, plane, None),
        P(),
        P(None, plane),
        P(None, plane),
        P(plane),
        P(plane, None),
        P(MEMBER, plane, None),
        P(MEMBER, plane, None),
        P(MEMBER, plane, None),
        P(MEMBER, None, plane),
        P(),
        P(),
    )
    out_specs = (P(MEMBER, plane, None), P(MEMBER, plane, None), P(MEMBER, plane, None))
    return jax.shard_map(
        shards, mesh=finer, in_specs=in_specs, out_specs=out_specs, check_vma=False
    )
```

time: 455 us -> 363 us (0.80)
  matrix products: 86.4 us -> 3.31 us
  Pallas kernels: 0 us -> 62.8 us
  local copies, waits for them, and re-layouts: 93.1 us -> 30.4 us
  blocking collectives: 61.4 us -> 8.1 us
  starting transfers between devices: 43.6 us -> 77.8 us
  waiting for transfers between devices: 132 us -> 153 us
  other arithmetic: 33.4 us -> 24.6 us
    ppermute x0 -> x36, waiting for transfers between devices: none -> 151 us  [the longest x12 101 us: delivered(): lax.ppermute(x, axis, [(i, (i + distance) % SIDE) for i in range(SIDE)])]
    all_to_all x3 -> x0, waiting for transfers between devices: 132 us -> none  [cut_exchange(): lax.all_to_all(section, axis, split_axis=0, concat_axis=0, tiled=True)]
    dot_general x83 -> x2, matrix products: 84 us -> 0.94 us  [the longest x1 0.47 us: shards(): jnp.einsum('wc,mtc->mwt', decoder_matrix, grad_rows, preferred_element_ty...]
    ppermute x0 -> x36, starting transfers between devices: none -> 69.8 us  [the longest x24 45.5 us: fetched(): lax.ppermute(x, axis, [(i, (i - distance) % SIDE) for i in range(SIDE)])]
    pallas_call x0 -> x2, Pallas kernels: none -> 62.8 us  [attention_tiles(): pl.pallas_call(tile_kernel, out_shape=[jax.ShapeDtypeStruct((2, rows, wid...]
    all_to_all x1 -> x0, blocking collectives: 53.3 us -> none  [cut_exchange(): lax.all_to_all(section, axis, split_axis=0, concat_axis=0, tiled=True)]
    all_to_all x3 -> x0, starting transfers between devices: 34.3 us -> none  [cut_exchange(): lax.all_to_all(section, axis, split_axis=0, concat_axis=0, tiled=True)]
    squeeze x17 -> x2, local copies, waits for them, and re-layouts: 22 us -> 1.29 us  [the longest x1 1.27 us: shards(): own = query[m]]
  transfers between devices with their start and end apart: 5 -> 38, of which waited for: 3 -> 17; matrix products, arithmetic and copies ran while one was open for 10% -> 10% of each run, Pallas kernels for 0% -> 17%
where the time goes in v1:
time: 363 us; the launch traced here: 361 us
  waiting for transfers between devices  153 us (42%)
  starting transfers between devices  77.8 us (21%)
  Pallas kernels  62.8 us (17%)
  local copies, waits for them, and re-layouts  30.4 us (8%)
  other arithmetic  24.6 us (7%)
  blocking collectives  8.1 us (2%)
    ppermute x12, waiting for transfers between devices, delivered(): lax.ppermute(x, axis, [(i, (i + distance) % SIDE) for i in range(SIDE)])  101 us
    pallas_call x2, Pallas kernels, attention_tiles(): pl.pallas_call(tile_kernel, out_shape=[jax.ShapeDtypeStruct((2, rows, wid...  62.8 us
    ppermute x24, waiting for transfers between devices, fetched(): lax.ppermute(x, axis, [(i, (i - distance) % SIDE) for i in range(SIDE)])  49.1 us
    ppermute x24, starting transfers between devices, fetched(): lax.ppermute(x, axis, [(i, (i - distance) % SIDE) for i in range(SIDE)])  45.5 us
    ppermute x12, starting transfers between devices, delivered(): lax.ppermute(x, axis, [(i, (i + distance) % SIDE) for i in range(SIDE)])  24.3 us
    unnamed x73, local copies, waits for them, and re-layouts  17 us
    all_to_all x2, blocking collectives, moved_by_axis(): filled = lax.all_to_all(filled, axes[k], k, k, tiled=True)  8.1 us
    all_to_all x2, starting transfers between devices, moved_by_axis(): filled = lax.all_to_all(filled, axes[k], k, k, tiled=True)  7.94 us
  transfers between devices with their start and end apart: 38, of which 17 were waited for; matrix products, arithmetic and copies ran while one was open for 10% of the time, Pallas kernels for 17%

profile of v1, /device:TPU:2, one launch (start us, length us, event | category | flops | bytes accessed | tf_op | source)
XLA Modules:
  0.0 360.7 jit_solution(13250276598489824299)
XLA Ops:
  0.6 1.2 copy-done
  1.9 1.4 fusion.2
  3.5 4.2 %all_to_all.20 = f32[4,2,2,96,64]{3,4,2,0,1:T(8,128)S(1)} all-to-all(f32[4,2,2,96,64]{3,4,2,0,1:T(8,128)S(1)} %copy.96), channel_id=1, replica_groups=mesh['y'=4,'core'=2,'x'=4,'z'=4] {'core'}, dimensions={1} | all-to-all | bytes 786432 | tf_op jit(solution)/shard_map/all_to_all | solution.py:38
  8.5 4.5 %all-to-all-start.1 = ((f32[4,2,2,96,64]{3,4,2,1,0:T(8,128)}), f32[4,2,2,96,64]{3,4,2,1,0:T(8,128)}, u32[]{:S(2)}, u32[]{:S(2)}) async-start(f32[4,2,2,96,64]{3,4,2,1,0:T(8,128)} %copy.97), calls=%async_computation.1 | async-start | bytes 1048576 | tf_op jit(solution)/shard_map/all_to_all | solution.py:38
  13.0 1.3 slice_bitcast_fusion.1
  14.3 2.0 collective-permute-start.5
  16.3 3.6 collective-permute-start.4
  21.6 1.3 all-to-all-done.1
  22.9 1.3 multiply_reduce_fusion
  24.2 3.4 fusion.1
  27.7 3.9 %fusion = f32[16,96,64]{1,2,0:T(8,128)S(1)} fusion(f32[16,16,64]{2,1,0:T(8,128)S(1)} %add_sqrt_fusion, f32[16,96,64]{1,2,0:T(8,128)} %bitcast.11), kind=kLoop, calls=%fused_computation.6 | loop fusion | flops 4620288 | bytes 851968 | tf_op jit(solution)/shard_map/reduce_sum | solution.py:57
  31.7 1.3 multiply_convert_fusion
  33.0 3.9 %all_to_all.21 = bf16[4,2,2,96,64]{3,4,2,0,1:T(8,128)(2,1)S(1)} all-to-all(bf16[4,2,2,96,64]{3,4,2,0,1:T(8,128)(2,1)S(1)} %copy.99), channel_id=1, replica_groups=mesh['y'=4,'core'=2,'x'=4,'z'=4] {'core'}, dimensions={1} | all-to-all | bytes 393216 | tf_op jit(solution)/shard_map/all_to_all | solution.py:38
  37.6 3.5 all-to-all-start.3
  41.1 2.6 fusion.25
  43.7 1.1 pad_maximum_fusion.4.refs_0_
  44.8 1.9 collective-permute-start.17
  49.9 1.0 bitcast_reduce_fusion
  51.0 2.0 collective-permute-start.11
  53.0 3.6 collective-permute-start.10
  56.6 16.6 %collective-permute-done.11.refs_15_ = f32[4,2,1024]{2,1,0:T(2,128)S(1)} collective-permute-done((f32[4,2,1024]{2,1,0:T(2,128)S(1)}, f32[4,2,1024]{2,1,0:T(2,128)S(1)}, u32[]{:S(2)}, u32[]{:S(2)}) %collective-permute-start.11) | collective-permute-done | bytes 32800 | tf_op jit(solution)/shard_map/ppermute | solution.py:65
  73.8 2.1 collective-permute-start.9
  77.1 1.5 collective-permute-start.26
  79.2 1.2 collective-permute-start.25
  81.6 2.0 collective-permute-start.24
  84.6 2.4 collective-permute-start.3
  87.0 1.6 collective-permute-start.20
  88.6 1.0 collective-permute-start.19
  89.7 2.1 collective-permute-start.18
  91.8 1.1 copy.103
  92.9 2.9 collective-permute-done.3.refs_5_
  96.5 9.3 %collective-permute-done.20.refs_7_ = bf16[512,512]{1,0:T(8,128)(2,1)} collective-permute-done((bf16[512,512]{1,0:T(8,128)(2,1)S(1)}, bf16[512,512]{1,0:T(8,128)(2,1)}, u32[]{:S(2)}, u32[]{:S(2)}) %collective-permute-start.20) | collective-permute-done | bytes 524320 | tf_op jit(solution)/shard_map/ppermute | solution.py:65
  105.7 2.7 collective-permute-start.23
  109.4 2.0 collective-permute-done.18.refs_5_
  111.8 2.9 collective-permute-start.22
  114.7 1.9 collective-permute-start.21
  116.6 2.3 pad_maximum_fusion.3.refs_0_
  119.7 1.3 collective-permute-start.2
  121.2 3.5 collective-permute-start.1
  125.2 1.0 copy.106.refs_16_
  129.0 1.0 collective-permute-start.7
  130.0 16.5 %collective-permute-done.15.refs_1_ = bf16[2,512,512]{2,1,0:T(8,128)(2,1)} collective-permute-done((bf16[2,512,512]{2,1,0:T(8,128)(2,1)}, bf16[2,512,512]{2,1,0:T(8,128)(2,1)}, u32[]{:S(2)}, u32[]{:S(2)}) %collective-permute-start.15) | collective-permute-done | bytes 1048608 | tf_op jit(solution)/shard_map/ppermute | solution.py:65
  146.5 2.7 collective-permute-start.6
  149.1 1.3 pad_clamp_fusion.1
  150.4 1.4 gather_fusion.3
  155.9 31.2 %attention_tiles.3 = (f32[2,512,512]{2,1,0:T(8,128)}, bf16[2,512,512]{2,1,0:T(8,128)(2,1)S(1)}, bf16[2,512,512]{2,1,0:T(8,128)(2,1)}, bf16[2,512,512]{2,1,0:T(8,...) custom-call(s32[16]{0:T(128)S(1)} %reshape.170.table, ...), custom_call_target="tpu_custom_call" | custom-call | tf_op jit(solution)/shard_map/attention_tiles/pallas_call | solution.py:146
  187.1 1.0 copy-done.20
  188.9 8.6 %collective-permute-start.27 = (bf16[512,512]{1,0:T(8,128)(2,1)}, bf16[512,512]{1,0:T(8,128)(2,1)S(1)}, u32[]{:S(2)}, u32[]{:S(2)}) collective-permute-start(bf16[512,512]{1,0:T(8,128)(2,1)} %get-tuple-element.24), channel_id=1, source_target_pairs={{0,4},{4,8},{8,12},{12,0},{1,5},{5,9},{9,13},{13,1},{2,6},{6,10},{... | collective-permute-start | bytes 1572872 | tf_op jit(solution)/shard_map/ppermute | solution.py:69
  197.5 3.8 %collective-permute-start.28 = (bf16[512,512]{1,0:T(8,128)(2,1)}, bf16[512,512]{1,0:T(8,128)(2,1)}, u32[]{:S(2)}, u32[]{:S(2)}) collective-permute-start(bf16[512,512]{1,0:T(8,128)(2,1)} %get-tuple-element.25), channel_id=1, source_target_pairs={{0,8},{4,12},{8,0},{12,4},{1,9},{5,13},{9,1},{13,5},{2,10},{6,14},... | collective-permute-start | bytes 1572872 | tf_op jit(solution)/shard_map/ppermute | solution.py:69
  206.1 31.6 %attention_tiles.2 = (f32[2,512,512]{2,1,0:T(8,128)}, bf16[2,512,512]{2,1,0:T(8,128)(2,1)S(1)}, bf16[2,512,512]{2,1,0:T(8,128)(2,1)}, bf16[2,512,512]{2,1,0:T(8,...) custom-call(s32[16]{0:T(128)S(1)} %reshape.165.table, ...), custom_call_target="tpu_custom_call" | custom-call | tf_op jit(solution)/shard_map/attention_tiles/pallas_call | solution.py:146
  237.8 1.8 collective-permute-start.33
  240.4 2.9 collective-permute-start.34
  243.7 1.1 collective-permute-start.13
  244.9 9.0 %collective-permute-done.12 = bf16[512,512]{1,0:T(8,128)(2,1)S(1)} collective-permute-done((bf16[512,512]{1,0:T(8,128)(2,1)S(1)}, bf16[512,512]{1,0:T(8,128)(2,1)S(1)}, u32[]{:S(2)}, u32[]{:S(2)}) %collective-permute-start.12) | collective-permute-done | bytes 524320 | tf_op jit(solution)/shard_map/ppermute | solution.py:69
  253.9 1.5 add_bitcast_fusion
  255.3 51.9 %collective-permute-done.13 = bf16[512,512]{1,0:T(8,128)(2,1)S(1)} collective-permute-done((bf16[512,512]{1,0:T(8,128)(2,1)S(1)}, bf16[512,512]{1,0:T(8,128)(2,1)S(1)}, u32[]{:S(2)}, u32[]{:S(2)}) %collective-permute-start.13) | collective-permute-done | bytes 524320 | tf_op jit(solution)/shard_map/ppermute | solution.py:69
  307.2 1.7 collective-permute-start.30
  310.7 2.9 collective-permute-start.32
  313.9 1.5 pad_maximum_fusion
  317.1 16.2 %collective-permute-done.30 = bf16[2,512,512]{2,1,0:T(8,128)(2,1)S(1)} collective-permute-done((bf16[2,512,512]{2,1,0:T(8,128)(2,1)S(1)}, bf16[2,512,512]{2,1,0:T(8,128)(2,1)S(1)}, u32[]{:S(2)}, u32[]{:S(2)}) %collective-permute-start.30) | collective-permute-done | bytes 1048608 | tf_op jit(solution)/shard_map/ppermute | solution.py:69
  333.3 4.1 %collective-permute-done.31 = bf16[2,512,512]{2,1,0:T(8,128)(2,1)S(1)} collective-permute-done((bf16[2,512,512]{2,1,0:T(8,128)(2,1)S(1)}, bf16[2,512,512]{2,1,0:T(8,128)(2,1)S(1)}, u32[]{:S(2)}, u32[]{:S(2)}) %collective-permute-start.31) | collective-permute-done | bytes 1048608 | tf_op jit(solution)/shard_map/ppermute | solution.py:69
  337.4 19.5 %collective-permute-done.32 = bf16[2,512,512]{2,1,0:T(8,128)(2,1)S(1)} collective-permute-done((bf16[2,512,512]{2,1,0:T(8,128)(2,1)S(1)}, bf16[2,512,512]{2,1,0:T(8,128)(2,1)S(1)}, u32[]{:S(2)}, u32[]{:S(2)}) %collective-permute-start.32) | collective-permute-done | bytes 1048608 | tf_op jit(solution)/shard_map/ppermute | solution.py:69
  357.7 1.5 pad_maximum_fusion.2
  359.2 1.5 pad_maximum_fusion.1
  (141 shorter events, 33.3 us)
Async XLA Ops:
  0.6 1.2 copy-start
  8.5 14.3 %all-to-all-start.1 = ((f32[4,2,2,96,64]{3,4,2,1,0:T(8,128)}), f32[4,2,2,96,64]{3,4,2,1,0:T(8,128)}, u32[]{:S(2)}, u32[]{:S(2)}) async-start(f32[4,2,2,96,64]{3,4,2,1,0:T(8,128)} %copy.97), calls=%async_computation.1 | async-start | bytes 1048576 | tf_op jit(solution)/shard_map/all_to_all | solution.py:38
  14.3 74.4 %collective-permute-start.5 = (bf16[512,512]{1,0:T(8,128)(2,1)S(1)}, bf16[512,512]{1,0:T(8,128)(2,1)S(1)}, u32[]{:S(2)}, u32[]{:S(2)}) collective-permute-start(bf16[512,512]{1,0:T(8,128)(2,1)S(1)} %get-tuple-element.39.refs_4_), channel_id=1, source_target_pairs={{0,1},{1,2},{2,3},{3,0},{4,5},{5,6},{6,7},{7,4},{8,9},{9,10},{10,1... | collective-permute-start | bytes 1572872 | tf_op jit(solution)/shard_map/ppermute | solution.py:65
  16.3 73.4 %collective-permute-start.4 = (bf16[512,512]{1,0:T(8,128)(2,1)S(1)}, bf16[512,512]{1,0:T(8,128)(2,1)S(1)}, u32[]{:S(2)}, u32[]{:S(2)}) collective-permute-start(bf16[512,512]{1,0:T(8,128)(2,1)S(1)} %get-tuple-element.39.refs_4_), channel_id=1, source_target_pairs={{0,2},{1,3},{2,0},{3,1},{4,6},{5,7},{6,4},{7,5},{8,10},{9,11},{10,... | collective-permute-start | bytes 1572872 | tf_op jit(solution)/shard_map/ppermute | solution.py:65
  37.6 10.6 %all-to-all-start.3 = ((bf16[4,2,2,96,64]{3,4,2,1,0:T(8,128)(2,1)}), bf16[4,2,2,96,64]{3,4,2,1,0:T(8,128)(2,1)S(1)}, u32[]{:S(2)}, u32[]{:S(2)}) async-start(bf16[4,2,2,96,64]{3,4,2,1,0:T(8,128)(2,1)} %copy.100), calls=%async_computation.3 | async-start | bytes 524288 | tf_op jit(solution)/shard_map/all_to_all | solution.py:38
  43.7 4.6 %copy-start.35 = (s32[1,512]{1,0:T(1,128)S(1)}, s32[1,512]{1,0:T(1,128)}, u32[]{:S(2)}) copy-start(s32[1,512]{1,0:T(1,128)} %param.17) | copy-start | bytes 6148
  43.7 5.7 %copy-start.27 = (bf16[512,96]{0,1:T(8,128)(2,1)S(1)}, bf16[512,96]{0,1:T(8,128)(2,1)}, u32[]{:S(2)}) copy-start(bf16[512,96]{0,1:T(8,128)(2,1)} %param.13) | copy-start | bytes 294916
  44.8 79.9 %collective-permute-start.17 = (bf16[2,512,512]{2,1,0:T(8,128)(2,1)}, bf16[2,512,512]{2,1,0:T(8,128)(2,1)}, u32[]{:S(2)}, u32[]{:S(2)}) collective-permute-start(bf16[2,512,512]{2,1,0:T(8,128)(2,1)} %pad_maximum_fusion.4.refs_0_), channel_id=1, source_target_pairs={{0,1},{1,2},{2,3},{3,0},{4,5},{5,6},{6,7},{7,4},{8,9},{9,10},{10,1... | collective-permute-start | bytes 3145736 | tf_op jit(solution)/shard_map/ppermute | solution.py:65
  51.0 22.1 %collective-permute-start.11 = (f32[4,2,1024]{2,1,0:T(2,128)S(1)}, f32[4,2,1024]{2,1,0:T(2,128)S(1)}, u32[]{:S(2)}, u32[]{:S(2)}) collective-permute-start(f32[4,2,1024]{2,1,0:T(2,128)S(1)} %get-tuple-element.47.refs_12_), channel_id=1, source_target_pairs={{0,1},{1,2},{2,3},{3,0},{4,5},{5,6},{6,7},{7,4},{8,9},{9,10},{10,1... | collective-permute-start | bytes 98312 | tf_op jit(solution)/shard_map/ppermute | solution.py:65
  53.0 23.5 %collective-permute-start.10 = (f32[4,2,1024]{2,1,0:T(2,128)S(1)}, f32[4,2,1024]{2,1,0:T(2,128)S(1)}, u32[]{:S(2)}, u32[]{:S(2)}) collective-permute-start(f32[4,2,1024]{2,1,0:T(2,128)S(1)} %get-tuple-element.47.refs_12_), channel_id=1, source_target_pairs={{0,2},{1,3},{2,0},{3,1},{4,6},{5,7},{6,4},{7,5},{8,10},{9,11},{10,... | collective-permute-start | bytes 98312 | tf_op jit(solution)/shard_map/ppermute | solution.py:65
  73.8 4.8 %collective-permute-start.9 = (f32[4,2,1024]{2,1,0:T(2,128)S(1)}, f32[4,2,1024]{2,1,0:T(2,128)S(1)}, u32[]{:S(2)}, u32[]{:S(2)}) collective-permute-start(f32[4,2,1024]{2,1,0:T(2,128)S(1)} %get-tuple-element.47.refs_12_), channel_id=1, source_target_pairs={{0,3},{1,0},{2,1},{3,2},{4,7},{5,4},{6,5},{7,6},{8,11},{9,8},{10,9... | collective-permute-start | bytes 98312 | tf_op jit(solution)/shard_map/ppermute | solution.py:65
  77.1 3.9 %collective-permute-start.26 = (f32[4,2,1024]{2,1,0:T(2,128)S(1)}, f32[4,2,1024]{2,1,0:T(2,128)S(1)}, u32[]{:S(2)}, u32[]{:S(2)}) collective-permute-start(f32[4,2,1024]{2,1,0:T(2,128)S(1)} %get-tuple-element.48.refs_12_), channel_id=1, source_target_pairs={{0,4},{4,8},{8,12},{12,0},{1,5},{5,9},{9,13},{13,1},{2,6},{6,10},{... | collective-permute-start | bytes 98312 | tf_op jit(solution)/shard_map/ppermute | solution.py:65
  79.2 5.4 %collective-permute-start.25 = (f32[4,2,1024]{2,1,0:T(2,128)S(1)}, f32[4,2,1024]{2,1,0:T(2,128)S(1)}, u32[]{:S(2)}, u32[]{:S(2)}) collective-permute-start(f32[4,2,1024]{2,1,0:T(2,128)S(1)} %get-tuple-element.48.refs_12_), channel_id=1, source_target_pairs={{0,8},{4,12},{8,0},{12,4},{1,9},{5,13},{9,1},{13,5},{2,10},{6,14},... | collective-permute-start | bytes 98312 | tf_op jit(solution)/shard_map/ppermute | solution.py:65
  81.6 5.4 %collective-permute-start.24 = (f32[4,2,1024]{2,1,0:T(2,128)S(1)}, f32[4,2,1024]{2,1,0:T(2,128)S(1)}, u32[]{:S(2)}, u32[]{:S(2)}) collective-permute-start(f32[4,2,1024]{2,1,0:T(2,128)S(1)} %get-tuple-element.48.refs_12_), channel_id=1, source_target_pairs={{0,12},{4,0},{8,4},{12,8},{1,13},{5,1},{9,5},{13,9},{2,14},{6,2},{... | collective-permute-start | bytes 98312 | tf_op jit(solution)/shard_map/ppermute | solution.py:65
  84.6 11.2 %copy-start.16 = (f32[4,2,1024]{2,1,0:T(2,128)}, f32[4,2,1024]{2,1,0:T(2,128)S(1)}, u32[]{:S(2)}) copy-start(f32[4,2,1024]{2,1,0:T(2,128)S(1)} %collective-permute-done.25.refs_14_) | copy-start | bytes 98308
  84.6 11.2 %collective-permute-start.3 = (bf16[512,512]{1,0:T(8,128)(2,1)S(1)}, bf16[512,512]{1,0:T(8,128)(2,1)S(1)}, u32[]{:S(2)}, u32[]{:S(2)}) collective-permute-start(bf16[512,512]{1,0:T(8,128)(2,1)S(1)} %get-tuple-element.39.refs_4_), channel_id=1, source_target_pairs={{0,3},{1,0},{2,1},{3,2},{4,7},{5,4},{6,5},{7,6},{8,11},{9,8},{10,9... | collective-permute-start | bytes 1572872 | tf_op jit(solution)/shard_map/ppermute | solution.py:65
  87.0 8.8 %copy-start.18 = (f32[4,2,1024]{2,1,0:T(2,128)}, f32[4,2,1024]{2,1,0:T(2,128)S(1)}, u32[]{:S(2)}) copy-start(f32[4,2,1024]{2,1,0:T(2,128)S(1)} %collective-permute-done.24.refs_13_) | copy-start | bytes 98308
  87.0 18.7 %collective-permute-start.20 = (bf16[512,512]{1,0:T(8,128)(2,1)S(1)}, bf16[512,512]{1,0:T(8,128)(2,1)}, u32[]{:S(2)}, u32[]{:S(2)}) collective-permute-start(bf16[512,512]{1,0:T(8,128)(2,1)S(1)} %get-tuple-element.40.refs_4_), channel_id=1, source_target_pairs={{0,4},{4,8},{8,12},{12,0},{1,5},{5,9},{9,13},{13,1},{2,6},{6,10},{... | collective-permute-start | bytes 1572872 | tf_op jit(solution)/shard_map/ppermute | solution.py:65
  88.6 19.8 %collective-permute-start.19 = (bf16[512,512]{1,0:T(8,128)(2,1)S(1)}, bf16[512,512]{1,0:T(8,128)(2,1)}, u32[]{:S(2)}, u32[]{:S(2)}) collective-permute-start(bf16[512,512]{1,0:T(8,128)(2,1)S(1)} %get-tuple-element.40.refs_4_), channel_id=1, source_target_pairs={{0,8},{4,12},{8,0},{12,4},{1,9},{5,13},{9,1},{13,5},{2,10},{6,14},... | collective-permute-start | bytes 1572872 | tf_op jit(solution)/shard_map/ppermute | solution.py:65
  89.7 21.7 %collective-permute-start.18 = (bf16[512,512]{1,0:T(8,128)(2,1)S(1)}, bf16[512,512]{1,0:T(8,128)(2,1)}, u32[]{:S(2)}, u32[]{:S(2)}) collective-permute-start(bf16[512,512]{1,0:T(8,128)(2,1)S(1)} %get-tuple-element.40.refs_4_), channel_id=1, source_target_pairs={{0,12},{4,0},{8,4},{12,8},{1,13},{5,1},{9,5},{13,9},{2,14},{6,2},{... | collective-permute-start | bytes 1572872 | tf_op jit(solution)/shard_map/ppermute | solution.py:65
  95.8 15.9 %collective-permute-start.8 = (bf16[512,96]{1,0:T(8,128)(2,1)S(1)}, bf16[512,96]{1,0:T(8,128)(2,1)S(1)}, u32[]{:S(2)}, u32[]{:S(2)}) collective-permute-start(bf16[512,96]{1,0:T(8,128)(2,1)S(1)} %get-tuple-element.45.refs_8_), channel_id=1, source_target_pairs={{0,1},{1,2},{2,3},{3,0},{4,5},{5,6},{6,7},{7,4},{8,9},{9,10},{10,1... | collective-permute-start | bytes 294920 | tf_op jit(solution)/shard_map/ppermute | solution.py:65
  105.7 9.0 %collective-permute-start.23 = (bf16[512,96]{1,0:T(8,128)(2,1)S(1)}, bf16[512,96]{1,0:T(8,128)(2,1)S(1)}, u32[]{:S(2)}, u32[]{:S(2)}) collective-permute-start(bf16[512,96]{1,0:T(8,128)(2,1)S(1)} %get-tuple-element.46.refs_8_), channel_id=1, source_target_pairs={{0,4},{4,8},{8,12},{12,0},{1,5},{5,9},{9,13},{13,1},{2,6},{6,10},{... | collective-permute-start | bytes 294920 | tf_op jit(solution)/shard_map/ppermute | solution.py:65
  108.4 20.5 %collective-permute-start.16 = (bf16[2,512,512]{2,1,0:T(8,128)(2,1)}, bf16[2,512,512]{2,1,0:T(8,128)(2,1)}, u32[]{:S(2)}, u32[]{:S(2)}) collective-permute-start(bf16[2,512,512]{2,1,0:T(8,128)(2,1)} %pad_maximum_fusion.4.refs_0_), channel_id=1, source_target_pairs={{0,2},{1,3},{2,0},{3,1},{4,6},{5,7},{6,4},{7,5},{8,10},{9,11},{10,... | collective-permute-start | bytes 3145736 | tf_op jit(solution)/shard_map/ppermute | solution.py:65
  111.3 35.1 %collective-permute-start.15 = (bf16[2,512,512]{2,1,0:T(8,128)(2,1)}, bf16[2,512,512]{2,1,0:T(8,128)(2,1)}, u32[]{:S(2)}, u32[]{:S(2)}) collective-permute-start(bf16[2,512,512]{2,1,0:T(8,128)(2,1)} %pad_maximum_fusion.4.refs_0_), channel_id=1, source_target_pairs={{0,3},{1,0},{2,1},{3,2},{4,7},{5,4},{6,5},{7,6},{8,11},{9,8},{10,9... | collective-permute-start | bytes 3145736 | tf_op jit(solution)/shard_map/ppermute | solution.py:65
  111.8 7.9 %collective-permute-start.22 = (bf16[512,96]{1,0:T(8,128)(2,1)S(1)}, bf16[512,96]{1,0:T(8,128)(2,1)S(1)}, u32[]{:S(2)}, u32[]{:S(2)}) collective-permute-start(bf16[512,96]{1,0:T(8,128)(2,1)S(1)} %get-tuple-element.46.refs_8_), channel_id=1, source_target_pairs={{0,8},{4,12},{8,0},{12,4},{1,9},{5,13},{9,1},{13,5},{2,10},{6,14},... | collective-permute-start | bytes 294920 | tf_op jit(solution)/shard_map/ppermute | solution.py:65
  114.7 6.6 %collective-permute-start.21 = (bf16[512,96]{1,0:T(8,128)(2,1)S(1)}, bf16[512,96]{1,0:T(8,128)(2,1)S(1)}, u32[]{:S(2)}, u32[]{:S(2)}) collective-permute-start(bf16[512,96]{1,0:T(8,128)(2,1)S(1)} %get-tuple-element.46.refs_8_), channel_id=1, source_target_pairs={{0,12},{4,0},{8,4},{12,8},{1,13},{5,1},{9,5},{13,9},{2,14},{6,2},{... | collective-permute-start | bytes 294920 | tf_op jit(solution)/shard_map/ppermute | solution.py:65
  119.7 83.3 %collective-permute-start.2 = (bf16[2,512,512]{2,1,0:T(8,128)(2,1)}, bf16[2,512,512]{2,1,0:T(8,128)(2,1)}, u32[]{:S(2)}, u32[]{:S(2)}) collective-permute-start(bf16[2,512,512]{2,1,0:T(8,128)(2,1)} %pad_maximum_fusion.3.refs_0_), channel_id=1, source_target_pairs={{0,4},{4,8},{8,12},{12,0},{1,5},{5,9},{9,13},{13,1},{2,6},{6,10},{... | collective-permute-start | bytes 3145736 | tf_op jit(solution)/shard_map/ppermute | solution.py:65
  121.2 7.7 %copy-start.2 = (bf16[512,96]{1,0:T(8,128)(2,1)}, bf16[512,96]{1,0:T(8,128)(2,1)S(1)}, u32[]{:S(2)}) copy-start(bf16[512,96]{1,0:T(8,128)(2,1)S(1)} %collective-permute-done.21.refs_9_) | copy-start | bytes 294916
  121.2 81.8 %collective-permute-start.1 = (bf16[2,512,512]{2,1,0:T(8,128)(2,1)}, bf16[2,512,512]{2,1,0:T(8,128)(2,1)}, u32[]{:S(2)}, u32[]{:S(2)}) collective-permute-start(bf16[2,512,512]{2,1,0:T(8,128)(2,1)} %pad_maximum_fusion.3.refs_0_), channel_id=1, source_target_pairs={{0,8},{4,12},{8,0},{12,4},{1,9},{5,13},{9,1},{13,5},{2,10},{6,14},... | collective-permute-start | bytes 3145736 | tf_op jit(solution)/shard_map/ppermute | solution.py:65
  124.7 78.3 %collective-permute-start = (bf16[2,512,512]{2,1,0:T(8,128)(2,1)}, bf16[2,512,512]{2,1,0:T(8,128)(2,1)}, u32[]{:S(2)}, u32[]{:S(2)}) collective-permute-start(bf16[2,512,512]{2,1,0:T(8,128)(2,1)} %pad_maximum_fusion.3.refs_0_), channel_id=1, source_target_pairs={{0,12},{4,0},{8,4},{12,8},{1,13},{5,1},{9,5},{13,9},{2,14},{6,2},{... | collective-permute-start | bytes 3145736 | tf_op jit(solution)/shard_map/ppermute | solution.py:65
  126.8 25.0 %copy-start.30 = (s32[1024]{0:T(1024)}, s32[1024]{0:T(1024)S(1)}, u32[]{:S(2)}) copy-start(s32[1024]{0:T(1024)S(1)} %pad_clamp_fusion) | copy-start | bytes 12292
  129.0 60.0 %collective-permute-start.7 = (bf16[512,96]{1,0:T(8,128)(2,1)S(1)}, bf16[512,96]{1,0:T(8,128)(2,1)S(1)}, u32[]{:S(2)}, u32[]{:S(2)}) collective-permute-start(bf16[512,96]{1,0:T(8,128)(2,1)S(1)} %get-tuple-element.45.refs_8_), channel_id=1, source_target_pairs={{0,2},{1,3},{2,0},{3,1},{4,6},{5,7},{6,4},{7,5},{8,10},{9,11},{10,... | collective-permute-start | bytes 294920 | tf_op jit(solution)/shard_map/ppermute | solution.py:65
  146.5 51.1 %collective-permute-start.6 = (bf16[512,96]{1,0:T(8,128)(2,1)S(1)}, bf16[512,96]{1,0:T(8,128)(2,1)}, u32[]{:S(2)}, u32[]{:S(2)}) collective-permute-start(bf16[512,96]{1,0:T(8,128)(2,1)S(1)} %get-tuple-element.45.refs_8_), channel_id=1, source_target_pairs={{0,3},{1,0},{2,1},{3,2},{4,7},{5,4},{6,5},{7,6},{8,11},{9,8},{10,9... | collective-permute-start | bytes 294920 | tf_op jit(solution)/shard_map/ppermute | solution.py:65
  152.0 0.9 copy-start.3
  152.9 0.8 copy-start.7
  153.6 0.8 copy-start.15
  154.4 0.8 copy-start.17
  155.2 0.8 copy-start.19
  187.1 1.0 copy-start.20
  188.1 0.8 copy-start.22
  188.9 50.7 %collective-permute-start.27 = (bf16[512,512]{1,0:T(8,128)(2,1)}, bf16[512,512]{1,0:T(8,128)(2,1)S(1)}, u32[]{:S(2)}, u32[]{:S(2)}) collective-permute-start(bf16[512,512]{1,0:T(8,128)(2,1)} %get-tuple-element.24), channel_id=1, source_target_pairs={{0,4},{4,8},{8,12},{12,0},{1,5},{5,9},{9,13},{13,1},{2,6},{6,10},{... | collective-permute-start | bytes 1572872 | tf_op jit(solution)/shard_map/ppermute | solution.py:69
  197.5 45.8 %collective-permute-start.28 = (bf16[512,512]{1,0:T(8,128)(2,1)}, bf16[512,512]{1,0:T(8,128)(2,1)}, u32[]{:S(2)}, u32[]{:S(2)}) collective-permute-start(bf16[512,512]{1,0:T(8,128)(2,1)} %get-tuple-element.25), channel_id=1, source_target_pairs={{0,8},{4,12},{8,0},{12,4},{1,9},{5,13},{9,1},{13,5},{2,10},{6,14},... | collective-permute-start | bytes 1572872 | tf_op jit(solution)/shard_map/ppermute | solution.py:69
  203.0 40.7 %collective-permute-start.29 = (bf16[512,512]{1,0:T(8,128)(2,1)}, bf16[512,512]{1,0:T(8,128)(2,1)S(1)}, u32[]{:S(2)}, u32[]{:S(2)}) collective-permute-start(bf16[512,512]{1,0:T(8,128)(2,1)} %copy-done.22), channel_id=1, source_target_pairs={{0,12},{4,0},{8,4},{12,8},{1,13},{5,1},{9,5},{13,9},{2,14},{6,2},{... | collective-permute-start | bytes 1572872 | tf_op jit(solution)/shard_map/ppermute | solution.py:69
  203.0 0.8 copy-start.5
  206.1 31.7 %copy-start.21 = (bf16[2,512,512]{2,1,0:T(8,128)(2,1)S(1)}, bf16[2,512,512]{2,1,0:T(8,128)(2,1)}, u32[]{:S(2)}) copy-start(bf16[2,512,512]{2,1,0:T(8,128)(2,1)} %copy-done.20) | copy-start | bytes 3145732
  206.1 34.4 %copy-start.32 = (bf16[2,512,512]{2,1,0:T(8,128)(2,1)S(1)}, bf16[2,512,512]{2,1,0:T(8,128)(2,1)}, u32[]{:S(2)}) copy-start(bf16[2,512,512]{2,1,0:T(8,128)(2,1)} %get-tuple-element.33) | copy-start | bytes 3145732
  206.1 37.2 %copy-start.31 = (bf16[2,512,512]{2,1,0:T(8,128)(2,1)S(1)}, bf16[2,512,512]{2,1,0:T(8,128)(2,1)}, u32[]{:S(2)}) copy-start(bf16[2,512,512]{2,1,0:T(8,128)(2,1)} %get-tuple-element.34) | copy-start | bytes 3145732
  206.1 47.8 %copy-start.25 = (f32[512,512]{1,0:T(8,128)S(1)}, f32[512,512]{1,0:T(8,128)}, u32[]{:S(2)}) copy-start(f32[512,512]{1,0:T(8,128)} %get-tuple-element.23) | copy-start | bytes 3145732
  237.7 72.1 %copy-start.34 = (bf16[2,512,512]{2,1,0:T(8,128)(2,1)S(1)}, bf16[2,512,512]{2,1,0:T(8,128)(2,1)}, u32[]{:S(2)}) copy-start(bf16[2,512,512]{2,1,0:T(8,128)(2,1)} %get-tuple-element.29) | copy-start | bytes 3145732
  237.7 73.0 %copy-start.33 = (bf16[2,512,512]{2,1,0:T(8,128)(2,1)S(1)}, bf16[2,512,512]{2,1,0:T(8,128)(2,1)}, u32[]{:S(2)}) copy-start(bf16[2,512,512]{2,1,0:T(8,128)(2,1)} %get-tuple-element.30) | copy-start | bytes 3145732
  237.7 75.9 %copy-start.26 = (f32[512,512]{1,0:T(8,128)S(1)}, f32[512,512]{1,0:T(8,128)}, u32[]{:S(2)}) copy-start(f32[512,512]{1,0:T(8,128)} %get-tuple-element.19) | copy-start | bytes 3145732
  237.7 16.1 %collective-permute-start.12 = (bf16[512,512]{1,0:T(8,128)(2,1)S(1)}, bf16[512,512]{1,0:T(8,128)(2,1)S(1)}, u32[]{:S(2)}, u32[]{:S(2)}) collective-permute-start(bf16[512,512]{1,0:T(8,128)(2,1)S(1)} %get-tuple-element.20), channel_id=1, source_target_pairs={{0,1},{1,2},{2,3},{3,0},{4,5},{5,6},{6,7},{7,4},{8,9},{9,10},{10,1... | collective-permute-start | bytes 1572872 | tf_op jit(solution)/shard_map/ppermute | solution.py:69
  237.8 72.9 %collective-permute-start.33 = (bf16[2,512,512]{2,1,0:T(8,128)(2,1)S(1)}, bf16[2,512,512]{2,1,0:T(8,128)(2,1)S(1)}, u32[]{:S(2)}, u32[]{:S(2)}) collective-permute-start(bf16[2,512,512]{2,1,0:T(8,128)(2,1)S(1)} %copy-done.21), channel_id=1, source_target_pairs={{0,1},{1,2},{2,3},{3,0},{4,5},{5,6},{6,7},{7,4},{8,9},{9,10},{10,1... | collective-permute-start | bytes 3145736 | tf_op jit(solution)/shard_map/ppermute | solution.py:69
  239.6 0.8 copy-start.29
  240.4 75.0 %collective-permute-start.34 = (bf16[2,512,512]{2,1,0:T(8,128)(2,1)S(1)}, bf16[2,512,512]{2,1,0:T(8,128)(2,1)S(1)}, u32[]{:S(2)}, u32[]{:S(2)}) collective-permute-start(bf16[2,512,512]{2,1,0:T(8,128)(2,1)S(1)} %copy-done.32), channel_id=1, source_target_pairs={{0,2},{1,3},{2,0},{3,1},{4,6},{5,7},{6,4},{7,5},{8,10},{9,11},{10,... | collective-permute-start | bytes 3145736 | tf_op jit(solution)/shard_map/ppermute | solution.py:69
  243.3 72.1 %collective-permute-start.35 = (bf16[2,512,512]{2,1,0:T(8,128)(2,1)S(1)}, bf16[2,512,512]{2,1,0:T(8,128)(2,1)S(1)}, u32[]{:S(2)}, u32[]{:S(2)}) collective-permute-start(bf16[2,512,512]{2,1,0:T(8,128)(2,1)S(1)} %copy-done.31), channel_id=1, source_target_pairs={{0,3},{1,0},{2,1},{3,2},{4,7},{5,4},{6,5},{7,6},{8,11},{9,8},{10,9... | collective-permute-start | bytes 3145736 | tf_op jit(solution)/shard_map/ppermute | solution.py:69
  243.7 63.5 %collective-permute-start.13 = (bf16[512,512]{1,0:T(8,128)(2,1)S(1)}, bf16[512,512]{1,0:T(8,128)(2,1)S(1)}, u32[]{:S(2)}, u32[]{:S(2)}) collective-permute-start(bf16[512,512]{1,0:T(8,128)(2,1)S(1)} %get-tuple-element.21), channel_id=1, source_target_pairs={{0,2},{1,3},{2,0},{3,1},{4,6},{5,7},{6,4},{7,5},{8,10},{9,11},{10,... | collective-permute-start | bytes 1572872 | tf_op jit(solution)/shard_map/ppermute | solution.py:69
  253.9 55.9 %collective-permute-start.14 = (bf16[512,512]{1,0:T(8,128)(2,1)S(1)}, bf16[512,512]{1,0:T(8,128)(2,1)S(1)}, u32[]{:S(2)}, u32[]{:S(2)}) collective-permute-start(bf16[512,512]{1,0:T(8,128)(2,1)S(1)} %get-tuple-element.22), channel_id=1, source_target_pairs={{0,3},{1,0},{2,1},{3,2},{4,7},{5,4},{6,5},{7,6},{8,11},{9,8},{10,9... | collective-permute-start | bytes 1572872 | tf_op jit(solution)/shard_map/ppermute | solution.py:69
  307.2 26.1 %collective-permute-start.30 = (bf16[2,512,512]{2,1,0:T(8,128)(2,1)S(1)}, bf16[2,512,512]{2,1,0:T(8,128)(2,1)S(1)}, u32[]{:S(2)}, u32[]{:S(2)}) collective-permute-start(bf16[2,512,512]{2,1,0:T(8,128)(2,1)S(1)} %get-tuple-element.28), channel_id=1, source_target_pairs={{0,4},{4,8},{8,12},{12,0},{1,5},{5,9},{9,13},{13,1},{2,6},{6,10},{... | collective-permute-start | bytes 3145736 | tf_op jit(solution)/shard_map/ppermute | solution.py:69
  309.8 27.6 %collective-permute-start.31 = (bf16[2,512,512]{2,1,0:T(8,128)(2,1)S(1)}, bf16[2,512,512]{2,1,0:T(8,128)(2,1)S(1)}, u32[]{:S(2)}, u32[]{:S(2)}) collective-permute-start(bf16[2,512,512]{2,1,0:T(8,128)(2,1)S(1)} %copy-done.34), channel_id=1, source_target_pairs={{0,8},{4,12},{8,0},{12,4},{1,9},{5,13},{9,1},{13,5},{2,10},{6,14},... | collective-permute-start | bytes 3145736 | tf_op jit(solution)/shard_map/ppermute | solution.py:69
  310.7 46.2 %collective-permute-start.32 = (bf16[2,512,512]{2,1,0:T(8,128)(2,1)S(1)}, bf16[2,512,512]{2,1,0:T(8,128)(2,1)S(1)}, u32[]{:S(2)}, u32[]{:S(2)}) collective-permute-start(bf16[2,512,512]{2,1,0:T(8,128)(2,1)S(1)} %copy-done.33), channel_id=1, source_target_pairs={{0,12},{4,0},{8,4},{12,8},{1,13},{5,1},{9,5},{13,9},{2,14},{6,2},{... | collective-permute-start | bytes 3145736 | tf_op jit(solution)/shard_map/ppermute | solution.py:69
  313.9 2.4 copy-start.23
  316.9 40.0 %copy-start.24 = (f32[2,512,512]{2,1,0:T(8,128)S(1)}, f32[2,512,512]{2,1,0:T(8,128)}, u32[]{:S(2)}) copy-start(f32[2,512,512]{2,1,0:T(8,128)} %get-tuple-element.27) | copy-start | bytes 6291460
  359.2 1.5 copy-start.1
  (10 other events, 6.6 us)

commit v2 on v1

v2 whole, which is shorter than its diff:
```python
import functools
import math

import jax
import jax.numpy as jnp
from jax import lax
from jax.experimental import pallas as pl
from jax.experimental.pallas import tpu as pltpu
from jax.sharding import Mesh
from jax.sharding import PartitionSpec as P

KB = 128
SIDE = 4
MEMBER = ("y", "core")
LOSS_SCALE = 4096.0
FAIR_EPS = 0.05
NORM_EPS = 1e-06
LOG2E = math.log2(math.e)
F32 = jnp.float32
BF16 = jnp.bfloat16


def cut_along(x, dim, length):
    dims = x.shape
    tiles = x.reshape(*dims[:dim], length, dims[dim] // length, *dims[dim + 1 :])
    return jnp.moveaxis(tiles, dim, 0)


def in_order(tiles, dim):
    tiles = jnp.moveaxis(tiles, 0, dim)
    dims = tiles.shape
    return tiles.reshape(*dims[:dim], dims[dim] * dims[dim + 1], *dims[dim + 2 :])


def moved_by_axis(tiles, axes, sequence):
    inside = tiles.shape[1:]
    filled = tiles.reshape(*(lax.axis_size(a) for a in axes), *inside)
    for k in sequence:
        filled = lax.all_to_all(filled, axes[k], k, k, tiled=True)
    return filled.reshape(-1, *inside)


def exchange_by_axis(x, axes, sequence, split_dim, concat_dim):
    tiles = cut_along(x, split_dim, lax.axis_size(axes))
    return in_order(moved_by_axis(tiles, axes, sequence), concat_dim)


def unit_scaled_lines(differences):
    return differences / jnp.sqrt(
        jnp.sum(differences * differences, axis=-2, keepdims=True) + NORM_EPS
    )


def outlook_derivative(forecasts, truth_field, cell_surface_share):
    count = forecasts.shape[0]
    polarity_unit = unit_scaled_lines(forecasts - truth_field[None])
    differences = forecasts[:, None] - forecasts[None]
    couple_total = jnp.sum(unit_scaled_lines(differences), axis=1)
    weight = LOSS_SCALE * cell_surface_share[None, None, :]
    return weight * (
        polarity_unit / count - (1.0 - FAIR_EPS) / (count * (count - 1)) * couple_total
    )


def fetched(x, axis, distance):
    return lax.ppermute(x, axis, [(i, (i - distance) % SIDE) for i in range(SIDE)])


def delivered(x, axis, distance):
    return lax.ppermute(x, axis, [(i, (i + distance) % SIDE) for i in range(SIDE)])


def head_pair_tiles(table, base, kv, queries, lates, decoder, out, scratch):
    q_stack, g_stack, stat_rows, dk_acc, dv_acc, dq_acc = scratch
    rows = q_stack.shape[1] // 2
    channels = decoder.shape[1]
    head = pl.program_id(0) * 2 + base
    head_dim = 64
    score_scale = head_dim ** (-0.5)
    lane = lax.broadcasted_iota(jnp.int32, (rows, 2 * head_dim), 1)
    first = lane < head_dim
    nt = (((1,), (1,)), ((), ()))
    tn = (((0,), (1,)), ((), ()))
    for t in range(SIDE):
        q = queries[t][...].astype(F32)
        g = lax.dot_general(
            lates[t][:channels, :].astype(BF16), decoder[...], tn, preferred_element_type=F32
        )
        q_stack[t, :rows] = jnp.where(first, q, 0.0).astype(BF16)
        q_stack[t, rows:] = jnp.where(first, 0.0, q).astype(BF16)
        g_stack[t, :rows] = jnp.where(first, g, 0.0).astype(BF16)
        g_stack[t, rows:] = jnp.where(first, 0.0, g).astype(BF16)
        for n in range(2):
            stat_rows[t, n : n + 1, :rows] = lates[t][pl.ds(channels + 8 * n + head, 1), :]
            stat_rows[t, n : n + 1, rows:] = lates[t][pl.ds(channels + 8 * n + head + 1, 1), :]
    dk_acc[...] = jnp.zeros_like(dk_acc)
    dv_acc[...] = jnp.zeros_like(dv_acc)

    def one_query_block(t, carry):
        q = q_stack[t]
        g = g_stack[t]
        lse = stat_rows[t, 0:1, :] * LOG2E
        delta = stat_rows[t, 1:2, :]
        dq_acc[...] = jnp.zeros_like(dq_acc)
        for pair in ((0, 1), (2, 3)):
            starts = [pl.multiple_of(table[t * SIDE + a] * KB, KB) for a in pair]
            k = jnp.concatenate([kv[a][0][pl.ds(s, KB), :] for a, s in zip(pair, starts)], axis=0)
            v = jnp.concatenate([kv[a][1][pl.ds(s, KB), :] for a, s in zip(pair, starts)], axis=0)
            scores = lax.dot_general(k, q, nt, preferred_element_type=F32)
            p = jnp.exp2(scores * (score_scale * LOG2E) - lse)
            dp = lax.dot_general(v, g, nt, preferred_element_type=F32)
            ds = (p * (dp - delta)).astype(BF16)
            dv = jnp.dot(p.astype(BF16), g, preferred_element_type=F32)
            dk = jnp.dot(ds, q, preferred_element_type=F32)
            for n, (a, s) in enumerate(zip(pair, starts)):
                dv_acc[a, pl.ds(s, KB), :] += dv[n * KB : (n + 1) * KB]
                dk_acc[a, pl.ds(s, KB), :] += dk[n * KB : (n + 1) * KB]
            kt = k.T
            dq_acc[:head_dim] += jnp.dot(kt[:head_dim], ds[:, :rows], preferred_element_type=F32)
            dq_acc[head_dim:] += jnp.dot(kt[head_dim:], ds[:, rows:], preferred_element_type=F32)
        dq = dq_acc[...].T * score_scale
        for n in range(SIDE):

            @pl.when(t == n)
            def _():
                out(2, n, dq)

        return carry

    lax.fori_loop(0, SIDE, one_query_block, 0)
    for a in range(SIDE):
        out(0, a, dk_acc[a] * score_scale)
        out(1, a, dv_acc[a])


def tile_kernel(table, *refs, base):
    key_own, value_own, query_own, late_own, decoder = refs[0:5]
    fetch_x, fetch_z = refs[5:8], refs[8:11]
    late_x, late_z = refs[11:14], refs[14:17]
    own_out = refs[17]
    send_x, send_z = refs[18:21], refs[21:24]
    scratch = refs[24:]
    sides = ((fetch_x, send_x, late_x), (fetch_z, send_z, late_z))
    for m in range(2):
        key_fetch, key_send, _ = sides[m]
        query_fetch, query_send, late = sides[1 - m]
        kv = [(key_own.at[m], value_own.at[m])] + [(r.at[0], r.at[1]) for r in key_fetch]
        queries = [query_own.at[m]] + [r.at[2] for r in query_fetch]
        lates = [late_own.at[m]] + list(late)

        def out(kind, n, value, m=m, key_send=key_send, query_send=query_send):
            if n == 0:
                own_out[kind, m] = value
            else:
                ref = (query_send if kind == 2 else key_send)[n - 1]
                ref[kind] = value.astype(BF16)

        head_pair_tiles(
            table.at[m], base, kv, queries, lates, decoder, out, scratch
        )


def attention_tiles(half, tables, key_rows, value_rows, query, fetched_x, fetched_z, late_own, late_x, late_z, decoder_matrix):
    members, rows, width = key_rows.shape
    stats, channels = late_own.shape[1], decoder_matrix.shape[1]
    pairs = width // 256
    base = half * pairs
    own_spec = pl.BlockSpec((members, rows, 128), lambda h, tab: (0, 0, base + h))
    near_spec = pl.BlockSpec((None, 3, rows, 128), lambda h, tab: (half, 0, 0, h))
    far_spec = pl.BlockSpec((3, rows, 128), lambda h, tab: (0, 0, h))
    fetch_specs = [near_spec, far_spec, near_spec]
    late_spec = pl.BlockSpec((stats, rows), lambda h, tab: (0, 0))
    out = pl.pallas_call(
        functools.partial(tile_kernel, base=2 * base),
        out_shape=[jax.ShapeDtypeStruct((3, members, rows, width // 2), F32)]
        + [jax.ShapeDtypeStruct((3, rows, width // 2), BF16)] * 6,
        grid_spec=pltpu.PrefetchScalarGridSpec(
            num_scalar_prefetch=1,
            grid=(pairs,),
            in_specs=[own_spec] * 3
            + [
                pl.BlockSpec((members, stats, rows), lambda h, tab: (0, 0, 0)),
                pl.BlockSpec((128, channels), lambda h, tab: (base + h, 0)),
            ]
            + fetch_specs * 2
            + [late_spec] * 6,
            out_specs=[pl.BlockSpec((3, members, rows, 128), lambda h, tab: (0, 0, 0, h))]
            + [far_spec] * 6,
            scratch_shapes=[
                pltpu.VMEM((SIDE, 2 * rows, 128), BF16),
                pltpu.VMEM((SIDE, 2 * rows, 128), BF16),
                pltpu.VMEM((SIDE, 2, 2 * rows), F32),
                pltpu.VMEM((SIDE, rows, 128), F32),
                pltpu.VMEM((SIDE, rows, 128), F32),
                pltpu.VMEM((128, rows), F32),
            ],
        ),
        compiler_params=pltpu.CompilerParams(
            dimension_semantics=("arbitrary",), vmem_limit_bytes=50 * 1024 * 1024
        ),
        name="attention_tiles",
    )(tables, key_rows, value_rows, query, late_own, decoder_matrix, *fetched_x, *fetched_z, *late_x, *late_z)
    return out[0], out[1:4], out[4:7]


def sum_kernel(*refs):
    own = refs[0]
    got_x, got_z = refs[1:4], refs[4:7]
    outs = refs[-3:]
    for kind, ref in enumerate(outs):
        for m in range(2):
            got = (got_x, got_z)[m if kind < 2 else 1 - m]
            total = own[kind, m]
            for g in got:
                total = total + g[kind].astype(F32)
            ref[m] = total


def summed(half, own, got_x, got_z, outs):
    _, members, rows, lanes = own.shape
    grid = (2,)
    own_spec = pl.BlockSpec((3, members, rows // 2, lanes), lambda r: (0, 0, r, 0))
    got_spec = pl.BlockSpec((3, rows // 2, lanes), lambda r: (0, r, 0))
    out_spec = pl.BlockSpec((members, rows // 2, lanes), lambda r: (0, r, half))
    shape = jax.ShapeDtypeStruct((members, rows, 2 * lanes), F32)
    kept = list(outs) if outs else []
    return pl.pallas_call(
        sum_kernel,
        out_shape=[shape] * 3,
        grid=grid,
        in_specs=[own_spec] + [got_spec] * 6 + [pl.BlockSpec(memory_space=pl.ANY)] * len(kept),
        out_specs=[out_spec] * 3,
        input_output_aliases={7 + n: n for n in range(len(kept))},
        compiler_params=pltpu.CompilerParams(vmem_limit_bytes=50 * 1024 * 1024),
        name="summed",
    )(own, *got_x, *got_z, *kept)


def ring_fetched(own, axis):
    after, before = fetched(own, axis, 1), fetched(own, axis, 3)
    return after, (fetched(after[0], axis, 1), fetched(before[1], axis, 3)), before


def outgoing(keys, values, queries):
    stacked = jnp.stack([keys, values, queries])
    kinds, rows, width = stacked.shape
    return jnp.stack([stacked[..., : width // 2], stacked[..., width // 2 :]])


def shards(
    hidden_embedding,
    decoder_matrix,
    baseline_field,
    truth_field,
    cell_surface_share,
    node_order,
    query,
    key_rows,
    value_rows,
    row_lse,
    kv_owner,
    kv_local,
):
    members, nodes, width = hidden_embedding.shape
    heads = row_lse.shape[1]
    x_at = lax.axis_index("x")
    z_at = lax.axis_index("z")

    x_after, x_far, x_before = ring_fetched(outgoing(key_rows[0], value_rows[0], query[1]), "x")
    z_after, z_far, z_before = ring_fetched(outgoing(key_rows[1], value_rows[1], query[0]), "z")

    forecast = baseline_field[None] + jnp.einsum(
        "mou,ut->mto", hidden_embedding, decoder_matrix, preferred_element_type=F32
    )
    groups = lax.axis_size(MEMBER)
    member_index = lax.axis_index(MEMBER)
    everyone = exchange_by_axis(forecast, MEMBER, (1, 0), 2, 0)
    span = nodes // groups
    offset = member_index * span
    observed = lax.dynamic_slice_in_dim(truth_field, offset, span, 1)
    area = lax.dynamic_slice_in_dim(cell_surface_share, offset, span, 0)
    derivative = outlook_derivative(everyone, observed, area).astype(BF16)
    grad_forecast = exchange_by_axis(derivative, MEMBER, (1, 0), 0, 2)

    shard_ids = jnp.arange(SIDE * SIDE, dtype=jnp.int32)
    around = jnp.arange(SIDE, dtype=jnp.int32)
    named = jnp.sum(
        jnp.where(kv_owner[:, :, None] == shard_ids[None, None, :], kv_local[:, :, None], 0), axis=1
    ).reshape(SIDE, SIDE, SIDE, SIDE)
    x_near = ((x_at + around) % SIDE)[:, None] == around[None, :]
    z_near = ((z_at + around) % SIDE)[:, None] == around[None, :]
    x_here, z_here = x_near[0], z_near[0]

    def picked(sx, sz, ox, oz):
        chosen = (
            sx[:, None, None, None, :, None, None, None]
            & sz[None, :, None, None, None, :, None, None]
            & ox[None, None, :, None, None, None, :, None]
            & oz[None, None, None, :, None, None, None, :]
        )
        return jnp.sum(jnp.where(chosen, named, 0), axis=(4, 5, 6, 7)).reshape(-1)

    tables = jnp.stack(
        [
            picked(x_here[None], z_near, x_near, z_here[None]),
            picked(x_near, z_here[None], x_here[None], z_near),
        ]
    )

    permuter = (node_order[0][:, None] == jnp.arange(nodes, dtype=jnp.int32)[None, :]).astype(BF16)
    grad_columns = jnp.einsum(
        "mcg,tg->mct", grad_forecast, permuter, preferred_element_type=F32
    )
    grad_latent = jnp.einsum(
        "wc,mct->mwt", decoder_matrix, grad_columns.astype(BF16), preferred_element_type=F32
    ).astype(BF16)
    saved = jnp.einsum("mgw,tg->mwt", hidden_embedding, permuter, preferred_element_type=F32).astype(
        BF16
    )
    split = (members, heads, width // heads, nodes)
    delta = jnp.sum(
        grad_latent.astype(F32).reshape(split) * saved.astype(F32).reshape(split), axis=2
    )
    late_own = jnp.concatenate([grad_columns, row_lse, delta], axis=1)
    late_z = [fetched(late_own[0], "z", d) for d in (1, 2, 3)]
    late_x = [fetched(late_own[1], "x", d) for d in (1, 2, 3)]

    outs = None
    parts = []
    for half in range(2):
        own, send_x, send_z = attention_tiles(
            half,
            tables,
            key_rows,
            value_rows,
            query,
            (x_after, x_far[half], x_before),
            (z_after, z_far[half], z_before),
            late_own,
            late_x,
            late_z,
            decoder_matrix,
        )
        got_x = [delivered(send_x[d - 1], "x", d) for d in (1, 2, 3)]
        got_z = [delivered(send_z[d - 1], "z", d) for d in (1, 2, 3)]
        parts.append((own, got_x, got_z))
    for half, (own, got_x, got_z) in enumerate(parts):
        outs = summed(half, own, got_x, got_z, outs)
    grad_key, grad_value, grad_query = outs
    return grad_query, grad_key, grad_value


def solution(mesh):
    finer = Mesh(mesh.devices.reshape(4, 2, SIDE, SIDE), ("y", "core", "x", "z"))
    plane = ("x", "z")
    in_specs = (
        P(MEMBER, plane, None),
        P(),
        P(None, plane),
        P(None, plane),
        P(plane),
        P(plane, None),
        P(MEMBER, plane, None),
        P(MEMBER, plane, None),
        P(MEMBER, plane, None),
        P(MEMBER, None, plane),
        P(),
        P(),
    )
    out_specs = (P(MEMBER, plane, None), P(MEMBER, plane, None), P(MEMBER, plane, None))
    return jax.shard_map(
        shards, mesh=finer, in_specs=in_specs, out_specs=out_specs, check_vma=False
    )
```

time: 363 us -> 234 us (0.64)
  waiting for transfers between devices: 153 us -> 62.1 us
  local copies, waits for them, and re-layouts: 30.4 us -> 13.6 us
  starting transfers between devices: 77.8 us -> 62.7 us
  other arithmetic: 24.6 us -> 11.1 us
  Pallas kernels: 62.8 us -> 71.8 us
    ppermute x12, waiting for transfers between devices: 101 us -> 36.6 us  [delivered(): lax.ppermute(x, axis, [(i, (i + distance) % SIDE) for i in range(SIDE)])]
    ppermute x24 -> x14, waiting for transfers between devices: 49.1 us -> 12 us  [fetched(): lax.ppermute(x, axis, [(i, (i - distance) % SIDE) for i in range(SIDE)])]
    unnamed x73 -> x39, local copies, waits for them, and re-layouts: 17 us -> 2.38 us
    all_to_all x2, waiting for transfers between devices: 2.14 us -> 13.5 us  [moved_by_axis(): filled = lax.all_to_all(filled, axes[k], k, k, tiled=True)]
    pallas_call x2 -> x4, Pallas kernels: 62.8 us -> 71.8 us  [the longest x2 64.6 us: attention_tiles(): pl.pallas_call(functools.partial(tile_kernel, base=2 * base), out_shape=[...]
    ppermute x24 -> x14, starting transfers between devices: 45.5 us -> 36.9 us  [fetched(): lax.ppermute(x, axis, [(i, (i - distance) % SIDE) for i in range(SIDE)])]
    another operation x7 -> x4, other arithmetic: 9.7 us -> 2.91 us  [the longest x2 2.56 us: outgoing(): return jnp.stack([stacked[..., :width // 2], stacked[..., width // 2:]])]
    ppermute x12, starting transfers between devices: 24.3 us -> 17.9 us  [delivered(): lax.ppermute(x, axis, [(i, (i + distance) % SIDE) for i in range(SIDE)])]
  transfers between devices with their start and end apart: 38 -> 28, of which waited for: 17 -> 9; matrix products, arithmetic and copies ran while one was open for 10% -> 10% of each run, Pallas kernels for 17% -> 29%
where the time goes in v2:
time: 234 us
  Pallas kernels  71.8 us (31%)
  starting transfers between devices  62.7 us (27%)
  waiting for transfers between devices  62.1 us (27%)
  local copies, waits for them, and re-layouts  13.6 us (6%)
  other arithmetic  11.1 us (5%)
  blocking collectives  8.1 us (3%)
  matrix products  3.11 us (1%)
    pallas_call x2, Pallas kernels, attention_tiles(): pl.pallas_call(functools.partial(tile_kernel, base=2 * base), out_shape=[...  64.6 us
    ppermute x14, starting transfers between devices, fetched(): lax.ppermute(x, axis, [(i, (i - distance) % SIDE) for i in range(SIDE)])  36.9 us
    ppermute x12, waiting for transfers between devices, delivered(): lax.ppermute(x, axis, [(i, (i + distance) % SIDE) for i in range(SIDE)])  36.6 us
    ppermute x12, starting transfers between devices, delivered(): lax.ppermute(x, axis, [(i, (i + distance) % SIDE) for i in range(SIDE)])  17.9 us
    all_to_all x2, waiting for transfers between devices, moved_by_axis(): filled = lax.all_to_all(filled, axes[k], k, k, tiled=True)  13.5 us
    ppermute x14, waiting for transfers between devices, fetched(): lax.ppermute(x, axis, [(i, (i - distance) % SIDE) for i in range(SIDE)])  12 us
    all_to_all x2, blocking collectives, moved_by_axis(): filled = lax.all_to_all(filled, axes[k], k, k, tiled=True)  8.1 us
    all_to_all x2, starting transfers between devices, moved_by_axis(): filled = lax.all_to_all(filled, axes[k], k, k, tiled=True)  7.87 us
  transfers between devices with their start and end apart: 28, of which 9 were waited for; matrix products, arithmetic and copies ran while one was open for 10% of the time, Pallas kernels for 29%

profile of v2, /device:TPU:2, one launch (start us, length us, event | category | flops | bytes accessed | tf_op | source)
XLA Modules:
  0.0 233.7 jit_solution(17828083799523472480)
XLA Ops:
  0.7 1.4 fusion.16
  2.1 0.2 copy-done.3
  2.3 0.2 copy-done.4
  2.7 0.3 pad_maximum_fusion
  3.1 1.3 pad_maximum_fusion.3
  4.4 4.0 %collective-permute-start.3 = (bf16[2,3,512,256]{3,2,1,0:T(8,128)(2,1)}, bf16[2,3,512,256]{3,2,1,0:T(8,128)(2,1)S(1)}, u32[]{:S(2)}, u32[]{:S(2)}) collective-permute-start(bf16[2,3,512,256]{3,2,1,0:T(8,128)(2,1)} %pad_maximum_fusion.3), channel_id=1, source_target_pairs={{0,3},{1,0},{2,1},{3,2},{4,7},{5,4},{6,5},{7,6},{8,11},{9,8},{10,9... | collective-permute-start | bytes 4718600 | tf_op jit(solution)/shard_map/ppermute | solution.py:66
  8.6 1.3 pad_maximum_fusion.1
  9.9 0.5 collective-permute-start
  10.4 1.5 collective-permute-start.1
  11.9 1.2 fusion.2
  13.1 1.2 copy.55
  14.4 4.2 %all_to_all.20 = f32[4,2,2,96,64]{3,4,2,0,1:T(8,128)S(1)} all-to-all(f32[4,2,2,96,64]{3,4,2,0,1:T(8,128)S(1)} %copy.56), channel_id=1, replica_groups=mesh['y'=4,'core'=2,'x'=4,'z'=4] {'core'}, dimensions={1} | all-to-all | bytes 786432 | tf_op jit(solution)/shard_map/all_to_all | solution.py:39
  18.5 0.8 copy.57
  19.4 4.5 %all-to-all-start.1 = ((f32[4,2,2,96,64]{3,4,2,1,0:T(8,128)}), f32[4,2,2,96,64]{3,4,2,1,0:T(8,128)S(1)}, u32[]{:S(2)}, u32[]{:S(2)}) async-start(f32[4,2,2,96,64]{3,4,2,1,0:T(8,128)} %copy.57), calls=%async_computation.1 | async-start | bytes 1048576 | tf_op jit(solution)/shard_map/all_to_all | solution.py:39
  23.9 0.9 constant_dynamic-slice_fusion
  25.5 0.7 select_reduce_fusion.1
  26.3 0.8 dynamic-slice_multiply_fusion
  27.2 6.4 %all-to-all-done.1 = f32[4,2,2,96,64]{3,4,2,1,0:T(8,128)S(1)} async-done(((f32[4,2,2,96,64]{3,4,2,1,0:T(8,128)}), f32[4,2,2,96,64]{3,4,2,1,0:T(8,128)S(1)}, u32[]{:S(2)}, u32[]{:S(2)}) %all-to-all-start.1) | async-done | bytes 393248 | tf_op jit(solution)/shard_map/all_to_all | solution.py:39
  33.6 2.2 fusion.1
  35.9 2.6 %fusion = f32[16,96,64]{1,2,0:T(8,128)S(1)} fusion(f32[16,16,64]{2,1,0:T(8,128)S(1)} %add_sqrt_fusion, f32[16,96,64]{1,2,0:T(8,128)S(1)} %bitcast.61), kind=kLoop, calls=%fused_computation.2 | loop fusion | flops 4620288 | bytes 851968 | tf_op jit(solution)/shard_map/reduce_sum | solution.py:58
  38.5 0.2 multiply_reduce_fusion
  38.8 0.2 multiply_convert_fusion
  39.0 3.9 %all_to_all.21 = bf16[4,2,2,96,64]{3,4,2,0,1:T(8,128)(2,1)S(1)} all-to-all(bf16[4,2,2,96,64]{3,4,2,0,1:T(8,128)(2,1)S(1)} %copy.59), channel_id=1, replica_groups=mesh['y'=4,'core'=2,'x'=4,'z'=4] {'core'}, dimensions={1} | all-to-all | bytes 393216 | tf_op jit(solution)/shard_map/all_to_all | solution.py:39
  43.0 0.7 copy.60
  43.7 3.4 %all-to-all-start.3 = ((bf16[4,2,2,96,64]{3,4,2,1,0:T(8,128)(2,1)}), bf16[4,2,2,96,64]{3,4,2,1,0:T(8,128)(2,1)S(1)}, u32[]{:S(2)}, u32[]{:S(2)}) async-start(bf16[4,2,2,96,64]{3,4,2,1,0:T(8,128)(2,1)} %copy.60), calls=%async_computation.3 | async-start | bytes 524288 | tf_op jit(solution)/shard_map/all_to_all | solution.py:39
  47.2 7.1 %all-to-all-done.3 = bf16[4,2,2,96,64]{3,4,2,1,0:T(8,128)(2,1)S(1)} async-done(((bf16[4,2,2,96,64]{3,4,2,1,0:T(8,128)(2,1)}), bf16[4,2,2,96,64]{3,4,2,1,0:T(8,128)(2,1)S(1)}, u32[]{:S(2)}, u32[]{:S(2)}) %all-to-all-start.3) | async-done | bytes 196640 | tf_op jit(solution)/shard_map/all_to_all | solution.py:39
  54.4 0.5 fusion.5
  54.9 0.5 convolution_convert_fusion.1
  55.4 1.0 bitcast_reduce_fusion
  56.4 1.0 slice_bitcast_fusion
  57.4 3.2 %collective-permute-start.19 = (bf16[3,512,256]{2,1,0:T(8,128)(2,1)}, bf16[3,512,256]{2,1,0:T(8,128)(2,1)S(1)}, u32[]{:S(2)}, u32[]{:S(2)}) collective-permute-start(bf16[3,512,256]{2,1,0:T(8,128)(2,1)} %slice_bitcast_fusion), channel_id=1, source_target_pairs={{0,3},{1,0},{2,1},{3,2},{4,7},{5,4},{6,5},{7,6},{8,11},{9,8},{10,9... | collective-permute-start | bytes 2359304 | tf_op jit(solution)/shard_map/ppermute | solution.py:66
  60.6 2.1 slice_bitcast_fusion.1
  62.7 1.3 collective-permute-start.18
  64.1 0.6 select_reduce_fusion
  64.9 6.8 %collective-permute-done.10.refs_15_ = f32[112,512]{1,0:T(8,128)S(1)} collective-permute-done((f32[112,512]{1,0:T(8,128)S(1)}, f32[112,512]{1,0:T(8,128)S(1)}, u32[]{:S(2)}, u32[]{:S(2)}) %collective-permute-start.10) | collective-permute-done | bytes 229408 | tf_op jit(solution)/shard_map/ppermute | solution.py:66
  71.6 11.7 %collective-permute-start.11 = (f32[112,512]{1,0:T(8,128)S(1)}, f32[112,512]{1,0:T(8,128)S(1)}, u32[]{:S(2)}, u32[]{:S(2)}) collective-permute-start(f32[112,512]{1,0:T(8,128)S(1)} %get-tuple-element.53), channel_id=1, source_target_pairs={{0,1},{1,2},{2,3},{3,0},{4,5},{5,6},{6,7},{7,4},{8,9},{9,10},{10,1... | collective-permute-start | bytes 688136 | tf_op jit(solution)/shard_map/ppermute | solution.py:66
  83.3 1.3 collective-permute-start.6
  84.6 1.2 slice_bitcast_fusion.2
  85.8 2.0 collective-permute-done.11.refs_16_
  87.8 3.3 %collective-permute-start.7 = (f32[112,512]{1,0:T(8,128)S(1)}, f32[112,512]{1,0:T(8,128)S(1)}, u32[]{:S(2)}, u32[]{:S(2)}) collective-permute-start(f32[112,512]{1,0:T(8,128)S(1)} %get-tuple-element.54), channel_id=1, source_target_pairs={{0,8},{4,12},{8,0},{12,4},{1,9},{5,13},{9,1},{13,5},{2,10},{6,14},... | collective-permute-start | bytes 688136 | tf_op jit(solution)/shard_map/ppermute | solution.py:66
  91.1 1.7 collective-permute-start.8
  92.8 0.4 collective-permute-start.9
  93.2 1.2 slice_bitcast_fusion.5
  94.4 1.2 collective-permute-done.7.refs_12_
  95.6 1.3 collective-permute-start.5
  96.9 2.0 collective-permute-done.8.refs_13_
  98.9 6.5 %collective-permute-start.2 = (bf16[3,512,256]{2,1,0:T(8,128)(2,1)S(1)}, bf16[3,512,256]{2,1,0:T(8,128)(2,1)S(1)}, u32[]{:S(2)}, u32[]{:S(2)}) collective-permute-start(bf16[3,512,256]{2,1,0:T(8,128)(2,1)S(1)} %slice_bitcast_fusion.5), channel_id=1, source_target_pairs={{0,4},{4,8},{8,12},{12,0},{1,5},{5,9},{9,13},{13,1},{2,6},{6,10},{... | collective-permute-start | bytes 2359304 | tf_op jit(solution)/shard_map/ppermute | solution.py:66
  105.4 0.9 copy-done.6
  106.3 32.3 %attention_tiles.3 = (f32[3,2,512,256]{3,2,1,0:T(8,128)}, bf16[3,512,256]{2,1,0:T(8,128)(2,1)S(1)}, bf16[3,512,256]{2,1,0:T(8,128)(2,1)S(1)}, bf16[3,512,256]{2,...) custom-call(s32[2,16]{1,0:T(2,128)S(1)} %pad_add_fusion.table, ...), custom_call_target="tpu_custom_call" | custom-call | tf_op jit(solution)/shard_map/attention_tiles/pallas_call | solution.py:173
  138.6 2.5 %collective-permute-start.20 = (bf16[3,512,256]{2,1,0:T(8,128)(2,1)S(1)}, bf16[3,512,256]{2,1,0:T(8,128)(2,1)S(1)}, u32[]{:S(2)}, u32[]{:S(2)}) collective-permute-start(bf16[3,512,256]{2,1,0:T(8,128)(2,1)S(1)} %get-tuple-element.31), channel_id=1, source_target_pairs={{0,4},{4,8},{8,12},{12,0},{1,5},{5,9},{9,13},{13,1},{2,6},{6,10},{... | collective-permute-start | bytes 2359304 | tf_op jit(solution)/shard_map/ppermute | solution.py:70
  141.1 0.4 collective-permute-start.21
  141.6 2.5 %collective-permute-start.22 = (bf16[3,512,256]{2,1,0:T(8,128)(2,1)}, bf16[3,512,256]{2,1,0:T(8,128)(2,1)S(1)}, u32[]{:S(2)}, u32[]{:S(2)}) collective-permute-start(bf16[3,512,256]{2,1,0:T(8,128)(2,1)} %get-tuple-element.33), channel_id=1, source_target_pairs={{0,12},{4,0},{8,4},{12,8},{1,13},{5,1},{9,5},{13,9},{2,14},{6,2},{... | collective-permute-start | bytes 2359304 | tf_op jit(solution)/shard_map/ppermute | solution.py:70
  144.1 2.5 %collective-permute-start.24 = (bf16[3,512,256]{2,1,0:T(8,128)(2,1)}, bf16[3,512,256]{2,1,0:T(8,128)(2,1)S(1)}, u32[]{:S(2)}, u32[]{:S(2)}) collective-permute-start(bf16[3,512,256]{2,1,0:T(8,128)(2,1)} %get-tuple-element.35), channel_id=1, source_target_pairs={{0,2},{1,3},{2,0},{3,1},{4,6},{5,7},{6,4},{7,5},{8,10},{9,11},{10,... | collective-permute-start | bytes 2359304 | tf_op jit(solution)/shard_map/ppermute | solution.py:70
  146.6 32.3 %attention_tiles.2 = (f32[3,2,512,256]{3,2,1,0:T(8,128)}, bf16[3,512,256]{2,1,0:T(8,128)(2,1)S(1)}, bf16[3,512,256]{2,1,0:T(8,128)(2,1)S(1)}, bf16[3,512,256]{2,...) custom-call(s32[2,16]{1,0:T(2,128)S(1)} %pad_add_fusion.table, ...), custom_call_target="tpu_custom_call" | custom-call | tf_op jit(solution)/shard_map/attention_tiles/pallas_call | solution.py:173
  178.9 2.4 %collective-permute-start.25 = (bf16[3,512,256]{2,1,0:T(8,128)(2,1)S(1)}, bf16[3,512,256]{2,1,0:T(8,128)(2,1)S(1)}, u32[]{:S(2)}, u32[]{:S(2)}) collective-permute-start(bf16[3,512,256]{2,1,0:T(8,128)(2,1)S(1)} %copy-done.17), channel_id=1, source_target_pairs={{0,3},{1,0},{2,1},{3,2},{4,7},{5,4},{6,5},{7,6},{8,11},{9,8},{10,9... | collective-permute-start | bytes 2359304 | tf_op jit(solution)/shard_map/ppermute | solution.py:70
  181.3 3.5 %collective-permute-start.13 = (bf16[3,512,256]{2,1,0:T(8,128)(2,1)S(1)}, bf16[3,512,256]{2,1,0:T(8,128)(2,1)S(1)}, u32[]{:S(2)}, u32[]{:S(2)}) collective-permute-start(bf16[3,512,256]{2,1,0:T(8,128)(2,1)S(1)} %get-tuple-element.25), channel_id=1, source_target_pairs={{0,8},{4,12},{8,0},{12,4},{1,9},{5,13},{9,1},{13,5},{2,10},{6,14},... | collective-permute-start | bytes 2359304 | tf_op jit(solution)/shard_map/ppermute | solution.py:70
  184.9 21.1 %collective-permute-done.25.refs_6_ = bf16[3,512,256]{2,1,0:T(8,128)(2,1)S(1)} collective-permute-done((bf16[3,512,256]{2,1,0:T(8,128)(2,1)S(1)}, bf16[3,512,256]{2,1,0:T(8,128)(2,1)S(1)}, u32[]{:S(2)}, u32[]{:S(2)}) %collective-permute-start.25) | collective-permute-done | bytes 786464 | tf_op jit(solution)/shard_map/ppermute | solution.py:70
  205.9 0.9 collective-permute-start.16
  206.9 3.1 %collective-permute-start.17 = (bf16[3,512,256]{2,1,0:T(8,128)(2,1)}, bf16[3,512,256]{2,1,0:T(8,128)(2,1)S(1)}, u32[]{:S(2)}, u32[]{:S(2)}) collective-permute-start(bf16[3,512,256]{2,1,0:T(8,128)(2,1)} %get-tuple-element.29), channel_id=1, source_target_pairs={{0,3},{1,0},{2,1},{3,2},{4,7},{5,4},{6,5},{7,6},{8,11},{9,8},{10,9... | collective-permute-start | bytes 2359304 | tf_op jit(solution)/shard_map/ppermute | solution.py:70
  210.0 3.6 %summed.2 = (f32[2,512,512]{2,1,0:T(8,128)}, f32[2,512,512]{2,1,0:T(8,128)}, f32[2,512,512]{2,1,0:T(8,128)}) custom-call(f32[3,2,512,256]{3,2,1,0:T(8,128)} %get-tuple-element.30.refs_0_, bf16[3,512,256]{2,1,0:T(8,128)(2,1)S(1)} %collective-permute-done.20.refs_1_, bf16[3,512,256]{2,1,0:T(8,128)(2,1)S(1)} %collective-permute-done.21.refs_2_, ...), custom_call_target="tpu_custom_call" | custom-call | tf_op jit(solution)/shard_map/summed/pallas_call | solution.py:227
  213.6 6.1 %collective-permute-done.16.refs_5_ = bf16[3,512,256]{2,1,0:T(8,128)(2,1)S(1)} collective-permute-done((bf16[3,512,256]{2,1,0:T(8,128)(2,1)}, bf16[3,512,256]{2,1,0:T(8,128)(2,1)S(1)}, u32[]{:S(2)}, u32[]{:S(2)}) %collective-permute-start.16) | collective-permute-done | bytes 786464 | tf_op jit(solution)/shard_map/ppermute | solution.py:70
  219.6 9.5 %collective-permute-done.17.refs_6_ = bf16[3,512,256]{2,1,0:T(8,128)(2,1)S(1)} collective-permute-done((bf16[3,512,256]{2,1,0:T(8,128)(2,1)}, bf16[3,512,256]{2,1,0:T(8,128)(2,1)S(1)}, u32[]{:S(2)}, u32[]{:S(2)}) %collective-permute-start.17) | collective-permute-done | bytes 786464 | tf_op jit(solution)/shard_map/ppermute | solution.py:70
  229.1 0.9 copy-done.9
  230.0 3.6 %summed.3 = (f32[2,512,512]{2,1,0:T(8,128)}, f32[2,512,512]{2,1,0:T(8,128)}, f32[2,512,512]{2,1,0:T(8,128)}) custom-call(f32[3,2,512,256]{3,2,1,0:T(8,128)} %get-tuple-element.23.refs_0_, bf16[3,512,256]{2,1,0:T(8,128)(2,1)S(1)} %collective-permute-done.12.refs_1_, ...), custom_call_target="tpu_custom_call", output_to_operand_aliasing={{0}: (7, {}), {1}: (8, {}), {2}: (9, {})} | custom-call | tf_op jit(solution)/shard_map/summed/pallas_call | solution.py:227
  (88 shorter events, 2.0 us)
Async XLA Ops:
  0.6 11.3 %copy-start = (bf16[2,512,512]{2,1,0:T(8,128)(2,1)S(1)}, bf16[2,512,512]{2,1,0:T(8,128)(2,1)}, u32[]{:S(2)}) copy-start(bf16[2,512,512]{2,1,0:T(8,128)(2,1)} %param.12) | copy-start | bytes 3145732
  0.6 1.6 copy-start.3
  0.7 1.9 copy-start.4
  4.4 52.0 %collective-permute-start.3 = (bf16[2,3,512,256]{3,2,1,0:T(8,128)(2,1)}, bf16[2,3,512,256]{3,2,1,0:T(8,128)(2,1)S(1)}, u32[]{:S(2)}, u32[]{:S(2)}) collective-permute-start(bf16[2,3,512,256]{3,2,1,0:T(8,128)(2,1)} %pad_maximum_fusion.3), channel_id=1, source_target_pairs={{0,3},{1,0},{2,1},{3,2},{4,7},{5,4},{6,5},{7,6},{8,11},{9,8},{10,9... | collective-permute-start | bytes 4718600 | tf_op jit(solution)/shard_map/ppermute | solution.py:66
  8.4 74.9 %collective-permute-start.4 = (bf16[2,3,512,256]{3,2,1,0:T(8,128)(2,1)}, bf16[2,3,512,256]{3,2,1,0:T(8,128)(2,1)}, u32[]{:S(2)}, u32[]{:S(2)}) collective-permute-start(bf16[2,3,512,256]{3,2,1,0:T(8,128)(2,1)} %pad_maximum_fusion.3), channel_id=1, source_target_pairs={{0,1},{1,2},{2,3},{3,0},{4,5},{5,6},{6,7},{7,4},{8,9},{9,10},{10,1... | collective-permute-start | bytes 4718600 | tf_op jit(solution)/shard_map/ppermute | solution.py:66
  8.6 3.3 %copy-start.5 = (bf16[512,96]{0,1:T(8,128)(2,1)S(1)}, bf16[512,96]{0,1:T(8,128)(2,1)}, u32[]{:S(2)}) copy-start(bf16[512,96]{0,1:T(8,128)(2,1)} %param.13) | copy-start | bytes 294916
  8.6 3.3 %copy-start.13 = (f32[96,512]{1,0:T(8,128)S(1)}, f32[96,512]{1,0:T(8,128)}, u32[]{:S(2)}) copy-start(f32[96,512]{1,0:T(8,128)} %param.14) | copy-start | bytes 589828
  9.9 50.8 %collective-permute-start = (bf16[2,3,512,256]{3,2,1,0:T(8,128)(2,1)}, bf16[2,3,512,256]{3,2,1,0:T(8,128)(2,1)}, u32[]{:S(2)}, u32[]{:S(2)}) collective-permute-start(bf16[2,3,512,256]{3,2,1,0:T(8,128)(2,1)} %pad_maximum_fusion.1), channel_id=1, source_target_pairs={{0,12},{4,0},{8,4},{12,8},{1,13},{5,1},{9,5},{13,9},{2,14},{6,2},{... | collective-permute-start | bytes 4718600 | tf_op jit(solution)/shard_map/ppermute | solution.py:66
  10.4 82.5 %collective-permute-start.1 = (bf16[2,3,512,256]{3,2,1,0:T(8,128)(2,1)}, bf16[2,3,512,256]{3,2,1,0:T(8,128)(2,1)}, u32[]{:S(2)}, u32[]{:S(2)}) collective-permute-start(bf16[2,3,512,256]{3,2,1,0:T(8,128)(2,1)} %pad_maximum_fusion.1), channel_id=1, source_target_pairs={{0,4},{4,8},{8,12},{12,0},{1,5},{5,9},{9,13},{13,1},{2,6},{6,10},{... | collective-permute-start | bytes 4718600 | tf_op jit(solution)/shard_map/ppermute | solution.py:66
  14.3 10.9 %copy-start.15 = (s32[16,16]{1,0:T(8,128)S(1)}, s32[16,16]{1,0:T(8,128)}, u32[]{:S(2)}) copy-start(s32[16,16]{1,0:T(8,128)} %param.23) | copy-start | bytes 3076
  14.4 10.9 %copy-start.16 = (s32[16,16]{1,0:T(8,128)S(1)}, s32[16,16]{1,0:T(8,128)}, u32[]{:S(2)}) copy-start(s32[16,16]{1,0:T(8,128)} %param.22) | copy-start | bytes 3076
  19.4 14.2 %all-to-all-start.1 = ((f32[4,2,2,96,64]{3,4,2,1,0:T(8,128)}), f32[4,2,2,96,64]{3,4,2,1,0:T(8,128)S(1)}, u32[]{:S(2)}, u32[]{:S(2)}) async-start(f32[4,2,2,96,64]{3,4,2,1,0:T(8,128)} %copy.57), calls=%async_computation.1 | async-start | bytes 1048576 | tf_op jit(solution)/shard_map/all_to_all | solution.py:39
  25.5 12.9 %copy-start.11 = (s32[4,4,4,4]{3,2,1,0:T(4,128)}, s32[4,4,4,4]{3,2,1,0:T(4,128)S(1)}, u32[]{:S(2)}) copy-start(s32[4,4,4,4]{3,2,1,0:T(4,128)S(1)} %reshape.221) | copy-start | bytes 3076
  39.0 15.4 %copy-start.18 = (s32[1,512]{1,0:T(1,128)S(1)}, s32[1,512]{1,0:T(1,128)}, u32[]{:S(2)}) copy-start(s32[1,512]{1,0:T(1,128)} %param.17) | copy-start | bytes 6148
  43.7 10.6 %all-to-all-start.3 = ((bf16[4,2,2,96,64]{3,4,2,1,0:T(8,128)(2,1)}), bf16[4,2,2,96,64]{3,4,2,1,0:T(8,128)(2,1)S(1)}, u32[]{:S(2)}, u32[]{:S(2)}) async-start(bf16[4,2,2,96,64]{3,4,2,1,0:T(8,128)(2,1)} %copy.60), calls=%async_computation.3 | async-start | bytes 524288 | tf_op jit(solution)/shard_map/all_to_all | solution.py:39
  55.4 1.0 copy-start.14
  56.4 6.3 %copy-start.2 = (bf16[2,3,512,256]{3,2,1,0:T(8,128)(2,1)}, bf16[2,3,512,256]{3,2,1,0:T(8,128)(2,1)S(1)}, u32[]{:S(2)}) copy-start(bf16[2,3,512,256]{3,2,1,0:T(8,128)(2,1)S(1)} %collective-permute-done.3.refs_8_) | copy-start | bytes 4718596
  57.4 6.7 %copy-start.12 = (s32[4,4,4,4]{3,2,1,0:T(4,128)S(1)}, s32[4,4,4,4]{3,2,1,0:T(4,128)}, u32[]{:S(2)}) copy-start(s32[4,4,4,4]{3,2,1,0:T(4,128)} %copy-done.11) | copy-start | bytes 3076
  57.4 48.0 %collective-permute-start.19 = (bf16[3,512,256]{2,1,0:T(8,128)(2,1)}, bf16[3,512,256]{2,1,0:T(8,128)(2,1)S(1)}, u32[]{:S(2)}, u32[]{:S(2)}) collective-permute-start(bf16[3,512,256]{2,1,0:T(8,128)(2,1)} %slice_bitcast_fusion), channel_id=1, source_target_pairs={{0,3},{1,0},{2,1},{3,2},{4,7},{5,4},{6,5},{7,6},{8,11},{9,8},{10,9... | collective-permute-start | bytes 2359304 | tf_op jit(solution)/shard_map/ppermute | solution.py:66
  62.7 42.7 %collective-permute-start.18 = (bf16[3,512,256]{2,1,0:T(8,128)(2,1)}, bf16[3,512,256]{2,1,0:T(8,128)(2,1)}, u32[]{:S(2)}, u32[]{:S(2)}) collective-permute-start(bf16[3,512,256]{2,1,0:T(8,128)(2,1)} %slice_bitcast_fusion.1), channel_id=1, source_target_pairs={{0,12},{4,0},{8,4},{12,8},{1,13},{5,1},{9,5},{13,9},{2,14},{6,2},{... | collective-permute-start | bytes 2359304 | tf_op jit(solution)/shard_map/ppermute | solution.py:66
  64.0 7.6 %collective-permute-start.10 = (f32[112,512]{1,0:T(8,128)S(1)}, f32[112,512]{1,0:T(8,128)S(1)}, u32[]{:S(2)}, u32[]{:S(2)}) collective-permute-start(f32[112,512]{1,0:T(8,128)S(1)} %get-tuple-element.53), channel_id=1, source_target_pairs={{0,2},{1,3},{2,0},{3,1},{4,6},{5,7},{6,4},{7,5},{8,10},{9,11},{10,... | collective-permute-start | bytes 688136 | tf_op jit(solution)/shard_map/ppermute | solution.py:66
  71.6 16.1 %collective-permute-start.11 = (f32[112,512]{1,0:T(8,128)S(1)}, f32[112,512]{1,0:T(8,128)S(1)}, u32[]{:S(2)}, u32[]{:S(2)}) collective-permute-start(f32[112,512]{1,0:T(8,128)S(1)} %get-tuple-element.53), channel_id=1, source_target_pairs={{0,1},{1,2},{2,3},{3,0},{4,5},{5,6},{6,7},{7,4},{8,9},{9,10},{10,1... | collective-permute-start | bytes 688136 | tf_op jit(solution)/shard_map/ppermute | solution.py:66
  83.3 7.8 %collective-permute-start.6 = (f32[112,512]{1,0:T(8,128)S(1)}, f32[112,512]{1,0:T(8,128)S(1)}, u32[]{:S(2)}, u32[]{:S(2)}) collective-permute-start(f32[112,512]{1,0:T(8,128)S(1)} %get-tuple-element.54), channel_id=1, source_target_pairs={{0,12},{4,0},{8,4},{12,8},{1,13},{5,1},{9,5},{13,9},{2,14},{6,2},{... | collective-permute-start | bytes 688136 | tf_op jit(solution)/shard_map/ppermute | solution.py:66
  87.8 7.8 %collective-permute-start.7 = (f32[112,512]{1,0:T(8,128)S(1)}, f32[112,512]{1,0:T(8,128)S(1)}, u32[]{:S(2)}, u32[]{:S(2)}) collective-permute-start(f32[112,512]{1,0:T(8,128)S(1)} %get-tuple-element.54), channel_id=1, source_target_pairs={{0,8},{4,12},{8,0},{12,4},{1,9},{5,13},{9,1},{13,5},{2,10},{6,14},... | collective-permute-start | bytes 688136 | tf_op jit(solution)/shard_map/ppermute | solution.py:66
  91.1 7.8 %collective-permute-start.8 = (f32[112,512]{1,0:T(8,128)S(1)}, f32[112,512]{1,0:T(8,128)S(1)}, u32[]{:S(2)}, u32[]{:S(2)}) collective-permute-start(f32[112,512]{1,0:T(8,128)S(1)} %get-tuple-element.54), channel_id=1, source_target_pairs={{0,4},{4,8},{8,12},{12,0},{1,5},{5,9},{9,13},{13,1},{2,6},{6,10},{... | collective-permute-start | bytes 688136 | tf_op jit(solution)/shard_map/ppermute | solution.py:66
  92.8 12.6 %collective-permute-start.9 = (f32[112,512]{1,0:T(8,128)S(1)}, f32[112,512]{1,0:T(8,128)S(1)}, u32[]{:S(2)}, u32[]{:S(2)}) collective-permute-start(f32[112,512]{1,0:T(8,128)S(1)} %get-tuple-element.53), channel_id=1, source_target_pairs={{0,3},{1,0},{2,1},{3,2},{4,7},{5,4},{6,5},{7,6},{8,11},{9,8},{10,9... | collective-permute-start | bytes 688136 | tf_op jit(solution)/shard_map/ppermute | solution.py:66
  95.6 48.5 %collective-permute-start.5 = (bf16[3,512,256]{2,1,0:T(8,128)(2,1)S(1)}, bf16[3,512,256]{2,1,0:T(8,128)(2,1)S(1)}, u32[]{:S(2)}, u32[]{:S(2)}) collective-permute-start(bf16[3,512,256]{2,1,0:T(8,128)(2,1)S(1)} %slice_bitcast_fusion.2), channel_id=1, source_target_pairs={{0,1},{1,2},{2,3},{3,0},{4,5},{5,6},{6,7},{7,4},{8,9},{9,10},{10,1... | collective-permute-start | bytes 2359304 | tf_op jit(solution)/shard_map/ppermute | solution.py:66
  98.9 45.2 %collective-permute-start.2 = (bf16[3,512,256]{2,1,0:T(8,128)(2,1)S(1)}, bf16[3,512,256]{2,1,0:T(8,128)(2,1)S(1)}, u32[]{:S(2)}, u32[]{:S(2)}) collective-permute-start(bf16[3,512,256]{2,1,0:T(8,128)(2,1)S(1)} %slice_bitcast_fusion.5), channel_id=1, source_target_pairs={{0,4},{4,8},{8,12},{12,0},{1,5},{5,9},{9,13},{13,1},{2,6},{6,10},{... | collective-permute-start | bytes 2359304 | tf_op jit(solution)/shard_map/ppermute | solution.py:66
  105.4 0.9 copy-start.6
  138.6 40.3 %collective-permute-start.20 = (bf16[3,512,256]{2,1,0:T(8,128)(2,1)S(1)}, bf16[3,512,256]{2,1,0:T(8,128)(2,1)S(1)}, u32[]{:S(2)}, u32[]{:S(2)}) collective-permute-start(bf16[3,512,256]{2,1,0:T(8,128)(2,1)S(1)} %get-tuple-element.31), channel_id=1, source_target_pairs={{0,4},{4,8},{8,12},{12,0},{1,5},{5,9},{9,13},{13,1},{2,6},{6,10},{... | collective-permute-start | bytes 2359304 | tf_op jit(solution)/shard_map/ppermute | solution.py:70
  141.1 40.2 %collective-permute-start.21 = (bf16[3,512,256]{2,1,0:T(8,128)(2,1)S(1)}, bf16[3,512,256]{2,1,0:T(8,128)(2,1)S(1)}, u32[]{:S(2)}, u32[]{:S(2)}) collective-permute-start(bf16[3,512,256]{2,1,0:T(8,128)(2,1)S(1)} %get-tuple-element.32), channel_id=1, source_target_pairs={{0,8},{4,12},{8,0},{12,4},{1,9},{5,13},{9,1},{13,5},{2,10},{6,14},... | collective-permute-start | bytes 2359304 | tf_op jit(solution)/shard_map/ppermute | solution.py:70
  141.6 39.8 %collective-permute-start.22 = (bf16[3,512,256]{2,1,0:T(8,128)(2,1)}, bf16[3,512,256]{2,1,0:T(8,128)(2,1)S(1)}, u32[]{:S(2)}, u32[]{:S(2)}) collective-permute-start(bf16[3,512,256]{2,1,0:T(8,128)(2,1)} %get-tuple-element.33), channel_id=1, source_target_pairs={{0,12},{4,0},{8,4},{12,8},{1,13},{5,1},{9,5},{13,9},{2,14},{6,2},{... | collective-permute-start | bytes 2359304 | tf_op jit(solution)/shard_map/ppermute | solution.py:70
  144.1 2.5 %copy-start.7 = (bf16[3,512,256]{2,1,0:T(8,128)(2,1)}, bf16[3,512,256]{2,1,0:T(8,128)(2,1)S(1)}, u32[]{:S(2)}) copy-start(bf16[3,512,256]{2,1,0:T(8,128)(2,1)S(1)} %collective-permute-done.5.refs_9_) | copy-start | bytes 2359300
  144.1 40.7 %collective-permute-start.23 = (bf16[3,512,256]{2,1,0:T(8,128)(2,1)}, bf16[3,512,256]{2,1,0:T(8,128)(2,1)S(1)}, u32[]{:S(2)}, u32[]{:S(2)}) collective-permute-start(bf16[3,512,256]{2,1,0:T(8,128)(2,1)} %get-tuple-element.34), channel_id=1, source_target_pairs={{0,1},{1,2},{2,3},{3,0},{4,5},{5,6},{6,7},{7,4},{8,9},{9,10},{10,1... | collective-permute-start | bytes 2359304 | tf_op jit(solution)/shard_map/ppermute | solution.py:70
  144.1 2.5 %copy-start.8 = (bf16[3,512,256]{2,1,0:T(8,128)(2,1)}, bf16[3,512,256]{2,1,0:T(8,128)(2,1)S(1)}, u32[]{:S(2)}) copy-start(bf16[3,512,256]{2,1,0:T(8,128)(2,1)S(1)} %collective-permute-done.2.refs_6_) | copy-start | bytes 2359300
  144.1 34.8 %copy-start.17 = (bf16[3,512,256]{2,1,0:T(8,128)(2,1)S(1)}, bf16[3,512,256]{2,1,0:T(8,128)(2,1)}, u32[]{:S(2)}) copy-start(bf16[3,512,256]{2,1,0:T(8,128)(2,1)} %get-tuple-element.36) | copy-start | bytes 2359300
  144.1 40.6 %collective-permute-start.24 = (bf16[3,512,256]{2,1,0:T(8,128)(2,1)}, bf16[3,512,256]{2,1,0:T(8,128)(2,1)S(1)}, u32[]{:S(2)}, u32[]{:S(2)}) collective-permute-start(bf16[3,512,256]{2,1,0:T(8,128)(2,1)} %get-tuple-element.35), channel_id=1, source_target_pairs={{0,2},{1,3},{2,0},{3,1},{4,6},{5,7},{6,4},{7,5},{8,10},{9,11},{10,... | collective-permute-start | bytes 2359304 | tf_op jit(solution)/shard_map/ppermute | solution.py:70
  178.9 27.0 %collective-permute-start.25 = (bf16[3,512,256]{2,1,0:T(8,128)(2,1)S(1)}, bf16[3,512,256]{2,1,0:T(8,128)(2,1)S(1)}, u32[]{:S(2)}, u32[]{:S(2)}) collective-permute-start(bf16[3,512,256]{2,1,0:T(8,128)(2,1)S(1)} %copy-done.17), channel_id=1, source_target_pairs={{0,3},{1,0},{2,1},{3,2},{4,7},{5,4},{6,5},{7,6},{8,11},{9,8},{10,9... | collective-permute-start | bytes 2359304 | tf_op jit(solution)/shard_map/ppermute | solution.py:70
  181.3 25.6 %collective-permute-start.12 = (bf16[3,512,256]{2,1,0:T(8,128)(2,1)S(1)}, bf16[3,512,256]{2,1,0:T(8,128)(2,1)S(1)}, u32[]{:S(2)}, u32[]{:S(2)}) collective-permute-start(bf16[3,512,256]{2,1,0:T(8,128)(2,1)S(1)} %get-tuple-element.24), channel_id=1, source_target_pairs={{0,4},{4,8},{8,12},{12,0},{1,5},{5,9},{9,13},{13,1},{2,6},{6,10},{... | collective-permute-start | bytes 2359304 | tf_op jit(solution)/shard_map/ppermute | solution.py:70
  181.3 32.2 %collective-permute-start.13 = (bf16[3,512,256]{2,1,0:T(8,128)(2,1)S(1)}, bf16[3,512,256]{2,1,0:T(8,128)(2,1)S(1)}, u32[]{:S(2)}, u32[]{:S(2)}) collective-permute-start(bf16[3,512,256]{2,1,0:T(8,128)(2,1)S(1)} %get-tuple-element.25), channel_id=1, source_target_pairs={{0,8},{4,12},{8,0},{12,4},{1,9},{5,13},{9,1},{13,5},{2,10},{6,14},... | collective-permute-start | bytes 2359304 | tf_op jit(solution)/shard_map/ppermute | solution.py:70
  184.8 28.8 %collective-permute-start.14 = (bf16[3,512,256]{2,1,0:T(8,128)(2,1)}, bf16[3,512,256]{2,1,0:T(8,128)(2,1)S(1)}, u32[]{:S(2)}, u32[]{:S(2)}) collective-permute-start(bf16[3,512,256]{2,1,0:T(8,128)(2,1)} %get-tuple-element.26), channel_id=1, source_target_pairs={{0,12},{4,0},{8,4},{12,8},{1,13},{5,1},{9,5},{13,9},{2,14},{6,2},{... | collective-permute-start | bytes 2359304 | tf_op jit(solution)/shard_map/ppermute | solution.py:70
  184.8 28.8 %collective-permute-start.15 = (bf16[3,512,256]{2,1,0:T(8,128)(2,1)}, bf16[3,512,256]{2,1,0:T(8,128)(2,1)S(1)}, u32[]{:S(2)}, u32[]{:S(2)}) collective-permute-start(bf16[3,512,256]{2,1,0:T(8,128)(2,1)} %get-tuple-element.27), channel_id=1, source_target_pairs={{0,1},{1,2},{2,3},{3,0},{4,5},{5,6},{6,7},{7,4},{8,9},{9,10},{10,1... | collective-permute-start | bytes 2359304 | tf_op jit(solution)/shard_map/ppermute | solution.py:70
  205.9 4.0 %copy-start.10 = (bf16[3,512,256]{2,1,0:T(8,128)(2,1)}, bf16[3,512,256]{2,1,0:T(8,128)(2,1)S(1)}, u32[]{:S(2)}) copy-start(bf16[3,512,256]{2,1,0:T(8,128)(2,1)S(1)} %collective-permute-done.25.refs_6_) | copy-start | bytes 2359300
  205.9 13.7 %collective-permute-start.16 = (bf16[3,512,256]{2,1,0:T(8,128)(2,1)}, bf16[3,512,256]{2,1,0:T(8,128)(2,1)S(1)}, u32[]{:S(2)}, u32[]{:S(2)}) collective-permute-start(bf16[3,512,256]{2,1,0:T(8,128)(2,1)} %get-tuple-element.28), channel_id=1, source_target_pairs={{0,2},{1,3},{2,0},{3,1},{4,6},{5,7},{6,4},{7,5},{8,10},{9,11},{10,... | collective-permute-start | bytes 2359304 | tf_op jit(solution)/shard_map/ppermute | solution.py:70
  206.9 22.2 %collective-permute-start.17 = (bf16[3,512,256]{2,1,0:T(8,128)(2,1)}, bf16[3,512,256]{2,1,0:T(8,128)(2,1)S(1)}, u32[]{:S(2)}, u32[]{:S(2)}) collective-permute-start(bf16[3,512,256]{2,1,0:T(8,128)(2,1)} %get-tuple-element.29), channel_id=1, source_target_pairs={{0,3},{1,0},{2,1},{3,2},{4,7},{5,4},{6,5},{7,6},{8,11},{9,8},{10,9... | collective-permute-start | bytes 2359304 | tf_op jit(solution)/shard_map/ppermute | solution.py:70
  229.1 0.9 copy-start.9
  230.0 3.6 %copy-start.1 = (bf16[2,512,512]{2,1,0:T(8,128)(2,1)S(1)}, bf16[2,512,512]{2,1,0:T(8,128)(2,1)}, u32[]{:S(2)}) copy-start(bf16[2,512,512]{2,1,0:T(8,128)(2,1)} %param.12) | copy-start | bytes 3145732

commit v3 on v2

v3 whole, which is shorter than its diff:
```python
import functools
import math

import jax
import jax.numpy as jnp
from jax import lax
from jax.experimental import pallas as pl
from jax.experimental.pallas import tpu as pltpu
from jax.sharding import Mesh
from jax.sharding import PartitionSpec as P

KB = 128
SIDE = 4
MEMBER = ("y", "core")
LOSS_SCALE = 4096.0
FAIR_EPS = 0.05
NORM_EPS = 1e-06
LOG2E = math.log2(math.e)
F32 = jnp.float32
BF16 = jnp.bfloat16


def score_kernel(forecast_ref, truth_ref, area_ref, out_ref):
    groups, _, lanes = forecast_ref.shape
    count = 2 * groups
    swapped = [pltpu.roll(forecast_ref[j], lanes // 2, 1) for j in range(groups)]

    def unit(x):
        return x * (1.0 / jnp.sqrt(jnp.sum(x * x, axis=0, keepdims=True) + NORM_EPS))

    weight = LOSS_SCALE * area_ref[...]
    for j in range(groups):
        one = forecast_ref[j]
        total = unit(one - swapped[j])
        for k in range(groups):
            if k != j:
                total = total + unit(one - forecast_ref[k]) + unit(one - swapped[k])
        gradient = weight * (
            unit(one - truth_ref[...]) / count - (1.0 - FAIR_EPS) / (count * (count - 1)) * total
        )
        out_ref[j] = gradient.astype(BF16)


def score_gradient(forecasts, truth, area):
    return pl.pallas_call(
        score_kernel, out_shape=jax.ShapeDtypeStruct(forecasts.shape, BF16), name="score_gradient"
    )(forecasts, truth, area)


def two_parts(x):
    high = x.astype(BF16)
    return [high, (x - lax.reduce_precision(x, 8, 7)).astype(BF16)]


def fetched(x, axis, distance):
    return lax.ppermute(x, axis, [(i, (i - distance) % SIDE) for i in range(SIDE)])


def delivered(x, axis, distance):
    return lax.ppermute(x, axis, [(i, (i + distance) % SIDE) for i in range(SIDE)])


def head_pair_tiles(table, base, kv, queries, lates, decoder, out, scratch):
    q_stack, g_stack, stat_rows, joined, dk_acc, dv_acc, dq_acc = scratch
    rows = q_stack.shape[1] // 2
    channels = decoder.shape[1]
    head = pl.program_id(0) * 2 + base
    head_dim = 64
    score_scale = head_dim ** (-0.5)
    lane = lax.broadcasted_iota(jnp.int32, (rows, 2 * head_dim), 1)
    first = lane < head_dim
    nt = (((1,), (1,)), ((), ()))
    tn = (((0,), (1,)), ((), ()))
    for t in range(SIDE):
        q = queries[t][...].astype(F32)
        g = lax.dot_general(
            lates[t][:channels, :], decoder[...], tn, preferred_element_type=F32
        )
        q_stack[t, :rows] = jnp.where(first, q, 0.0).astype(BF16)
        q_stack[t, rows:] = jnp.where(first, 0.0, q).astype(BF16)
        g_stack[t, :rows] = jnp.where(first, g, 0.0).astype(BF16)
        g_stack[t, rows:] = jnp.where(first, 0.0, g).astype(BF16)
        stat = lates[t][channels:, :].astype(F32)
        joined[: stat.shape[0] // 2] = stat[: stat.shape[0] // 2] + stat[stat.shape[0] // 2 :]
        for n in range(2):
            stat_rows[t, n : n + 1, :rows] = joined[pl.ds(8 * n + head, 1), :]
            stat_rows[t, n : n + 1, rows:] = joined[pl.ds(8 * n + head + 1, 1), :]
    dk_acc[...] = jnp.zeros_like(dk_acc)
    dv_acc[...] = jnp.zeros_like(dv_acc)

    def one_query_block(t, carry):
        q = q_stack[t]
        g = g_stack[t]
        lse = stat_rows[t, 0:1, :] * LOG2E
        delta = stat_rows[t, 1:2, :]
        dq_acc[...] = jnp.zeros_like(dq_acc)
        for pair in ((0, 1), (2, 3)):
            starts = [pl.multiple_of(table[t * SIDE + a] * KB, KB) for a in pair]
            k = jnp.concatenate([kv[a][0][pl.ds(s, KB), :] for a, s in zip(pair, starts)], axis=0)
            v = jnp.concatenate([kv[a][1][pl.ds(s, KB), :] for a, s in zip(pair, starts)], axis=0)
            scores = lax.dot_general(k, q, nt, preferred_element_type=F32)
            p = jnp.exp2(scores * (score_scale * LOG2E) - lse)
            dp = lax.dot_general(v, g, nt, preferred_element_type=F32)
            ds = (p * (dp - delta)).astype(BF16)
            dv = jnp.dot(p.astype(BF16), g, preferred_element_type=F32)
            dk = jnp.dot(ds, q, preferred_element_type=F32)
            for n, (a, s) in enumerate(zip(pair, starts)):
                dv_acc[a, pl.ds(s, KB), :] += dv[n * KB : (n + 1) * KB]
                dk_acc[a, pl.ds(s, KB), :] += dk[n * KB : (n + 1) * KB]
            kt = k.T
            dq_acc[:head_dim] += jnp.dot(kt[:head_dim], ds[:, :rows], preferred_element_type=F32)
            dq_acc[head_dim:] += jnp.dot(kt[head_dim:], ds[:, rows:], preferred_element_type=F32)
        dq = dq_acc[...].T * score_scale
        for n in range(SIDE):

            @pl.when(t == n)
            def _():
                out(2, n, dq)

        return carry

    lax.fori_loop(0, SIDE, one_query_block, 0)
    for a in range(SIDE):
        out(0, a, dk_acc[a] * score_scale)
        out(1, a, dv_acc[a])


def tile_kernel(table, *refs, base):
    key_own, value_own, query_own, late_own, decoder = refs[0:5]
    fetch_x, fetch_z = refs[5:8], refs[8:11]
    late_x, late_z = refs[11:14], refs[14:17]
    send_x, own_z, send_z = refs[17], refs[18], refs[19:22]
    scratch = refs[22:]
    sides = ((fetch_x, late_x), (fetch_z, late_z))
    for m in range(2):
        key_fetch = sides[m][0]
        query_fetch, late = sides[1 - m]
        kv = [(key_own.at[m], value_own.at[m])] + [(r.at[0], r.at[1]) for r in key_fetch]
        queries = [query_own.at[m]] + [r.at[2] for r in query_fetch]
        lates = [late_own.at[m]] + list(late)

        def out(kind, n, value, m=m):
            if m == (1 if kind == 2 else 0):
                send_x[table[2, n], kind] = value.astype(BF16)
            elif n == 0:
                own_z[kind] = value
            else:
                send_z[n - 1][kind] = value.astype(BF16)

        head_pair_tiles(
            table.at[m], base, kv, queries, lates, decoder, out, scratch
        )


def attention_tiles(half, tables, key_rows, value_rows, query, fetched_x, fetched_z, late_own, late_x, late_z, decoder_matrix):
    members, rows, width = key_rows.shape
    stats, channels = late_own.shape[1], decoder_matrix.shape[1]
    pairs = width // 256
    base = half * pairs
    own_spec = pl.BlockSpec((members, rows, 128), lambda h, tab: (0, 0, base + h))
    near_spec = pl.BlockSpec((None, 3, rows, 128), lambda h, tab: (half, 0, 0, h))
    once_spec = pl.BlockSpec((None, 3, rows, 128), lambda h, tab: (0, 0, 0, h))
    far_spec = pl.BlockSpec((3, rows, 128), lambda h, tab: (0, 0, h))
    fetch_specs = [near_spec, once_spec, near_spec]
    late_spec = pl.BlockSpec((stats, rows), lambda h, tab: (0, 0))
    out = pl.pallas_call(
        functools.partial(tile_kernel, base=2 * base),
        out_shape=[
            jax.ShapeDtypeStruct((SIDE, 3, rows, width // 2), BF16),
            jax.ShapeDtypeStruct((3, rows, width // 2), F32),
        ]
        + [jax.ShapeDtypeStruct((3, rows, width // 2), BF16)] * 3,
        grid_spec=pltpu.PrefetchScalarGridSpec(
            num_scalar_prefetch=1,
            grid=(pairs,),
            in_specs=[own_spec] * 3
            + [
                pl.BlockSpec((members, stats, rows), lambda h, tab: (0, 0, 0)),
                pl.BlockSpec((128, channels), lambda h, tab: (base + h, 0)),
            ]
            + fetch_specs * 2
            + [late_spec] * 6,
            out_specs=[pl.BlockSpec((SIDE, 3, rows, 128), lambda h, tab: (0, 0, 0, h))]
            + [far_spec] * 4,
            scratch_shapes=[
                pltpu.VMEM((SIDE, 2 * rows, 128), BF16),
                pltpu.VMEM((SIDE, 2 * rows, 128), BF16),
                pltpu.VMEM((SIDE, 2, 2 * rows), F32),
                pltpu.VMEM((16, rows), F32),
                pltpu.VMEM((SIDE, rows, 128), F32),
                pltpu.VMEM((SIDE, rows, 128), F32),
                pltpu.VMEM((128, rows), F32),
            ],
        ),
        compiler_params=pltpu.CompilerParams(
            dimension_semantics=("arbitrary",), vmem_limit_bytes=50 * 1024 * 1024
        ),
        cost_estimate=pl.CostEstimate(
            flops=5 * 2 * (SIDE * SIDE * KB) * rows * 128 * 4 * pairs * members,
            transcendentals=SIDE * SIDE * KB * rows * 2 * pairs * members,
            bytes_accessed=20 * 1024 * 1024,
        ),
        name="attention_tiles",
    )(tables, key_rows, value_rows, query, late_own, decoder_matrix, *fetched_x, *fetched_z, *late_x, *late_z)
    return out[0], out[1], out[2:]


def sum_kernel(got_x, own_z, *refs):
    got_z, outs = refs[:3], refs[-3:]
    for kind, ref in enumerate(outs):
        along_x = got_x[0, kind].astype(F32)
        for n in range(1, SIDE):
            along_x = along_x + got_x[n, kind].astype(F32)
        along_z = own_z[kind]
        for got in got_z:
            along_z = along_z + got[kind].astype(F32)
        ref[1 if kind == 2 else 0] = along_x
        ref[0 if kind == 2 else 1] = along_z


def summed(half, got_x, own_z, got_z, outs):
    _, rows, lanes = own_z.shape
    z_spec = pl.BlockSpec((3, rows // 2, lanes), lambda r: (0, r, 0))
    shape = jax.ShapeDtypeStruct((2, rows, 2 * lanes), F32)
    kept = list(outs) if outs else []
    return pl.pallas_call(
        sum_kernel,
        out_shape=[shape] * 3,
        grid=(2,),
        in_specs=[pl.BlockSpec((SIDE, 3, rows // 2, lanes), lambda r: (0, 0, r, 0))]
        + [z_spec] * 4
        + [pl.BlockSpec(memory_space=pl.ANY)] * len(kept),
        out_specs=[pl.BlockSpec((2, rows // 2, lanes), lambda r: (0, r, half))] * 3,
        input_output_aliases={5 + n: n for n in range(len(kept))},
        compiler_params=pltpu.CompilerParams(vmem_limit_bytes=50 * 1024 * 1024),
        name="summed",
    )(got_x, own_z, *got_z, *kept)


def ring_far(after, before, axis):
    return fetched(after[0:1], axis, 1), fetched(before[1:2], axis, 3)


def outgoing(keys, values, queries):
    stacked = jnp.stack([keys, values, queries])
    kinds, rows, width = stacked.shape
    return jnp.stack([stacked[..., : width // 2], stacked[..., width // 2 :]])


def shards(
    hidden_embedding,
    decoder_matrix,
    baseline_field,
    truth_field,
    cell_surface_share,
    node_order,
    query,
    key_rows,
    value_rows,
    row_lse,
    kv_owner,
    kv_local,
):
    members, nodes, width = hidden_embedding.shape
    heads = row_lse.shape[1]
    x_at = lax.axis_index("x")
    z_at = lax.axis_index("z")

    own_x = outgoing(key_rows[0], value_rows[0], query[1])
    own_z = outgoing(key_rows[1], value_rows[1], query[0])
    near = [fetched(own_x, "x", 1), fetched(own_x, "x", 3), fetched(own_z, "z", 1), fetched(own_z, "z", 3)]

    forecast = baseline_field[None] + jnp.einsum(
        "mou,ut->mto", hidden_embedding, decoder_matrix, preferred_element_type=F32
    )
    groups = lax.axis_size(MEMBER)
    span = nodes // groups
    channels = forecast.shape[1]
    offset = lax.axis_index(MEMBER) * span
    by_node = forecast.reshape(members, channels, groups, span).transpose(2, 1, 0, 3)
    everyone = lax.all_to_all(
        by_node.reshape(groups, channels, members * span), MEMBER, 0, 0, tiled=True
    )
    observed = lax.dynamic_slice_in_dim(truth_field, offset, span, 1)
    area = lax.dynamic_slice_in_dim(cell_surface_share, offset, span, 0)
    derivative = score_gradient(
        everyone, jnp.tile(observed, (1, members)), jnp.tile(area[None], (1, members))
    )
    returned = lax.all_to_all(derivative, MEMBER, 0, 0, tiled=True)
    returned, *near = lax.optimization_barrier((returned, *near))
    x_after, x_before, z_after, z_before = near
    x_far, z_far = ring_far(x_after, x_before, "x"), ring_far(z_after, z_before, "z")
    grad_forecast = (
        returned.reshape(groups, channels, members, span)
        .transpose(2, 1, 0, 3)
        .reshape(members, channels, nodes)
    )

    shard_ids = jnp.arange(SIDE * SIDE, dtype=jnp.int32)
    around = jnp.arange(SIDE, dtype=jnp.int32)
    named = jnp.sum(
        jnp.where(kv_owner[:, :, None] == shard_ids[None, None, :], kv_local[:, :, None], 0), axis=1
    ).reshape(SIDE, SIDE, SIDE, SIDE)
    x_near = ((x_at + around) % SIDE)[:, None] == around[None, :]
    z_near = ((z_at + around) % SIDE)[:, None] == around[None, :]
    x_here, z_here = x_near[0], z_near[0]

    def picked(sx, sz, ox, oz):
        chosen = (
            sx[:, None, None, None, :, None, None, None]
            & sz[None, :, None, None, None, :, None, None]
            & ox[None, None, :, None, None, None, :, None]
            & oz[None, None, None, :, None, None, None, :]
        )
        return jnp.sum(jnp.where(chosen, named, 0), axis=(4, 5, 6, 7)).reshape(-1)

    tables = jnp.stack(
        [
            picked(x_here[None], z_near, x_near, z_here[None]),
            picked(x_near, z_here[None], x_here[None], z_near),
            jnp.pad((x_at + around) % SIDE, (0, SIDE * (SIDE - 1))),
        ]
    )

    permuter = (node_order[0][:, None] == jnp.arange(nodes, dtype=jnp.int32)[None, :]).astype(BF16)
    grad_columns = jnp.einsum(
        "mcg,tg->mct", grad_forecast, permuter, preferred_element_type=F32
    ).astype(BF16)
    grad_latent = jnp.einsum(
        "wc,mct->mwt", decoder_matrix, grad_columns, preferred_element_type=F32
    ).astype(BF16)
    saved = jnp.einsum("mgw,tg->mwt", hidden_embedding, permuter, preferred_element_type=F32).astype(
        BF16
    )
    split = (members, heads, width // heads, nodes)
    delta = jnp.sum(
        grad_latent.astype(F32).reshape(split) * saved.astype(F32).reshape(split), axis=2
    )
    late_own = jnp.concatenate(
        [grad_columns] + [part[n] for n in range(2) for part in (two_parts(row_lse), two_parts(delta))],
        axis=1,
    )
    late_z = [fetched(late_own[0], "z", d) for d in (1, 2, 3)]
    late_x = [fetched(late_own[1], "x", d) for d in (1, 2, 3)]

    outs = None
    parts = []
    for half in range(2):
        send_x, own, send_z = attention_tiles(
            half,
            tables,
            key_rows,
            value_rows,
            query,
            (x_after, x_far[half], x_before),
            (z_after, z_far[half], z_before),
            late_own,
            late_x,
            late_z,
            decoder_matrix,
        )
        if parts:
            (first_x, first_own, first_z) = parts[0]
            send_x, send_z, first_x, first_z = lax.optimization_barrier(
                (send_x, send_z, first_x, first_z)
            )
            parts[0] = (first_x, first_own, first_z)
        got_x = lax.all_to_all(send_x, "x", 0, 0, tiled=True)
        got_z = [delivered(send_z[d - 1], "z", d) for d in (1, 2, 3)]
        parts.append((got_x, own, got_z))
    for half, part in enumerate(parts):
        outs = summed(half, *part, outs)
    grad_key, grad_value, grad_query = outs
    return grad_query, grad_key, grad_value


def solution(mesh):
    finer = Mesh(mesh.devices.reshape(4, 2, SIDE, SIDE), ("y", "core", "x", "z"))
    plane = ("x", "z")
    in_specs = (
        P(MEMBER, plane, None),
        P(),
        P(None, plane),
        P(None, plane),
        P(plane),
        P(plane, None),
        P(MEMBER, plane, None),
        P(MEMBER, plane, None),
        P(MEMBER, plane, None),
        P(MEMBER, None, plane),
        P(),
        P(),
    )
    out_specs = (P(MEMBER, plane, None), P(MEMBER, plane, None), P(MEMBER, plane, None))
    return jax.shard_map(
        shards, mesh=finer, in_specs=in_specs, out_specs=out_specs, check_vma=False
    )
```

time: 234 us -> 210 us (0.90)
  local copies, waits for them, and re-layouts: 13.6 us -> 29.8 us
  starting transfers between devices: 62.7 us -> 48 us
  waiting for transfers between devices: 62.1 us -> 48.3 us
  blocking collectives: 8.1 us -> 0 us
  other arithmetic: 11.1 us -> 4.93 us
  Pallas kernels: 71.8 us -> 74.3 us
    ppermute x14, starting transfers between devices: 36.9 us -> 20.4 us  [fetched(): lax.ppermute(x, axis, [(i, (i - distance) % SIDE) for i in range(SIDE)])]
    ppermute x12 -> x6, waiting for transfers between devices: 36.6 us -> 20.7 us  [delivered(): lax.ppermute(x, axis, [(i, (i + distance) % SIDE) for i in range(SIDE)])]
    unnamed x39 -> x57, local copies, waits for them, and re-layouts: 2.38 us -> 16 us
    all_to_all x2 -> x4, starting transfers between devices: 7.87 us -> 18.4 us  [the longest x2 10.5 us: shards(): got_x = lax.all_to_all(send_x, 'x', 0, 0, tiled=True)]
    ppermute x12 -> x6, starting transfers between devices: 17.9 us -> 9.29 us  [delivered(): lax.ppermute(x, axis, [(i, (i + distance) % SIDE) for i in range(SIDE)])]
    all_to_all x2 -> x0, blocking collectives: 8.1 us -> none  [moved_by_axis(): filled = lax.all_to_all(filled, axes[k], k, k, tiled=True)]
    slice x3 -> x7, local copies, waits for them, and re-layouts: 1.56 us -> 8.94 us  [the longest x4 7.38 us: ring_far(): return (fetched(after[0:1], axis, 1), fetched(before[1:2], axis, 3))]
    squeeze x4 -> x0, local copies, waits for them, and re-layouts: 5.44 us -> none  [the longest x2 3.07 us: ring_fetched(): after[0]]
  transfers between devices with their start and end apart: 28 -> 24, of which waited for: 9 -> 9; matrix products, arithmetic and copies ran while one was open for 10% -> 7% of each run, Pallas kernels for 29% -> 34%
where the time goes in v3:
time: 210 us; the launch traced here: 209 us
  Pallas kernels  74.3 us (35%)
  waiting for transfers between devices  48.3 us (23%)
  starting transfers between devices  48 us (23%)
  local copies, waits for them, and re-layouts  29.8 us (14%)
  other arithmetic  4.93 us (2%)
  matrix products  2.35 us (1%)
    pallas_call x2, Pallas kernels, attention_tiles(): pl.pallas_call(functools.partial(tile_kernel, base=2 * base), out_shape=[...  64 us
    ppermute x6, waiting for transfers between devices, delivered(): lax.ppermute(x, axis, [(i, (i + distance) % SIDE) for i in range(SIDE)])  20.7 us
    ppermute x14, starting transfers between devices, fetched(): lax.ppermute(x, axis, [(i, (i - distance) % SIDE) for i in range(SIDE)])  20.4 us
    ppermute x14, waiting for transfers between devices, fetched(): lax.ppermute(x, axis, [(i, (i - distance) % SIDE) for i in range(SIDE)])  16.5 us
    unnamed x57, local copies, waits for them, and re-layouts  16 us
    all_to_all x2, starting transfers between devices, shards(): got_x = lax.all_to_all(send_x, 'x', 0, 0, tiled=True)  10.5 us
    ppermute x6, starting transfers between devices, delivered(): lax.ppermute(x, axis, [(i, (i + distance) % SIDE) for i in range(SIDE)])  9.29 us
    slice x4, local copies, waits for them, and re-layouts, ring_far(): return (fetched(after[0:1], axis, 1), fetched(before[1:2], axis, 3))  7.38 us
  transfers between devices with their start and end apart: 24, of which 9 were waited for; matrix products, arithmetic and copies ran while one was open for 7% of the time, Pallas kernels for 34%

profile of v3, /device:TPU:2, one launch (start us, length us, event | category | flops | bytes accessed | tf_op | source)
XLA Modules:
  0.0 208.7 jit_solution(13360667439027551884)
XLA Ops:
  0.7 1.4 fusion.18
  3.1 1.3 pad_maximum_fusion.3
  4.4 1.9 collective-permute-start.3
  6.3 2.1 %collective-permute-start.2 = (bf16[2,3,512,256]{3,2,1,0:T(8,128)(2,1)}, bf16[2,3,512,256]{3,2,1,0:T(8,128)(2,1)}, u32[]{:S(2)}, u32[]{:S(2)}) collective-permute-start(bf16[2,3,512,256]{3,2,1,0:T(8,128)(2,1)} %pad_maximum_fusion.3), channel_id=1, source_target_pairs={{0,3},{1,0},{2,1},{3,2},{4,7},{5,4},{6,5},{7,6},{8,11},{9,8},{10,9... | collective-permute-start | bytes 4718600 | tf_op jit(solution)/shard_map/ppermute | solution.py:56
  8.6 1.3 pad_maximum_fusion.1
  9.9 1.5 collective-permute-start.1
  12.6 0.9 copy.36
  13.6 4.5 %all-to-all-start = ((f32[8,96,128]{2,1,0:T(8,128)}), f32[8,96,128]{2,1,0:T(8,128)S(1)}, u32[]{:S(2)}, u32[]{:S(2)}) async-start(f32[8,96,128]{2,1,0:T(8,128)} %copy.36), calls=%async_computation | async-start | bytes 786432 | tf_op jit(solution)/shard_map/all_to_all | solution.py:281
  18.4 0.9 constant_dynamic-slice_fusion
  19.2 0.8 dynamic_slice.7
  20.0 0.7 tile.20.area_ref
  20.8 0.7 copy.38.truth_ref
  21.9 5.1 %all-to-all-done.forecast_ref = f32[8,96,128]{2,1,0:T(8,128)S(1)} async-done(((f32[8,96,128]{2,1,0:T(8,128)}), f32[8,96,128]{2,1,0:T(8,128)S(1)}, u32[]{:S(2)}, u32[]{:S(2)}) %all-to-all-start) | async-done | bytes 393248 | tf_op jit(solution)/shard_map/all_to_all | solution.py:281
  27.0 0.7 copy-done.19
  27.7 3.3 %score_gradient.1 = bf16[8,96,128]{2,1,0:T(8,128)(2,1)} custom-call(f32[8,96,128]{2,1,0:T(8,128)} %copy-done.19, f32[96,128]{1,0:T(8,128)} %copy.38.truth_ref, f32[1,128]{1,0:T(1,128)} %tile.20.area_ref), custom_call_target="tpu_custom_call" | custom-call | tf_op jit(solution)/shard_map/score_gradient/pallas_call | solution.py:45
  31.0 3.4 %all-to-all-start.1 = ((bf16[8,96,128]{2,1,0:T(8,128)(2,1)}), bf16[8,96,128]{2,1,0:T(8,128)(2,1)S(1)}, u32[]{:S(2)}, u32[]{:S(2)}) async-start(bf16[8,96,128]{2,1,0:T(8,128)(2,1)} %score_gradient.1), calls=%async_computation.1 | async-start | bytes 393216 | tf_op jit(solution)/shard_map/all_to_all | solution.py:289
  34.4 0.7 select_reduce_fusion.1
  35.1 6.0 %all-to-all-done.1 = bf16[8,96,128]{2,1,0:T(8,128)(2,1)S(1)} async-done(((bf16[8,96,128]{2,1,0:T(8,128)(2,1)}), bf16[8,96,128]{2,1,0:T(8,128)(2,1)S(1)}, u32[]{:S(2)}, u32[]{:S(2)}) %all-to-all-start.1) | async-done | bytes 196640 | tf_op jit(solution)/shard_map/all_to_all | solution.py:289
  41.1 2.0 collective-permute-done.3.refs_10_
  43.2 2.9 %collective-permute-done.1.refs_7_ = bf16[2,3,512,256]{3,2,1,0:T(8,128)(2,1)} collective-permute-done((bf16[2,3,512,256]{3,2,1,0:T(8,128)(2,1)}, bf16[2,3,512,256]{3,2,1,0:T(8,128)(2,1)}, u32[]{:S(2)}, u32[]{:S(2)}) %collective-permute-start.1) | collective-permute-done | bytes 1572896 | tf_op jit(solution)/shard_map/ppermute | solution.py:56
  46.0 1.2 collective-permute-done.refs_5_
  47.5 1.2 slice.74
  48.7 2.1 slice.75
  50.7 1.7 collective-permute-start.13
  54.0 1.0 bitcast_reduce_fusion
  55.4 1.6 collective-permute-start.10
  57.0 1.4 collective-permute-start.9
  58.3 0.6 select_reduce_fusion
  59.0 3.7 %collective-permute-done.11.refs_16_ = bf16[128,512]{1,0:T(8,128)(2,1)S(1)} collective-permute-done((bf16[128,512]{1,0:T(8,128)(2,1)S(1)}, bf16[128,512]{1,0:T(8,128)(2,1)S(1)}, u32[]{:S(2)}, u32[]{:S(2)}) %collective-permute-start.11) | collective-permute-done | bytes 131104 | tf_op jit(solution)/shard_map/ppermute | solution.py:56
  62.7 1.5 collective-permute-start.8
  64.2 3.5 %collective-permute-start.7 = (bf16[128,512]{1,0:T(8,128)(2,1)S(1)}, bf16[128,512]{1,0:T(8,128)(2,1)S(1)}, u32[]{:S(2)}, u32[]{:S(2)}) collective-permute-start(bf16[128,512]{1,0:T(8,128)(2,1)S(1)} %get-tuple-element.72), channel_id=1, source_target_pairs={{0,8},{4,12},{8,0},{12,4},{1,9},{5,13},{9,1},{13,5},{2,10},{6,14},... | collective-permute-start | bytes 393224 | tf_op jit(solution)/shard_map/ppermute | solution.py:56
  67.7 6.7 %collective-permute-done.9.refs_14_ = bf16[128,512]{1,0:T(8,128)(2,1)S(1)} collective-permute-done((bf16[128,512]{1,0:T(8,128)(2,1)S(1)}, bf16[128,512]{1,0:T(8,128)(2,1)S(1)}, u32[]{:S(2)}, u32[]{:S(2)}) %collective-permute-start.9) | collective-permute-done | bytes 131104 | tf_op jit(solution)/shard_map/ppermute | solution.py:56
  74.4 0.8 collective-permute-start.6
  75.5 2.1 slice.70
  77.6 2.1 slice.71
  79.7 1.8 collective-permute-start.5
  81.5 1.1 collective-permute-start.4
  82.5 0.7 copy-done.16
  83.2 0.9 copy-done.17
  84.1 31.9 %attention_tiles.3 = (bf16[4,3,512,256]{3,2,1,0:T(8,128)(2,1)}, f32[3,512,256]{2,1,0:T(8,128)}, bf16[3,512,256]{2,1,0:T(8,128)(2,1)S(1)}, bf16[3,512,256]{2,1,0:T(8,128)(2,1)S(1)}, bf16[3,512,256]{2,1,0:T(8,128)(2,1)S(1)}) custom-call(s32[3,16]{1,0:T(4,128)S(1)} %pad_add_fusion.table, bf16[2,512,512]{2,1,0:T(8,128)(2,1)} %refs_0_.3, ...), custom_call_target="tpu_custom_call" | custom-call | flops 21474836480 | bytes 20971520 | tf_op jit(solution)/shard_map/attention_tiles/pallas_call | solution.py:166
  116.0 5.6 %all-to-all-start.2 = ((bf16[4,3,512,256]{3,2,1,0:T(8,128)(2,1)}), bf16[4,3,512,256]{3,2,1,0:T(8,128)(2,1)}, u32[]{:S(2)}, u32[]{:S(2)}) async-start(bf16[4,3,512,256]{3,2,1,0:T(8,128)(2,1)} %get-tuple-element.41), calls=%async_computation.2 | async-start | bytes 6291456 | tf_op jit(solution)/shard_map/all_to_all | solution.py:368
  121.7 3.4 %collective-permute-start.15 = (bf16[3,512,256]{2,1,0:T(8,128)(2,1)S(1)}, bf16[3,512,256]{2,1,0:T(8,128)(2,1)S(1)}, u32[]{:S(2)}, u32[]{:S(2)}) collective-permute-start(bf16[3,512,256]{2,1,0:T(8,128)(2,1)S(1)} %get-tuple-element.43), channel_id=1, source_target_pairs={{0,2},{1,3},{2,0},{3,1},{4,6},{5,7},{6,4},{7,5},{8,10},{9,11},{10,... | collective-permute-start | bytes 2359304 | tf_op jit(solution)/shard_map/ppermute | solution.py:60
  125.1 2.5 %collective-permute-start.16 = (bf16[3,512,256]{2,1,0:T(8,128)(2,1)S(1)}, bf16[3,512,256]{2,1,0:T(8,128)(2,1)S(1)}, u32[]{:S(2)}, u32[]{:S(2)}) collective-permute-start(bf16[3,512,256]{2,1,0:T(8,128)(2,1)S(1)} %get-tuple-element.44), channel_id=1, source_target_pairs={{0,3},{1,0},{2,1},{3,2},{4,7},{5,4},{6,5},{7,6},{8,11},{9,8},{10,9... | collective-permute-start | bytes 2359304 | tf_op jit(solution)/shard_map/ppermute | solution.py:60
  127.6 0.9 copy-done.18
  128.5 32.1 %attention_tiles.2 = (bf16[4,3,512,256]{3,2,1,0:T(8,128)(2,1)}, f32[3,512,256]{2,1,0:T(8,128)}, bf16[3,512,256]{2,1,0:T(8,128)(2,1)}, bf16[3,512,256]{2,1,0:T(8,128)(2,1)}, bf16[3,512,256]{2,1,0:T(8,128)(2,1)}) custom-call(s32[3,16]{1,0:T(4,128)S(1)} %pad_add_fusion.table, bf16[2,512,512]{2,1,0:T(8,128)(2,1)} %refs_0_.3, bf16[2,512,512]{2,1,0:T(8,128)(2,1)} %refs_1_.3, ...), custom_call_target="tpu_custom_call" | custom-call | flops 21474836480 | bytes 20971520 | tf_op jit(solution)/shard_map/attention_tiles/pallas_call | solution.py:166
  160.7 0.9 copy-done.4
  161.6 0.9 copy-done.6
  162.4 0.9 copy-done.8
  163.3 4.9 %all-to-all-start.3 = ((bf16[4,3,512,256]{3,2,1,0:T(8,128)(2,1)}), bf16[4,3,512,256]{3,2,1,0:T(8,128)(2,1)}, u32[]{:S(2)}, u32[]{:S(2)}) async-start(bf16[4,3,512,256]{3,2,1,0:T(8,128)(2,1)} %get-tuple-element.45), calls=%async_computation.3 | async-start | bytes 6291456 | tf_op jit(solution)/shard_map/all_to_all | solution.py:368
  168.3 1.5 collective-permute-start.18
  169.7 1.8 collective-permute-start.19
  171.5 1.1 copy-done.5
  172.6 1.1 copy-done.7
  173.8 1.1 copy-done.9
  174.9 3.5 %summed.2 = (f32[2,512,512]{2,1,0:T(8,128)}, f32[2,512,512]{2,1,0:T(8,128)}, f32[2,512,512]{2,1,0:T(8,128)}) custom-call(bf16[4,3,512,256]{3,2,1,0:T(8,128)(2,1)} %all-to-all-done.2.got_x, f32[3,512,256]{2,1,0:T(8,128)S(1)} %copy-done.2, bf16[3,512,256]{2,1,0:T(8,128)(2,1)S(1)} %copy-done.5, bf16[3,512,256]{2,1,0:T(8,128)(2,1)S(1)} %copy-done.7, ...), custom_call_target="tpu_custom_call" | custom-call | tf_op jit(solution)/shard_map/summed/pallas_call | solution.py:226
  178.4 9.3 %collective-permute-done.17.refs_0_ = bf16[3,512,256]{2,1,0:T(8,128)(2,1)S(1)} collective-permute-done((bf16[3,512,256]{2,1,0:T(8,128)(2,1)}, bf16[3,512,256]{2,1,0:T(8,128)(2,1)S(1)}, u32[]{:S(2)}, u32[]{:S(2)}) %collective-permute-start.17) | collective-permute-done | bytes 786464 | tf_op jit(solution)/shard_map/ppermute | solution.py:60
  187.7 0.9 copy-done.10
  188.6 11.4 %collective-permute-done.18.refs_1_ = bf16[3,512,256]{2,1,0:T(8,128)(2,1)S(1)} collective-permute-done((bf16[3,512,256]{2,1,0:T(8,128)(2,1)}, bf16[3,512,256]{2,1,0:T(8,128)(2,1)S(1)}, u32[]{:S(2)}, u32[]{:S(2)}) %collective-permute-start.18) | collective-permute-done | bytes 786464 | tf_op jit(solution)/shard_map/ppermute | solution.py:60
  200.0 0.9 copy-done.12
  200.9 0.9 copy-done.14
  201.8 1.1 copy-done.11
  202.9 1.1 copy-done.13
  204.1 1.1 copy-done.15
  205.2 3.5 %summed.3 = (f32[2,512,512]{2,1,0:T(8,128)}, f32[2,512,512]{2,1,0:T(8,128)}, f32[2,512,512]{2,1,0:T(8,128)}) custom-call(bf16[4,3,512,256]{3,2,1,0:T(8,128)(2,1)} %all-to-all-done.3.got_x, f32[3,512,256]{2,1,0:T(8,128)S(1)} %copy-done.3, bf16[3,512,256]{2,1,0:T(8,128)(2,1)S(1)} %copy-done.11, ...), custom_call_target="tpu_custom_call", output_to_operand_aliasing={{0}: (5, {}), {1}: (6, {}), {2}: (7, {})} | custom-call | tf_op jit(solution)/shard_map/summed/pallas_call | solution.py:226
  (97 shorter events, 5.8 us)
Async XLA Ops:
  0.6 11.3 %copy-start = (bf16[2,512,512]{2,1,0:T(8,128)(2,1)S(1)}, bf16[2,512,512]{2,1,0:T(8,128)(2,1)}, u32[]{:S(2)}) copy-start(bf16[2,512,512]{2,1,0:T(8,128)(2,1)} %param.12) | copy-start | bytes 3145732
  0.6 1.6 copy-start.20
  0.7 1.9 copy-start.21
  4.4 38.7 %collective-permute-start.3 = (bf16[2,3,512,256]{3,2,1,0:T(8,128)(2,1)}, bf16[2,3,512,256]{3,2,1,0:T(8,128)(2,1)}, u32[]{:S(2)}, u32[]{:S(2)}) collective-permute-start(bf16[2,3,512,256]{3,2,1,0:T(8,128)(2,1)} %pad_maximum_fusion.3), channel_id=1, source_target_pairs={{0,1},{1,2},{2,3},{3,0},{4,5},{5,6},{6,7},{7,4},{8,9},{9,10},{10,1... | collective-permute-start | bytes 4718600 | tf_op jit(solution)/shard_map/ppermute | solution.py:56
  6.3 36.8 %collective-permute-start.2 = (bf16[2,3,512,256]{3,2,1,0:T(8,128)(2,1)}, bf16[2,3,512,256]{3,2,1,0:T(8,128)(2,1)}, u32[]{:S(2)}, u32[]{:S(2)}) collective-permute-start(bf16[2,3,512,256]{3,2,1,0:T(8,128)(2,1)} %pad_maximum_fusion.3), channel_id=1, source_target_pairs={{0,3},{1,0},{2,1},{3,2},{4,7},{5,4},{6,5},{7,6},{8,11},{9,8},{10,9... | collective-permute-start | bytes 4718600 | tf_op jit(solution)/shard_map/ppermute | solution.py:56
  8.6 3.3 %copy-start.22 = (bf16[512,96]{0,1:T(8,128)(2,1)S(1)}, bf16[512,96]{0,1:T(8,128)(2,1)}, u32[]{:S(2)}) copy-start(bf16[512,96]{0,1:T(8,128)(2,1)} %param.13) | copy-start | bytes 294916
  8.6 3.3 %copy-start.23 = (f32[96,512]{1,0:T(8,128)S(1)}, f32[96,512]{1,0:T(8,128)}, u32[]{:S(2)}) copy-start(f32[96,512]{1,0:T(8,128)} %param.14) | copy-start | bytes 589828
  9.9 36.2 %collective-permute-start.1 = (bf16[2,3,512,256]{3,2,1,0:T(8,128)(2,1)}, bf16[2,3,512,256]{3,2,1,0:T(8,128)(2,1)}, u32[]{:S(2)}, u32[]{:S(2)}) collective-permute-start(bf16[2,3,512,256]{3,2,1,0:T(8,128)(2,1)} %pad_maximum_fusion.1), channel_id=1, source_target_pairs={{0,4},{4,8},{8,12},{12,0},{1,5},{5,9},{9,13},{13,1},{2,6},{6,10},{... | collective-permute-start | bytes 4718600 | tf_op jit(solution)/shard_map/ppermute | solution.py:56
  11.3 35.9 %collective-permute-start = (bf16[2,3,512,256]{3,2,1,0:T(8,128)(2,1)}, bf16[2,3,512,256]{3,2,1,0:T(8,128)(2,1)}, u32[]{:S(2)}, u32[]{:S(2)}) collective-permute-start(bf16[2,3,512,256]{3,2,1,0:T(8,128)(2,1)} %pad_maximum_fusion.1), channel_id=1, source_target_pairs={{0,12},{4,0},{8,4},{12,8},{1,13},{5,1},{9,5},{13,9},{2,14},{6,2},{... | collective-permute-start | bytes 4718600 | tf_op jit(solution)/shard_map/ppermute | solution.py:56
  12.5 5.7 %copy-start.25 = (s32[16,16]{1,0:T(8,128)S(1)}, s32[16,16]{1,0:T(8,128)}, u32[]{:S(2)}) copy-start(s32[16,16]{1,0:T(8,128)} %param.23) | copy-start | bytes 3076
  12.6 5.7 %copy-start.26 = (s32[16,16]{1,0:T(8,128)S(1)}, s32[16,16]{1,0:T(8,128)}, u32[]{:S(2)}) copy-start(s32[16,16]{1,0:T(8,128)} %param.22) | copy-start | bytes 3076
  13.6 13.4 %all-to-all-start = ((f32[8,96,128]{2,1,0:T(8,128)}), f32[8,96,128]{2,1,0:T(8,128)S(1)}, u32[]{:S(2)}, u32[]{:S(2)}) async-start(f32[8,96,128]{2,1,0:T(8,128)} %copy.36), calls=%async_computation | async-start | bytes 786432 | tf_op jit(solution)/shard_map/all_to_all | solution.py:281
  27.0 0.7 copy-start.19
  31.0 10.2 %all-to-all-start.1 = ((bf16[8,96,128]{2,1,0:T(8,128)(2,1)}), bf16[8,96,128]{2,1,0:T(8,128)(2,1)S(1)}, u32[]{:S(2)}, u32[]{:S(2)}) async-start(bf16[8,96,128]{2,1,0:T(8,128)(2,1)} %score_gradient.1), calls=%async_computation.1 | async-start | bytes 393216 | tf_op jit(solution)/shard_map/all_to_all | solution.py:289
  47.4 5.6 %copy-start.27 = (s32[1,512]{1,0:T(1,128)S(1)}, s32[1,512]{1,0:T(1,128)}, u32[]{:S(2)}) copy-start(s32[1,512]{1,0:T(1,128)} %param.17) | copy-start | bytes 6148
  50.7 32.5 %collective-permute-start.13 = (bf16[1,3,512,256]{3,2,1,0:T(8,128)(2,1)}, bf16[1,3,512,256]{3,2,1,0:T(8,128)(2,1)}, u32[]{:S(2)}, u32[]{:S(2)}) collective-permute-start(bf16[1,3,512,256]{3,2,1,0:T(8,128)(2,1)} %slice.75), channel_id=1, source_target_pairs={{0,3},{1,0},{2,1},{3,2},{4,7},{5,4},{6,5},{7,6},{8,11},{9,8},{10,9... | collective-permute-start | bytes 2359304 | tf_op jit(solution)/shard_map/ppermute | solution.py:56
  52.5 30.8 %collective-permute-start.12 = (bf16[1,3,512,256]{3,2,1,0:T(8,128)(2,1)S(1)}, bf16[1,3,512,256]{3,2,1,0:T(8,128)(2,1)}, u32[]{:S(2)}, u32[]{:S(2)}) collective-permute-start(bf16[1,3,512,256]{3,2,1,0:T(8,128)(2,1)S(1)} %slice.74), channel_id=1, source_target_pairs={{0,12},{4,0},{8,4},{12,8},{1,13},{5,1},{9,5},{13,9},{2,14},{6,2},{... | collective-permute-start | bytes 2359304 | tf_op jit(solution)/shard_map/ppermute | solution.py:56
  54.0 1.0 copy-start.24
  55.0 7.7 %collective-permute-start.11 = (bf16[128,512]{1,0:T(8,128)(2,1)S(1)}, bf16[128,512]{1,0:T(8,128)(2,1)S(1)}, u32[]{:S(2)}, u32[]{:S(2)}) collective-permute-start(bf16[128,512]{1,0:T(8,128)(2,1)S(1)} %get-tuple-element.71), channel_id=1, source_target_pairs={{0,1},{1,2},{2,3},{3,0},{4,5},{5,6},{6,7},{7,4},{8,9},{9,10},{10,1... | collective-permute-start | bytes 393224 | tf_op jit(solution)/shard_map/ppermute | solution.py:56
  55.4 8.8 %collective-permute-start.10 = (bf16[128,512]{1,0:T(8,128)(2,1)S(1)}, bf16[128,512]{1,0:T(8,128)(2,1)S(1)}, u32[]{:S(2)}, u32[]{:S(2)}) collective-permute-start(bf16[128,512]{1,0:T(8,128)(2,1)S(1)} %get-tuple-element.71), channel_id=1, source_target_pairs={{0,2},{1,3},{2,0},{3,1},{4,6},{5,7},{6,4},{7,5},{8,10},{9,11},{10,... | collective-permute-start | bytes 393224 | tf_op jit(solution)/shard_map/ppermute | solution.py:56
  57.0 17.4 %collective-permute-start.9 = (bf16[128,512]{1,0:T(8,128)(2,1)S(1)}, bf16[128,512]{1,0:T(8,128)(2,1)S(1)}, u32[]{:S(2)}, u32[]{:S(2)}) collective-permute-start(bf16[128,512]{1,0:T(8,128)(2,1)S(1)} %get-tuple-element.71), channel_id=1, source_target_pairs={{0,3},{1,0},{2,1},{3,2},{4,7},{5,4},{6,5},{7,6},{8,11},{9,8},{10,9... | collective-permute-start | bytes 393224 | tf_op jit(solution)/shard_map/ppermute | solution.py:56
  62.7 17.0 %collective-permute-start.8 = (bf16[128,512]{1,0:T(8,128)(2,1)S(1)}, bf16[128,512]{1,0:T(8,128)(2,1)S(1)}, u32[]{:S(2)}, u32[]{:S(2)}) collective-permute-start(bf16[128,512]{1,0:T(8,128)(2,1)S(1)} %get-tuple-element.72), channel_id=1, source_target_pairs={{0,4},{4,8},{8,12},{12,0},{1,5},{5,9},{9,13},{13,1},{2,6},{6,10},{... | collective-permute-start | bytes 393224 | tf_op jit(solution)/shard_map/ppermute | solution.py:56
  64.2 17.3 %collective-permute-start.7 = (bf16[128,512]{1,0:T(8,128)(2,1)S(1)}, bf16[128,512]{1,0:T(8,128)(2,1)S(1)}, u32[]{:S(2)}, u32[]{:S(2)}) collective-permute-start(bf16[128,512]{1,0:T(8,128)(2,1)S(1)} %get-tuple-element.72), channel_id=1, source_target_pairs={{0,8},{4,12},{8,0},{12,4},{1,9},{5,13},{9,1},{13,5},{2,10},{6,14},... | collective-permute-start | bytes 393224 | tf_op jit(solution)/shard_map/ppermute | solution.py:56
  74.4 8.2 %collective-permute-start.6 = (bf16[128,512]{1,0:T(8,128)(2,1)S(1)}, bf16[128,512]{1,0:T(8,128)(2,1)S(1)}, u32[]{:S(2)}, u32[]{:S(2)}) collective-permute-start(bf16[128,512]{1,0:T(8,128)(2,1)S(1)} %get-tuple-element.72), channel_id=1, source_target_pairs={{0,12},{4,0},{8,4},{12,8},{1,13},{5,1},{9,5},{13,9},{2,14},{6,2},{... | collective-permute-start | bytes 393224 | tf_op jit(solution)/shard_map/ppermute | solution.py:56
  79.7 48.0 %collective-permute-start.5 = (bf16[1,3,512,256]{3,2,1,0:T(8,128)(2,1)}, bf16[1,3,512,256]{3,2,1,0:T(8,128)(2,1)}, u32[]{:S(2)}, u32[]{:S(2)}) collective-permute-start(bf16[1,3,512,256]{3,2,1,0:T(8,128)(2,1)} %slice.71), channel_id=1, source_target_pairs={{0,1},{1,2},{2,3},{3,0},{4,5},{5,6},{6,7},{7,4},{8,9},{9,10},{10,1... | collective-permute-start | bytes 2359304 | tf_op jit(solution)/shard_map/ppermute | solution.py:56
  81.5 46.2 %collective-permute-start.4 = (bf16[1,3,512,256]{3,2,1,0:T(8,128)(2,1)}, bf16[1,3,512,256]{3,2,1,0:T(8,128)(2,1)}, u32[]{:S(2)}, u32[]{:S(2)}) collective-permute-start(bf16[1,3,512,256]{3,2,1,0:T(8,128)(2,1)} %slice.70), channel_id=1, source_target_pairs={{0,4},{4,8},{8,12},{12,0},{1,5},{5,9},{9,13},{13,1},{2,6},{6,10},{... | collective-permute-start | bytes 2359304 | tf_op jit(solution)/shard_map/ppermute | solution.py:56
  82.5 0.7 copy-start.16
  83.2 0.9 copy-start.17
  116.0 47.3 %all-to-all-start.2 = ((bf16[4,3,512,256]{3,2,1,0:T(8,128)(2,1)}), bf16[4,3,512,256]{3,2,1,0:T(8,128)(2,1)}, u32[]{:S(2)}, u32[]{:S(2)}) async-start(bf16[4,3,512,256]{3,2,1,0:T(8,128)(2,1)} %get-tuple-element.41), calls=%async_computation.2 | async-start | bytes 6291456 | tf_op jit(solution)/shard_map/all_to_all | solution.py:368
  121.6 39.1 %collective-permute-start.14 = (bf16[3,512,256]{2,1,0:T(8,128)(2,1)S(1)}, bf16[3,512,256]{2,1,0:T(8,128)(2,1)S(1)}, u32[]{:S(2)}, u32[]{:S(2)}) collective-permute-start(bf16[3,512,256]{2,1,0:T(8,128)(2,1)S(1)} %get-tuple-element.42), channel_id=1, source_target_pairs={{0,1},{1,2},{2,3},{3,0},{4,5},{5,6},{6,7},{7,4},{8,9},{9,10},{10,1... | collective-permute-start | bytes 2359304 | tf_op jit(solution)/shard_map/ppermute | solution.py:60
  121.7 39.9 %collective-permute-start.15 = (bf16[3,512,256]{2,1,0:T(8,128)(2,1)S(1)}, bf16[3,512,256]{2,1,0:T(8,128)(2,1)S(1)}, u32[]{:S(2)}, u32[]{:S(2)}) collective-permute-start(bf16[3,512,256]{2,1,0:T(8,128)(2,1)S(1)} %get-tuple-element.43), channel_id=1, source_target_pairs={{0,2},{1,3},{2,0},{3,1},{4,6},{5,7},{6,4},{7,5},{8,10},{9,11},{10,... | collective-permute-start | bytes 2359304 | tf_op jit(solution)/shard_map/ppermute | solution.py:60
  125.1 37.3 %collective-permute-start.16 = (bf16[3,512,256]{2,1,0:T(8,128)(2,1)S(1)}, bf16[3,512,256]{2,1,0:T(8,128)(2,1)S(1)}, u32[]{:S(2)}, u32[]{:S(2)}) collective-permute-start(bf16[3,512,256]{2,1,0:T(8,128)(2,1)S(1)} %get-tuple-element.44), channel_id=1, source_target_pairs={{0,3},{1,0},{2,1},{3,2},{4,7},{5,4},{6,5},{7,6},{8,11},{9,8},{10,9... | collective-permute-start | bytes 2359304 | tf_op jit(solution)/shard_map/ppermute | solution.py:60
  127.6 0.9 copy-start.18
  160.7 0.9 copy-start.4
  161.6 0.9 copy-start.6
  162.4 0.9 copy-start.8
  163.3 8.2 %copy-start.2 = (f32[3,512,256]{2,1,0:T(8,128)S(1)}, f32[3,512,256]{2,1,0:T(8,128)}, u32[]{:S(2)}) copy-start(f32[3,512,256]{2,1,0:T(8,128)} %get-tuple-element.51.own_z) | copy-start | bytes 4718596
  163.3 38.5 %all-to-all-start.3 = ((bf16[4,3,512,256]{3,2,1,0:T(8,128)(2,1)}), bf16[4,3,512,256]{3,2,1,0:T(8,128)(2,1)}, u32[]{:S(2)}, u32[]{:S(2)}) async-start(bf16[4,3,512,256]{3,2,1,0:T(8,128)(2,1)} %get-tuple-element.45), calls=%async_computation.3 | async-start | bytes 6291456 | tf_op jit(solution)/shard_map/all_to_all | solution.py:368
  168.3 19.5 %collective-permute-start.17 = (bf16[3,512,256]{2,1,0:T(8,128)(2,1)}, bf16[3,512,256]{2,1,0:T(8,128)(2,1)S(1)}, u32[]{:S(2)}, u32[]{:S(2)}) collective-permute-start(bf16[3,512,256]{2,1,0:T(8,128)(2,1)} %get-tuple-element.47), channel_id=1, source_target_pairs={{0,1},{1,2},{2,3},{3,0},{4,5},{5,6},{6,7},{7,4},{8,9},{9,10},{10,1... | collective-permute-start | bytes 2359304 | tf_op jit(solution)/shard_map/ppermute | solution.py:60
  168.3 31.7 %collective-permute-start.18 = (bf16[3,512,256]{2,1,0:T(8,128)(2,1)}, bf16[3,512,256]{2,1,0:T(8,128)(2,1)S(1)}, u32[]{:S(2)}, u32[]{:S(2)}) collective-permute-start(bf16[3,512,256]{2,1,0:T(8,128)(2,1)} %get-tuple-element.48), channel_id=1, source_target_pairs={{0,2},{1,3},{2,0},{3,1},{4,6},{5,7},{6,4},{7,5},{8,10},{9,11},{10,... | collective-permute-start | bytes 2359304 | tf_op jit(solution)/shard_map/ppermute | solution.py:60
  169.7 31.2 %collective-permute-start.19 = (bf16[3,512,256]{2,1,0:T(8,128)(2,1)}, bf16[3,512,256]{2,1,0:T(8,128)(2,1)S(1)}, u32[]{:S(2)}, u32[]{:S(2)}) collective-permute-start(bf16[3,512,256]{2,1,0:T(8,128)(2,1)} %get-tuple-element.49), channel_id=1, source_target_pairs={{0,3},{1,0},{2,1},{3,2},{4,7},{5,4},{6,5},{7,6},{8,11},{9,8},{10,9... | collective-permute-start | bytes 2359304 | tf_op jit(solution)/shard_map/ppermute | solution.py:60
  171.5 1.1 copy-start.5
  172.6 1.1 copy-start.7
  173.8 1.1 copy-start.9
  174.9 26.9 %copy-start.3 = (f32[3,512,256]{2,1,0:T(8,128)S(1)}, f32[3,512,256]{2,1,0:T(8,128)}, u32[]{:S(2)}) copy-start(f32[3,512,256]{2,1,0:T(8,128)} %get-tuple-element.46.own_z) | copy-start | bytes 4718596
  187.7 0.9 copy-start.10
  200.0 0.9 copy-start.12
  200.9 0.9 copy-start.14
  201.8 1.1 copy-start.11
  202.9 1.1 copy-start.13
  204.1 1.1 copy-start.15
  205.2 3.5 %copy-start.1 = (bf16[2,512,512]{2,1,0:T(8,128)(2,1)S(1)}, bf16[2,512,512]{2,1,0:T(8,128)(2,1)}, u32[]{:S(2)}) copy-start(bf16[2,512,512]{2,1,0:T(8,128)(2,1)} %param.12) | copy-start | bytes 3145732

commit v4 on v3

--- a/solution.py
+++ b/solution.py
@@ -158,10 +158,7 @@
     pairs = width // 256
     base = half * pairs
     own_spec = pl.BlockSpec((members, rows, 128), lambda h, tab: (0, 0, base + h))
-    near_spec = pl.BlockSpec((None, 3, rows, 128), lambda h, tab: (half, 0, 0, h))
-    once_spec = pl.BlockSpec((None, 3, rows, 128), lambda h, tab: (0, 0, 0, h))
     far_spec = pl.BlockSpec((3, rows, 128), lambda h, tab: (0, 0, h))
-    fetch_specs = [near_spec, once_spec, near_spec]
     late_spec = pl.BlockSpec((stats, rows), lambda h, tab: (0, 0))
     out = pl.pallas_call(
         functools.partial(tile_kernel, base=2 * base),
@@ -178,7 +175,7 @@
                 pl.BlockSpec((members, stats, rows), lambda h, tab: (0, 0, 0)),
                 pl.BlockSpec((128, channels), lambda h, tab: (base + h, 0)),
             ]
-            + fetch_specs * 2
+            + [far_spec] * 6
             + [late_spec] * 6,
             out_specs=[pl.BlockSpec((SIDE, 3, rows, 128), lambda h, tab: (0, 0, 0, h))]
             + [far_spec] * 4,
@@ -201,7 +198,11 @@
             bytes_accessed=20 * 1024 * 1024,
         ),
         name="attention_tiles",
-    )(tables, key_rows, value_rows, query, late_own, decoder_matrix, *fetched_x, *fetched_z, *late_x, *late_z)
+    )(
+        tables,
+        *in_hbm(key_rows, value_rows, query, late_own, decoder_matrix),
+        *in_hbm(*fetched_x, *fetched_z, *late_x, *late_z),
+    )
     return out[0], out[1], out[2:]
 
 
@@ -234,17 +235,16 @@
         input_output_aliases={5 + n: n for n in range(len(kept))},
         compiler_params=pltpu.CompilerParams(vmem_limit_bytes=50 * 1024 * 1024),
         name="summed",
-    )(got_x, own_z, *got_z, *kept)
-
-
-def ring_far(after, before, axis):
-    return fetched(after[0:1], axis, 1), fetched(before[1:2], axis, 3)
-
-
-def outgoing(keys, values, queries):
-    stacked = jnp.stack([keys, values, queries])
-    kinds, rows, width = stacked.shape
-    return jnp.stack([stacked[..., : width // 2], stacked[..., width // 2 :]])
+    )(*in_hbm(got_x, own_z, *got_z), *kept)
+
+
+def outgoing(half, *arrays):
+    lanes = arrays[0].shape[-1] // 2
+    return jnp.stack([a[:, half * lanes : (half + 1) * lanes] for a in arrays])
+
+
+def in_hbm(*arrays):
+    return [pltpu.with_memory_space_constraint(a, pltpu.HBM) for a in arrays]
 
 
 def shards(
@@ -266,9 +266,11 @@
     x_at = lax.axis_index("x")
     z_at = lax.axis_index("z")
 
-    own_x = outgoing(key_rows[0], value_rows[0], query[1])
-    own_z = outgoing(key_rows[1], value_rows[1], query[0])
-    near = [fetched(own_x, "x", 1), fetched(own_x, "x", 3), fetched(own_z, "z", 1), fetched(own_z, "z", 3)]
+    own = [
+        (outgoing(h, key_rows[0], value_rows[0], query[1]), outgoing(h, key_rows[1], value_rows[1], query[0]))
+        for h in range(2)
+    ]
+    near = [fetched(a, axis, d) for a, axis in zip(own[0], ("x", "z")) for d in (1, 3)]
 
     forecast = baseline_field[None] + jnp.einsum(
         "mou,ut->mto", hidden_embedding, decoder_matrix, preferred_element_type=F32
@@ -286,10 +288,11 @@
     derivative = score_gradient(
         everyone, jnp.tile(observed, (1, members)), jnp.tile(area[None], (1, members))
     )
+    derivative, own_1, near = lax.optimization_barrier((derivative, own[1], near))
     returned = lax.all_to_all(derivative, MEMBER, 0, 0, tiled=True)
-    returned, *near = lax.optimization_barrier((returned, *near))
-    x_after, x_before, z_after, z_before = near
-    x_far, z_far = ring_far(x_after, x_before, "x"), ring_far(z_after, z_before, "z")
+    far = [fetched(near[0], "x", 1), fetched(near[2], "z", 1)]
+    before = [fetched(a, axis, 3) for a, axis in zip(own_1, ("x", "z"))]
+    returned, own_1, before = lax.optimization_barrier((returned, own_1, before))
     grad_forecast = (
         returned.reshape(groups, channels, members, span)
         .transpose(2, 1, 0, 3)
@@ -342,6 +345,13 @@
     )
     late_z = [fetched(late_own[0], "z", d) for d in (1, 2, 3)]
     late_x = [fetched(late_own[1], "x", d) for d in (1, 2, 3)]
+    late_own, own_1, before = lax.optimization_barrier((late_own, own_1, before))
+    after = [fetched(a, axis, 1) for a, axis in zip(own_1, ("x", "z"))]
+    last = [fetched(before[0], "x", 3), fetched(before[1], "z", 3)]
+    came = (
+        ((near[0], far[0], near[1]), (near[2], far[1], near[3])),
+        ((after[0], last[0], before[0]), (after[1], last[1], before[1])),
+    )
 
     outs = None
     parts = []
@@ -352,8 +362,7 @@
             key_rows,
             value_rows,
             query,
-            (x_after, x_far[half], x_before),
-            (z_after, z_far[half], z_before),
+            *came[half],
             late_own,
             late_x,
             late_z,

time: 210 us -> 196 us (0.933)
  local copies, waits for them, and re-layouts: 29.8 us -> 13.4 us
  waiting for transfers between devices: 48.3 us -> 38.8 us
  starting transfers between devices: 48 us -> 55.7 us
  Pallas kernels: 74.3 us -> 77.2 us
    unnamed x57 -> x41, local copies, waits for them, and re-layouts: 16 us -> 6.22 us
    slice x7 -> x0, local copies, waits for them, and re-layouts: 8.94 us -> none  [the longest x4 7.38 us: ring_far(): return (fetched(after[0:1], axis, 1), fetched(before[1:2], axis, 3))]
    ppermute x14 -> x18, waiting for transfers between devices: 16.5 us -> 9.6 us  [fetched(): lax.ppermute(x, axis, [(i, (i - distance) % SIDE) for i in range(SIDE)])]
    ppermute x14 -> x18, starting transfers between devices: 20.4 us -> 25.9 us  [fetched(): lax.ppermute(x, axis, [(i, (i - distance) % SIDE) for i in range(SIDE)])]
    all_to_all x1, waiting for transfers between devices: 6.04 us -> 2.69 us  [shards(): returned = lax.all_to_all(derivative, MEMBER, 0, 0, tiled=True)]
    ppermute x6, waiting for transfers between devices: 20.7 us -> 24 us  [delivered(): lax.ppermute(x, axis, [(i, (i + distance) % SIDE) for i in range(SIDE)])]
    all_to_all x1, waiting for transfers between devices: 5.08 us -> 2.46 us  [shards(): lax.all_to_all(by_node.reshape(groups, channels, members * span), MEMBER,...]
    another operation x3 -> x4, other arithmetic: 2.9 us -> 4.83 us  [outgoing(): return jnp.stack([a[:, half * lanes:(half + 1) * lanes] for a in arrays])]
  transfers between devices with their start and end apart: 24 -> 28, of which waited for: 9 -> 7; matrix products, arithmetic and copies ran while one was open for 7% -> 7% of each run, Pallas kernels for 34% -> 37%
where the time goes in v4:
time: 196 us; the launch traced here: 195 us
  Pallas kernels  77.2 us (39%)
  starting transfers between devices  55.7 us (28%)
  waiting for transfers between devices  38.8 us (20%)
  local copies, waits for them, and re-layouts  13.4 us (7%)
  other arithmetic  6.85 us (3%)
  matrix products  2.36 us (1%)
    pallas_call x2, Pallas kernels, attention_tiles(): pl.pallas_call(functools.partial(tile_kernel, base=2 * base), out_shape=[...  65 us
    ppermute x18, starting transfers between devices, fetched(): lax.ppermute(x, axis, [(i, (i - distance) % SIDE) for i in range(SIDE)])  25.9 us
    ppermute x6, waiting for transfers between devices, delivered(): lax.ppermute(x, axis, [(i, (i + distance) % SIDE) for i in range(SIDE)])  24 us
    all_to_all x2, starting transfers between devices, shards(): got_x = lax.all_to_all(send_x, 'x', 0, 0, tiled=True)  11.6 us
    ppermute x6, starting transfers between devices, delivered(): lax.ppermute(x, axis, [(i, (i + distance) % SIDE) for i in range(SIDE)])  9.89 us
    ppermute x18, waiting for transfers between devices, fetched(): lax.ppermute(x, axis, [(i, (i - distance) % SIDE) for i in range(SIDE)])  9.6 us
    pallas_call x2, Pallas kernels, summed(): pl.pallas_call(sum_kernel, out_shape=[shape] * 3, grid=(2,), in_specs=[pl...  8.94 us
    unnamed x41, local copies, waits for them, and re-layouts  6.22 us
  transfers between devices with their start and end apart: 28, of which 7 were waited for; matrix products, arithmetic and copies ran while one was open for 7% of the time, Pallas kernels for 37%

profile of v4, /device:TPU:2, one launch (start us, length us, event | category | flops | bytes accessed | tf_op | source)
XLA Modules:
  0.0 195.3 jit_solution(6498274260628016810)
XLA Ops:
  0.7 1.4 slice_bitcast_fusion
  2.1 0.2 copy-done.6
  2.3 0.2 copy-done.7
  2.8 0.8 slice_bitcast_fusion.7
  3.6 1.0 pad_maximum_fusion.2
  4.6 1.5 collective-permute-start.1
  6.1 0.5 collective-permute-start
  6.6 1.0 pad_maximum_fusion.3
  7.6 1.9 collective-permute-start.3
  9.5 2.1 %collective-permute-start.2 = (bf16[3,512,256]{2,1,0:T(8,128)(2,1)}, bf16[3,512,256]{2,1,0:T(8,128)(2,1)}, u32[]{:S(2)}, u32[]{:S(2)}) collective-permute-start(bf16[3,512,256]{2,1,0:T(8,128)(2,1)} %pad_maximum_fusion.3), channel_id=1, source_target_pairs={{0,3},{1,0},{2,1},{3,2},{4,7},{5,4},{6,5},{7,6},{8,11},{9,8},{10,9... | collective-permute-start | bytes 2359304 | tf_op jit(solution)/shard_map/ppermute | solution.py:56
  11.6 0.4 fusion
  12.1 0.2 copy.34
  12.4 0.9 copy.36
  13.3 4.5 %all-to-all-start = ((f32[8,96,128]{2,1,0:T(8,128)}), f32[8,96,128]{2,1,0:T(8,128)S(1)}, u32[]{:S(2)}, u32[]{:S(2)}) async-start(f32[8,96,128]{2,1,0:T(8,128)} %copy.36), calls=%async_computation | async-start | bytes 786432 | tf_op jit(solution)/shard_map/all_to_all | solution.py:283
  17.9 0.8 dynamic_slice.7
  18.7 0.7 tile.20.area_ref
  19.4 0.1 select_reduce_fusion.2
  19.6 0.9 constant_dynamic-slice_fusion
  20.6 0.7 copy.38.truth_ref
  21.3 1.9 pad_maximum_fusion.1
  23.2 1.0 pad_maximum_fusion
  24.3 2.5 %all-to-all-done.forecast_ref = f32[8,96,128]{2,1,0:T(8,128)S(1)} async-done(((f32[8,96,128]{2,1,0:T(8,128)}), f32[8,96,128]{2,1,0:T(8,128)S(1)}, u32[]{:S(2)}, u32[]{:S(2)}) %all-to-all-start) | async-done | bytes 393248 | tf_op jit(solution)/shard_map/all_to_all | solution.py:283
  26.7 0.7 copy-done.5
  27.5 3.3 %score_gradient.1 = bf16[8,96,128]{2,1,0:T(8,128)(2,1)} custom-call(f32[8,96,128]{2,1,0:T(8,128)} %copy-done.5, f32[96,128]{1,0:T(8,128)} %copy.38.truth_ref, f32[1,128]{1,0:T(1,128)} %tile.20.area_ref), custom_call_target="tpu_custom_call" | custom-call | tf_op jit(solution)/shard_map/score_gradient/pallas_call | solution.py:45
  30.8 1.6 collective-permute-start.4
  32.5 0.1 broadcast_and_fusion
  32.6 3.8 %all-to-all-start.1 = ((bf16[8,96,128]{2,1,0:T(8,128)(2,1)}), bf16[8,96,128]{2,1,0:T(8,128)(2,1)S(1)}, u32[]{:S(2)}, u32[]{:S(2)}) async-start(bf16[8,96,128]{2,1,0:T(8,128)(2,1)} %score_gradient.1), calls=%async_computation.1 | async-start | bytes 393216 | tf_op jit(solution)/shard_map/all_to_all | solution.py:292
  36.4 0.7 select_reduce_fusion.1
  37.1 0.6 collective-permute-start.16
  37.7 2.8 %collective-permute-start.17 = (bf16[3,512,256]{2,1,0:T(8,128)(2,1)}, bf16[3,512,256]{2,1,0:T(8,128)(2,1)}, u32[]{:S(2)}, u32[]{:S(2)}) collective-permute-start(bf16[3,512,256]{2,1,0:T(8,128)(2,1)} %collective-permute-done.2.refs_8_), channel_id=1, source_target_pairs={{0,3},{1,0},{2,1},{3,2},{4,7},{5,4},{6,5},{7,6},{8,11},{9,8},{10,9... | collective-permute-start | bytes 2359304 | tf_op jit(solution)/shard_map/ppermute | solution.py:56
  40.6 2.7 %all-to-all-done.1 = bf16[8,96,128]{2,1,0:T(8,128)(2,1)S(1)} async-done(((bf16[8,96,128]{2,1,0:T(8,128)(2,1)}), bf16[8,96,128]{2,1,0:T(8,128)(2,1)S(1)}, u32[]{:S(2)}, u32[]{:S(2)}) %all-to-all-start.1) | async-done | bytes 196640 | tf_op jit(solution)/shard_map/all_to_all | solution.py:292
  43.2 7.0 %collective-permute-done.4.refs_7_ = bf16[3,512,256]{2,1,0:T(8,128)(2,1)} collective-permute-done((bf16[3,512,256]{2,1,0:T(8,128)(2,1)}, bf16[3,512,256]{2,1,0:T(8,128)(2,1)}, u32[]{:S(2)}, u32[]{:S(2)}) %collective-permute-start.4) | collective-permute-done | bytes 786464 | tf_op jit(solution)/shard_map/ppermute | solution.py:56
  50.2 2.4 %collective-permute-done.5.refs_10_ = bf16[3,512,256]{2,1,0:T(8,128)(2,1)} collective-permute-done((bf16[3,512,256]{2,1,0:T(8,128)(2,1)}, bf16[3,512,256]{2,1,0:T(8,128)(2,1)}, u32[]{:S(2)}, u32[]{:S(2)}) %collective-permute-start.5) | collective-permute-done | bytes 786464 | tf_op jit(solution)/shard_map/ppermute | solution.py:56
  52.7 0.2 copy.39
  52.9 0.5 constant_dynamic-update-slice_fusion
  53.4 0.5 convolution_convert_fusion.1
  53.9 1.0 bitcast_reduce_fusion
  55.0 0.6 select_reduce_fusion
  55.6 2.3 %collective-permute-start.14 = (bf16[128,512]{1,0:T(8,128)(2,1)S(1)}, bf16[128,512]{1,0:T(8,128)(2,1)}, u32[]{:S(2)}, u32[]{:S(2)}) collective-permute-start(bf16[128,512]{1,0:T(8,128)(2,1)S(1)} %get-tuple-element.103), channel_id=1, source_target_pairs={{0,2},{1,3},{2,0},{3,1},{4,6},{5,7},{6,4},{7,5},{8,10},{9,11},{10,... | collective-permute-start | bytes 393224 | tf_op jit(solution)/shard_map/ppermute | solution.py:56
  58.0 1.0 collective-permute-start.13
  59.0 1.2 collective-permute-start.12
  60.2 2.6 %collective-permute-start.11 = (bf16[128,512]{1,0:T(8,128)(2,1)S(1)}, bf16[128,512]{1,0:T(8,128)(2,1)}, u32[]{:S(2)}, u32[]{:S(2)}) collective-permute-start(bf16[128,512]{1,0:T(8,128)(2,1)S(1)} %get-tuple-element.104), channel_id=1, source_target_pairs={{0,8},{4,12},{8,0},{12,4},{1,9},{5,13},{9,1},{13,5},{2,10},{6,14},... | collective-permute-start | bytes 393224 | tf_op jit(solution)/shard_map/ppermute | solution.py:56
  62.8 0.2 collective-permute-done.15.refs_16_
  63.0 1.5 collective-permute-start.10
  64.5 0.8 copy.43.refs_4_
  65.4 2.3 %collective-permute-start.6 = (bf16[3,512,256]{2,1,0:T(8,128)(2,1)}, bf16[3,512,256]{2,1,0:T(8,128)(2,1)S(1)}, u32[]{:S(2)}, u32[]{:S(2)}) collective-permute-start(bf16[3,512,256]{2,1,0:T(8,128)(2,1)} %pad_maximum_fusion), channel_id=1, source_target_pairs={{0,12},{4,0},{8,4},{12,8},{1,13},{5,1},{9,5},{13,9},{2,14},{6,2},{... | collective-permute-start | bytes 2359304 | tf_op jit(solution)/shard_map/ppermute | solution.py:56
  67.7 1.9 collective-permute-start.8
  69.6 1.9 collective-permute-start.7
  71.6 32.5 %attention_tiles.3 = (bf16[4,3,512,256]{3,2,1,0:T(8,128)(2,1)}, f32[3,512,256]{2,1,0:T(8,128)S(1)}, bf16[3,512,256]{2,1,0:T(8,128)(2,1)}, bf16[3,512,256]{2,1,0:T(8,128)(2,1)}, bf16[3,512,256]{2,1,0:T(8,128)(2,1)S(1)}) custom-call(s32[3,16]{1,0:T(4,128)S(1)} %pad_add_fusion.table, bf16[2,512,512]{2,1,0:T(8,128)(2,1)} %refs_0_.3, ...), custom_call_target="tpu_custom_call" | custom-call | flops 21474836480 | bytes 20971520 | tf_op jit(solution)/shard_map/attention_tiles/pallas_call | solution.py:163
  104.1 1.1 copy-done.1
  105.3 6.7 %all-to-all-start.2 = ((bf16[4,3,512,256]{3,2,1,0:T(8,128)(2,1)}), bf16[4,3,512,256]{3,2,1,0:T(8,128)(2,1)}, u32[]{:S(2)}, u32[]{:S(2)}) async-start(bf16[4,3,512,256]{3,2,1,0:T(8,128)(2,1)} %get-tuple-element.65), calls=%async_computation.2 | async-start | bytes 6291456 | tf_op jit(solution)/shard_map/all_to_all | solution.py:377
  112.0 4.6 %collective-permute-start.19 = (bf16[3,512,256]{2,1,0:T(8,128)(2,1)}, bf16[3,512,256]{2,1,0:T(8,128)(2,1)}, u32[]{:S(2)}, u32[]{:S(2)}) collective-permute-start(bf16[3,512,256]{2,1,0:T(8,128)(2,1)} %get-tuple-element.67), channel_id=1, source_target_pairs={{0,2},{1,3},{2,0},{3,1},{4,6},{5,7},{6,4},{7,5},{8,10},{9,11},{10,... | collective-permute-start | bytes 2359304 | tf_op jit(solution)/shard_map/ppermute | solution.py:60
  116.6 2.0 %collective-permute-start.20 = (bf16[3,512,256]{2,1,0:T(8,128)(2,1)S(1)}, bf16[3,512,256]{2,1,0:T(8,128)(2,1)}, u32[]{:S(2)}, u32[]{:S(2)}) collective-permute-start(bf16[3,512,256]{2,1,0:T(8,128)(2,1)S(1)} %get-tuple-element.68), channel_id=1, source_target_pairs={{0,3},{1,0},{2,1},{3,2},{4,7},{5,4},{6,5},{7,6},{8,11},{9,8},{10,9... | collective-permute-start | bytes 2359304 | tf_op jit(solution)/shard_map/ppermute | solution.py:60
  118.6 32.5 %attention_tiles.2 = (bf16[4,3,512,256]{3,2,1,0:T(8,128)(2,1)}, f32[3,512,256]{2,1,0:T(8,128)S(1)}, bf16[3,512,256]{2,1,0:T(8,128)(2,1)S(1)}, bf16[3,512,256]{2,1,0:T(8,128)(2,1)S(1)}, bf16[3,512,256]{2,1,0:T(8,128)(2,1)S(1)}) custom-call(s32[3,16]{1,0:T(4,128)S(1)} %pad_add_fusion.table, bf16[2,512,512]{2,1,0:T(8,128)(2,1)} %refs_0_.3, ...), custom_call_target="tpu_custom_call" | custom-call | flops 21474836480 | bytes 20971520 | tf_op jit(solution)/shard_map/attention_tiles/pallas_call | solution.py:163
  151.1 1.2 copy-done.2
  152.3 0.9 copy-done.3
  153.2 4.9 %all-to-all-start.3 = ((bf16[4,3,512,256]{3,2,1,0:T(8,128)(2,1)}), bf16[4,3,512,256]{3,2,1,0:T(8,128)(2,1)}, u32[]{:S(2)}, u32[]{:S(2)}) async-start(bf16[4,3,512,256]{3,2,1,0:T(8,128)(2,1)} %get-tuple-element.69), calls=%async_computation.3 | async-start | bytes 6291456 | tf_op jit(solution)/shard_map/all_to_all | solution.py:377
  158.2 1.5 collective-permute-start.22
  159.7 1.8 collective-permute-start.23
  161.4 4.5 %summed.2 = (f32[2,512,512]{2,1,0:T(8,128)}, f32[2,512,512]{2,1,0:T(8,128)}, f32[2,512,512]{2,1,0:T(8,128)}) custom-call(bf16[4,3,512,256]{3,2,1,0:T(8,128)(2,1)} %all-to-all-done.2.got_x, f32[3,512,256]{2,1,0:T(8,128)} %copy-done.1, bf16[3,512,256]{2,1,0:T(8,128)(2,1)} %collective-permute-done.18.refs_0_, ...), custom_call_target="tpu_custom_call" | custom-call | tf_op jit(solution)/shard_map/summed/pallas_call | solution.py:227
  165.9 10.9 %collective-permute-done.21.refs_0_ = bf16[3,512,256]{2,1,0:T(8,128)(2,1)S(1)} collective-permute-done((bf16[3,512,256]{2,1,0:T(8,128)(2,1)S(1)}, bf16[3,512,256]{2,1,0:T(8,128)(2,1)S(1)}, u32[]{:S(2)}, u32[]{:S(2)}) %collective-permute-start.21) | collective-permute-done | bytes 786464 | tf_op jit(solution)/shard_map/ppermute | solution.py:60
  176.8 13.0 %collective-permute-done.22.refs_1_ = bf16[3,512,256]{2,1,0:T(8,128)(2,1)S(1)} collective-permute-done((bf16[3,512,256]{2,1,0:T(8,128)(2,1)S(1)}, bf16[3,512,256]{2,1,0:T(8,128)(2,1)S(1)}, u32[]{:S(2)}, u32[]{:S(2)}) %collective-permute-start.22) | collective-permute-done | bytes 786464 | tf_op jit(solution)/shard_map/ppermute | solution.py:60
  189.9 1.0 copy-done.10
  190.9 4.5 %summed.3 = (f32[2,512,512]{2,1,0:T(8,128)}, f32[2,512,512]{2,1,0:T(8,128)}, f32[2,512,512]{2,1,0:T(8,128)}) custom-call(bf16[4,3,512,256]{3,2,1,0:T(8,128)(2,1)} %all-to-all-done.3.got_x, f32[3,512,256]{2,1,0:T(8,128)} %copy-done.2, bf16[3,512,256]{2,1,0:T(8,128)(2,1)} %copy-done.9, ...), custom_call_target="tpu_custom_call", output_to_operand_aliasing={{0}: (5, {}), {1}: (6, {}), {2}: (7, {})} | custom-call | tf_op jit(solution)/shard_map/summed/pallas_call | solution.py:227
  (87 shorter events, 1.4 us)
Async XLA Ops:
  0.6 11.0 %copy-start = (bf16[2,512,512]{2,1,0:T(8,128)(2,1)S(1)}, bf16[2,512,512]{2,1,0:T(8,128)(2,1)}, u32[]{:S(2)}) copy-start(bf16[2,512,512]{2,1,0:T(8,128)(2,1)} %param.12) | copy-start | bytes 3145732
  0.6 1.6 copy-start.6
  0.7 1.9 copy-start.7
  3.6 8.0 %copy-start.8 = (bf16[512,96]{0,1:T(8,128)(2,1)S(1)}, bf16[512,96]{0,1:T(8,128)(2,1)}, u32[]{:S(2)}) copy-start(bf16[512,96]{0,1:T(8,128)(2,1)} %param.13) | copy-start | bytes 294916
  3.6 8.0 %copy-start.12 = (f32[96,512]{1,0:T(8,128)S(1)}, f32[96,512]{1,0:T(8,128)}, u32[]{:S(2)}) copy-start(f32[96,512]{1,0:T(8,128)} %param.14) | copy-start | bytes 589828
  4.6 26.2 %collective-permute-start.1 = (bf16[3,512,256]{2,1,0:T(8,128)(2,1)}, bf16[3,512,256]{2,1,0:T(8,128)(2,1)}, u32[]{:S(2)}, u32[]{:S(2)}) collective-permute-start(bf16[3,512,256]{2,1,0:T(8,128)(2,1)} %pad_maximum_fusion.2), channel_id=1, source_target_pairs={{0,4},{4,8},{8,12},{12,0},{1,5},{5,9},{9,13},{13,1},{2,6},{6,10},{... | collective-permute-start | bytes 2359304 | tf_op jit(solution)/shard_map/ppermute | solution.py:56
  6.1 24.7 %collective-permute-start = (bf16[3,512,256]{2,1,0:T(8,128)(2,1)}, bf16[3,512,256]{2,1,0:T(8,128)(2,1)}, u32[]{:S(2)}, u32[]{:S(2)}) collective-permute-start(bf16[3,512,256]{2,1,0:T(8,128)(2,1)} %pad_maximum_fusion.2), channel_id=1, source_target_pairs={{0,12},{4,0},{8,4},{12,8},{1,13},{5,1},{9,5},{13,9},{2,14},{6,2},{... | collective-permute-start | bytes 2359304 | tf_op jit(solution)/shard_map/ppermute | solution.py:56
  7.6 23.2 %collective-permute-start.3 = (bf16[3,512,256]{2,1,0:T(8,128)(2,1)}, bf16[3,512,256]{2,1,0:T(8,128)(2,1)}, u32[]{:S(2)}, u32[]{:S(2)}) collective-permute-start(bf16[3,512,256]{2,1,0:T(8,128)(2,1)} %pad_maximum_fusion.3), channel_id=1, source_target_pairs={{0,1},{1,2},{2,3},{3,0},{4,5},{5,6},{6,7},{7,4},{8,9},{9,10},{10,1... | collective-permute-start | bytes 2359304 | tf_op jit(solution)/shard_map/ppermute | solution.py:56
  9.5 21.3 %collective-permute-start.2 = (bf16[3,512,256]{2,1,0:T(8,128)(2,1)}, bf16[3,512,256]{2,1,0:T(8,128)(2,1)}, u32[]{:S(2)}, u32[]{:S(2)}) collective-permute-start(bf16[3,512,256]{2,1,0:T(8,128)(2,1)} %pad_maximum_fusion.3), channel_id=1, source_target_pairs={{0,3},{1,0},{2,1},{3,2},{4,7},{5,4},{6,5},{7,6},{8,11},{9,8},{10,9... | collective-permute-start | bytes 2359304 | tf_op jit(solution)/shard_map/ppermute | solution.py:56
  12.1 7.3 %copy-start.14 = (s32[16,16]{1,0:T(8,128)S(1)}, s32[16,16]{1,0:T(8,128)}, u32[]{:S(2)}) copy-start(s32[16,16]{1,0:T(8,128)} %param.23) | copy-start | bytes 3076
  12.1 7.3 %copy-start.15 = (s32[16,16]{1,0:T(8,128)S(1)}, s32[16,16]{1,0:T(8,128)}, u32[]{:S(2)}) copy-start(s32[16,16]{1,0:T(8,128)} %param.22) | copy-start | bytes 3076
  13.3 13.4 %all-to-all-start = ((f32[8,96,128]{2,1,0:T(8,128)}), f32[8,96,128]{2,1,0:T(8,128)S(1)}, u32[]{:S(2)}, u32[]{:S(2)}) async-start(f32[8,96,128]{2,1,0:T(8,128)} %copy.36), calls=%async_computation | async-start | bytes 786432 | tf_op jit(solution)/shard_map/all_to_all | solution.py:283
  23.2 29.7 %copy-start.19 = (s32[1,512]{1,0:T(1,128)S(1)}, s32[1,512]{1,0:T(1,128)}, u32[]{:S(2)}) copy-start(s32[1,512]{1,0:T(1,128)} %param.17) | copy-start | bytes 6148
  26.7 0.7 copy-start.5
  30.8 19.5 %collective-permute-start.4 = (bf16[3,512,256]{2,1,0:T(8,128)(2,1)}, bf16[3,512,256]{2,1,0:T(8,128)(2,1)}, u32[]{:S(2)}, u32[]{:S(2)}) collective-permute-start(bf16[3,512,256]{2,1,0:T(8,128)(2,1)} %pad_maximum_fusion), channel_id=1, source_target_pairs={{0,4},{4,8},{8,12},{12,0},{1,5},{5,9},{9,13},{13,1},{2,6},{6,10},{... | collective-permute-start | bytes 2359304 | tf_op jit(solution)/shard_map/ppermute | solution.py:56
  32.3 20.3 %collective-permute-start.5 = (bf16[3,512,256]{2,1,0:T(8,128)(2,1)}, bf16[3,512,256]{2,1,0:T(8,128)(2,1)}, u32[]{:S(2)}, u32[]{:S(2)}) collective-permute-start(bf16[3,512,256]{2,1,0:T(8,128)(2,1)} %pad_maximum_fusion.1), channel_id=1, source_target_pairs={{0,1},{1,2},{2,3},{3,0},{4,5},{5,6},{6,7},{7,4},{8,9},{9,10},{10,1... | collective-permute-start | bytes 2359304 | tf_op jit(solution)/shard_map/ppermute | solution.py:56
  32.6 10.7 %all-to-all-start.1 = ((bf16[8,96,128]{2,1,0:T(8,128)(2,1)}), bf16[8,96,128]{2,1,0:T(8,128)(2,1)S(1)}, u32[]{:S(2)}, u32[]{:S(2)}) async-start(bf16[8,96,128]{2,1,0:T(8,128)(2,1)} %score_gradient.1), calls=%async_computation.1 | async-start | bytes 393216 | tf_op jit(solution)/shard_map/all_to_all | solution.py:292
  37.1 21.9 %collective-permute-start.16 = (bf16[3,512,256]{2,1,0:T(8,128)(2,1)}, bf16[3,512,256]{2,1,0:T(8,128)(2,1)S(1)}, u32[]{:S(2)}, u32[]{:S(2)}) collective-permute-start(bf16[3,512,256]{2,1,0:T(8,128)(2,1)} %collective-permute-done.refs_5_), channel_id=1, source_target_pairs={{0,12},{4,0},{8,4},{12,8},{1,13},{5,1},{9,5},{13,9},{2,14},{6,2},{... | collective-permute-start | bytes 2359304 | tf_op jit(solution)/shard_map/ppermute | solution.py:56
  37.7 22.5 %collective-permute-start.17 = (bf16[3,512,256]{2,1,0:T(8,128)(2,1)}, bf16[3,512,256]{2,1,0:T(8,128)(2,1)}, u32[]{:S(2)}, u32[]{:S(2)}) collective-permute-start(bf16[3,512,256]{2,1,0:T(8,128)(2,1)} %collective-permute-done.2.refs_8_), channel_id=1, source_target_pairs={{0,3},{1,0},{2,1},{3,2},{4,7},{5,4},{6,5},{7,6},{8,11},{9,8},{10,9... | collective-permute-start | bytes 2359304 | tf_op jit(solution)/shard_map/ppermute | solution.py:56
  53.8 1.0 copy-start.13
  54.9 16.7 %copy-start.11 = (bf16[2,128,512]{2,1,0:T(8,128)(2,1)}, bf16[2,128,512]{2,1,0:T(8,128)(2,1)S(1)}, u32[]{:S(2)}) copy-start(bf16[2,128,512]{2,1,0:T(8,128)(2,1)S(1)} %fusion.12.refs_3_) | copy-start | bytes 786436
  54.9 8.1 %collective-permute-start.15 = (bf16[128,512]{1,0:T(8,128)(2,1)S(1)}, bf16[128,512]{1,0:T(8,128)(2,1)S(1)}, u32[]{:S(2)}, u32[]{:S(2)}) collective-permute-start(bf16[128,512]{1,0:T(8,128)(2,1)S(1)} %get-tuple-element.103), channel_id=1, source_target_pairs={{0,1},{1,2},{2,3},{3,0},{4,5},{5,6},{6,7},{7,4},{8,9},{9,10},{10,1... | collective-permute-start | bytes 393224 | tf_op jit(solution)/shard_map/ppermute | solution.py:56
  55.6 9.8 %collective-permute-start.14 = (bf16[128,512]{1,0:T(8,128)(2,1)S(1)}, bf16[128,512]{1,0:T(8,128)(2,1)}, u32[]{:S(2)}, u32[]{:S(2)}) collective-permute-start(bf16[128,512]{1,0:T(8,128)(2,1)S(1)} %get-tuple-element.103), channel_id=1, source_target_pairs={{0,2},{1,3},{2,0},{3,1},{4,6},{5,7},{6,4},{7,5},{8,10},{9,11},{10,... | collective-permute-start | bytes 393224 | tf_op jit(solution)/shard_map/ppermute | solution.py:56
  58.0 9.7 %collective-permute-start.13 = (bf16[128,512]{1,0:T(8,128)(2,1)S(1)}, bf16[128,512]{1,0:T(8,128)(2,1)}, u32[]{:S(2)}, u32[]{:S(2)}) collective-permute-start(bf16[128,512]{1,0:T(8,128)(2,1)S(1)} %get-tuple-element.103), channel_id=1, source_target_pairs={{0,3},{1,0},{2,1},{3,2},{4,7},{5,4},{6,5},{7,6},{8,11},{9,8},{10,9... | collective-permute-start | bytes 393224 | tf_op jit(solution)/shard_map/ppermute | solution.py:56
  59.0 12.5 %copy-start.16 = (bf16[3,512,256]{2,1,0:T(8,128)(2,1)}, bf16[3,512,256]{2,1,0:T(8,128)(2,1)S(1)}, u32[]{:S(2)}) copy-start(bf16[3,512,256]{2,1,0:T(8,128)(2,1)S(1)} %collective-permute-done.16.refs_6_) | copy-start | bytes 2359300
  59.0 10.6 %collective-permute-start.12 = (bf16[128,512]{1,0:T(8,128)(2,1)S(1)}, bf16[128,512]{1,0:T(8,128)(2,1)}, u32[]{:S(2)}, u32[]{:S(2)}) collective-permute-start(bf16[128,512]{1,0:T(8,128)(2,1)S(1)} %get-tuple-element.104), channel_id=1, source_target_pairs={{0,4},{4,8},{8,12},{12,0},{1,5},{5,9},{9,13},{13,1},{2,6},{6,10},{... | collective-permute-start | bytes 393224 | tf_op jit(solution)/shard_map/ppermute | solution.py:56
  60.2 11.3 %collective-permute-start.11 = (bf16[128,512]{1,0:T(8,128)(2,1)S(1)}, bf16[128,512]{1,0:T(8,128)(2,1)}, u32[]{:S(2)}, u32[]{:S(2)}) collective-permute-start(bf16[128,512]{1,0:T(8,128)(2,1)S(1)} %get-tuple-element.104), channel_id=1, source_target_pairs={{0,8},{4,12},{8,0},{12,4},{1,9},{5,13},{9,1},{13,5},{2,10},{6,14},... | collective-permute-start | bytes 393224 | tf_op jit(solution)/shard_map/ppermute | solution.py:56
  63.0 8.6 %copy-start.18 = (bf16[128,512]{1,0:T(8,128)(2,1)}, bf16[128,512]{1,0:T(8,128)(2,1)S(1)}, u32[]{:S(2)}) copy-start(bf16[128,512]{1,0:T(8,128)(2,1)S(1)} %collective-permute-done.15.refs_16_) | copy-start | bytes 393220
  63.0 8.6 %collective-permute-start.10 = (bf16[128,512]{1,0:T(8,128)(2,1)S(1)}, bf16[128,512]{1,0:T(8,128)(2,1)}, u32[]{:S(2)}, u32[]{:S(2)}) collective-permute-start(bf16[128,512]{1,0:T(8,128)(2,1)S(1)} %get-tuple-element.104), channel_id=1, source_target_pairs={{0,12},{4,0},{8,4},{12,8},{1,13},{5,1},{9,5},{13,9},{2,14},{6,2},{... | collective-permute-start | bytes 393224 | tf_op jit(solution)/shard_map/ppermute | solution.py:56
  65.4 46.5 %collective-permute-start.6 = (bf16[3,512,256]{2,1,0:T(8,128)(2,1)}, bf16[3,512,256]{2,1,0:T(8,128)(2,1)S(1)}, u32[]{:S(2)}, u32[]{:S(2)}) collective-permute-start(bf16[3,512,256]{2,1,0:T(8,128)(2,1)} %pad_maximum_fusion), channel_id=1, source_target_pairs={{0,12},{4,0},{8,4},{12,8},{1,13},{5,1},{9,5},{13,9},{2,14},{6,2},{... | collective-permute-start | bytes 2359304 | tf_op jit(solution)/shard_map/ppermute | solution.py:56
  67.7 48.9 %collective-permute-start.8 = (bf16[3,512,256]{2,1,0:T(8,128)(2,1)}, bf16[3,512,256]{2,1,0:T(8,128)(2,1)}, u32[]{:S(2)}, u32[]{:S(2)}) collective-permute-start(bf16[3,512,256]{2,1,0:T(8,128)(2,1)} %pad_maximum_fusion.1), channel_id=1, source_target_pairs={{0,3},{1,0},{2,1},{3,2},{4,7},{5,4},{6,5},{7,6},{8,11},{9,8},{10,9... | collective-permute-start | bytes 2359304 | tf_op jit(solution)/shard_map/ppermute | solution.py:56
  69.6 49.0 %collective-permute-start.7 = (bf16[3,512,256]{2,1,0:T(8,128)(2,1)}, bf16[3,512,256]{2,1,0:T(8,128)(2,1)}, u32[]{:S(2)}, u32[]{:S(2)}) collective-permute-start(bf16[3,512,256]{2,1,0:T(8,128)(2,1)} %collective-permute-done.4.refs_7_), channel_id=1, source_target_pairs={{0,4},{4,8},{8,12},{12,0},{1,5},{5,9},{9,13},{13,1},{2,6},{6,10},{... | collective-permute-start | bytes 2359304 | tf_op jit(solution)/shard_map/ppermute | solution.py:56
  71.5 47.1 %collective-permute-start.9 = (bf16[3,512,256]{2,1,0:T(8,128)(2,1)}, bf16[3,512,256]{2,1,0:T(8,128)(2,1)}, u32[]{:S(2)}, u32[]{:S(2)}) collective-permute-start(bf16[3,512,256]{2,1,0:T(8,128)(2,1)} %collective-permute-done.5.refs_10_), channel_id=1, source_target_pairs={{0,1},{1,2},{2,3},{3,0},{4,5},{5,6},{6,7},{7,4},{8,9},{9,10},{10,1... | collective-permute-start | bytes 2359304 | tf_op jit(solution)/shard_map/ppermute | solution.py:56
  104.1 1.1 copy-start.1
  105.3 48.0 %all-to-all-start.2 = ((bf16[4,3,512,256]{3,2,1,0:T(8,128)(2,1)}), bf16[4,3,512,256]{3,2,1,0:T(8,128)(2,1)}, u32[]{:S(2)}, u32[]{:S(2)}) async-start(bf16[4,3,512,256]{3,2,1,0:T(8,128)(2,1)} %get-tuple-element.65), calls=%async_computation.2 | async-start | bytes 6291456 | tf_op jit(solution)/shard_map/all_to_all | solution.py:377
  111.9 41.3 %collective-permute-start.18 = (bf16[3,512,256]{2,1,0:T(8,128)(2,1)}, bf16[3,512,256]{2,1,0:T(8,128)(2,1)}, u32[]{:S(2)}, u32[]{:S(2)}) collective-permute-start(bf16[3,512,256]{2,1,0:T(8,128)(2,1)} %get-tuple-element.66), channel_id=1, source_target_pairs={{0,1},{1,2},{2,3},{3,0},{4,5},{5,6},{6,7},{7,4},{8,9},{9,10},{10,1... | collective-permute-start | bytes 2359304 | tf_op jit(solution)/shard_map/ppermute | solution.py:60
  111.9 6.7 %copy-start.17 = (bf16[3,512,256]{2,1,0:T(8,128)(2,1)}, bf16[3,512,256]{2,1,0:T(8,128)(2,1)S(1)}, u32[]{:S(2)}) copy-start(bf16[3,512,256]{2,1,0:T(8,128)(2,1)S(1)} %collective-permute-done.6.refs_5_) | copy-start | bytes 2359300
  112.0 41.3 %collective-permute-start.19 = (bf16[3,512,256]{2,1,0:T(8,128)(2,1)}, bf16[3,512,256]{2,1,0:T(8,128)(2,1)}, u32[]{:S(2)}, u32[]{:S(2)}) collective-permute-start(bf16[3,512,256]{2,1,0:T(8,128)(2,1)} %get-tuple-element.67), channel_id=1, source_target_pairs={{0,2},{1,3},{2,0},{3,1},{4,6},{5,7},{6,4},{7,5},{8,10},{9,11},{10,... | collective-permute-start | bytes 2359304 | tf_op jit(solution)/shard_map/ppermute | solution.py:60
  116.6 36.6 %collective-permute-start.20 = (bf16[3,512,256]{2,1,0:T(8,128)(2,1)S(1)}, bf16[3,512,256]{2,1,0:T(8,128)(2,1)}, u32[]{:S(2)}, u32[]{:S(2)}) collective-permute-start(bf16[3,512,256]{2,1,0:T(8,128)(2,1)S(1)} %get-tuple-element.68), channel_id=1, source_target_pairs={{0,3},{1,0},{2,1},{3,2},{4,7},{5,4},{6,5},{7,6},{8,11},{9,8},{10,9... | collective-permute-start | bytes 2359304 | tf_op jit(solution)/shard_map/ppermute | solution.py:60
  151.1 1.2 copy-start.2
  152.3 0.9 copy-start.3
  153.2 5.0 %copy-start.4 = (bf16[3,512,256]{2,1,0:T(8,128)(2,1)S(1)}, bf16[3,512,256]{2,1,0:T(8,128)(2,1)}, u32[]{:S(2)}) copy-start(bf16[3,512,256]{2,1,0:T(8,128)(2,1)} %copy-done.3) | copy-start | bytes 2359300
  153.2 37.6 %all-to-all-start.3 = ((bf16[4,3,512,256]{3,2,1,0:T(8,128)(2,1)}), bf16[4,3,512,256]{3,2,1,0:T(8,128)(2,1)}, u32[]{:S(2)}, u32[]{:S(2)}) async-start(bf16[4,3,512,256]{3,2,1,0:T(8,128)(2,1)} %get-tuple-element.69), calls=%async_computation.3 | async-start | bytes 6291456 | tf_op jit(solution)/shard_map/all_to_all | solution.py:377
  158.2 18.7 %collective-permute-start.21 = (bf16[3,512,256]{2,1,0:T(8,128)(2,1)S(1)}, bf16[3,512,256]{2,1,0:T(8,128)(2,1)S(1)}, u32[]{:S(2)}, u32[]{:S(2)}) collective-permute-start(bf16[3,512,256]{2,1,0:T(8,128)(2,1)S(1)} %copy-done.4), channel_id=1, source_target_pairs={{0,1},{1,2},{2,3},{3,0},{4,5},{5,6},{6,7},{7,4},{8,9},{9,10},{10,1... | collective-permute-start | bytes 2359304 | tf_op jit(solution)/shard_map/ppermute | solution.py:60
  158.2 31.7 %collective-permute-start.22 = (bf16[3,512,256]{2,1,0:T(8,128)(2,1)S(1)}, bf16[3,512,256]{2,1,0:T(8,128)(2,1)S(1)}, u32[]{:S(2)}, u32[]{:S(2)}) collective-permute-start(bf16[3,512,256]{2,1,0:T(8,128)(2,1)S(1)} %get-tuple-element.72), channel_id=1, source_target_pairs={{0,2},{1,3},{2,0},{3,1},{4,6},{5,7},{6,4},{7,5},{8,10},{9,11},{10,... | collective-permute-start | bytes 2359304 | tf_op jit(solution)/shard_map/ppermute | solution.py:60
  159.7 31.2 %collective-permute-start.23 = (bf16[3,512,256]{2,1,0:T(8,128)(2,1)S(1)}, bf16[3,512,256]{2,1,0:T(8,128)(2,1)}, u32[]{:S(2)}, u32[]{:S(2)}) collective-permute-start(bf16[3,512,256]{2,1,0:T(8,128)(2,1)S(1)} %get-tuple-element.73), channel_id=1, source_target_pairs={{0,3},{1,0},{2,1},{3,2},{4,7},{5,4},{6,5},{7,6},{8,11},{9,8},{10,9... | collective-permute-start | bytes 2359304 | tf_op jit(solution)/shard_map/ppermute | solution.py:60
  176.8 13.1 %copy-start.9 = (bf16[3,512,256]{2,1,0:T(8,128)(2,1)}, bf16[3,512,256]{2,1,0:T(8,128)(2,1)S(1)}, u32[]{:S(2)}) copy-start(bf16[3,512,256]{2,1,0:T(8,128)(2,1)S(1)} %collective-permute-done.21.refs_0_) | copy-start | bytes 2359300
  189.9 1.0 copy-start.10

commit v5 on v4

--- a/solution.py
+++ b/solution.py
@@ -11,6 +11,7 @@
 
 KB = 128
 SIDE = 4
+GROUP = 2
 MEMBER = ("y", "core")
 LOSS_SCALE = 4096.0
 FAIR_EPS = 0.05
@@ -20,30 +21,36 @@
 BF16 = jnp.bfloat16
 
 
-def score_kernel(forecast_ref, truth_ref, area_ref, out_ref):
+def score_kernel(forecast_ref, truth_ref, area_ref, out_ref, swapped_ref):
     groups, _, lanes = forecast_ref.shape
     count = 2 * groups
-    swapped = [pltpu.roll(forecast_ref[j], lanes // 2, 1) for j in range(groups)]
+    for k in range(groups):
+        swapped_ref[k] = pltpu.roll(forecast_ref[k], lanes // 2, 1)
+    weight = LOSS_SCALE * area_ref[...]
 
     def unit(x):
         return x * (1.0 / jnp.sqrt(jnp.sum(x * x, axis=0, keepdims=True) + NORM_EPS))
 
-    weight = LOSS_SCALE * area_ref[...]
-    for j in range(groups):
+    def one_group(j, carry):
         one = forecast_ref[j]
-        total = unit(one - swapped[j])
+        total = jnp.zeros_like(one)
         for k in range(groups):
-            if k != j:
-                total = total + unit(one - forecast_ref[k]) + unit(one - swapped[k])
+            total = total + unit(one - forecast_ref[k]) + unit(one - swapped_ref[k])
         gradient = weight * (
             unit(one - truth_ref[...]) / count - (1.0 - FAIR_EPS) / (count * (count - 1)) * total
         )
         out_ref[j] = gradient.astype(BF16)
+        return carry
+
+    lax.fori_loop(0, groups, one_group, 0)
 
 
 def score_gradient(forecasts, truth, area):
     return pl.pallas_call(
-        score_kernel, out_shape=jax.ShapeDtypeStruct(forecasts.shape, BF16), name="score_gradient"
+        score_kernel,
+        out_shape=jax.ShapeDtypeStruct(forecasts.shape, BF16),
+        scratch_shapes=[pltpu.VMEM(forecasts.shape, F32)],
+        name="score_gradient",
     )(forecasts, truth, area)
 
 
@@ -60,69 +67,53 @@
     return lax.ppermute(x, axis, [(i, (i + distance) % SIDE) for i in range(SIDE)])
 
 
-def head_pair_tiles(table, base, kv, queries, lates, decoder, out, scratch):
-    q_stack, g_stack, stat_rows, joined, dk_acc, dv_acc, dq_acc = scratch
-    rows = q_stack.shape[1] // 2
-    channels = decoder.shape[1]
-    head = pl.program_id(0) * 2 + base
+def head_pair_tiles(table, scratch):
+    kv_rows, q_rows, g_rows, lse_rows, delta_rows, dq_rows, dk_acc, dv_acc = scratch
     head_dim = 64
     score_scale = head_dim ** (-0.5)
-    lane = lax.broadcasted_iota(jnp.int32, (rows, 2 * head_dim), 1)
-    first = lane < head_dim
+    keys = GROUP * KB
+    first = lax.broadcasted_iota(jnp.int32, (keys, 2 * head_dim), 1) < head_dim
     nt = (((1,), (1,)), ((), ()))
-    tn = (((0,), (1,)), ((), ()))
-    for t in range(SIDE):
-        q = queries[t][...].astype(F32)
-        g = lax.dot_general(
-            lates[t][:channels, :], decoder[...], tn, preferred_element_type=F32
-        )
-        q_stack[t, :rows] = jnp.where(first, q, 0.0).astype(BF16)
-        q_stack[t, rows:] = jnp.where(first, 0.0, q).astype(BF16)
-        g_stack[t, :rows] = jnp.where(first, g, 0.0).astype(BF16)
-        g_stack[t, rows:] = jnp.where(first, 0.0, g).astype(BF16)
-        stat = lates[t][channels:, :].astype(F32)
-        joined[: stat.shape[0] // 2] = stat[: stat.shape[0] // 2] + stat[stat.shape[0] // 2 :]
-        for n in range(2):
-            stat_rows[t, n : n + 1, :rows] = joined[pl.ds(8 * n + head, 1), :]
-            stat_rows[t, n : n + 1, rows:] = joined[pl.ds(8 * n + head + 1, 1), :]
     dk_acc[...] = jnp.zeros_like(dk_acc)
     dv_acc[...] = jnp.zeros_like(dv_acc)
 
-    def one_query_block(t, carry):
-        q = q_stack[t]
-        g = g_stack[t]
-        lse = stat_rows[t, 0:1, :] * LOG2E
-        delta = stat_rows[t, 1:2, :]
-        dq_acc[...] = jnp.zeros_like(dq_acc)
-        for pair in ((0, 1), (2, 3)):
-            starts = [pl.multiple_of(table[t * SIDE + a] * KB, KB) for a in pair]
-            k = jnp.concatenate([kv[a][0][pl.ds(s, KB), :] for a, s in zip(pair, starts)], axis=0)
-            v = jnp.concatenate([kv[a][1][pl.ds(s, KB), :] for a, s in zip(pair, starts)], axis=0)
+    def by_head(x):
+        x = x.astype(F32)
+        return jnp.concatenate(
+            [jnp.where(first, x, 0.0).astype(BF16), jnp.where(first, 0.0, x).astype(BF16)], axis=0
+        )
+
+    for t in range(SIDE):
+        q, g = q_rows[t], g_rows[t]
+        dq = None
+        for start in range(0, SIDE, GROUP):
+            group = range(start, start + GROUP)
+            starts = [pl.multiple_of(table[t * SIDE + a] * KB, KB) for a in group]
+            k, v = (
+                by_head(
+                    jnp.concatenate([kv_rows[a, i, pl.ds(s, KB), :] for a, s in zip(group, starts)], axis=0)
+                )
+                for i in range(2)
+            )
             scores = lax.dot_general(k, q, nt, preferred_element_type=F32)
-            p = jnp.exp2(scores * (score_scale * LOG2E) - lse)
             dp = lax.dot_general(v, g, nt, preferred_element_type=F32)
-            ds = (p * (dp - delta)).astype(BF16)
-            dv = jnp.dot(p.astype(BF16), g, preferred_element_type=F32)
+            ps, dss = [], []
+            for n in range(2):
+                part = slice(n * keys, (n + 1) * keys)
+                p = jnp.exp2(scores[part] * (score_scale * LOG2E) - lse_rows[t, n : n + 1, :] * LOG2E)
+                ps.append(p.astype(BF16))
+                dss.append((p * (dp[part] - delta_rows[t, n : n + 1, :])).astype(BF16))
+            p, ds = jnp.concatenate(ps, axis=0), jnp.concatenate(dss, axis=0)
+            dv = jnp.dot(p, g, preferred_element_type=F32)
             dk = jnp.dot(ds, q, preferred_element_type=F32)
-            for n, (a, s) in enumerate(zip(pair, starts)):
+            dv = jnp.where(first, dv[:keys], dv[keys:])
+            dk = jnp.where(first, dk[:keys], dk[keys:])
+            for n, (a, s) in enumerate(zip(group, starts)):
                 dv_acc[a, pl.ds(s, KB), :] += dv[n * KB : (n + 1) * KB]
                 dk_acc[a, pl.ds(s, KB), :] += dk[n * KB : (n + 1) * KB]
-            kt = k.T
-            dq_acc[:head_dim] += jnp.dot(kt[:head_dim], ds[:, :rows], preferred_element_type=F32)
-            dq_acc[head_dim:] += jnp.dot(kt[head_dim:], ds[:, rows:], preferred_element_type=F32)
-        dq = dq_acc[...].T * score_scale
-        for n in range(SIDE):
-
-            @pl.when(t == n)
-            def _():
-                out(2, n, dq)
-
-        return carry
-
-    lax.fori_loop(0, SIDE, one_query_block, 0)
-    for a in range(SIDE):
-        out(0, a, dk_acc[a] * score_scale)
-        out(1, a, dv_acc[a])
+            part = jnp.dot(k.T, ds, preferred_element_type=F32)
+            dq = part if dq is None else dq + part
+        dq_rows[t] = dq.T
 
 
 def tile_kernel(table, *refs, base):
@@ -131,15 +122,35 @@
     late_x, late_z = refs[11:14], refs[14:17]
     send_x, own_z, send_z = refs[17], refs[18], refs[19:22]
     scratch = refs[22:]
+    kv_rows, q_rows, g_rows, lse_rows, delta_rows, dq_rows, dk_acc, dv_acc = scratch
     sides = ((fetch_x, late_x), (fetch_z, late_z))
-    for m in range(2):
+    channels = decoder.shape[1]
+    head = pl.program_id(0) * 2 + base
+    score_scale = 64 ** (-0.5)
+    tn = (((0,), (1,)), ((), ()))
+
+    def load(m):
         key_fetch = sides[m][0]
         query_fetch, late = sides[1 - m]
-        kv = [(key_own.at[m], value_own.at[m])] + [(r.at[0], r.at[1]) for r in key_fetch]
-        queries = [query_own.at[m]] + [r.at[2] for r in query_fetch]
-        lates = [late_own.at[m]] + list(late)
-
-        def out(kind, n, value, m=m):
+        for n in range(SIDE):
+            kv_rows[n, 0] = key_own[m] if n == 0 else key_fetch[n - 1][0]
+            kv_rows[n, 1] = value_own[m] if n == 0 else key_fetch[n - 1][1]
+            q_rows[n] = query_own[m] if n == 0 else query_fetch[n - 1][2]
+            package = late_own.at[m] if n == 0 else late[n - 1]
+            g_rows[n] = lax.dot_general(
+                package[:channels, :], decoder[...], tn, preferred_element_type=F32
+            ).astype(BF16)
+            stat = package[channels:, :].astype(F32)
+            stat = stat[: stat.shape[0] // 2] + stat[stat.shape[0] // 2 :]
+            lse_rows[n], delta_rows[n] = stat[:8], stat[8:]
+            for i in range(2):
+                lse_rows[n, i : i + 1, :], delta_rows[n, i : i + 1, :] = (
+                    lse_rows[n, pl.ds(head + i, 1), :],
+                    delta_rows[n, pl.ds(head + i, 1), :],
+                )
+
+    def store(m):
+        def out(kind, n, value):
             if m == (1 if kind == 2 else 0):
                 send_x[table[2, n], kind] = value.astype(BF16)
             elif n == 0:
@@ -147,9 +158,20 @@
             else:
                 send_z[n - 1][kind] = value.astype(BF16)
 
-        head_pair_tiles(
-            table.at[m], base, kv, queries, lates, decoder, out, scratch
-        )
+        for n in range(SIDE):
+            out(0, n, dk_acc[n] * score_scale)
+            out(1, n, dv_acc[n])
+            out(2, n, dq_rows[n] * score_scale)
+
+    def one_member(m, carry):
+        for n in range(2):
+            pl.when(m == n)(functools.partial(load, n))
+        head_pair_tiles(table.at[m], scratch)
+        for n in range(2):
+            pl.when(m == n)(functools.partial(store, n))
+        return carry
+
+    lax.fori_loop(0, 2, one_member, 0)
 
 
 def attention_tiles(half, tables, key_rows, value_rows, query, fetched_x, fetched_z, late_own, late_x, late_z, decoder_matrix):
@@ -180,13 +202,14 @@
             out_specs=[pl.BlockSpec((SIDE, 3, rows, 128), lambda h, tab: (0, 0, 0, h))]
             + [far_spec] * 4,
             scratch_shapes=[
-                pltpu.VMEM((SIDE, 2 * rows, 128), BF16),
-                pltpu.VMEM((SIDE, 2 * rows, 128), BF16),
-                pltpu.VMEM((SIDE, 2, 2 * rows), F32),
-                pltpu.VMEM((16, rows), F32),
+                pltpu.VMEM((SIDE, 2, rows, 128), BF16),
+                pltpu.VMEM((SIDE, rows, 128), BF16),
+                pltpu.VMEM((SIDE, rows, 128), BF16),
+                pltpu.VMEM((SIDE, 8, rows), F32),
+                pltpu.VMEM((SIDE, 8, rows), F32),
                 pltpu.VMEM((SIDE, rows, 128), F32),
                 pltpu.VMEM((SIDE, rows, 128), F32),
-                pltpu.VMEM((128, rows), F32),
+                pltpu.VMEM((SIDE, rows, 128), F32),
             ],
         ),
         compiler_params=pltpu.CompilerParams(
@@ -203,7 +226,7 @@
         *in_hbm(key_rows, value_rows, query, late_own, decoder_matrix),
         *in_hbm(*fetched_x, *fetched_z, *late_x, *late_z),
     )
-    return out[0], out[1], out[2:]
+    return in_hbm(out[0])[0], out[1], in_hbm(*out[2:])
 
 
 def sum_kernel(got_x, own_z, *refs):
@@ -221,26 +244,47 @@
 
 def summed(half, got_x, own_z, got_z, outs):
     _, rows, lanes = own_z.shape
-    z_spec = pl.BlockSpec((3, rows // 2, lanes), lambda r: (0, r, 0))
+    z_spec = pl.BlockSpec((3, rows // 4, lanes), lambda r: (0, r, 0))
     shape = jax.ShapeDtypeStruct((2, rows, 2 * lanes), F32)
     kept = list(outs) if outs else []
     return pl.pallas_call(
         sum_kernel,
         out_shape=[shape] * 3,
-        grid=(2,),
-        in_specs=[pl.BlockSpec((SIDE, 3, rows // 2, lanes), lambda r: (0, 0, r, 0))]
+        grid=(4,),
+        in_specs=[pl.BlockSpec((SIDE, 3, rows // 4, lanes), lambda r: (0, 0, r, 0))]
         + [z_spec] * 4
         + [pl.BlockSpec(memory_space=pl.ANY)] * len(kept),
-        out_specs=[pl.BlockSpec((2, rows // 2, lanes), lambda r: (0, r, half))] * 3,
+        out_specs=[pl.BlockSpec((2, rows // 4, lanes), lambda r: (0, r, half))] * 3,
         input_output_aliases={5 + n: n for n in range(len(kept))},
         compiler_params=pltpu.CompilerParams(vmem_limit_bytes=50 * 1024 * 1024),
         name="summed",
-    )(*in_hbm(got_x, own_z, *got_z), *kept)
-
-
-def outgoing(half, *arrays):
-    lanes = arrays[0].shape[-1] // 2
-    return jnp.stack([a[:, half * lanes : (half + 1) * lanes] for a in arrays])
+    )(*in_hbm(got_x), own_z, *in_hbm(*got_z), *kept)
+
+
+def pack_kernel(key_rows, value_rows, query, along_x, along_z, sems, *, half):
+    lanes = along_x.shape[-1]
+    part = pl.ds(half * lanes, lanes)
+    copies = []
+    for m, out in enumerate((along_x, along_z)):
+        for n, ref in enumerate((key_rows.at[m], value_rows.at[m], query.at[1 - m])):
+            copies.append(pltpu.make_async_copy(ref.at[:, part], out.at[n], sems.at[m, n]))
+    for copy in copies:
+        copy.start()
+    for copy in copies:
+        copy.wait()
+
+
+def outgoing(half, key_rows, value_rows, query):
+    _, rows, width = key_rows.shape
+    anywhere = pl.BlockSpec(memory_space=pl.ANY)
+    return pl.pallas_call(
+        functools.partial(pack_kernel, half=half),
+        out_shape=[jax.ShapeDtypeStruct((3, rows, width // 2), BF16)] * 2,
+        in_specs=[anywhere] * 3,
+        out_specs=[anywhere] * 2,
+        scratch_shapes=[pltpu.SemaphoreType.DMA((2, 3))],
+        name="outgoing",
+    )(*in_hbm(key_rows, value_rows, query))
 
 
 def in_hbm(*arrays):
@@ -266,11 +310,9 @@
     x_at = lax.axis_index("x")
     z_at = lax.axis_index("z")
 
-    own = [
-        (outgoing(h, key_rows[0], value_rows[0], query[1]), outgoing(h, key_rows[1], value_rows[1], query[0]))
-        for h in range(2)
-    ]
-    near = [fetched(a, axis, d) for a, axis in zip(own[0], ("x", "z")) for d in (1, 3)]
+    own_0 = outgoing(0, key_rows, value_rows, query)
+    near = [fetched(a, axis, d) for a, axis in zip(own_0, ("x", "z")) for d in (1, 3)]
+    own_1 = outgoing(1, key_rows, value_rows, query)
 
     forecast = baseline_field[None] + jnp.einsum(
         "mou,ut->mto", hidden_embedding, decoder_matrix, preferred_element_type=F32
@@ -288,11 +330,12 @@
     derivative = score_gradient(
         everyone, jnp.tile(observed, (1, members)), jnp.tile(area[None], (1, members))
     )
-    derivative, own_1, near = lax.optimization_barrier((derivative, own[1], near))
+    derivative, own_1, near, decoder_rows = lax.optimization_barrier(
+        (derivative, own_1, near, in_hbm(decoder_matrix)[0])
+    )
     returned = lax.all_to_all(derivative, MEMBER, 0, 0, tiled=True)
     far = [fetched(near[0], "x", 1), fetched(near[2], "z", 1)]
     before = [fetched(a, axis, 3) for a, axis in zip(own_1, ("x", "z"))]
-    returned, own_1, before = lax.optimization_barrier((returned, own_1, before))
     grad_forecast = (
         returned.reshape(groups, channels, members, span)
         .transpose(2, 1, 0, 3)
@@ -366,7 +409,7 @@
             late_own,
             late_x,
             late_z,
-            decoder_matrix,
+            decoder_rows,
         )
         if parts:
             (first_x, first_own, first_z) = parts[0]

time: 196 us -> 291 us (1.48)
  Pallas kernels: 77.2 us -> 167 us
  waiting for transfers between devices: 38.8 us -> 54.5 us
  other arithmetic: 6.85 us -> 2.02 us
  starting transfers between devices: 55.7 us -> 51.1 us
    pallas_call x2 -> x4, Pallas kernels: 8.94 us -> 107 us  [the longest x2 97.6 us: outgoing(): pl.pallas_call(functools.partial(pack_kernel, half=half), out_shape=[jax....]
    ppermute x18, waiting for transfers between devices: 9.6 us -> 27.2 us  [fetched(): lax.ppermute(x, axis, [(i, (i - distance) % SIDE) for i in range(SIDE)])]
    pallas_call x2, Pallas kernels: 65 us -> 56.8 us  [attention_tiles(): pl.pallas_call(functools.partial(tile_kernel, base=2 * base), out_shape=[...]
    another operation x4 -> x0, other arithmetic: 4.83 us -> none  [outgoing(): return jnp.stack([a[:, half * lanes:(half + 1) * lanes] for a in arrays])]
    ppermute x18, starting transfers between devices: 25.9 us -> 22.2 us  [fetched(): lax.ppermute(x, axis, [(i, (i - distance) % SIDE) for i in range(SIDE)])]
    unnamed x41 -> x40, local copies, waits for them, and re-layouts: 6.22 us -> 6.01 us
  transfers between devices with their start and end apart: 28 -> 28, of which waited for: 7 -> 7; matrix products, arithmetic and copies ran while one was open for 7% -> 3% of each run, Pallas kernels for 37% -> 39%
where the time goes in v5:
time: 291 us; the launch traced here: 290 us
  Pallas kernels  167 us (57%)
  waiting for transfers between devices  54.5 us (19%)
  starting transfers between devices  51.1 us (18%)
  local copies, waits for them, and re-layouts  11.5 us (4%)
    pallas_call x2, Pallas kernels, outgoing(): pl.pallas_call(functools.partial(pack_kernel, half=half), out_shape=[jax....  97.6 us
    pallas_call x2, Pallas kernels, attention_tiles(): pl.pallas_call(functools.partial(tile_kernel, base=2 * base), out_shape=[...  56.8 us
    ppermute x18, waiting for transfers between devices, fetched(): lax.ppermute(x, axis, [(i, (i - distance) % SIDE) for i in range(SIDE)])  27.2 us
    ppermute x6, waiting for transfers between devices, delivered(): lax.ppermute(x, axis, [(i, (i + distance) % SIDE) for i in range(SIDE)])  25.8 us
    ppermute x18, starting transfers between devices, fetched(): lax.ppermute(x, axis, [(i, (i - distance) % SIDE) for i in range(SIDE)])  22.2 us
    all_to_all x2, starting transfers between devices, shards(): got_x = lax.all_to_all(send_x, 'x', 0, 0, tiled=True)  9.97 us
    pallas_call x2, Pallas kernels, summed(): pl.pallas_call(sum_kernel, out_shape=[shape] * 3, grid=(4,), in_specs=[pl...  9.71 us
    ppermute x6, starting transfers between devices, delivered(): lax.ppermute(x, axis, [(i, (i + distance) % SIDE) for i in range(SIDE)])  9.55 us
  transfers between devices with their start and end apart: 28, of which 7 were waited for; matrix products, arithmetic and copies ran while one was open for 3% of the time, Pallas kernels for 39%

profile of v5, /device:TPU:2, one launch (start us, length us, event | category | flops | bytes accessed | tf_op | source)
XLA Modules:
  0.0 290.0 jit_solution(18173057818811706468)
XLA Ops:
  0.7 48.8 %outgoing.3 = (bf16[3,512,256]{2,1,0:T(8,128)(2,1)}, bf16[3,512,256]{2,1,0:T(8,128)(2,1)}) custom-call(bf16[2,512,512]{2,1,0:T(8,128)(2,1)} %refs_0_.3, bf16[2,512,512]{2,1,0:T(8,128)(2,1)} %refs_1_.3, bf16[2,512,512]{2,1,0:T(8,128)(2,1)} %refs_2_.3), custom_call_target="tpu_custom_call" | custom-call | tf_op jit(solution)/shard_map/outgoing/pallas_call | solution.py:280
  49.5 1.6 collective-permute-start.1
  51.0 0.5 collective-permute-start
  51.6 1.9 collective-permute-start.3
  53.5 2.1 collective-permute-start.2
  55.6 0.4 fusion
  56.1 0.2 copy.34
  56.3 0.9 copy.36
  57.3 4.6 %all-to-all-start = ((f32[8,96,128]{2,1,0:T(8,128)}), f32[8,96,128]{2,1,0:T(8,128)S(1)}, u32[]{:S(2)}, u32[]{:S(2)}) async-start(f32[8,96,128]{2,1,0:T(8,128)} %copy.36), calls=%async_computation | async-start | bytes 786432 | tf_op jit(solution)/shard_map/all_to_all | solution.py:325
  61.9 48.8 %outgoing.2 = (bf16[3,512,256]{2,1,0:T(8,128)(2,1)}, bf16[3,512,256]{2,1,0:T(8,128)(2,1)}) custom-call(bf16[2,512,512]{2,1,0:T(8,128)(2,1)} %refs_0_.3, bf16[2,512,512]{2,1,0:T(8,128)(2,1)} %refs_1_.3, bf16[2,512,512]{2,1,0:T(8,128)(2,1)} %refs_2_.3), custom_call_target="tpu_custom_call" | custom-call | tf_op jit(solution)/shard_map/outgoing/pallas_call | solution.py:280
  110.9 0.8 dynamic_slice.7
  111.7 0.6 tile.20.area_ref
  112.3 0.1 select_reduce_fusion.2
  112.4 0.1 reshape.206
  112.5 0.9 constant_dynamic-slice_fusion
  113.5 0.7 copy.38.truth_ref
  114.3 0.1 broadcast_and_fusion
  114.4 0.7 copy-done.5
  115.1 3.4 %score_gradient.1 = bf16[8,96,128]{2,1,0:T(8,128)(2,1)} custom-call(f32[8,96,128]{2,1,0:T(8,128)} %copy-done.5, f32[96,128]{1,0:T(8,128)} %copy.38.truth_ref, f32[1,128]{1,0:T(1,128)} %tile.20.area_ref), custom_call_target="tpu_custom_call" | custom-call | tf_op jit(solution)/shard_map/score_gradient/pallas_call | solution.py:49
  118.6 0.9 copy-done.12
  119.4 4.8 %all-to-all-start.1 = ((bf16[8,96,128]{2,1,0:T(8,128)(2,1)}), bf16[8,96,128]{2,1,0:T(8,128)(2,1)S(1)}, u32[]{:S(2)}, u32[]{:S(2)}) async-start(bf16[8,96,128]{2,1,0:T(8,128)(2,1)} %score_gradient.1), calls=%async_computation.1 | async-start | bytes 393216 | tf_op jit(solution)/shard_map/all_to_all | solution.py:336
  124.3 1.5 collective-permute-start.4
  125.8 0.6 collective-permute-start.16
  126.3 3.2 %collective-permute-start.17 = (bf16[3,512,256]{2,1,0:T(8,128)(2,1)}, bf16[3,512,256]{2,1,0:T(8,128)(2,1)}, u32[]{:S(2)}, u32[]{:S(2)}) collective-permute-start(bf16[3,512,256]{2,1,0:T(8,128)(2,1)} %collective-permute-done.2.refs_8_), channel_id=1, source_target_pairs={{0,3},{1,0},{2,1},{3,2},{4,7},{5,4},{6,5},{7,6},{8,11},{9,8},{10,9... | collective-permute-start | bytes 2359304 | tf_op jit(solution)/shard_map/ppermute | solution.py:63
  129.5 1.5 all-to-all-done.1
  131.0 0.2 copy.39
  131.3 0.5 constant_dynamic-update-slice_fusion
  131.7 0.5 convolution_convert_fusion.1
  132.2 1.0 bitcast_reduce_fusion
  133.4 0.1 broadcast_and_fusion.1
  133.5 16.2 %collective-permute-done.15.refs_16_ = bf16[128,512]{1,0:T(8,128)(2,1)S(1)} collective-permute-done((bf16[128,512]{1,0:T(8,128)(2,1)S(1)}, bf16[128,512]{1,0:T(8,128)(2,1)S(1)}, u32[]{:S(2)}, u32[]{:S(2)}) %collective-permute-start.15) | collective-permute-done | bytes 131104 | tf_op jit(solution)/shard_map/ppermute | solution.py:63
  149.7 0.7 collective-permute-start.14
  150.3 0.7 select_reduce_fusion.1
  151.0 5.1 %collective-permute-done.14.refs_15_ = bf16[128,512]{1,0:T(8,128)(2,1)S(1)} collective-permute-done((bf16[128,512]{1,0:T(8,128)(2,1)S(1)}, bf16[128,512]{1,0:T(8,128)(2,1)S(1)}, u32[]{:S(2)}, u32[]{:S(2)}) %collective-permute-start.14) | collective-permute-done | bytes 131104 | tf_op jit(solution)/shard_map/ppermute | solution.py:63
  156.2 0.8 collective-permute-start.13
  157.0 0.6 select_reduce_fusion
  157.6 3.5 %collective-permute-done.13.refs_14_ = bf16[128,512]{1,0:T(8,128)(2,1)S(1)} collective-permute-done((bf16[128,512]{1,0:T(8,128)(2,1)S(1)}, bf16[128,512]{1,0:T(8,128)(2,1)S(1)}, u32[]{:S(2)}, u32[]{:S(2)}) %collective-permute-start.13) | collective-permute-done | bytes 131104 | tf_op jit(solution)/shard_map/ppermute | solution.py:63
  161.1 1.2 collective-permute-start.12
  162.3 1.5 collective-permute-start.11
  163.8 2.3 collective-permute-start.10
  166.2 0.1 stack_reshape.6
  166.3 0.8 copy.43.refs_4_
  167.0 0.9 collective-permute-start.6
  168.0 2.3 collective-permute-done.11.refs_12_
  170.3 2.0 collective-permute-start.8
  172.3 1.3 collective-permute-start.7
  173.7 28.5 %attention_tiles.3 = (bf16[4,3,512,256]{3,2,1,0:T(8,128)(2,1)}, f32[3,512,256]{2,1,0:T(8,128)S(1)}, bf16[3,512,256]{2,1,0:T(8,128)(2,1)}, bf16[3,512,256]{2,1,0:T(8,128)(2,1)}, bf16[3,512,256]{2,1,0:T(8,128)(2,1)}) custom-call(s32[3,16]{1,0:T(4,128)S(1)} %pad_add_fusion.table, bf16[2,512,512]{2,1,0:T(8,128)(2,1)} %refs_0_.3, bf16[2,512,512]{2,1,0:T(8,128)(2,1)} %refs_1_.3, ...), custom_call_target="tpu_custom_call" | custom-call | flops 21474836480 | bytes 20971520 | tf_op jit(solution)/shard_map/attention_tiles/pallas_call | solution.py:185
  202.2 5.3 %all-to-all-start.2 = ((bf16[4,3,512,256]{3,2,1,0:T(8,128)(2,1)}), bf16[4,3,512,256]{3,2,1,0:T(8,128)(2,1)}, u32[]{:S(2)}, u32[]{:S(2)}) async-start(bf16[4,3,512,256]{3,2,1,0:T(8,128)(2,1)} %get-tuple-element.65), calls=%async_computation.2 | async-start | bytes 6291456 | tf_op jit(solution)/shard_map/all_to_all | solution.py:420
  207.5 0.1 collective-permute-start.18
  207.6 4.6 %collective-permute-start.19 = (bf16[3,512,256]{2,1,0:T(8,128)(2,1)}, bf16[3,512,256]{2,1,0:T(8,128)(2,1)}, u32[]{:S(2)}, u32[]{:S(2)}) collective-permute-start(bf16[3,512,256]{2,1,0:T(8,128)(2,1)} %get-tuple-element.67), channel_id=1, source_target_pairs={{0,2},{1,3},{2,0},{3,1},{4,6},{5,7},{6,4},{7,5},{8,10},{9,11},{10,... | collective-permute-start | bytes 2359304 | tf_op jit(solution)/shard_map/ppermute | solution.py:67
  212.2 0.9 collective-permute-start.20
  213.1 28.3 %attention_tiles.2 = (bf16[4,3,512,256]{3,2,1,0:T(8,128)(2,1)}, f32[3,512,256]{2,1,0:T(8,128)S(1)}, bf16[3,512,256]{2,1,0:T(8,128)(2,1)S(1)}, bf16[3,512,256]{2,1,0:T(8,128)(2,1)S(1)}, bf16[3,512,256]{2,1,0:T(8,128)(2,1)S(1)}) custom-call(s32[3,16]{1,0:T(4,128)S(1)} %pad_add_fusion.table, bf16[2,512,512]{2,1,0:T(8,128)(2,1)} %refs_0_.3, ...), custom_call_target="tpu_custom_call" | custom-call | flops 21474836480 | bytes 20971520 | tf_op jit(solution)/shard_map/attention_tiles/pallas_call | solution.py:185
  241.4 1.1 copy-done.1
  242.6 0.9 copy-done.3
  243.5 0.9 copy-done.4
  244.4 4.7 %all-to-all-start.3 = ((bf16[4,3,512,256]{3,2,1,0:T(8,128)(2,1)}), bf16[4,3,512,256]{3,2,1,0:T(8,128)(2,1)}, u32[]{:S(2)}, u32[]{:S(2)}) async-start(bf16[4,3,512,256]{3,2,1,0:T(8,128)(2,1)} %get-tuple-element.69), calls=%async_computation.3 | async-start | bytes 6291456 | tf_op jit(solution)/shard_map/all_to_all | solution.py:420
  249.1 1.2 collective-permute-start.21
  250.3 0.3 collective-permute-start.22
  250.6 2.4 collective-permute-start.23
  253.0 4.9 %summed.2 = (f32[2,512,512]{2,1,0:T(8,128)}, f32[2,512,512]{2,1,0:T(8,128)}, f32[2,512,512]{2,1,0:T(8,128)}) custom-call(bf16[4,3,512,256]{3,2,1,0:T(8,128)(2,1)} %all-to-all-done.2.got_x, f32[3,512,256]{2,1,0:T(8,128)S(1)} %get-tuple-element.75.own_z, bf16[3,512,256]{2,1,0:T(8,128)(2,1)} %collective-permute-done.18.refs_0_, ...), custom_call_target="tpu_custom_call" | custom-call | tf_op jit(solution)/shard_map/summed/pallas_call | solution.py:250
  257.9 10.8 %collective-permute-done.21.refs_0_ = bf16[3,512,256]{2,1,0:T(8,128)(2,1)} collective-permute-done((bf16[3,512,256]{2,1,0:T(8,128)(2,1)}, bf16[3,512,256]{2,1,0:T(8,128)(2,1)}, u32[]{:S(2)}, u32[]{:S(2)}) %collective-permute-start.21) | collective-permute-done | bytes 786464 | tf_op jit(solution)/shard_map/ppermute | solution.py:67
  268.6 15.1 %collective-permute-done.22.refs_1_ = bf16[3,512,256]{2,1,0:T(8,128)(2,1)} collective-permute-done((bf16[3,512,256]{2,1,0:T(8,128)(2,1)}, bf16[3,512,256]{2,1,0:T(8,128)(2,1)}, u32[]{:S(2)}, u32[]{:S(2)}) %collective-permute-start.22) | collective-permute-done | bytes 786464 | tf_op jit(solution)/shard_map/ppermute | solution.py:67
  283.7 1.4 copy-done.2
  285.1 4.9 %summed.3 = (f32[2,512,512]{2,1,0:T(8,128)}, f32[2,512,512]{2,1,0:T(8,128)}, f32[2,512,512]{2,1,0:T(8,128)}) custom-call(bf16[4,3,512,256]{3,2,1,0:T(8,128)(2,1)} %all-to-all-done.3.got_x, f32[3,512,256]{2,1,0:T(8,128)S(1)} %copy-done.2, ...), custom_call_target="tpu_custom_call", output_to_operand_aliasing={{0}: (5, {}), {1}: (6, {}), {2}: (7, {})} | custom-call | tf_op jit(solution)/shard_map/summed/pallas_call | solution.py:250
  (79 shorter events, 0.8 us)
Async XLA Ops:
  0.6 55.0 %copy-start = (bf16[2,512,512]{2,1,0:T(8,128)(2,1)S(1)}, bf16[2,512,512]{2,1,0:T(8,128)(2,1)}, u32[]{:S(2)}) copy-start(bf16[2,512,512]{2,1,0:T(8,128)(2,1)} %param.12) | copy-start | bytes 3145732
  0.6 55.0 %copy-start.6 = (bf16[512,96]{0,1:T(8,128)(2,1)S(1)}, bf16[512,96]{0,1:T(8,128)(2,1)}, u32[]{:S(2)}) copy-start(bf16[512,96]{0,1:T(8,128)(2,1)} %param.13) | copy-start | bytes 294916
  0.7 55.0 %copy-start.8 = (f32[96,512]{1,0:T(8,128)S(1)}, f32[96,512]{1,0:T(8,128)}, u32[]{:S(2)}) copy-start(f32[96,512]{1,0:T(8,128)} %param.14) | copy-start | bytes 589828
  49.5 69.0 %collective-permute-start.1 = (bf16[3,512,256]{2,1,0:T(8,128)(2,1)}, bf16[3,512,256]{2,1,0:T(8,128)(2,1)S(1)}, u32[]{:S(2)}, u32[]{:S(2)}) collective-permute-start(bf16[3,512,256]{2,1,0:T(8,128)(2,1)} %get-tuple-element.46), channel_id=1, source_target_pairs={{0,4},{4,8},{8,12},{12,0},{1,5},{5,9},{9,13},{13,1},{2,6},{6,10},{... | collective-permute-start | bytes 2359304 | tf_op jit(solution)/shard_map/ppermute | solution.py:63
  51.0 67.5 %collective-permute-start = (bf16[3,512,256]{2,1,0:T(8,128)(2,1)}, bf16[3,512,256]{2,1,0:T(8,128)(2,1)}, u32[]{:S(2)}, u32[]{:S(2)}) collective-permute-start(bf16[3,512,256]{2,1,0:T(8,128)(2,1)} %get-tuple-element.46), channel_id=1, source_target_pairs={{0,12},{4,0},{8,4},{12,8},{1,13},{5,1},{9,5},{13,9},{2,14},{6,2},{... | collective-permute-start | bytes 2359304 | tf_op jit(solution)/shard_map/ppermute | solution.py:63
  51.6 67.0 %collective-permute-start.3 = (bf16[3,512,256]{2,1,0:T(8,128)(2,1)}, bf16[3,512,256]{2,1,0:T(8,128)(2,1)}, u32[]{:S(2)}, u32[]{:S(2)}) collective-permute-start(bf16[3,512,256]{2,1,0:T(8,128)(2,1)} %get-tuple-element.47), channel_id=1, source_target_pairs={{0,1},{1,2},{2,3},{3,0},{4,5},{5,6},{6,7},{7,4},{8,9},{9,10},{10,1... | collective-permute-start | bytes 2359304 | tf_op jit(solution)/shard_map/ppermute | solution.py:63
  53.5 65.1 %collective-permute-start.2 = (bf16[3,512,256]{2,1,0:T(8,128)(2,1)}, bf16[3,512,256]{2,1,0:T(8,128)(2,1)}, u32[]{:S(2)}, u32[]{:S(2)}) collective-permute-start(bf16[3,512,256]{2,1,0:T(8,128)(2,1)} %get-tuple-element.47), channel_id=1, source_target_pairs={{0,3},{1,0},{2,1},{3,2},{4,7},{5,4},{6,5},{7,6},{8,11},{9,8},{10,9... | collective-permute-start | bytes 2359304 | tf_op jit(solution)/shard_map/ppermute | solution.py:63
  57.3 55.0 %copy-start.10 = (s32[16,16]{1,0:T(8,128)S(1)}, s32[16,16]{1,0:T(8,128)}, u32[]{:S(2)}) copy-start(s32[16,16]{1,0:T(8,128)} %param.23) | copy-start | bytes 3076
  57.3 55.0 %copy-start.11 = (s32[16,16]{1,0:T(8,128)S(1)}, s32[16,16]{1,0:T(8,128)}, u32[]{:S(2)}) copy-start(s32[16,16]{1,0:T(8,128)} %param.22) | copy-start | bytes 3076
  57.3 57.1 %all-to-all-start = ((f32[8,96,128]{2,1,0:T(8,128)}), f32[8,96,128]{2,1,0:T(8,128)S(1)}, u32[]{:S(2)}, u32[]{:S(2)}) async-start(f32[8,96,128]{2,1,0:T(8,128)} %copy.36), calls=%async_computation | async-start | bytes 786432 | tf_op jit(solution)/shard_map/all_to_all | solution.py:325
  61.9 69.4 %copy-start.19 = (s32[1,512]{1,0:T(1,128)S(1)}, s32[1,512]{1,0:T(1,128)}, u32[]{:S(2)}) copy-start(s32[1,512]{1,0:T(1,128)} %param.17) | copy-start | bytes 6148
  114.4 0.8 copy-start.5
  118.5 0.9 copy-start.12
  119.4 11.6 %all-to-all-start.1 = ((bf16[8,96,128]{2,1,0:T(8,128)(2,1)}), bf16[8,96,128]{2,1,0:T(8,128)(2,1)S(1)}, u32[]{:S(2)}, u32[]{:S(2)}) async-start(bf16[8,96,128]{2,1,0:T(8,128)(2,1)} %score_gradient.1), calls=%async_computation.1 | async-start | bytes 393216 | tf_op jit(solution)/shard_map/all_to_all | solution.py:336
  124.3 38.0 %collective-permute-start.4 = (bf16[3,512,256]{2,1,0:T(8,128)(2,1)}, bf16[3,512,256]{2,1,0:T(8,128)(2,1)}, u32[]{:S(2)}, u32[]{:S(2)}) collective-permute-start(bf16[3,512,256]{2,1,0:T(8,128)(2,1)} %get-tuple-element.53), channel_id=1, source_target_pairs={{0,4},{4,8},{8,12},{12,0},{1,5},{5,9},{9,13},{13,1},{2,6},{6,10},{... | collective-permute-start | bytes 2359304 | tf_op jit(solution)/shard_map/ppermute | solution.py:63
  125.8 38.0 %collective-permute-start.5 = (bf16[3,512,256]{2,1,0:T(8,128)(2,1)}, bf16[3,512,256]{2,1,0:T(8,128)(2,1)}, u32[]{:S(2)}, u32[]{:S(2)}) collective-permute-start(bf16[3,512,256]{2,1,0:T(8,128)(2,1)} %get-tuple-element.55), channel_id=1, source_target_pairs={{0,1},{1,2},{2,3},{3,0},{4,5},{5,6},{6,7},{7,4},{8,9},{9,10},{10,1... | collective-permute-start | bytes 2359304 | tf_op jit(solution)/shard_map/ppermute | solution.py:63
  125.8 47.9 %collective-permute-start.16 = (bf16[3,512,256]{2,1,0:T(8,128)(2,1)}, bf16[3,512,256]{2,1,0:T(8,128)(2,1)}, u32[]{:S(2)}, u32[]{:S(2)}) collective-permute-start(bf16[3,512,256]{2,1,0:T(8,128)(2,1)} %collective-permute-done.refs_5_), channel_id=1, source_target_pairs={{0,12},{4,0},{8,4},{12,8},{1,13},{5,1},{9,5},{13,9},{2,14},{6,2},{... | collective-permute-start | bytes 2359304 | tf_op jit(solution)/shard_map/ppermute | solution.py:63
  126.3 47.3 %collective-permute-start.17 = (bf16[3,512,256]{2,1,0:T(8,128)(2,1)}, bf16[3,512,256]{2,1,0:T(8,128)(2,1)}, u32[]{:S(2)}, u32[]{:S(2)}) collective-permute-start(bf16[3,512,256]{2,1,0:T(8,128)(2,1)} %collective-permute-done.2.refs_8_), channel_id=1, source_target_pairs={{0,3},{1,0},{2,1},{3,2},{4,7},{5,4},{6,5},{7,6},{8,11},{9,8},{10,9... | collective-permute-start | bytes 2359304 | tf_op jit(solution)/shard_map/ppermute | solution.py:63
  132.2 1.0 copy-start.9
  133.3 40.4 %copy-start.7 = (bf16[2,128,512]{2,1,0:T(8,128)(2,1)}, bf16[2,128,512]{2,1,0:T(8,128)(2,1)S(1)}, u32[]{:S(2)}) copy-start(bf16[2,128,512]{2,1,0:T(8,128)(2,1)S(1)} %fusion.12.refs_3_) | copy-start | bytes 786436
  133.3 16.4 %collective-permute-start.15 = (bf16[128,512]{1,0:T(8,128)(2,1)S(1)}, bf16[128,512]{1,0:T(8,128)(2,1)S(1)}, u32[]{:S(2)}, u32[]{:S(2)}) collective-permute-start(bf16[128,512]{1,0:T(8,128)(2,1)S(1)} %get-tuple-element.85), channel_id=1, source_target_pairs={{0,1},{1,2},{2,3},{3,0},{4,5},{5,6},{6,7},{7,4},{8,9},{9,10},{10,1... | collective-permute-start | bytes 393224 | tf_op jit(solution)/shard_map/ppermute | solution.py:63
  149.7 24.0 %copy-start.13 = (bf16[128,512]{1,0:T(8,128)(2,1)}, bf16[128,512]{1,0:T(8,128)(2,1)S(1)}, u32[]{:S(2)}) copy-start(bf16[128,512]{1,0:T(8,128)(2,1)S(1)} %collective-permute-done.15.refs_16_) | copy-start | bytes 393220
  149.7 6.5 %collective-permute-start.14 = (bf16[128,512]{1,0:T(8,128)(2,1)S(1)}, bf16[128,512]{1,0:T(8,128)(2,1)S(1)}, u32[]{:S(2)}, u32[]{:S(2)}) collective-permute-start(bf16[128,512]{1,0:T(8,128)(2,1)S(1)} %get-tuple-element.85), channel_id=1, source_target_pairs={{0,2},{1,3},{2,0},{3,1},{4,6},{5,7},{6,4},{7,5},{8,10},{9,11},{10,... | collective-permute-start | bytes 393224 | tf_op jit(solution)/shard_map/ppermute | solution.py:63
  156.2 17.5 %copy-start.14 = (bf16[128,512]{1,0:T(8,128)(2,1)}, bf16[128,512]{1,0:T(8,128)(2,1)S(1)}, u32[]{:S(2)}) copy-start(bf16[128,512]{1,0:T(8,128)(2,1)S(1)} %collective-permute-done.14.refs_15_) | copy-start | bytes 393220
  156.2 5.0 %collective-permute-start.13 = (bf16[128,512]{1,0:T(8,128)(2,1)S(1)}, bf16[128,512]{1,0:T(8,128)(2,1)S(1)}, u32[]{:S(2)}, u32[]{:S(2)}) collective-permute-start(bf16[128,512]{1,0:T(8,128)(2,1)S(1)} %get-tuple-element.85), channel_id=1, source_target_pairs={{0,3},{1,0},{2,1},{3,2},{4,7},{5,4},{6,5},{7,6},{8,11},{9,8},{10,9... | collective-permute-start | bytes 393224 | tf_op jit(solution)/shard_map/ppermute | solution.py:63
  161.1 12.6 %copy-start.15 = (bf16[128,512]{1,0:T(8,128)(2,1)}, bf16[128,512]{1,0:T(8,128)(2,1)S(1)}, u32[]{:S(2)}) copy-start(bf16[128,512]{1,0:T(8,128)(2,1)S(1)} %collective-permute-done.13.refs_14_) | copy-start | bytes 393220
  161.1 5.9 %collective-permute-start.12 = (bf16[128,512]{1,0:T(8,128)(2,1)S(1)}, bf16[128,512]{1,0:T(8,128)(2,1)S(1)}, u32[]{:S(2)}, u32[]{:S(2)}) collective-permute-start(bf16[128,512]{1,0:T(8,128)(2,1)S(1)} %get-tuple-element.86), channel_id=1, source_target_pairs={{0,4},{4,8},{8,12},{12,0},{1,5},{5,9},{9,13},{13,1},{2,6},{6,10},{... | collective-permute-start | bytes 393224 | tf_op jit(solution)/shard_map/ppermute | solution.py:63
  162.3 7.9 %collective-permute-start.11 = (bf16[128,512]{1,0:T(8,128)(2,1)S(1)}, bf16[128,512]{1,0:T(8,128)(2,1)S(1)}, u32[]{:S(2)}, u32[]{:S(2)}) collective-permute-start(bf16[128,512]{1,0:T(8,128)(2,1)S(1)} %get-tuple-element.86), channel_id=1, source_target_pairs={{0,8},{4,12},{8,0},{12,4},{1,9},{5,13},{9,1},{13,5},{2,10},{6,14},... | collective-permute-start | bytes 393224 | tf_op jit(solution)/shard_map/ppermute | solution.py:63
  163.8 8.5 %collective-permute-start.10 = (bf16[128,512]{1,0:T(8,128)(2,1)S(1)}, bf16[128,512]{1,0:T(8,128)(2,1)S(1)}, u32[]{:S(2)}, u32[]{:S(2)}) collective-permute-start(bf16[128,512]{1,0:T(8,128)(2,1)S(1)} %get-tuple-element.86), channel_id=1, source_target_pairs={{0,12},{4,0},{8,4},{12,8},{1,13},{5,1},{9,5},{13,9},{2,14},{6,2},{... | collective-permute-start | bytes 393224 | tf_op jit(solution)/shard_map/ppermute | solution.py:63
  167.0 6.7 %copy-start.16 = (bf16[128,512]{1,0:T(8,128)(2,1)}, bf16[128,512]{1,0:T(8,128)(2,1)S(1)}, u32[]{:S(2)}) copy-start(bf16[128,512]{1,0:T(8,128)(2,1)S(1)} %collective-permute-done.12.refs_13_) | copy-start | bytes 393220
  167.0 40.6 %collective-permute-start.6 = (bf16[3,512,256]{2,1,0:T(8,128)(2,1)}, bf16[3,512,256]{2,1,0:T(8,128)(2,1)}, u32[]{:S(2)}, u32[]{:S(2)}) collective-permute-start(bf16[3,512,256]{2,1,0:T(8,128)(2,1)} %get-tuple-element.53), channel_id=1, source_target_pairs={{0,12},{4,0},{8,4},{12,8},{1,13},{5,1},{9,5},{13,9},{2,14},{6,2},{... | collective-permute-start | bytes 2359304 | tf_op jit(solution)/shard_map/ppermute | solution.py:63
  170.3 3.4 %copy-start.17 = (bf16[128,512]{1,0:T(8,128)(2,1)}, bf16[128,512]{1,0:T(8,128)(2,1)S(1)}, u32[]{:S(2)}) copy-start(bf16[128,512]{1,0:T(8,128)(2,1)S(1)} %collective-permute-done.11.refs_12_) | copy-start | bytes 393220
  170.3 41.9 %collective-permute-start.8 = (bf16[3,512,256]{2,1,0:T(8,128)(2,1)}, bf16[3,512,256]{2,1,0:T(8,128)(2,1)}, u32[]{:S(2)}, u32[]{:S(2)}) collective-permute-start(bf16[3,512,256]{2,1,0:T(8,128)(2,1)} %get-tuple-element.55), channel_id=1, source_target_pairs={{0,3},{1,0},{2,1},{3,2},{4,7},{5,4},{6,5},{7,6},{8,11},{9,8},{10,9... | collective-permute-start | bytes 2359304 | tf_op jit(solution)/shard_map/ppermute | solution.py:63
  172.3 1.4 copy-start.18
  172.3 40.8 %collective-permute-start.7 = (bf16[3,512,256]{2,1,0:T(8,128)(2,1)}, bf16[3,512,256]{2,1,0:T(8,128)(2,1)}, u32[]{:S(2)}, u32[]{:S(2)}) collective-permute-start(bf16[3,512,256]{2,1,0:T(8,128)(2,1)} %collective-permute-done.4.refs_7_), channel_id=1, source_target_pairs={{0,4},{4,8},{8,12},{12,0},{1,5},{5,9},{9,13},{13,1},{2,6},{6,10},{... | collective-permute-start | bytes 2359304 | tf_op jit(solution)/shard_map/ppermute | solution.py:63
  173.6 39.5 %collective-permute-start.9 = (bf16[3,512,256]{2,1,0:T(8,128)(2,1)}, bf16[3,512,256]{2,1,0:T(8,128)(2,1)}, u32[]{:S(2)}, u32[]{:S(2)}) collective-permute-start(bf16[3,512,256]{2,1,0:T(8,128)(2,1)} %collective-permute-done.5.refs_10_), channel_id=1, source_target_pairs={{0,1},{1,2},{2,3},{3,0},{4,5},{5,6},{6,7},{7,4},{8,9},{9,10},{10,1... | collective-permute-start | bytes 2359304 | tf_op jit(solution)/shard_map/ppermute | solution.py:63
  202.2 42.2 %all-to-all-start.2 = ((bf16[4,3,512,256]{3,2,1,0:T(8,128)(2,1)}), bf16[4,3,512,256]{3,2,1,0:T(8,128)(2,1)}, u32[]{:S(2)}, u32[]{:S(2)}) async-start(bf16[4,3,512,256]{3,2,1,0:T(8,128)(2,1)} %get-tuple-element.65), calls=%async_computation.2 | async-start | bytes 6291456 | tf_op jit(solution)/shard_map/all_to_all | solution.py:420
  207.5 36.8 %collective-permute-start.18 = (bf16[3,512,256]{2,1,0:T(8,128)(2,1)}, bf16[3,512,256]{2,1,0:T(8,128)(2,1)}, u32[]{:S(2)}, u32[]{:S(2)}) collective-permute-start(bf16[3,512,256]{2,1,0:T(8,128)(2,1)} %get-tuple-element.66), channel_id=1, source_target_pairs={{0,1},{1,2},{2,3},{3,0},{4,5},{5,6},{6,7},{7,4},{8,9},{9,10},{10,1... | collective-permute-start | bytes 2359304 | tf_op jit(solution)/shard_map/ppermute | solution.py:67
  207.6 36.7 %collective-permute-start.19 = (bf16[3,512,256]{2,1,0:T(8,128)(2,1)}, bf16[3,512,256]{2,1,0:T(8,128)(2,1)}, u32[]{:S(2)}, u32[]{:S(2)}) collective-permute-start(bf16[3,512,256]{2,1,0:T(8,128)(2,1)} %get-tuple-element.67), channel_id=1, source_target_pairs={{0,2},{1,3},{2,0},{3,1},{4,6},{5,7},{6,4},{7,5},{8,10},{9,11},{10,... | collective-permute-start | bytes 2359304 | tf_op jit(solution)/shard_map/ppermute | solution.py:67
  212.2 32.2 %collective-permute-start.20 = (bf16[3,512,256]{2,1,0:T(8,128)(2,1)}, bf16[3,512,256]{2,1,0:T(8,128)(2,1)}, u32[]{:S(2)}, u32[]{:S(2)}) collective-permute-start(bf16[3,512,256]{2,1,0:T(8,128)(2,1)} %get-tuple-element.68), channel_id=1, source_target_pairs={{0,3},{1,0},{2,1},{3,2},{4,7},{5,4},{6,5},{7,6},{8,11},{9,8},{10,9... | collective-permute-start | bytes 2359304 | tf_op jit(solution)/shard_map/ppermute | solution.py:67
  241.4 1.1 copy-start.1
  242.6 0.9 copy-start.3
  243.5 0.9 copy-start.4
  244.4 39.3 %all-to-all-start.3 = ((bf16[4,3,512,256]{3,2,1,0:T(8,128)(2,1)}), bf16[4,3,512,256]{3,2,1,0:T(8,128)(2,1)}, u32[]{:S(2)}, u32[]{:S(2)}) async-start(bf16[4,3,512,256]{3,2,1,0:T(8,128)(2,1)} %get-tuple-element.69), calls=%async_computation.3 | async-start | bytes 6291456 | tf_op jit(solution)/shard_map/all_to_all | solution.py:420
  249.1 19.6 %collective-permute-start.21 = (bf16[3,512,256]{2,1,0:T(8,128)(2,1)}, bf16[3,512,256]{2,1,0:T(8,128)(2,1)}, u32[]{:S(2)}, u32[]{:S(2)}) collective-permute-start(bf16[3,512,256]{2,1,0:T(8,128)(2,1)} %copy-done.4), channel_id=1, source_target_pairs={{0,1},{1,2},{2,3},{3,0},{4,5},{5,6},{6,7},{7,4},{8,9},{9,10},{10,1... | collective-permute-start | bytes 2359304 | tf_op jit(solution)/shard_map/ppermute | solution.py:67
  250.3 33.4 %collective-permute-start.22 = (bf16[3,512,256]{2,1,0:T(8,128)(2,1)}, bf16[3,512,256]{2,1,0:T(8,128)(2,1)}, u32[]{:S(2)}, u32[]{:S(2)}) collective-permute-start(bf16[3,512,256]{2,1,0:T(8,128)(2,1)} %copy-done.3), channel_id=1, source_target_pairs={{0,2},{1,3},{2,0},{3,1},{4,6},{5,7},{6,4},{7,5},{8,10},{9,11},{10,... | collective-permute-start | bytes 2359304 | tf_op jit(solution)/shard_map/ppermute | solution.py:67
  250.6 33.1 %collective-permute-start.23 = (bf16[3,512,256]{2,1,0:T(8,128)(2,1)S(1)}, bf16[3,512,256]{2,1,0:T(8,128)(2,1)}, u32[]{:S(2)}, u32[]{:S(2)}) collective-permute-start(bf16[3,512,256]{2,1,0:T(8,128)(2,1)S(1)} %get-tuple-element.73), channel_id=1, source_target_pairs={{0,3},{1,0},{2,1},{3,2},{4,7},{5,4},{6,5},{7,6},{8,11},{9,8},{10,9... | collective-permute-start | bytes 2359304 | tf_op jit(solution)/shard_map/ppermute | solution.py:67
  283.7 1.4 copy-start.2

commit v6 on v5

--- a/solution.py
+++ b/solution.py
@@ -49,6 +49,8 @@
     return pl.pallas_call(
         score_kernel,
         out_shape=jax.ShapeDtypeStruct(forecasts.shape, BF16),
+        in_specs=[pl.BlockSpec(memory_space=pltpu.VMEM)] * 3,
+        out_specs=pl.BlockSpec(memory_space=pltpu.VMEM),
         scratch_shapes=[pltpu.VMEM(forecasts.shape, F32)],
         name="score_gradient",
     )(forecasts, truth, area)
@@ -185,10 +187,10 @@
     out = pl.pallas_call(
         functools.partial(tile_kernel, base=2 * base),
         out_shape=[
-            jax.ShapeDtypeStruct((SIDE, 3, rows, width // 2), BF16),
-            jax.ShapeDtypeStruct((3, rows, width // 2), F32),
+            pltpu.HBM((SIDE, 3, rows, width // 2), BF16),
+            pltpu.HBM((3, rows, width // 2), F32),
         ]
-        + [jax.ShapeDtypeStruct((3, rows, width // 2), BF16)] * 3,
+        + [pltpu.HBM((3, rows, width // 2), BF16)] * 3,
         grid_spec=pltpu.PrefetchScalarGridSpec(
             num_scalar_prefetch=1,
             grid=(pairs,),
@@ -226,7 +228,7 @@
         *in_hbm(key_rows, value_rows, query, late_own, decoder_matrix),
         *in_hbm(*fetched_x, *fetched_z, *late_x, *late_z),
     )
-    return in_hbm(out[0])[0], out[1], in_hbm(*out[2:])
+    return out[0], out[1], out[2:]
 
 
 def sum_kernel(got_x, own_z, *refs):
@@ -244,47 +246,29 @@
 
 def summed(half, got_x, own_z, got_z, outs):
     _, rows, lanes = own_z.shape
-    z_spec = pl.BlockSpec((3, rows // 4, lanes), lambda r: (0, r, 0))
+    z_spec = pl.BlockSpec((3, rows // 2, lanes), lambda r: (0, r, 0))
     shape = jax.ShapeDtypeStruct((2, rows, 2 * lanes), F32)
     kept = list(outs) if outs else []
     return pl.pallas_call(
         sum_kernel,
         out_shape=[shape] * 3,
-        grid=(4,),
-        in_specs=[pl.BlockSpec((SIDE, 3, rows // 4, lanes), lambda r: (0, 0, r, 0))]
+        grid=(2,),
+        in_specs=[pl.BlockSpec((SIDE, 3, rows // 2, lanes), lambda r: (0, 0, r, 0))]
         + [z_spec] * 4
         + [pl.BlockSpec(memory_space=pl.ANY)] * len(kept),
-        out_specs=[pl.BlockSpec((2, rows // 4, lanes), lambda r: (0, r, half))] * 3,
+        out_specs=[pl.BlockSpec((2, rows // 2, lanes), lambda r: (0, r, half))] * 3,
         input_output_aliases={5 + n: n for n in range(len(kept))},
         compiler_params=pltpu.CompilerParams(vmem_limit_bytes=50 * 1024 * 1024),
         name="summed",
-    )(*in_hbm(got_x), own_z, *in_hbm(*got_z), *kept)
-
-
-def pack_kernel(key_rows, value_rows, query, along_x, along_z, sems, *, half):
-    lanes = along_x.shape[-1]
-    part = pl.ds(half * lanes, lanes)
-    copies = []
-    for m, out in enumerate((along_x, along_z)):
-        for n, ref in enumerate((key_rows.at[m], value_rows.at[m], query.at[1 - m])):
-            copies.append(pltpu.make_async_copy(ref.at[:, part], out.at[n], sems.at[m, n]))
-    for copy in copies:
-        copy.start()
-    for copy in copies:
-        copy.wait()
+    )(*in_hbm(got_x, own_z, *got_z), *kept)
 
 
 def outgoing(half, key_rows, value_rows, query):
-    _, rows, width = key_rows.shape
-    anywhere = pl.BlockSpec(memory_space=pl.ANY)
-    return pl.pallas_call(
-        functools.partial(pack_kernel, half=half),
-        out_shape=[jax.ShapeDtypeStruct((3, rows, width // 2), BF16)] * 2,
-        in_specs=[anywhere] * 3,
-        out_specs=[anywhere] * 2,
-        scratch_shapes=[pltpu.SemaphoreType.DMA((2, 3))],
-        name="outgoing",
-    )(*in_hbm(key_rows, value_rows, query))
+    lanes = query.shape[-1] // 2
+    part = slice(half * lanes, (half + 1) * lanes)
+    return [
+        jnp.stack([key_rows[m, :, part], value_rows[m, :, part], query[1 - m, :, part]]) for m in range(2)
+    ]
 
 
 def in_hbm(*arrays):
@@ -335,7 +319,7 @@
     )
     returned = lax.all_to_all(derivative, MEMBER, 0, 0, tiled=True)
     far = [fetched(near[0], "x", 1), fetched(near[2], "z", 1)]
-    before = [fetched(a, axis, 3) for a, axis in zip(own_1, ("x", "z"))]
+    z_before = fetched(own_1[1], "z", 3)
     grad_forecast = (
         returned.reshape(groups, channels, members, span)
         .transpose(2, 1, 0, 3)
@@ -388,13 +372,10 @@
     )
     late_z = [fetched(late_own[0], "z", d) for d in (1, 2, 3)]
     late_x = [fetched(late_own[1], "x", d) for d in (1, 2, 3)]
-    late_own, own_1, before = lax.optimization_barrier((late_own, own_1, before))
-    after = [fetched(a, axis, 1) for a, axis in zip(own_1, ("x", "z"))]
-    last = [fetched(before[0], "x", 3), fetched(before[1], "z", 3)]
-    came = (
-        ((near[0], far[0], near[1]), (near[2], far[1], near[3])),
-        ((after[0], last[0], before[0]), (after[1], last[1], before[1])),
-    )
+    late_own, own_1, z_before = lax.optimization_barrier((late_own, own_1, z_before))
+    x_around = [fetched(own_1[0], "x", d) for d in (1, 2, 3)]
+    z_around = [fetched(own_1[1], "z", 1), fetched(z_before, "z", 3), z_before]
+    came = (((near[0], far[0], near[1]), (near[2], far[1], near[3])), (x_around, z_around))
 
     outs = None
     parts = []

time: 291 us -> 197 us (0.68)
  Pallas kernels: 167 us -> 69.7 us
  waiting for transfers between devices: 54.5 us -> 34.4 us
  starting transfers between devices: 51.1 us -> 68.9 us
  other arithmetic: 2.02 us -> 6.24 us
    pallas_call x4 -> x2, Pallas kernels: 107 us -> 8.93 us  [summed(): pl.pallas_call(sum_kernel, out_shape=[shape] * 3, grid=(2,), in_specs=[pl...]
    ppermute x18, starting transfers between devices: 22.2 us -> 37.4 us  [fetched(): lax.ppermute(x, axis, [(i, (i - distance) % SIDE) for i in range(SIDE)])]
    ppermute x18, waiting for transfers between devices: 27.2 us -> 14.9 us  [fetched(): lax.ppermute(x, axis, [(i, (i - distance) % SIDE) for i in range(SIDE)])]
    ppermute x6, waiting for transfers between devices: 25.8 us -> 15 us  [delivered(): lax.ppermute(x, axis, [(i, (i + distance) % SIDE) for i in range(SIDE)])]
    another operation x0 -> x3, other arithmetic: none -> 4.22 us  [outgoing(): jnp.stack([key_rows[m, :, part], value_rows[m, :, part], query[1 - m, :,...]
    slice x0 -> x3, local copies, waits for them, and re-layouts: none -> 3.78 us  [the longest x1 2.11 us: outgoing(): query[1 - m, :, part]]
    all_to_all x2, starting transfers between devices: 9.97 us -> 12.9 us  [shards(): got_x = lax.all_to_all(send_x, 'x', 0, 0, tiled=True)]
    unnamed x40 -> x52, local copies, waits for them, and re-layouts: 6.01 us -> 3.99 us
  transfers between devices with their start and end apart: 28 -> 28, of which waited for: 7 -> 8; matrix products, arithmetic and copies ran while one was open for 3% -> 7% of each run, Pallas kernels for 39% -> 33%
where the time goes in v6:
time: 197 us; the launch traced here: 196 us
  Pallas kernels  69.7 us (35%)
  starting transfers between devices  68.9 us (35%)
  waiting for transfers between devices  34.4 us (17%)
  local copies, waits for them, and re-layouts  13.3 us (7%)
  other arithmetic  6.24 us (3%)
  matrix products  2.37 us (1%)
    pallas_call x2, Pallas kernels, attention_tiles(): pl.pallas_call(functools.partial(tile_kernel, base=2 * base), out_shape=[...  57.4 us
    ppermute x18, starting transfers between devices, fetched(): lax.ppermute(x, axis, [(i, (i - distance) % SIDE) for i in range(SIDE)])  37.4 us
    ppermute x6, waiting for transfers between devices, delivered(): lax.ppermute(x, axis, [(i, (i + distance) % SIDE) for i in range(SIDE)])  15 us
    ppermute x18, waiting for transfers between devices, fetched(): lax.ppermute(x, axis, [(i, (i - distance) % SIDE) for i in range(SIDE)])  14.9 us
    all_to_all x2, starting transfers between devices, shards(): got_x = lax.all_to_all(send_x, 'x', 0, 0, tiled=True)  12.9 us
    ppermute x6, starting transfers between devices, delivered(): lax.ppermute(x, axis, [(i, (i + distance) % SIDE) for i in range(SIDE)])  10.7 us
    pallas_call x2, Pallas kernels, summed(): pl.pallas_call(sum_kernel, out_shape=[shape] * 3, grid=(2,), in_specs=[pl...  8.93 us
    all_to_all x1, starting transfers between devices, shards(): lax.all_to_all(by_node.reshape(groups, channels, members * span), MEMBER,...  4.47 us
  transfers between devices with their start and end apart: 28, of which 8 were waited for; matrix products, arithmetic and copies ran while one was open for 7% of the time, Pallas kernels for 33%

profile of v6, /device:TPU:2, one launch (start us, length us, event | category | flops | bytes accessed | tf_op | source)
XLA Modules:
  0.0 196.0 jit_solution(18006392577937089488)
XLA Ops:
  0.7 2.1 %fusion.18 = (bf16[1,512,256]{2,1,0:T(8,128)(2,1)S(1)}, bf16[1,512,256]{2,1,0:T(8,128)(2,1)S(1)}, bf16[1,512,256]{2,1,0:T(8,128)(2,1)S(1)}, bf16[1,512,256]{2,1,0:T(8,128)(2,1)}) fusion(bf16[2,512,512]{2,1,0:T(8,128)(2,1)} %refs_2_.3), kind=kLoop, calls=%fused_computation.53 | loop fusion | bytes 2097152 | tf_op jit(solution)/shard_map/slice | solution.py:270
  2.8 0.9 fusion.16
  3.7 0.8 fusion.17
  4.5 1.0 pad_maximum_fusion.2
  5.4 1.5 collective-permute-start.1
  6.9 0.5 collective-permute-start
  7.4 1.0 pad_maximum_fusion.3
  8.4 1.9 collective-permute-start.3
  10.4 2.1 %collective-permute-start.2 = (bf16[3,512,256]{2,1,0:T(8,128)(2,1)}, bf16[3,512,256]{2,1,0:T(8,128)(2,1)}, u32[]{:S(2)}, u32[]{:S(2)}) collective-permute-start(bf16[3,512,256]{2,1,0:T(8,128)(2,1)} %pad_maximum_fusion.3), channel_id=1, source_target_pairs={{0,3},{1,0},{2,1},{3,2},{4,7},{5,4},{6,5},{7,6},{8,11},{9,8},{10,9... | collective-permute-start | bytes 2359304 | tf_op jit(solution)/shard_map/ppermute | solution.py:65
  12.5 0.4 fusion
  13.3 1.0 copy.36
  14.2 4.5 %all-to-all-start = ((f32[8,96,128]{2,1,0:T(8,128)}), f32[8,96,128]{2,1,0:T(8,128)S(1)}, u32[]{:S(2)}, u32[]{:S(2)}) async-start(f32[8,96,128]{2,1,0:T(8,128)} %copy.36), calls=%async_computation | async-start | bytes 786432 | tf_op jit(solution)/shard_map/all_to_all | solution.py:309
  18.9 0.8 dynamic_slice.7
  19.6 0.7 tile.20.area_ref
  20.5 0.9 constant_dynamic-slice_fusion
  21.5 0.7 copy.38.truth_ref
  22.4 2.3 %pad_maximum_fusion = (bf16[3,512,256]{2,1,0:T(8,128)(2,1)}, bf16[3,512,256]{2,1,0:T(8,128)(2,1)}) fusion(bf16[1,512,256]{2,1,0:T(8,128)(2,1)S(1)} %copy-done.4, bf16[1,512,256]{2,1,0:T(8,128)(2,1)} %get-tuple-element.82, bf16[1,512,256]{2,1,0:T(8,128)(2,1)S(1)} %copy-done.6, bf16[1,512,256]{2,1,0:T(8,128)(2,1)S(1)} %get-tuple-element.85, ...), kind=kLoop, calls=%fused_computation.9 | loop fusion | flops 1572864 | bytes 3145728 | tf_op jit(solution)/shard_map/stack | solution.py:270
  24.8 2.9 %all-to-all-done.forecast_ref = f32[8,96,128]{2,1,0:T(8,128)S(1)} async-done(((f32[8,96,128]{2,1,0:T(8,128)}), f32[8,96,128]{2,1,0:T(8,128)S(1)}, u32[]{:S(2)}, u32[]{:S(2)}) %all-to-all-start) | async-done | bytes 393248 | tf_op jit(solution)/shard_map/all_to_all | solution.py:309
  27.7 0.8 copy-done.1
  28.4 3.4 %score_gradient.1 = bf16[8,96,128]{2,1,0:T(8,128)(2,1)} custom-call(f32[8,96,128]{2,1,0:T(8,128)} %copy-done.1, f32[96,128]{1,0:T(8,128)} %copy.38.truth_ref, f32[1,128]{1,0:T(1,128)} %tile.20.area_ref), custom_call_target="tpu_custom_call" | custom-call | tf_op jit(solution)/shard_map/score_gradient/pallas_call | solution.py:49
  31.8 3.4 %all-to-all-start.1 = ((bf16[8,96,128]{2,1,0:T(8,128)(2,1)}), bf16[8,96,128]{2,1,0:T(8,128)(2,1)S(1)}, u32[]{:S(2)}, u32[]{:S(2)}) async-start(bf16[8,96,128]{2,1,0:T(8,128)(2,1)} %score_gradient.1), calls=%async_computation.1 | async-start | bytes 393216 | tf_op jit(solution)/shard_map/all_to_all | solution.py:320
  35.3 0.3 collective-permute-start.4
  35.7 1.7 collective-permute-start.16
  37.4 3.0 %collective-permute-start.17 = (bf16[3,512,256]{2,1,0:T(8,128)(2,1)}, bf16[3,512,256]{2,1,0:T(8,128)(2,1)}, u32[]{:S(2)}, u32[]{:S(2)}) collective-permute-start(bf16[3,512,256]{2,1,0:T(8,128)(2,1)} %collective-permute-done.2.refs_8_), channel_id=1, source_target_pairs={{0,3},{1,0},{2,1},{3,2},{4,7},{5,4},{6,5},{7,6},{8,11},{9,8},{10,9... | collective-permute-start | bytes 2359304 | tf_op jit(solution)/shard_map/ppermute | solution.py:65
  40.4 1.6 all-to-all-done.1
  42.2 0.5 constant_dynamic-update-slice_fusion
  42.7 0.5 convolution_convert_fusion.1
  43.2 1.0 bitcast_reduce_fusion
  44.3 0.4 collective-permute-start.15
  44.7 0.7 select_reduce_fusion.1
  45.4 3.2 %collective-permute-start.14 = (bf16[128,512]{1,0:T(8,128)(2,1)S(1)}, bf16[128,512]{1,0:T(8,128)(2,1)S(1)}, u32[]{:S(2)}, u32[]{:S(2)}) collective-permute-start(bf16[128,512]{1,0:T(8,128)(2,1)S(1)} %get-tuple-element.87), channel_id=1, source_target_pairs={{0,2},{1,3},{2,0},{3,1},{4,6},{5,7},{6,4},{7,5},{8,10},{9,11},{10,... | collective-permute-start | bytes 393224 | tf_op jit(solution)/shard_map/ppermute | solution.py:65
  48.7 11.0 %collective-permute-done.15.refs_16_ = bf16[128,512]{1,0:T(8,128)(2,1)S(1)} collective-permute-done((bf16[128,512]{1,0:T(8,128)(2,1)S(1)}, bf16[128,512]{1,0:T(8,128)(2,1)S(1)}, u32[]{:S(2)}, u32[]{:S(2)}) %collective-permute-start.15) | collective-permute-done | bytes 131104 | tf_op jit(solution)/shard_map/ppermute | solution.py:65
  59.7 1.1 collective-permute-start.13
  60.8 0.6 select_reduce_fusion
  61.4 1.2 collective-permute-done.14.refs_15_
  62.6 1.5 collective-permute-start.12
  64.1 0.6 collective-permute-done.13.refs_14_
  64.7 2.1 %collective-permute-start.11 = (bf16[128,512]{1,0:T(8,128)(2,1)S(1)}, bf16[128,512]{1,0:T(8,128)(2,1)S(1)}, u32[]{:S(2)}, u32[]{:S(2)}) collective-permute-start(bf16[128,512]{1,0:T(8,128)(2,1)S(1)} %get-tuple-element.88), channel_id=1, source_target_pairs={{0,8},{4,12},{8,0},{12,4},{1,9},{5,13},{9,1},{13,5},{2,10},{6,14},... | collective-permute-start | bytes 393224 | tf_op jit(solution)/shard_map/ppermute | solution.py:65
  66.8 1.4 collective-permute-start.10
  68.4 0.8 copy.43.refs_4_
  69.2 0.6 collective-permute-start.7
  69.8 2.1 %collective-permute-done.11.refs_12_ = bf16[128,512]{1,0:T(8,128)(2,1)S(1)} collective-permute-done((bf16[128,512]{1,0:T(8,128)(2,1)S(1)}, bf16[128,512]{1,0:T(8,128)(2,1)S(1)}, u32[]{:S(2)}, u32[]{:S(2)}) %collective-permute-start.11) | collective-permute-done | bytes 131104 | tf_op jit(solution)/shard_map/ppermute | solution.py:65
  71.9 2.9 %collective-permute-start.6 = (bf16[3,512,256]{2,1,0:T(8,128)(2,1)}, bf16[3,512,256]{2,1,0:T(8,128)(2,1)}, u32[]{:S(2)}, u32[]{:S(2)}) collective-permute-start(bf16[3,512,256]{2,1,0:T(8,128)(2,1)} %get-tuple-element.44), channel_id=1, source_target_pairs={{0,8},{4,12},{8,0},{12,4},{1,9},{5,13},{9,1},{13,5},{2,10},{6,14},... | collective-permute-start | bytes 2359304 | tf_op jit(solution)/shard_map/ppermute | solution.py:65
  74.7 0.4 collective-permute-start.5
  75.2 3.3 %collective-permute-start.8 = (bf16[3,512,256]{2,1,0:T(8,128)(2,1)S(1)}, bf16[3,512,256]{2,1,0:T(8,128)(2,1)}, u32[]{:S(2)}, u32[]{:S(2)}) collective-permute-start(bf16[3,512,256]{2,1,0:T(8,128)(2,1)S(1)} %copy-done.14), channel_id=1, source_target_pairs={{0,3},{1,0},{2,1},{3,2},{4,7},{5,4},{6,5},{7,6},{8,11},{9,8},{10,9... | collective-permute-start | bytes 2359304 | tf_op jit(solution)/shard_map/ppermute | solution.py:65
  78.4 9.3 %collective-permute-start.9 = (bf16[3,512,256]{2,1,0:T(8,128)(2,1)}, bf16[3,512,256]{2,1,0:T(8,128)(2,1)}, u32[]{:S(2)}, u32[]{:S(2)}) collective-permute-start(bf16[3,512,256]{2,1,0:T(8,128)(2,1)} %collective-permute-done.4.refs_10_), channel_id=1, source_target_pairs={{0,1},{1,2},{2,3},{3,0},{4,5},{5,6},{6,7},{7,4},{8,9},{9,10},{10,1... | collective-permute-start | bytes 2359304 | tf_op jit(solution)/shard_map/ppermute | solution.py:65
  87.7 28.7 %attention_tiles.3 = (bf16[4,3,512,256]{3,2,1,0:T(8,128)(2,1)}, f32[3,512,256]{2,1,0:T(8,128)}, bf16[3,512,256]{2,1,0:T(8,128)(2,1)}, bf16[3,512,256]{2,1,0:T(8,128)(2,1)}, bf16[3,512,256]{2,1,0:T(8,128)(2,1)}) custom-call(s32[3,16]{1,0:T(4,128)S(1)} %pad_add_fusion.table, bf16[2,512,512]{2,1,0:T(8,128)(2,1)} %refs_0_.3, bf16[2,512,512]{2,1,0:T(8,128)(2,1)} %refs_1_.3, ...), custom_call_target="tpu_custom_call" | custom-call | flops 21474836480 | bytes 20971520 | tf_op jit(solution)/shard_map/attention_tiles/pallas_call | solution.py:187
  116.4 8.1 %all-to-all-start.2 = ((bf16[4,3,512,256]{3,2,1,0:T(8,128)(2,1)}), bf16[4,3,512,256]{3,2,1,0:T(8,128)(2,1)}, u32[]{:S(2)}, u32[]{:S(2)}) async-start(bf16[4,3,512,256]{3,2,1,0:T(8,128)(2,1)} %get-tuple-element.55), calls=%async_computation.2 | async-start | bytes 6291456 | tf_op jit(solution)/shard_map/all_to_all | solution.py:401
  124.5 3.1 %collective-permute-start.18 = (bf16[3,512,256]{2,1,0:T(8,128)(2,1)}, bf16[3,512,256]{2,1,0:T(8,128)(2,1)S(1)}, u32[]{:S(2)}, u32[]{:S(2)}) collective-permute-start(bf16[3,512,256]{2,1,0:T(8,128)(2,1)} %get-tuple-element.56), channel_id=1, source_target_pairs={{0,1},{1,2},{2,3},{3,0},{4,5},{5,6},{6,7},{7,4},{8,9},{9,10},{10,1... | collective-permute-start | bytes 2359304 | tf_op jit(solution)/shard_map/ppermute | solution.py:69
  127.6 1.9 collective-permute-start.19
  129.5 0.9 copy-done.20
  130.4 2.5 %collective-permute-start.20 = (bf16[3,512,256]{2,1,0:T(8,128)(2,1)}, bf16[3,512,256]{2,1,0:T(8,128)(2,1)S(1)}, u32[]{:S(2)}, u32[]{:S(2)}) collective-permute-start(bf16[3,512,256]{2,1,0:T(8,128)(2,1)} %get-tuple-element.58), channel_id=1, source_target_pairs={{0,3},{1,0},{2,1},{3,2},{4,7},{5,4},{6,5},{7,6},{8,11},{9,8},{10,9... | collective-permute-start | bytes 2359304 | tf_op jit(solution)/shard_map/ppermute | solution.py:69
  132.9 28.7 %attention_tiles.2 = (bf16[4,3,512,256]{3,2,1,0:T(8,128)(2,1)}, f32[3,512,256]{2,1,0:T(8,128)}, bf16[3,512,256]{2,1,0:T(8,128)(2,1)}, bf16[3,512,256]{2,1,0:T(8,128)(2,1)}, bf16[3,512,256]{2,1,0:T(8,128)(2,1)}) custom-call(s32[3,16]{1,0:T(4,128)S(1)} %pad_add_fusion.table, bf16[2,512,512]{2,1,0:T(8,128)(2,1)} %refs_0_.3, bf16[2,512,512]{2,1,0:T(8,128)(2,1)} %refs_1_.3, ...), custom_call_target="tpu_custom_call" | custom-call | flops 21474836480 | bytes 20971520 | tf_op jit(solution)/shard_map/attention_tiles/pallas_call | solution.py:187
  161.7 0.8 copy-done.8
  162.6 0.3 copy-done.9
  163.1 4.8 %all-to-all-start.3 = ((bf16[4,3,512,256]{3,2,1,0:T(8,128)(2,1)}), bf16[4,3,512,256]{3,2,1,0:T(8,128)(2,1)}, u32[]{:S(2)}, u32[]{:S(2)}) async-start(bf16[4,3,512,256]{3,2,1,0:T(8,128)(2,1)} %get-tuple-element.59), calls=%async_computation.3 | async-start | bytes 6291456 | tf_op jit(solution)/shard_map/all_to_all | solution.py:401
  167.9 1.5 collective-permute-start.22
  169.4 1.7 collective-permute-start.23
  171.1 4.5 %summed.2 = (f32[2,512,512]{2,1,0:T(8,128)}, f32[2,512,512]{2,1,0:T(8,128)}, f32[2,512,512]{2,1,0:T(8,128)}) custom-call(bf16[4,3,512,256]{3,2,1,0:T(8,128)(2,1)} %all-to-all-done.2.got_x, f32[3,512,256]{2,1,0:T(8,128)} %get-tuple-element.65.own_z, bf16[3,512,256]{2,1,0:T(8,128)(2,1)} %copy-done.8, bf16[3,512,256]{2,1,0:T(8,128)(2,1)} %copy-done.9, ...), custom_call_target="tpu_custom_call" | custom-call | tf_op jit(solution)/shard_map/summed/pallas_call | solution.py:252
  175.6 14.1 %collective-permute-done.21.refs_0_ = bf16[3,512,256]{2,1,0:T(8,128)(2,1)S(1)} collective-permute-done((bf16[3,512,256]{2,1,0:T(8,128)(2,1)}, bf16[3,512,256]{2,1,0:T(8,128)(2,1)S(1)}, u32[]{:S(2)}, u32[]{:S(2)}) %collective-permute-start.21) | collective-permute-done | bytes 786464 | tf_op jit(solution)/shard_map/ppermute | solution.py:69
  189.7 0.9 collective-permute-done.23.refs_2_
  190.6 0.3 copy-done.12
  191.0 0.5 copy-done.13
  191.5 4.5 %summed.3 = (f32[2,512,512]{2,1,0:T(8,128)}, f32[2,512,512]{2,1,0:T(8,128)}, f32[2,512,512]{2,1,0:T(8,128)}) custom-call(bf16[4,3,512,256]{3,2,1,0:T(8,128)(2,1)} %all-to-all-done.3.got_x, f32[3,512,256]{2,1,0:T(8,128)} %get-tuple-element.60.own_z, bf16[3,512,256]{2,1,0:T(8,128)(2,1)} %copy-done.11, ...), custom_call_target="tpu_custom_call", output_to_operand_aliasing={{0}: (5, {}), {1}: (6, {}), {2}: (7, {})} | custom-call | tf_op jit(solution)/shard_map/summed/pallas_call | solution.py:252
  (95 shorter events, 1.9 us)
Async XLA Ops:
  0.6 11.9 %copy-start = (bf16[2,512,512]{2,1,0:T(8,128)(2,1)S(1)}, bf16[2,512,512]{2,1,0:T(8,128)(2,1)}, u32[]{:S(2)}) copy-start(bf16[2,512,512]{2,1,0:T(8,128)(2,1)} %param.12) | copy-start | bytes 3145732
  0.6 2.1 %copy-start.2 = (bf16[2,512,512]{2,1,0:T(8,128)(2,1)S(1)}, bf16[2,512,512]{2,1,0:T(8,128)(2,1)}, u32[]{:S(2)}) copy-start(bf16[2,512,512]{2,1,0:T(8,128)(2,1)} %refs_0_.3) | copy-start | bytes 3145732
  0.7 3.0 %copy-start.3 = (bf16[2,512,512]{2,1,0:T(8,128)(2,1)S(1)}, bf16[2,512,512]{2,1,0:T(8,128)(2,1)}, u32[]{:S(2)}) copy-start(bf16[2,512,512]{2,1,0:T(8,128)(2,1)} %refs_1_.3) | copy-start | bytes 3145732
  4.5 8.0 %copy-start.7 = (bf16[512,96]{0,1:T(8,128)(2,1)S(1)}, bf16[512,96]{0,1:T(8,128)(2,1)}, u32[]{:S(2)}) copy-start(bf16[512,96]{0,1:T(8,128)(2,1)} %param.13) | copy-start | bytes 294916
  4.5 8.0 %copy-start.16 = (f32[96,512]{1,0:T(8,128)S(1)}, f32[96,512]{1,0:T(8,128)}, u32[]{:S(2)}) copy-start(f32[96,512]{1,0:T(8,128)} %param.14) | copy-start | bytes 589828
  5.4 26.4 %collective-permute-start.1 = (bf16[3,512,256]{2,1,0:T(8,128)(2,1)}, bf16[3,512,256]{2,1,0:T(8,128)(2,1)}, u32[]{:S(2)}, u32[]{:S(2)}) collective-permute-start(bf16[3,512,256]{2,1,0:T(8,128)(2,1)} %pad_maximum_fusion.2), channel_id=1, source_target_pairs={{0,4},{4,8},{8,12},{12,0},{1,5},{5,9},{9,13},{13,1},{2,6},{6,10},{... | collective-permute-start | bytes 2359304 | tf_op jit(solution)/shard_map/ppermute | solution.py:65
  6.9 24.9 %collective-permute-start = (bf16[3,512,256]{2,1,0:T(8,128)(2,1)}, bf16[3,512,256]{2,1,0:T(8,128)(2,1)}, u32[]{:S(2)}, u32[]{:S(2)}) collective-permute-start(bf16[3,512,256]{2,1,0:T(8,128)(2,1)} %pad_maximum_fusion.2), channel_id=1, source_target_pairs={{0,12},{4,0},{8,4},{12,8},{1,13},{5,1},{9,5},{13,9},{2,14},{6,2},{... | collective-permute-start | bytes 2359304 | tf_op jit(solution)/shard_map/ppermute | solution.py:65
  8.4 23.4 %collective-permute-start.3 = (bf16[3,512,256]{2,1,0:T(8,128)(2,1)}, bf16[3,512,256]{2,1,0:T(8,128)(2,1)}, u32[]{:S(2)}, u32[]{:S(2)}) collective-permute-start(bf16[3,512,256]{2,1,0:T(8,128)(2,1)} %pad_maximum_fusion.3), channel_id=1, source_target_pairs={{0,1},{1,2},{2,3},{3,0},{4,5},{5,6},{6,7},{7,4},{8,9},{9,10},{10,1... | collective-permute-start | bytes 2359304 | tf_op jit(solution)/shard_map/ppermute | solution.py:65
  10.4 21.5 %collective-permute-start.2 = (bf16[3,512,256]{2,1,0:T(8,128)(2,1)}, bf16[3,512,256]{2,1,0:T(8,128)(2,1)}, u32[]{:S(2)}, u32[]{:S(2)}) collective-permute-start(bf16[3,512,256]{2,1,0:T(8,128)(2,1)} %pad_maximum_fusion.3), channel_id=1, source_target_pairs={{0,3},{1,0},{2,1},{3,2},{4,7},{5,4},{6,5},{7,6},{8,11},{9,8},{10,9... | collective-permute-start | bytes 2359304 | tf_op jit(solution)/shard_map/ppermute | solution.py:65
  13.0 7.3 %copy-start.18 = (s32[16,16]{1,0:T(8,128)S(1)}, s32[16,16]{1,0:T(8,128)}, u32[]{:S(2)}) copy-start(s32[16,16]{1,0:T(8,128)} %param.23) | copy-start | bytes 3076
  13.0 7.3 %copy-start.19 = (s32[16,16]{1,0:T(8,128)S(1)}, s32[16,16]{1,0:T(8,128)}, u32[]{:S(2)}) copy-start(s32[16,16]{1,0:T(8,128)} %param.22) | copy-start | bytes 3076
  13.0 9.4 %copy-start.4 = (bf16[1,512,256]{2,1,0:T(8,128)(2,1)S(1)}, bf16[1,512,256]{2,1,0:T(8,128)(2,1)}, u32[]{:S(2)}) copy-start(bf16[1,512,256]{2,1,0:T(8,128)(2,1)} %get-tuple-element.86) | copy-start | bytes 786436
  13.0 9.4 %copy-start.5 = (bf16[1,512,256]{2,1,0:T(8,128)(2,1)S(1)}, bf16[1,512,256]{2,1,0:T(8,128)(2,1)}, u32[]{:S(2)}) copy-start(bf16[1,512,256]{2,1,0:T(8,128)(2,1)} %get-tuple-element.77) | copy-start | bytes 786436
  13.0 9.4 %copy-start.6 = (bf16[1,512,256]{2,1,0:T(8,128)(2,1)S(1)}, bf16[1,512,256]{2,1,0:T(8,128)(2,1)}, u32[]{:S(2)}) copy-start(bf16[1,512,256]{2,1,0:T(8,128)(2,1)} %get-tuple-element.78) | copy-start | bytes 786436
  14.2 13.4 %all-to-all-start = ((f32[8,96,128]{2,1,0:T(8,128)}), f32[8,96,128]{2,1,0:T(8,128)S(1)}, u32[]{:S(2)}, u32[]{:S(2)}) async-start(f32[8,96,128]{2,1,0:T(8,128)} %copy.36), calls=%async_computation | async-start | bytes 786432 | tf_op jit(solution)/shard_map/all_to_all | solution.py:309
  22.4 19.8 %copy-start.25 = (s32[1,512]{1,0:T(1,128)S(1)}, s32[1,512]{1,0:T(1,128)}, u32[]{:S(2)}) copy-start(s32[1,512]{1,0:T(1,128)} %param.17) | copy-start | bytes 6148
  27.6 0.8 copy-start.1
  31.8 10.2 %all-to-all-start.1 = ((bf16[8,96,128]{2,1,0:T(8,128)(2,1)}), bf16[8,96,128]{2,1,0:T(8,128)(2,1)S(1)}, u32[]{:S(2)}, u32[]{:S(2)}) async-start(bf16[8,96,128]{2,1,0:T(8,128)(2,1)} %score_gradient.1), calls=%async_computation.1 | async-start | bytes 393216 | tf_op jit(solution)/shard_map/all_to_all | solution.py:320
  35.3 31.5 %collective-permute-start.4 = (bf16[3,512,256]{2,1,0:T(8,128)(2,1)}, bf16[3,512,256]{2,1,0:T(8,128)(2,1)}, u32[]{:S(2)}, u32[]{:S(2)}) collective-permute-start(bf16[3,512,256]{2,1,0:T(8,128)(2,1)} %get-tuple-element.45), channel_id=1, source_target_pairs={{0,1},{1,2},{2,3},{3,0},{4,5},{5,6},{6,7},{7,4},{8,9},{9,10},{10,1... | collective-permute-start | bytes 2359304 | tf_op jit(solution)/shard_map/ppermute | solution.py:65
  35.7 39.5 %collective-permute-start.16 = (bf16[3,512,256]{2,1,0:T(8,128)(2,1)}, bf16[3,512,256]{2,1,0:T(8,128)(2,1)}, u32[]{:S(2)}, u32[]{:S(2)}) collective-permute-start(bf16[3,512,256]{2,1,0:T(8,128)(2,1)} %collective-permute-done.refs_5_), channel_id=1, source_target_pairs={{0,12},{4,0},{8,4},{12,8},{1,13},{5,1},{9,5},{13,9},{2,14},{6,2},{... | collective-permute-start | bytes 2359304 | tf_op jit(solution)/shard_map/ppermute | solution.py:65
  37.4 41.0 %collective-permute-start.17 = (bf16[3,512,256]{2,1,0:T(8,128)(2,1)}, bf16[3,512,256]{2,1,0:T(8,128)(2,1)}, u32[]{:S(2)}, u32[]{:S(2)}) collective-permute-start(bf16[3,512,256]{2,1,0:T(8,128)(2,1)} %collective-permute-done.2.refs_8_), channel_id=1, source_target_pairs={{0,3},{1,0},{2,1},{3,2},{4,7},{5,4},{6,5},{7,6},{8,11},{9,8},{10,9... | collective-permute-start | bytes 2359304 | tf_op jit(solution)/shard_map/ppermute | solution.py:65
  43.2 1.0 copy-start.17
  43.2 31.9 %copy-start.14 = (bf16[3,512,256]{2,1,0:T(8,128)(2,1)S(1)}, bf16[3,512,256]{2,1,0:T(8,128)(2,1)}, u32[]{:S(2)}) copy-start(bf16[3,512,256]{2,1,0:T(8,128)(2,1)} %get-tuple-element.45) | copy-start | bytes 2359300
  44.3 43.5 %copy-start.15 = (bf16[2,128,512]{2,1,0:T(8,128)(2,1)}, bf16[2,128,512]{2,1,0:T(8,128)(2,1)S(1)}, u32[]{:S(2)}) copy-start(bf16[2,128,512]{2,1,0:T(8,128)(2,1)S(1)} %fusion.12.refs_3_) | copy-start | bytes 786436
  44.3 15.4 %collective-permute-start.15 = (bf16[128,512]{1,0:T(8,128)(2,1)S(1)}, bf16[128,512]{1,0:T(8,128)(2,1)S(1)}, u32[]{:S(2)}, u32[]{:S(2)}) collective-permute-start(bf16[128,512]{1,0:T(8,128)(2,1)S(1)} %get-tuple-element.87), channel_id=1, source_target_pairs={{0,1},{1,2},{2,3},{3,0},{4,5},{5,6},{6,7},{7,4},{8,9},{9,10},{10,1... | collective-permute-start | bytes 393224 | tf_op jit(solution)/shard_map/ppermute | solution.py:65
  45.4 17.2 %collective-permute-start.14 = (bf16[128,512]{1,0:T(8,128)(2,1)S(1)}, bf16[128,512]{1,0:T(8,128)(2,1)S(1)}, u32[]{:S(2)}, u32[]{:S(2)}) collective-permute-start(bf16[128,512]{1,0:T(8,128)(2,1)S(1)} %get-tuple-element.87), channel_id=1, source_target_pairs={{0,2},{1,3},{2,0},{3,1},{4,6},{5,7},{6,4},{7,5},{8,10},{9,11},{10,... | collective-permute-start | bytes 393224 | tf_op jit(solution)/shard_map/ppermute | solution.py:65
  59.7 28.0 %copy-start.21 = (bf16[128,512]{1,0:T(8,128)(2,1)}, bf16[128,512]{1,0:T(8,128)(2,1)S(1)}, u32[]{:S(2)}) copy-start(bf16[128,512]{1,0:T(8,128)(2,1)S(1)} %collective-permute-done.15.refs_16_) | copy-start | bytes 393220
  59.7 5.0 %collective-permute-start.13 = (bf16[128,512]{1,0:T(8,128)(2,1)S(1)}, bf16[128,512]{1,0:T(8,128)(2,1)S(1)}, u32[]{:S(2)}, u32[]{:S(2)}) collective-permute-start(bf16[128,512]{1,0:T(8,128)(2,1)S(1)} %get-tuple-element.87), channel_id=1, source_target_pairs={{0,3},{1,0},{2,1},{3,2},{4,7},{5,4},{6,5},{7,6},{8,11},{9,8},{10,9... | collective-permute-start | bytes 393224 | tf_op jit(solution)/shard_map/ppermute | solution.py:65
  62.6 6.6 %copy-start.22 = (bf16[128,512]{1,0:T(8,128)(2,1)}, bf16[128,512]{1,0:T(8,128)(2,1)S(1)}, u32[]{:S(2)}) copy-start(bf16[128,512]{1,0:T(8,128)(2,1)S(1)} %collective-permute-done.14.refs_15_) | copy-start | bytes 393220
  62.6 6.6 %collective-permute-start.12 = (bf16[128,512]{1,0:T(8,128)(2,1)S(1)}, bf16[128,512]{1,0:T(8,128)(2,1)}, u32[]{:S(2)}, u32[]{:S(2)}) collective-permute-start(bf16[128,512]{1,0:T(8,128)(2,1)S(1)} %get-tuple-element.88), channel_id=1, source_target_pairs={{0,4},{4,8},{8,12},{12,0},{1,5},{5,9},{9,13},{13,1},{2,6},{6,10},{... | collective-permute-start | bytes 393224 | tf_op jit(solution)/shard_map/ppermute | solution.py:65
  64.7 3.6 %copy-start.23 = (bf16[128,512]{1,0:T(8,128)(2,1)}, bf16[128,512]{1,0:T(8,128)(2,1)S(1)}, u32[]{:S(2)}) copy-start(bf16[128,512]{1,0:T(8,128)(2,1)S(1)} %collective-permute-done.13.refs_14_) | copy-start | bytes 393220
  64.7 7.2 %collective-permute-start.11 = (bf16[128,512]{1,0:T(8,128)(2,1)S(1)}, bf16[128,512]{1,0:T(8,128)(2,1)S(1)}, u32[]{:S(2)}, u32[]{:S(2)}) collective-permute-start(bf16[128,512]{1,0:T(8,128)(2,1)S(1)} %get-tuple-element.88), channel_id=1, source_target_pairs={{0,8},{4,12},{8,0},{12,4},{1,9},{5,13},{9,1},{13,5},{2,10},{6,14},... | collective-permute-start | bytes 393224 | tf_op jit(solution)/shard_map/ppermute | solution.py:65
  66.8 7.9 %collective-permute-start.10 = (bf16[128,512]{1,0:T(8,128)(2,1)S(1)}, bf16[128,512]{1,0:T(8,128)(2,1)}, u32[]{:S(2)}, u32[]{:S(2)}) collective-permute-start(bf16[128,512]{1,0:T(8,128)(2,1)S(1)} %get-tuple-element.88), channel_id=1, source_target_pairs={{0,12},{4,0},{8,4},{12,8},{1,13},{5,1},{9,5},{13,9},{2,14},{6,2},{... | collective-permute-start | bytes 393224 | tf_op jit(solution)/shard_map/ppermute | solution.py:65
  69.2 60.3 %collective-permute-start.7 = (bf16[3,512,256]{2,1,0:T(8,128)(2,1)}, bf16[3,512,256]{2,1,0:T(8,128)(2,1)S(1)}, u32[]{:S(2)}, u32[]{:S(2)}) collective-permute-start(bf16[3,512,256]{2,1,0:T(8,128)(2,1)} %get-tuple-element.44), channel_id=1, source_target_pairs={{0,4},{4,8},{8,12},{12,0},{1,5},{5,9},{9,13},{13,1},{2,6},{6,10},{... | collective-permute-start | bytes 2359304 | tf_op jit(solution)/shard_map/ppermute | solution.py:65
  71.9 15.9 %copy-start.24 = (bf16[128,512]{1,0:T(8,128)(2,1)}, bf16[128,512]{1,0:T(8,128)(2,1)S(1)}, u32[]{:S(2)}) copy-start(bf16[128,512]{1,0:T(8,128)(2,1)S(1)} %collective-permute-done.11.refs_12_) | copy-start | bytes 393220
  71.9 61.0 %collective-permute-start.6 = (bf16[3,512,256]{2,1,0:T(8,128)(2,1)}, bf16[3,512,256]{2,1,0:T(8,128)(2,1)}, u32[]{:S(2)}, u32[]{:S(2)}) collective-permute-start(bf16[3,512,256]{2,1,0:T(8,128)(2,1)} %get-tuple-element.44), channel_id=1, source_target_pairs={{0,8},{4,12},{8,0},{12,4},{1,9},{5,13},{9,1},{13,5},{2,10},{6,14},... | collective-permute-start | bytes 2359304 | tf_op jit(solution)/shard_map/ppermute | solution.py:65
  74.7 58.2 %collective-permute-start.5 = (bf16[3,512,256]{2,1,0:T(8,128)(2,1)}, bf16[3,512,256]{2,1,0:T(8,128)(2,1)}, u32[]{:S(2)}, u32[]{:S(2)}) collective-permute-start(bf16[3,512,256]{2,1,0:T(8,128)(2,1)} %get-tuple-element.44), channel_id=1, source_target_pairs={{0,12},{4,0},{8,4},{12,8},{1,13},{5,1},{9,5},{13,9},{2,14},{6,2},{... | collective-permute-start | bytes 2359304 | tf_op jit(solution)/shard_map/ppermute | solution.py:65
  75.2 49.4 %collective-permute-start.8 = (bf16[3,512,256]{2,1,0:T(8,128)(2,1)S(1)}, bf16[3,512,256]{2,1,0:T(8,128)(2,1)}, u32[]{:S(2)}, u32[]{:S(2)}) collective-permute-start(bf16[3,512,256]{2,1,0:T(8,128)(2,1)S(1)} %copy-done.14), channel_id=1, source_target_pairs={{0,3},{1,0},{2,1},{3,2},{4,7},{5,4},{6,5},{7,6},{8,11},{9,8},{10,9... | collective-permute-start | bytes 2359304 | tf_op jit(solution)/shard_map/ppermute | solution.py:65
  78.4 49.2 %collective-permute-start.9 = (bf16[3,512,256]{2,1,0:T(8,128)(2,1)}, bf16[3,512,256]{2,1,0:T(8,128)(2,1)}, u32[]{:S(2)}, u32[]{:S(2)}) collective-permute-start(bf16[3,512,256]{2,1,0:T(8,128)(2,1)} %collective-permute-done.4.refs_10_), channel_id=1, source_target_pairs={{0,1},{1,2},{2,3},{3,0},{4,5},{5,6},{6,7},{7,4},{8,9},{9,10},{10,1... | collective-permute-start | bytes 2359304 | tf_op jit(solution)/shard_map/ppermute | solution.py:65
  116.4 45.3 %all-to-all-start.2 = ((bf16[4,3,512,256]{3,2,1,0:T(8,128)(2,1)}), bf16[4,3,512,256]{3,2,1,0:T(8,128)(2,1)}, u32[]{:S(2)}, u32[]{:S(2)}) async-start(bf16[4,3,512,256]{3,2,1,0:T(8,128)(2,1)} %get-tuple-element.55), calls=%async_computation.2 | async-start | bytes 6291456 | tf_op jit(solution)/shard_map/all_to_all | solution.py:401
  124.5 37.1 %collective-permute-start.18 = (bf16[3,512,256]{2,1,0:T(8,128)(2,1)}, bf16[3,512,256]{2,1,0:T(8,128)(2,1)S(1)}, u32[]{:S(2)}, u32[]{:S(2)}) collective-permute-start(bf16[3,512,256]{2,1,0:T(8,128)(2,1)} %get-tuple-element.56), channel_id=1, source_target_pairs={{0,1},{1,2},{2,3},{3,0},{4,5},{5,6},{6,7},{7,4},{8,9},{9,10},{10,1... | collective-permute-start | bytes 2359304 | tf_op jit(solution)/shard_map/ppermute | solution.py:69
  127.6 34.1 %collective-permute-start.19 = (bf16[3,512,256]{2,1,0:T(8,128)(2,1)}, bf16[3,512,256]{2,1,0:T(8,128)(2,1)S(1)}, u32[]{:S(2)}, u32[]{:S(2)}) collective-permute-start(bf16[3,512,256]{2,1,0:T(8,128)(2,1)} %get-tuple-element.57), channel_id=1, source_target_pairs={{0,2},{1,3},{2,0},{3,1},{4,6},{5,7},{6,4},{7,5},{8,10},{9,11},{10,... | collective-permute-start | bytes 2359304 | tf_op jit(solution)/shard_map/ppermute | solution.py:69
  129.5 0.9 copy-start.20
  130.4 31.3 %collective-permute-start.20 = (bf16[3,512,256]{2,1,0:T(8,128)(2,1)}, bf16[3,512,256]{2,1,0:T(8,128)(2,1)S(1)}, u32[]{:S(2)}, u32[]{:S(2)}) collective-permute-start(bf16[3,512,256]{2,1,0:T(8,128)(2,1)} %get-tuple-element.58), channel_id=1, source_target_pairs={{0,3},{1,0},{2,1},{3,2},{4,7},{5,4},{6,5},{7,6},{8,11},{9,8},{10,9... | collective-permute-start | bytes 2359304 | tf_op jit(solution)/shard_map/ppermute | solution.py:69
  161.7 0.9 copy-start.8
  161.7 1.1 copy-start.9
  161.7 1.4 copy-start.10
  163.1 27.5 %all-to-all-start.3 = ((bf16[4,3,512,256]{3,2,1,0:T(8,128)(2,1)}), bf16[4,3,512,256]{3,2,1,0:T(8,128)(2,1)}, u32[]{:S(2)}, u32[]{:S(2)}) async-start(bf16[4,3,512,256]{3,2,1,0:T(8,128)(2,1)} %get-tuple-element.59), calls=%async_computation.3 | async-start | bytes 6291456 | tf_op jit(solution)/shard_map/all_to_all | solution.py:401
  167.9 21.8 %collective-permute-start.21 = (bf16[3,512,256]{2,1,0:T(8,128)(2,1)}, bf16[3,512,256]{2,1,0:T(8,128)(2,1)S(1)}, u32[]{:S(2)}, u32[]{:S(2)}) collective-permute-start(bf16[3,512,256]{2,1,0:T(8,128)(2,1)} %get-tuple-element.61), channel_id=1, source_target_pairs={{0,1},{1,2},{2,3},{3,0},{4,5},{5,6},{6,7},{7,4},{8,9},{9,10},{10,1... | collective-permute-start | bytes 2359304 | tf_op jit(solution)/shard_map/ppermute | solution.py:69
  167.9 21.8 %collective-permute-start.22 = (bf16[3,512,256]{2,1,0:T(8,128)(2,1)}, bf16[3,512,256]{2,1,0:T(8,128)(2,1)S(1)}, u32[]{:S(2)}, u32[]{:S(2)}) collective-permute-start(bf16[3,512,256]{2,1,0:T(8,128)(2,1)} %get-tuple-element.62), channel_id=1, source_target_pairs={{0,2},{1,3},{2,0},{3,1},{4,6},{5,7},{6,4},{7,5},{8,10},{9,11},{10,... | collective-permute-start | bytes 2359304 | tf_op jit(solution)/shard_map/ppermute | solution.py:69
  169.4 21.2 %collective-permute-start.23 = (bf16[3,512,256]{2,1,0:T(8,128)(2,1)}, bf16[3,512,256]{2,1,0:T(8,128)(2,1)S(1)}, u32[]{:S(2)}, u32[]{:S(2)}) collective-permute-start(bf16[3,512,256]{2,1,0:T(8,128)(2,1)} %get-tuple-element.63), channel_id=1, source_target_pairs={{0,3},{1,0},{2,1},{3,2},{4,7},{5,4},{6,5},{7,6},{8,11},{9,8},{10,9... | collective-permute-start | bytes 2359304 | tf_op jit(solution)/shard_map/ppermute | solution.py:69
  189.7 0.9 copy-start.11
  189.7 1.2 copy-start.12
  190.6 0.9 copy-start.13

commit v7 on v6

--- a/solution.py
+++ b/solution.py
@@ -319,7 +319,8 @@
     )
     returned = lax.all_to_all(derivative, MEMBER, 0, 0, tiled=True)
     far = [fetched(near[0], "x", 1), fetched(near[2], "z", 1)]
-    z_before = fetched(own_1[1], "z", 3)
+    before = [fetched(a, axis, 3) for a, axis in zip(own_1, ("x", "z"))]
+    returned, own_1, before = lax.optimization_barrier((returned, own_1, before))
     grad_forecast = (
         returned.reshape(groups, channels, members, span)
         .transpose(2, 1, 0, 3)
@@ -372,10 +373,13 @@
     )
     late_z = [fetched(late_own[0], "z", d) for d in (1, 2, 3)]
     late_x = [fetched(late_own[1], "x", d) for d in (1, 2, 3)]
-    late_own, own_1, z_before = lax.optimization_barrier((late_own, own_1, z_before))
-    x_around = [fetched(own_1[0], "x", d) for d in (1, 2, 3)]
-    z_around = [fetched(own_1[1], "z", 1), fetched(z_before, "z", 3), z_before]
-    came = (((near[0], far[0], near[1]), (near[2], far[1], near[3])), (x_around, z_around))
+    late_own, own_1, before = lax.optimization_barrier((late_own, own_1, before))
+    after = [fetched(a, axis, 1) for a, axis in zip(own_1, ("x", "z"))]
+    last = [fetched(a, axis, 3) for a, axis in zip(before, ("x", "z"))]
+    came = (
+        ((near[0], far[0], near[1]), (near[2], far[1], near[3])),
+        ((after[0], last[0], before[0]), (after[1], last[1], before[1])),
+    )
 
     outs = None
     parts = []

time: 197 us -> 193 us (0.980)
  starting transfers between devices: 68.9 us -> 54 us
  waiting for transfers between devices: 34.4 us -> 44.1 us
    ppermute x6, waiting for transfers between devices: 15 us -> 29.5 us  [delivered(): lax.ppermute(x, axis, [(i, (i + distance) % SIDE) for i in range(SIDE)])]
    ppermute x18, starting transfers between devices: 37.4 us -> 24.4 us  [fetched(): lax.ppermute(x, axis, [(i, (i - distance) % SIDE) for i in range(SIDE)])]
    ppermute x18, waiting for transfers between devices: 14.9 us -> 9.49 us  [fetched(): lax.ppermute(x, axis, [(i, (i - distance) % SIDE) for i in range(SIDE)])]
    unnamed x52 -> x56, local copies, waits for them, and re-layouts: 3.99 us -> 4.55 us
  transfers between devices with their start and end apart: 28 -> 28, of which waited for: 8 -> 8; matrix products, arithmetic and copies ran while one was open for 7% -> 7% of each run, Pallas kernels for 33% -> 34%
where the time goes in v7:
time: 193 us; the launch traced here: 192 us
  Pallas kernels  69.7 us (36%)
  starting transfers between devices  54 us (28%)
  waiting for transfers between devices  44.1 us (23%)
  local copies, waits for them, and re-layouts  13.9 us (7%)
  other arithmetic  6.22 us (3%)
  matrix products  3.15 us (2%)
    pallas_call x2, Pallas kernels, attention_tiles(): pl.pallas_call(functools.partial(tile_kernel, base=2 * base), out_shape=[...  57.4 us
    ppermute x6, waiting for transfers between devices, delivered(): lax.ppermute(x, axis, [(i, (i + distance) % SIDE) for i in range(SIDE)])  29.5 us
    ppermute x18, starting transfers between devices, fetched(): lax.ppermute(x, axis, [(i, (i - distance) % SIDE) for i in range(SIDE)])  24.4 us
    all_to_all x2, starting transfers between devices, shards(): got_x = lax.all_to_all(send_x, 'x', 0, 0, tiled=True)  12.1 us
    ppermute x18, waiting for transfers between devices, fetched(): lax.ppermute(x, axis, [(i, (i - distance) % SIDE) for i in range(SIDE)])  9.49 us
    ppermute x6, starting transfers between devices, delivered(): lax.ppermute(x, axis, [(i, (i + distance) % SIDE) for i in range(SIDE)])  9.34 us
    pallas_call x2, Pallas kernels, summed(): pl.pallas_call(sum_kernel, out_shape=[shape] * 3, grid=(2,), in_specs=[pl...  8.93 us
    unnamed x56, local copies, waits for them, and re-layouts  4.55 us
  transfers between devices with their start and end apart: 28, of which 8 were waited for; matrix products, arithmetic and copies ran while one was open for 7% of the time, Pallas kernels for 34%

profile of v7, /device:TPU:2, one launch (start us, length us, event | category | flops | bytes accessed | tf_op | source)
XLA Modules:
  0.0 192.1 jit_solution(13596416902395194324)
XLA Ops:
  0.7 2.1 %fusion.18 = (bf16[1,512,256]{2,1,0:T(8,128)(2,1)S(1)}, bf16[1,512,256]{2,1,0:T(8,128)(2,1)S(1)}, bf16[1,512,256]{2,1,0:T(8,128)(2,1)S(1)}, bf16[1,512,256]{2,1,0:T(8,128)(2,1)}) fusion(bf16[2,512,512]{2,1,0:T(8,128)(2,1)} %refs_2_.3), kind=kLoop, calls=%fused_computation.53 | loop fusion | bytes 2097152 | tf_op jit(solution)/shard_map/slice | solution.py:270
  2.8 0.9 fusion.16
  3.7 0.8 fusion.17
  4.5 1.0 pad_maximum_fusion.2
  5.4 1.5 collective-permute-start.1
  6.9 0.5 collective-permute-start
  7.4 1.0 pad_maximum_fusion.3
  8.4 1.9 collective-permute-start.3
  10.3 2.1 %collective-permute-start.2 = (bf16[3,512,256]{2,1,0:T(8,128)(2,1)}, bf16[3,512,256]{2,1,0:T(8,128)(2,1)}, u32[]{:S(2)}, u32[]{:S(2)}) collective-permute-start(bf16[3,512,256]{2,1,0:T(8,128)(2,1)} %pad_maximum_fusion.3), channel_id=1, source_target_pairs={{0,3},{1,0},{2,1},{3,2},{4,7},{5,4},{6,5},{7,6},{8,11},{9,8},{10,9... | collective-permute-start | bytes 2359304 | tf_op jit(solution)/shard_map/ppermute | solution.py:65
  12.5 0.4 fusion
  13.2 1.0 copy.36
  14.2 4.5 %all-to-all-start = ((f32[8,96,128]{2,1,0:T(8,128)}), f32[8,96,128]{2,1,0:T(8,128)S(1)}, u32[]{:S(2)}, u32[]{:S(2)}) async-start(f32[8,96,128]{2,1,0:T(8,128)} %copy.36), calls=%async_computation | async-start | bytes 786432 | tf_op jit(solution)/shard_map/all_to_all | solution.py:309
  18.9 0.4 copy-done.26
  19.3 0.8 dynamic_slice.7
  20.1 0.7 tile.20.area_ref
  21.0 0.9 constant_dynamic-slice_fusion
  21.9 0.7 copy.38.truth_ref
  22.7 2.3 %pad_maximum_fusion = (bf16[3,512,256]{2,1,0:T(8,128)(2,1)}, bf16[3,512,256]{2,1,0:T(8,128)(2,1)}) fusion(bf16[1,512,256]{2,1,0:T(8,128)(2,1)S(1)} %copy-done.4, bf16[1,512,256]{2,1,0:T(8,128)(2,1)} %get-tuple-element.94, bf16[1,512,256]{2,1,0:T(8,128)(2,1)S(1)} %copy-done.6, bf16[1,512,256]{2,1,0:T(8,128)(2,1)S(1)} %get-tuple-element.97, ...), kind=kLoop, calls=%fused_computation.9 | loop fusion | flops 1572864 | bytes 3145728 | tf_op jit(solution)/shard_map/stack | solution.py:270
  25.0 2.6 %all-to-all-done.forecast_ref = f32[8,96,128]{2,1,0:T(8,128)S(1)} async-done(((f32[8,96,128]{2,1,0:T(8,128)}), f32[8,96,128]{2,1,0:T(8,128)S(1)}, u32[]{:S(2)}, u32[]{:S(2)}) %all-to-all-start) | async-done | bytes 393248 | tf_op jit(solution)/shard_map/all_to_all | solution.py:309
  27.6 0.8 copy-done.1
  28.4 3.4 %score_gradient.1 = bf16[8,96,128]{2,1,0:T(8,128)(2,1)} custom-call(f32[8,96,128]{2,1,0:T(8,128)} %copy-done.1, f32[96,128]{1,0:T(8,128)} %copy.38.truth_ref, f32[1,128]{1,0:T(1,128)} %tile.20.area_ref), custom_call_target="tpu_custom_call" | custom-call | tf_op jit(solution)/shard_map/score_gradient/pallas_call | solution.py:49
  31.8 1.6 collective-permute-start.4
  33.6 3.6 %all-to-all-start.1 = ((bf16[8,96,128]{2,1,0:T(8,128)(2,1)}), bf16[8,96,128]{2,1,0:T(8,128)(2,1)S(1)}, u32[]{:S(2)}, u32[]{:S(2)}) async-start(bf16[8,96,128]{2,1,0:T(8,128)(2,1)} %score_gradient.1), calls=%async_computation.1 | async-start | bytes 393216 | tf_op jit(solution)/shard_map/all_to_all | solution.py:320
  37.3 0.7 select_reduce_fusion.1
  38.0 0.6 collective-permute-start.16
  38.6 3.0 %collective-permute-start.17 = (bf16[3,512,256]{2,1,0:T(8,128)(2,1)}, bf16[3,512,256]{2,1,0:T(8,128)(2,1)}, u32[]{:S(2)}, u32[]{:S(2)}) collective-permute-start(bf16[3,512,256]{2,1,0:T(8,128)(2,1)} %collective-permute-done.2.refs_8_), channel_id=1, source_target_pairs={{0,3},{1,0},{2,1},{3,2},{4,7},{5,4},{6,5},{7,6},{8,11},{9,8},{10,9... | collective-permute-start | bytes 2359304 | tf_op jit(solution)/shard_map/ppermute | solution.py:65
  41.6 2.5 %all-to-all-done.1 = bf16[8,96,128]{2,1,0:T(8,128)(2,1)S(1)} async-done(((bf16[8,96,128]{2,1,0:T(8,128)(2,1)}), bf16[8,96,128]{2,1,0:T(8,128)(2,1)S(1)}, u32[]{:S(2)}, u32[]{:S(2)}) %all-to-all-start.1) | async-done | bytes 196640 | tf_op jit(solution)/shard_map/all_to_all | solution.py:320
  44.1 7.1 %collective-permute-done.4.refs_7_ = bf16[3,512,256]{2,1,0:T(8,128)(2,1)S(1)} collective-permute-done((bf16[3,512,256]{2,1,0:T(8,128)(2,1)}, bf16[3,512,256]{2,1,0:T(8,128)(2,1)S(1)}, u32[]{:S(2)}, u32[]{:S(2)}) %collective-permute-start.4) | collective-permute-done | bytes 786464 | tf_op jit(solution)/shard_map/ppermute | solution.py:65
  51.2 0.9 copy-done.23
  52.1 1.6 collective-permute-done.5.refs_10_
  53.9 0.5 constant_dynamic-update-slice_fusion
  54.4 0.5 convolution_convert_fusion.1
  54.9 1.8 bitcast_reduce_fusion
  56.9 0.6 select_reduce_fusion
  57.5 2.3 %collective-permute-start.14 = (bf16[128,512]{1,0:T(8,128)(2,1)S(1)}, bf16[128,512]{1,0:T(8,128)(2,1)}, u32[]{:S(2)}, u32[]{:S(2)}) collective-permute-start(bf16[128,512]{1,0:T(8,128)(2,1)S(1)} %get-tuple-element.99), channel_id=1, source_target_pairs={{0,2},{1,3},{2,0},{3,1},{4,6},{5,7},{6,4},{7,5},{8,10},{9,11},{10,... | collective-permute-start | bytes 393224 | tf_op jit(solution)/shard_map/ppermute | solution.py:65
  59.9 1.0 collective-permute-start.13
  60.9 1.2 collective-permute-start.12
  62.1 3.4 %collective-permute-start.11 = (bf16[128,512]{1,0:T(8,128)(2,1)S(1)}, bf16[128,512]{1,0:T(8,128)(2,1)}, u32[]{:S(2)}, u32[]{:S(2)}) collective-permute-start(bf16[128,512]{1,0:T(8,128)(2,1)S(1)} %get-tuple-element.100), channel_id=1, source_target_pairs={{0,8},{4,12},{8,0},{12,4},{1,9},{5,13},{9,1},{13,5},{2,10},{6,14},... | collective-permute-start | bytes 393224 | tf_op jit(solution)/shard_map/ppermute | solution.py:65
  65.5 0.4 collective-permute-start.10
  66.1 0.8 copy.43.refs_4_
  66.8 2.5 %collective-permute-start.6 = (bf16[3,512,256]{2,1,0:T(8,128)(2,1)S(1)}, bf16[3,512,256]{2,1,0:T(8,128)(2,1)}, u32[]{:S(2)}, u32[]{:S(2)}) collective-permute-start(bf16[3,512,256]{2,1,0:T(8,128)(2,1)S(1)} %copy-done.15), channel_id=1, source_target_pairs={{0,12},{4,0},{8,4},{12,8},{1,13},{5,1},{9,5},{13,9},{2,14},{6,2},{... | collective-permute-start | bytes 2359304 | tf_op jit(solution)/shard_map/ppermute | solution.py:65
  69.3 1.7 collective-permute-start.7
  71.1 0.5 collective-permute-start.9
  71.6 0.7 collective-permute-done.10.refs_11_
  72.4 28.7 %attention_tiles.3 = (bf16[4,3,512,256]{3,2,1,0:T(8,128)(2,1)}, f32[3,512,256]{2,1,0:T(8,128)}, bf16[3,512,256]{2,1,0:T(8,128)(2,1)}, bf16[3,512,256]{2,1,0:T(8,128)(2,1)}, bf16[3,512,256]{2,1,0:T(8,128)(2,1)}) custom-call(s32[3,16]{1,0:T(4,128)S(1)} %pad_add_fusion.table, bf16[2,512,512]{2,1,0:T(8,128)(2,1)} %refs_0_.3, bf16[2,512,512]{2,1,0:T(8,128)(2,1)} %refs_1_.3, ...), custom_call_target="tpu_custom_call" | custom-call | flops 21474836480 | bytes 20971520 | tf_op jit(solution)/shard_map/attention_tiles/pallas_call | solution.py:187
  101.0 7.1 %all-to-all-start.2 = ((bf16[4,3,512,256]{3,2,1,0:T(8,128)(2,1)}), bf16[4,3,512,256]{3,2,1,0:T(8,128)(2,1)}, u32[]{:S(2)}, u32[]{:S(2)}) async-start(bf16[4,3,512,256]{3,2,1,0:T(8,128)(2,1)} %get-tuple-element.67), calls=%async_computation.2 | async-start | bytes 6291456 | tf_op jit(solution)/shard_map/all_to_all | solution.py:405
  108.1 1.0 collective-permute-start.18
  109.1 2.2 %collective-permute-start.19 = (bf16[3,512,256]{2,1,0:T(8,128)(2,1)}, bf16[3,512,256]{2,1,0:T(8,128)(2,1)S(1)}, u32[]{:S(2)}, u32[]{:S(2)}) collective-permute-start(bf16[3,512,256]{2,1,0:T(8,128)(2,1)} %get-tuple-element.69), channel_id=1, source_target_pairs={{0,2},{1,3},{2,0},{3,1},{4,6},{5,7},{6,4},{7,5},{8,10},{9,11},{10,... | collective-permute-start | bytes 2359304 | tf_op jit(solution)/shard_map/ppermute | solution.py:69
  111.3 2.0 %collective-permute-start.20 = (bf16[3,512,256]{2,1,0:T(8,128)(2,1)}, bf16[3,512,256]{2,1,0:T(8,128)(2,1)S(1)}, u32[]{:S(2)}, u32[]{:S(2)}) collective-permute-start(bf16[3,512,256]{2,1,0:T(8,128)(2,1)} %get-tuple-element.70), channel_id=1, source_target_pairs={{0,3},{1,0},{2,1},{3,2},{4,7},{5,4},{6,5},{7,6},{8,11},{9,8},{10,9... | collective-permute-start | bytes 2359304 | tf_op jit(solution)/shard_map/ppermute | solution.py:69
  113.3 28.7 %attention_tiles.2 = (bf16[4,3,512,256]{3,2,1,0:T(8,128)(2,1)}, f32[3,512,256]{2,1,0:T(8,128)}, bf16[3,512,256]{2,1,0:T(8,128)(2,1)}, bf16[3,512,256]{2,1,0:T(8,128)(2,1)}, bf16[3,512,256]{2,1,0:T(8,128)(2,1)}) custom-call(s32[3,16]{1,0:T(4,128)S(1)} %pad_add_fusion.table, bf16[2,512,512]{2,1,0:T(8,128)(2,1)} %refs_0_.3, bf16[2,512,512]{2,1,0:T(8,128)(2,1)} %refs_1_.3, ...), custom_call_target="tpu_custom_call" | custom-call | flops 21474836480 | bytes 20971520 | tf_op jit(solution)/shard_map/attention_tiles/pallas_call | solution.py:187
  142.1 0.5 collective-permute-done.19.refs_1_
  142.6 0.4 copy-done.8
  143.0 0.5 copy-done.9
  143.5 0.3 copy-done.10
  143.7 5.0 %all-to-all-start.3 = ((bf16[4,3,512,256]{3,2,1,0:T(8,128)(2,1)}), bf16[4,3,512,256]{3,2,1,0:T(8,128)(2,1)}, u32[]{:S(2)}, u32[]{:S(2)}) async-start(bf16[4,3,512,256]{3,2,1,0:T(8,128)(2,1)} %get-tuple-element.71), calls=%async_computation.3 | async-start | bytes 6291456 | tf_op jit(solution)/shard_map/all_to_all | solution.py:405
  148.7 0.9 collective-permute-start.21
  149.6 2.5 %collective-permute-start.22 = (bf16[3,512,256]{2,1,0:T(8,128)(2,1)}, bf16[3,512,256]{2,1,0:T(8,128)(2,1)S(1)}, u32[]{:S(2)}, u32[]{:S(2)}) collective-permute-start(bf16[3,512,256]{2,1,0:T(8,128)(2,1)} %get-tuple-element.74), channel_id=1, source_target_pairs={{0,2},{1,3},{2,0},{3,1},{4,6},{5,7},{6,4},{7,5},{8,10},{9,11},{10,... | collective-permute-start | bytes 2359304 | tf_op jit(solution)/shard_map/ppermute | solution.py:69
  152.1 0.7 collective-permute-start.23
  152.9 4.5 %summed.2 = (f32[2,512,512]{2,1,0:T(8,128)}, f32[2,512,512]{2,1,0:T(8,128)}, f32[2,512,512]{2,1,0:T(8,128)}) custom-call(bf16[4,3,512,256]{3,2,1,0:T(8,128)(2,1)} %all-to-all-done.2.got_x, f32[3,512,256]{2,1,0:T(8,128)} %get-tuple-element.77.own_z, bf16[3,512,256]{2,1,0:T(8,128)(2,1)} %copy-done.8, bf16[3,512,256]{2,1,0:T(8,128)(2,1)} %copy-done.9, ...), custom_call_target="tpu_custom_call" | custom-call | tf_op jit(solution)/shard_map/summed/pallas_call | solution.py:252
  157.4 11.1 %collective-permute-done.21.refs_0_ = bf16[3,512,256]{2,1,0:T(8,128)(2,1)S(1)} collective-permute-done((bf16[3,512,256]{2,1,0:T(8,128)(2,1)}, bf16[3,512,256]{2,1,0:T(8,128)(2,1)S(1)}, u32[]{:S(2)}, u32[]{:S(2)}) %collective-permute-start.21) | collective-permute-done | bytes 786464 | tf_op jit(solution)/shard_map/ppermute | solution.py:69
  168.4 18.0 %collective-permute-done.22.refs_1_ = bf16[3,512,256]{2,1,0:T(8,128)(2,1)S(1)} collective-permute-done((bf16[3,512,256]{2,1,0:T(8,128)(2,1)}, bf16[3,512,256]{2,1,0:T(8,128)(2,1)S(1)}, u32[]{:S(2)}, u32[]{:S(2)}) %collective-permute-start.22) | collective-permute-done | bytes 786464 | tf_op jit(solution)/shard_map/ppermute | solution.py:69
  186.4 0.9 copy-done.12
  187.3 0.3 copy-done.13
  187.6 4.5 %summed.3 = (f32[2,512,512]{2,1,0:T(8,128)}, f32[2,512,512]{2,1,0:T(8,128)}, f32[2,512,512]{2,1,0:T(8,128)}) custom-call(bf16[4,3,512,256]{3,2,1,0:T(8,128)(2,1)} %all-to-all-done.3.got_x, f32[3,512,256]{2,1,0:T(8,128)} %get-tuple-element.72.own_z, bf16[3,512,256]{2,1,0:T(8,128)(2,1)} %copy-done.11, ...), custom_call_target="tpu_custom_call", output_to_operand_aliasing={{0}: (5, {}), {1}: (6, {}), {2}: (7, {})} | custom-call | tf_op jit(solution)/shard_map/summed/pallas_call | solution.py:252
  (99 shorter events, 1.7 us)
Async XLA Ops:
  0.6 11.8 %copy-start = (bf16[2,512,512]{2,1,0:T(8,128)(2,1)S(1)}, bf16[2,512,512]{2,1,0:T(8,128)(2,1)}, u32[]{:S(2)}) copy-start(bf16[2,512,512]{2,1,0:T(8,128)(2,1)} %param.12) | copy-start | bytes 3145732
  0.6 2.1 %copy-start.2 = (bf16[2,512,512]{2,1,0:T(8,128)(2,1)S(1)}, bf16[2,512,512]{2,1,0:T(8,128)(2,1)}, u32[]{:S(2)}) copy-start(bf16[2,512,512]{2,1,0:T(8,128)(2,1)} %refs_0_.3) | copy-start | bytes 3145732
  0.7 3.0 %copy-start.3 = (bf16[2,512,512]{2,1,0:T(8,128)(2,1)S(1)}, bf16[2,512,512]{2,1,0:T(8,128)(2,1)}, u32[]{:S(2)}) copy-start(bf16[2,512,512]{2,1,0:T(8,128)(2,1)} %refs_1_.3) | copy-start | bytes 3145732
  4.5 8.0 %copy-start.7 = (bf16[512,96]{0,1:T(8,128)(2,1)S(1)}, bf16[512,96]{0,1:T(8,128)(2,1)}, u32[]{:S(2)}) copy-start(bf16[512,96]{0,1:T(8,128)(2,1)} %param.13) | copy-start | bytes 294916
  4.5 8.0 %copy-start.17 = (f32[96,512]{1,0:T(8,128)S(1)}, f32[96,512]{1,0:T(8,128)}, u32[]{:S(2)}) copy-start(f32[96,512]{1,0:T(8,128)} %param.14) | copy-start | bytes 589828
  5.4 26.4 %collective-permute-start.1 = (bf16[3,512,256]{2,1,0:T(8,128)(2,1)}, bf16[3,512,256]{2,1,0:T(8,128)(2,1)}, u32[]{:S(2)}, u32[]{:S(2)}) collective-permute-start(bf16[3,512,256]{2,1,0:T(8,128)(2,1)} %pad_maximum_fusion.2), channel_id=1, source_target_pairs={{0,4},{4,8},{8,12},{12,0},{1,5},{5,9},{9,13},{13,1},{2,6},{6,10},{... | collective-permute-start | bytes 2359304 | tf_op jit(solution)/shard_map/ppermute | solution.py:65
  6.9 24.9 %collective-permute-start = (bf16[3,512,256]{2,1,0:T(8,128)(2,1)}, bf16[3,512,256]{2,1,0:T(8,128)(2,1)}, u32[]{:S(2)}, u32[]{:S(2)}) collective-permute-start(bf16[3,512,256]{2,1,0:T(8,128)(2,1)} %pad_maximum_fusion.2), channel_id=1, source_target_pairs={{0,12},{4,0},{8,4},{12,8},{1,13},{5,1},{9,5},{13,9},{2,14},{6,2},{... | collective-permute-start | bytes 2359304 | tf_op jit(solution)/shard_map/ppermute | solution.py:65
  8.4 23.4 %collective-permute-start.3 = (bf16[3,512,256]{2,1,0:T(8,128)(2,1)}, bf16[3,512,256]{2,1,0:T(8,128)(2,1)}, u32[]{:S(2)}, u32[]{:S(2)}) collective-permute-start(bf16[3,512,256]{2,1,0:T(8,128)(2,1)} %pad_maximum_fusion.3), channel_id=1, source_target_pairs={{0,1},{1,2},{2,3},{3,0},{4,5},{5,6},{6,7},{7,4},{8,9},{9,10},{10,1... | collective-permute-start | bytes 2359304 | tf_op jit(solution)/shard_map/ppermute | solution.py:65
  10.3 21.5 %collective-permute-start.2 = (bf16[3,512,256]{2,1,0:T(8,128)(2,1)}, bf16[3,512,256]{2,1,0:T(8,128)(2,1)}, u32[]{:S(2)}, u32[]{:S(2)}) collective-permute-start(bf16[3,512,256]{2,1,0:T(8,128)(2,1)} %pad_maximum_fusion.3), channel_id=1, source_target_pairs={{0,3},{1,0},{2,1},{3,2},{4,7},{5,4},{6,5},{7,6},{8,11},{9,8},{10,9... | collective-permute-start | bytes 2359304 | tf_op jit(solution)/shard_map/ppermute | solution.py:65
  12.9 7.8 %copy-start.19 = (s32[16,16]{1,0:T(8,128)S(1)}, s32[16,16]{1,0:T(8,128)}, u32[]{:S(2)}) copy-start(s32[16,16]{1,0:T(8,128)} %param.23) | copy-start | bytes 3076
  12.9 7.8 %copy-start.20 = (s32[16,16]{1,0:T(8,128)S(1)}, s32[16,16]{1,0:T(8,128)}, u32[]{:S(2)}) copy-start(s32[16,16]{1,0:T(8,128)} %param.22) | copy-start | bytes 3076
  13.0 9.7 %copy-start.4 = (bf16[1,512,256]{2,1,0:T(8,128)(2,1)S(1)}, bf16[1,512,256]{2,1,0:T(8,128)(2,1)}, u32[]{:S(2)}) copy-start(bf16[1,512,256]{2,1,0:T(8,128)(2,1)} %get-tuple-element.98) | copy-start | bytes 786436
  13.0 9.7 %copy-start.5 = (bf16[1,512,256]{2,1,0:T(8,128)(2,1)S(1)}, bf16[1,512,256]{2,1,0:T(8,128)(2,1)}, u32[]{:S(2)}) copy-start(bf16[1,512,256]{2,1,0:T(8,128)(2,1)} %get-tuple-element.89) | copy-start | bytes 786436
  13.0 9.7 %copy-start.6 = (bf16[1,512,256]{2,1,0:T(8,128)(2,1)S(1)}, bf16[1,512,256]{2,1,0:T(8,128)(2,1)}, u32[]{:S(2)}) copy-start(bf16[1,512,256]{2,1,0:T(8,128)(2,1)} %get-tuple-element.90) | copy-start | bytes 786436
  14.2 13.4 %all-to-all-start = ((f32[8,96,128]{2,1,0:T(8,128)}), f32[8,96,128]{2,1,0:T(8,128)S(1)}, u32[]{:S(2)}, u32[]{:S(2)}) async-start(f32[8,96,128]{2,1,0:T(8,128)} %copy.36), calls=%async_computation | async-start | bytes 786432 | tf_op jit(solution)/shard_map/all_to_all | solution.py:309
  18.7 0.6 copy-start.26
  18.8 14.6 %copy-start.21 = (pred[4,4]{1,0:T(4,128)(4,1)}, pred[4,4]{1,0:T(4,128)(4,1)S(1)}, u32[]{:S(2)}) copy-start(pred[4,4]{1,0:T(4,128)(4,1)S(1)} %iota_compare_fusion.2) | copy-start | bytes 52
  22.7 31.2 %copy-start.25 = (s32[1,512]{1,0:T(1,128)S(1)}, s32[1,512]{1,0:T(1,128)}, u32[]{:S(2)}) copy-start(s32[1,512]{1,0:T(1,128)} %param.17) | copy-start | bytes 6148
  27.6 0.8 copy-start.1
  31.8 19.4 %collective-permute-start.4 = (bf16[3,512,256]{2,1,0:T(8,128)(2,1)}, bf16[3,512,256]{2,1,0:T(8,128)(2,1)S(1)}, u32[]{:S(2)}, u32[]{:S(2)}) collective-permute-start(bf16[3,512,256]{2,1,0:T(8,128)(2,1)} %get-tuple-element.55), channel_id=1, source_target_pairs={{0,4},{4,8},{8,12},{12,0},{1,5},{5,9},{9,13},{13,1},{2,6},{6,10},{... | collective-permute-start | bytes 2359304 | tf_op jit(solution)/shard_map/ppermute | solution.py:65
  33.4 20.3 %collective-permute-start.5 = (bf16[3,512,256]{2,1,0:T(8,128)(2,1)}, bf16[3,512,256]{2,1,0:T(8,128)(2,1)}, u32[]{:S(2)}, u32[]{:S(2)}) collective-permute-start(bf16[3,512,256]{2,1,0:T(8,128)(2,1)} %get-tuple-element.57), channel_id=1, source_target_pairs={{0,1},{1,2},{2,3},{3,0},{4,5},{5,6},{6,7},{7,4},{8,9},{9,10},{10,1... | collective-permute-start | bytes 2359304 | tf_op jit(solution)/shard_map/ppermute | solution.py:65
  33.6 10.5 %all-to-all-start.1 = ((bf16[8,96,128]{2,1,0:T(8,128)(2,1)}), bf16[8,96,128]{2,1,0:T(8,128)(2,1)S(1)}, u32[]{:S(2)}, u32[]{:S(2)}) async-start(bf16[8,96,128]{2,1,0:T(8,128)(2,1)} %score_gradient.1), calls=%async_computation.1 | async-start | bytes 393216 | tf_op jit(solution)/shard_map/all_to_all | solution.py:320
  38.0 22.9 %collective-permute-start.16 = (bf16[3,512,256]{2,1,0:T(8,128)(2,1)}, bf16[3,512,256]{2,1,0:T(8,128)(2,1)}, u32[]{:S(2)}, u32[]{:S(2)}) collective-permute-start(bf16[3,512,256]{2,1,0:T(8,128)(2,1)} %collective-permute-done.refs_5_), channel_id=1, source_target_pairs={{0,12},{4,0},{8,4},{12,8},{1,13},{5,1},{9,5},{13,9},{2,14},{6,2},{... | collective-permute-start | bytes 2359304 | tf_op jit(solution)/shard_map/ppermute | solution.py:65
  38.6 23.5 %collective-permute-start.17 = (bf16[3,512,256]{2,1,0:T(8,128)(2,1)}, bf16[3,512,256]{2,1,0:T(8,128)(2,1)}, u32[]{:S(2)}, u32[]{:S(2)}) collective-permute-start(bf16[3,512,256]{2,1,0:T(8,128)(2,1)} %collective-permute-done.2.refs_8_), channel_id=1, source_target_pairs={{0,3},{1,0},{2,1},{3,2},{4,7},{5,4},{6,5},{7,6},{8,11},{9,8},{10,9... | collective-permute-start | bytes 2359304 | tf_op jit(solution)/shard_map/ppermute | solution.py:65
  51.2 0.9 copy-start.23
  54.9 1.8 copy-start.18
  54.9 2.0 %copy-start.22 = (pred[4,4]{1,0:T(4,128)(4,1)S(1)}, pred[4,4]{1,0:T(4,128)(4,1)}, u32[]{:S(2)}) copy-start(pred[4,4]{1,0:T(4,128)(4,1)} %copy-done.21) | copy-start | bytes 52
  54.9 11.0 %copy-start.27 = (s32[4]{0:T(128)S(1)}, s32[4]{0:T(128)}, u32[]{:S(2)}) copy-start(s32[4]{0:T(128)} %copy-done.26) | copy-start | bytes 52
  54.9 11.9 %copy-start.15 = (bf16[3,512,256]{2,1,0:T(8,128)(2,1)S(1)}, bf16[3,512,256]{2,1,0:T(8,128)(2,1)}, u32[]{:S(2)}) copy-start(bf16[3,512,256]{2,1,0:T(8,128)(2,1)} %get-tuple-element.55) | copy-start | bytes 2359300
  54.9 14.4 %copy-start.14 = (bf16[3,512,256]{2,1,0:T(8,128)(2,1)S(1)}, bf16[3,512,256]{2,1,0:T(8,128)(2,1)}, u32[]{:S(2)}) copy-start(bf16[3,512,256]{2,1,0:T(8,128)(2,1)} %get-tuple-element.57) | copy-start | bytes 2359300
  56.8 15.6 %copy-start.16 = (bf16[2,128,512]{2,1,0:T(8,128)(2,1)}, bf16[2,128,512]{2,1,0:T(8,128)(2,1)S(1)}, u32[]{:S(2)}) copy-start(bf16[2,128,512]{2,1,0:T(8,128)(2,1)S(1)} %fusion.12.refs_3_) | copy-start | bytes 786436
  56.8 8.7 %collective-permute-start.15 = (bf16[128,512]{1,0:T(8,128)(2,1)S(1)}, bf16[128,512]{1,0:T(8,128)(2,1)S(1)}, u32[]{:S(2)}, u32[]{:S(2)}) collective-permute-start(bf16[128,512]{1,0:T(8,128)(2,1)S(1)} %get-tuple-element.99), channel_id=1, source_target_pairs={{0,1},{1,2},{2,3},{3,0},{4,5},{5,6},{6,7},{7,4},{8,9},{9,10},{10,1... | collective-permute-start | bytes 393224 | tf_op jit(solution)/shard_map/ppermute | solution.py:65
  57.5 9.3 %collective-permute-start.14 = (bf16[128,512]{1,0:T(8,128)(2,1)S(1)}, bf16[128,512]{1,0:T(8,128)(2,1)}, u32[]{:S(2)}, u32[]{:S(2)}) collective-permute-start(bf16[128,512]{1,0:T(8,128)(2,1)S(1)} %get-tuple-element.99), channel_id=1, source_target_pairs={{0,2},{1,3},{2,0},{3,1},{4,6},{5,7},{6,4},{7,5},{8,10},{9,11},{10,... | collective-permute-start | bytes 393224 | tf_op jit(solution)/shard_map/ppermute | solution.py:65
  59.9 9.5 %collective-permute-start.13 = (bf16[128,512]{1,0:T(8,128)(2,1)S(1)}, bf16[128,512]{1,0:T(8,128)(2,1)}, u32[]{:S(2)}, u32[]{:S(2)}) collective-permute-start(bf16[128,512]{1,0:T(8,128)(2,1)S(1)} %get-tuple-element.99), channel_id=1, source_target_pairs={{0,3},{1,0},{2,1},{3,2},{4,7},{5,4},{6,5},{7,6},{8,11},{9,8},{10,9... | collective-permute-start | bytes 393224 | tf_op jit(solution)/shard_map/ppermute | solution.py:65
  60.9 8.4 %collective-permute-start.12 = (bf16[128,512]{1,0:T(8,128)(2,1)S(1)}, bf16[128,512]{1,0:T(8,128)(2,1)}, u32[]{:S(2)}, u32[]{:S(2)}) collective-permute-start(bf16[128,512]{1,0:T(8,128)(2,1)S(1)} %get-tuple-element.100), channel_id=1, source_target_pairs={{0,4},{4,8},{8,12},{12,0},{1,5},{5,9},{9,13},{13,1},{2,6},{6,10},{... | collective-permute-start | bytes 393224 | tf_op jit(solution)/shard_map/ppermute | solution.py:65
  62.1 9.0 %collective-permute-start.11 = (bf16[128,512]{1,0:T(8,128)(2,1)S(1)}, bf16[128,512]{1,0:T(8,128)(2,1)}, u32[]{:S(2)}, u32[]{:S(2)}) collective-permute-start(bf16[128,512]{1,0:T(8,128)(2,1)S(1)} %get-tuple-element.100), channel_id=1, source_target_pairs={{0,8},{4,12},{8,0},{12,4},{1,9},{5,13},{9,1},{13,5},{2,10},{6,14},... | collective-permute-start | bytes 393224 | tf_op jit(solution)/shard_map/ppermute | solution.py:65
  65.5 6.9 %copy-start.24 = (bf16[128,512]{1,0:T(8,128)(2,1)}, bf16[128,512]{1,0:T(8,128)(2,1)S(1)}, u32[]{:S(2)}) copy-start(bf16[128,512]{1,0:T(8,128)(2,1)S(1)} %collective-permute-done.15.refs_16_) | copy-start | bytes 393220
  65.5 6.9 %collective-permute-start.10 = (bf16[128,512]{1,0:T(8,128)(2,1)S(1)}, bf16[128,512]{1,0:T(8,128)(2,1)}, u32[]{:S(2)}, u32[]{:S(2)}) collective-permute-start(bf16[128,512]{1,0:T(8,128)(2,1)S(1)} %get-tuple-element.100), channel_id=1, source_target_pairs={{0,12},{4,0},{8,4},{12,8},{1,13},{5,1},{9,5},{13,9},{2,14},{6,2},{... | collective-permute-start | bytes 393224 | tf_op jit(solution)/shard_map/ppermute | solution.py:65
  66.8 42.3 %collective-permute-start.6 = (bf16[3,512,256]{2,1,0:T(8,128)(2,1)S(1)}, bf16[3,512,256]{2,1,0:T(8,128)(2,1)}, u32[]{:S(2)}, u32[]{:S(2)}) collective-permute-start(bf16[3,512,256]{2,1,0:T(8,128)(2,1)S(1)} %copy-done.15), channel_id=1, source_target_pairs={{0,12},{4,0},{8,4},{12,8},{1,13},{5,1},{9,5},{13,9},{2,14},{6,2},{... | collective-permute-start | bytes 2359304 | tf_op jit(solution)/shard_map/ppermute | solution.py:65
  69.3 42.0 %collective-permute-start.8 = (bf16[3,512,256]{2,1,0:T(8,128)(2,1)S(1)}, bf16[3,512,256]{2,1,0:T(8,128)(2,1)}, u32[]{:S(2)}, u32[]{:S(2)}) collective-permute-start(bf16[3,512,256]{2,1,0:T(8,128)(2,1)S(1)} %copy-done.14), channel_id=1, source_target_pairs={{0,3},{1,0},{2,1},{3,2},{4,7},{5,4},{6,5},{7,6},{8,11},{9,8},{10,9... | collective-permute-start | bytes 2359304 | tf_op jit(solution)/shard_map/ppermute | solution.py:65
  69.3 44.0 %collective-permute-start.7 = (bf16[3,512,256]{2,1,0:T(8,128)(2,1)}, bf16[3,512,256]{2,1,0:T(8,128)(2,1)}, u32[]{:S(2)}, u32[]{:S(2)}) collective-permute-start(bf16[3,512,256]{2,1,0:T(8,128)(2,1)} %copy-done.23), channel_id=1, source_target_pairs={{0,4},{4,8},{8,12},{12,0},{1,5},{5,9},{9,13},{13,1},{2,6},{6,10},{... | collective-permute-start | bytes 2359304 | tf_op jit(solution)/shard_map/ppermute | solution.py:65
  71.1 42.3 %collective-permute-start.9 = (bf16[3,512,256]{2,1,0:T(8,128)(2,1)}, bf16[3,512,256]{2,1,0:T(8,128)(2,1)}, u32[]{:S(2)}, u32[]{:S(2)}) collective-permute-start(bf16[3,512,256]{2,1,0:T(8,128)(2,1)} %collective-permute-done.5.refs_10_), channel_id=1, source_target_pairs={{0,1},{1,2},{2,3},{3,0},{4,5},{5,6},{6,7},{7,4},{8,9},{9,10},{10,1... | collective-permute-start | bytes 2359304 | tf_op jit(solution)/shard_map/ppermute | solution.py:65
  101.0 41.6 %all-to-all-start.2 = ((bf16[4,3,512,256]{3,2,1,0:T(8,128)(2,1)}), bf16[4,3,512,256]{3,2,1,0:T(8,128)(2,1)}, u32[]{:S(2)}, u32[]{:S(2)}) async-start(bf16[4,3,512,256]{3,2,1,0:T(8,128)(2,1)} %get-tuple-element.67), calls=%async_computation.2 | async-start | bytes 6291456 | tf_op jit(solution)/shard_map/all_to_all | solution.py:405
  108.1 34.0 %collective-permute-start.18 = (bf16[3,512,256]{2,1,0:T(8,128)(2,1)}, bf16[3,512,256]{2,1,0:T(8,128)(2,1)S(1)}, u32[]{:S(2)}, u32[]{:S(2)}) collective-permute-start(bf16[3,512,256]{2,1,0:T(8,128)(2,1)} %get-tuple-element.68), channel_id=1, source_target_pairs={{0,1},{1,2},{2,3},{3,0},{4,5},{5,6},{6,7},{7,4},{8,9},{9,10},{10,1... | collective-permute-start | bytes 2359304 | tf_op jit(solution)/shard_map/ppermute | solution.py:69
  109.1 33.4 %collective-permute-start.19 = (bf16[3,512,256]{2,1,0:T(8,128)(2,1)}, bf16[3,512,256]{2,1,0:T(8,128)(2,1)S(1)}, u32[]{:S(2)}, u32[]{:S(2)}) collective-permute-start(bf16[3,512,256]{2,1,0:T(8,128)(2,1)} %get-tuple-element.69), channel_id=1, source_target_pairs={{0,2},{1,3},{2,0},{3,1},{4,6},{5,7},{6,4},{7,5},{8,10},{9,11},{10,... | collective-permute-start | bytes 2359304 | tf_op jit(solution)/shard_map/ppermute | solution.py:69
  111.3 31.2 %collective-permute-start.20 = (bf16[3,512,256]{2,1,0:T(8,128)(2,1)}, bf16[3,512,256]{2,1,0:T(8,128)(2,1)S(1)}, u32[]{:S(2)}, u32[]{:S(2)}) collective-permute-start(bf16[3,512,256]{2,1,0:T(8,128)(2,1)} %get-tuple-element.70), channel_id=1, source_target_pairs={{0,3},{1,0},{2,1},{3,2},{4,7},{5,4},{6,5},{7,6},{8,11},{9,8},{10,9... | collective-permute-start | bytes 2359304 | tf_op jit(solution)/shard_map/ppermute | solution.py:69
  142.1 0.9 copy-start.8
  142.6 0.9 copy-start.9
  142.6 1.2 copy-start.10
  143.7 42.6 %all-to-all-start.3 = ((bf16[4,3,512,256]{3,2,1,0:T(8,128)(2,1)}), bf16[4,3,512,256]{3,2,1,0:T(8,128)(2,1)}, u32[]{:S(2)}, u32[]{:S(2)}) async-start(bf16[4,3,512,256]{3,2,1,0:T(8,128)(2,1)} %get-tuple-element.71), calls=%async_computation.3 | async-start | bytes 6291456 | tf_op jit(solution)/shard_map/all_to_all | solution.py:405
  148.7 19.7 %collective-permute-start.21 = (bf16[3,512,256]{2,1,0:T(8,128)(2,1)}, bf16[3,512,256]{2,1,0:T(8,128)(2,1)S(1)}, u32[]{:S(2)}, u32[]{:S(2)}) collective-permute-start(bf16[3,512,256]{2,1,0:T(8,128)(2,1)} %get-tuple-element.73), channel_id=1, source_target_pairs={{0,1},{1,2},{2,3},{3,0},{4,5},{5,6},{6,7},{7,4},{8,9},{9,10},{10,1... | collective-permute-start | bytes 2359304 | tf_op jit(solution)/shard_map/ppermute | solution.py:69
  149.6 36.8 %collective-permute-start.22 = (bf16[3,512,256]{2,1,0:T(8,128)(2,1)}, bf16[3,512,256]{2,1,0:T(8,128)(2,1)S(1)}, u32[]{:S(2)}, u32[]{:S(2)}) collective-permute-start(bf16[3,512,256]{2,1,0:T(8,128)(2,1)} %get-tuple-element.74), channel_id=1, source_target_pairs={{0,2},{1,3},{2,0},{3,1},{4,6},{5,7},{6,4},{7,5},{8,10},{9,11},{10,... | collective-permute-start | bytes 2359304 | tf_op jit(solution)/shard_map/ppermute | solution.py:69
  152.1 34.2 %collective-permute-start.23 = (bf16[3,512,256]{2,1,0:T(8,128)(2,1)}, bf16[3,512,256]{2,1,0:T(8,128)(2,1)S(1)}, u32[]{:S(2)}, u32[]{:S(2)}) collective-permute-start(bf16[3,512,256]{2,1,0:T(8,128)(2,1)} %get-tuple-element.75), channel_id=1, source_target_pairs={{0,3},{1,0},{2,1},{3,2},{4,7},{5,4},{6,5},{7,6},{8,11},{9,8},{10,9... | collective-permute-start | bytes 2359304 | tf_op jit(solution)/shard_map/ppermute | solution.py:69
  168.4 18.0 %copy-start.11 = (bf16[3,512,256]{2,1,0:T(8,128)(2,1)}, bf16[3,512,256]{2,1,0:T(8,128)(2,1)S(1)}, u32[]{:S(2)}) copy-start(bf16[3,512,256]{2,1,0:T(8,128)(2,1)S(1)} %collective-permute-done.21.refs_0_) | copy-start | bytes 2359300
  186.4 0.9 copy-start.12
  186.4 1.2 copy-start.13

commit v8 on v7

--- a/solution.py
+++ b/solution.py
@@ -126,10 +126,10 @@
     scratch = refs[22:]
     kv_rows, q_rows, g_rows, lse_rows, delta_rows, dq_rows, dk_acc, dv_acc = scratch
     sides = ((fetch_x, late_x), (fetch_z, late_z))
-    channels = decoder.shape[1]
+    channels = decoder.shape[0]
     head = pl.program_id(0) * 2 + base
     score_scale = 64 ** (-0.5)
-    tn = (((0,), (1,)), ((), ()))
+    tn = (((0,), (0,)), ((), ()))
 
     def load(m):
         key_fetch = sides[m][0]
@@ -178,7 +178,7 @@
 
 def attention_tiles(half, tables, key_rows, value_rows, query, fetched_x, fetched_z, late_own, late_x, late_z, decoder_matrix):
     members, rows, width = key_rows.shape
-    stats, channels = late_own.shape[1], decoder_matrix.shape[1]
+    stats, channels = late_own.shape[1], decoder_matrix.shape[0]
     pairs = width // 256
     base = half * pairs
     own_spec = pl.BlockSpec((members, rows, 128), lambda h, tab: (0, 0, base + h))
@@ -197,7 +197,7 @@
             in_specs=[own_spec] * 3
             + [
                 pl.BlockSpec((members, stats, rows), lambda h, tab: (0, 0, 0)),
-                pl.BlockSpec((128, channels), lambda h, tab: (base + h, 0)),
+                pl.BlockSpec((channels, 128), lambda h, tab: (0, base + h)),
             ]
             + [far_spec] * 6
             + [late_spec] * 6,
@@ -263,12 +263,25 @@
     )(*in_hbm(got_x, own_z, *got_z), *kept)
 
 
+def pack_kernel(key_rows, value_rows, query, along_x, along_z):
+    for m, out in enumerate((along_x, along_z)):
+        out[0] = key_rows[m]
+        out[1] = value_rows[m]
+        out[2] = query[1 - m]
+
+
 def outgoing(half, key_rows, value_rows, query):
-    lanes = query.shape[-1] // 2
-    part = slice(half * lanes, (half + 1) * lanes)
-    return [
-        jnp.stack([key_rows[m, :, part], value_rows[m, :, part], query[1 - m, :, part]]) for m in range(2)
-    ]
+    members, rows, width = query.shape
+    lanes = width // 2
+    block = pl.BlockSpec((members, rows // 4, lanes), lambda r: (0, r, half))
+    return pl.pallas_call(
+        pack_kernel,
+        out_shape=[pltpu.HBM((3, rows, lanes), BF16)] * 2,
+        grid=(4,),
+        in_specs=[block] * 3,
+        out_specs=[pl.BlockSpec((3, rows // 4, lanes), lambda r: (0, r, 0))] * 2,
+        name="outgoing",
+    )(*in_hbm(key_rows, value_rows, query))
 
 
 def in_hbm(*arrays):
@@ -315,12 +328,11 @@
         everyone, jnp.tile(observed, (1, members)), jnp.tile(area[None], (1, members))
     )
     derivative, own_1, near, decoder_rows = lax.optimization_barrier(
-        (derivative, own_1, near, in_hbm(decoder_matrix)[0])
+        (derivative, own_1, near, decoder_matrix.T)
     )
     returned = lax.all_to_all(derivative, MEMBER, 0, 0, tiled=True)
     far = [fetched(near[0], "x", 1), fetched(near[2], "z", 1)]
     before = [fetched(a, axis, 3) for a, axis in zip(own_1, ("x", "z"))]
-    returned, own_1, before = lax.optimization_barrier((returned, own_1, before))
     grad_forecast = (
         returned.reshape(groups, channels, members, span)
         .transpose(2, 1, 0, 3)
@@ -371,6 +383,7 @@
         [grad_columns] + [part[n] for n in range(2) for part in (two_parts(row_lse), two_parts(delta))],
         axis=1,
     )
+    late_own, own_1, before, far = lax.optimization_barrier((late_own, own_1, before, far))
     late_z = [fetched(late_own[0], "z", d) for d in (1, 2, 3)]
     late_x = [fetched(late_own[1], "x", d) for d in (1, 2, 3)]
     late_own, own_1, before = lax.optimization_barrier((late_own, own_1, before))

time: 193 us -> 194 us (level)
  Pallas kernels: 69.7 us -> 77 us
  local copies, waits for them, and re-layouts: 13.9 us -> 8.78 us
  other arithmetic: 6.22 us -> 2.03 us
  waiting for transfers between devices: 44.1 us -> 46.3 us
    pallas_call x0 -> x2, Pallas kernels: none -> 7.36 us  [outgoing(): pl.pallas_call(pack_kernel, out_shape=[pltpu.HBM((3, rows, lanes), BF16)]...]
    ppermute x18, waiting for transfers between devices: 9.49 us -> 15.2 us  [fetched(): lax.ppermute(x, axis, [(i, (i - distance) % SIDE) for i in range(SIDE)])]
    another operation x3 -> x0, other arithmetic: 4.2 us -> none  [outgoing(): jnp.stack([key_rows[m, :, part], value_rows[m, :, part], query[1 - m, :,...]
    slice x3 -> x0, local copies, waits for them, and re-layouts: 3.78 us -> none  [the longest x1 2.11 us: outgoing(): query[1 - m, :, part]]
    ppermute x18, starting transfers between devices: 24.4 us -> 27.2 us  [fetched(): lax.ppermute(x, axis, [(i, (i - distance) % SIDE) for i in range(SIDE)])]
    unnamed x56 -> x46, local copies, waits for them, and re-layouts: 4.55 us -> 4.02 us
  transfers between devices with their start and end apart: 28 -> 28, of which waited for: 8 -> 8; matrix products, arithmetic and copies ran while one was open for 7% -> 5% of each run, Pallas kernels for 34% -> 36%
where the time goes in v8:
time: 194 us; the launch traced here: 193 us
  Pallas kernels  77 us (40%)
  starting transfers between devices  55.9 us (29%)
  waiting for transfers between devices  46.3 us (24%)
  local copies, waits for them, and re-layouts  8.78 us (5%)
  matrix products  2.36 us (1%)
  other arithmetic  2.03 us (1%)
    pallas_call x2, Pallas kernels, attention_tiles(): pl.pallas_call(functools.partial(tile_kernel, base=2 * base), out_shape=[...  57.3 us
    ppermute x6, waiting for transfers between devices, delivered(): lax.ppermute(x, axis, [(i, (i + distance) % SIDE) for i in range(SIDE)])  28.9 us
    ppermute x18, starting transfers between devices, fetched(): lax.ppermute(x, axis, [(i, (i - distance) % SIDE) for i in range(SIDE)])  27.2 us
    ppermute x18, waiting for transfers between devices, fetched(): lax.ppermute(x, axis, [(i, (i - distance) % SIDE) for i in range(SIDE)])  15.2 us
    all_to_all x2, starting transfers between devices, shards(): got_x = lax.all_to_all(send_x, 'x', 0, 0, tiled=True)  12 us
    pallas_call x2, Pallas kernels, summed(): pl.pallas_call(sum_kernel, out_shape=[shape] * 3, grid=(2,), in_specs=[pl...  8.93 us
    ppermute x6, starting transfers between devices, delivered(): lax.ppermute(x, axis, [(i, (i + distance) % SIDE) for i in range(SIDE)])  8.75 us
    pallas_call x2, Pallas kernels, outgoing(): pl.pallas_call(pack_kernel, out_shape=[pltpu.HBM((3, rows, lanes), BF16)]...  7.36 us
  transfers between devices with their start and end apart: 28, of which 8 were waited for; matrix products, arithmetic and copies ran while one was open for 5% of the time, Pallas kernels for 36%

profile of v8, /device:TPU:2, one launch (start us, length us, event | category | flops | bytes accessed | tf_op | source)
XLA Modules:
  0.0 193.4 jit_solution(9296879324247630978)
XLA Ops:
  0.7 3.7 %outgoing.3 = (bf16[3,512,256]{2,1,0:T(8,128)(2,1)}, bf16[3,512,256]{2,1,0:T(8,128)(2,1)}) custom-call(bf16[2,512,512]{2,1,0:T(8,128)(2,1)} %refs_0_.3, bf16[2,512,512]{2,1,0:T(8,128)(2,1)} %refs_1_.3, bf16[2,512,512]{2,1,0:T(8,128)(2,1)} %refs_2_.3), custom_call_target="tpu_custom_call" | custom-call | tf_op jit(solution)/shard_map/outgoing/pallas_call | solution.py:277
  4.4 1.5 collective-permute-start.1
  5.9 0.5 collective-permute-start
  6.4 1.9 collective-permute-start.3
  8.3 2.1 %collective-permute-start.2 = (bf16[3,512,256]{2,1,0:T(8,128)(2,1)}, bf16[3,512,256]{2,1,0:T(8,128)(2,1)}, u32[]{:S(2)}, u32[]{:S(2)}) collective-permute-start(bf16[3,512,256]{2,1,0:T(8,128)(2,1)} %get-tuple-element.54), channel_id=1, source_target_pairs={{0,3},{1,0},{2,1},{3,2},{4,7},{5,4},{6,5},{7,6},{8,11},{9,8},{10,9... | collective-permute-start | bytes 2359304 | tf_op jit(solution)/shard_map/ppermute | solution.py:65
  10.5 0.4 fusion
  10.9 0.2 copy.30
  11.2 0.9 copy.32
  12.1 4.6 %all-to-all-start = ((f32[8,96,128]{2,1,0:T(8,128)}), f32[8,96,128]{2,1,0:T(8,128)S(1)}, u32[]{:S(2)}, u32[]{:S(2)}) async-start(f32[8,96,128]{2,1,0:T(8,128)} %copy.32), calls=%async_computation | async-start | bytes 786432 | tf_op jit(solution)/shard_map/all_to_all | solution.py:322
  16.7 3.6 %outgoing.2 = (bf16[3,512,256]{2,1,0:T(8,128)(2,1)}, bf16[3,512,256]{2,1,0:T(8,128)(2,1)}) custom-call(bf16[2,512,512]{2,1,0:T(8,128)(2,1)} %refs_0_.3, bf16[2,512,512]{2,1,0:T(8,128)(2,1)} %refs_1_.3, bf16[2,512,512]{2,1,0:T(8,128)(2,1)} %refs_2_.3), custom_call_target="tpu_custom_call" | custom-call | tf_op jit(solution)/shard_map/outgoing/pallas_call | solution.py:277
  20.6 0.8 dynamic_slice.7
  21.3 0.7 tile.20.area_ref
  22.0 0.1 select_reduce_fusion.2
  22.1 0.1 reshape.206
  22.2 0.9 constant_dynamic-slice_fusion
  23.2 0.7 copy.34.truth_ref
  24.0 0.1 broadcast_and_fusion.1
  24.2 0.1 broadcast_and_fusion
  24.3 1.4 all-to-all-done.forecast_ref
  25.7 0.7 copy-done.1
  26.4 3.4 %score_gradient.1 = bf16[8,96,128]{2,1,0:T(8,128)(2,1)} custom-call(f32[8,96,128]{2,1,0:T(8,128)} %copy-done.1, f32[96,128]{1,0:T(8,128)} %copy.34.truth_ref, f32[1,128]{1,0:T(1,128)} %tile.20.area_ref), custom_call_target="tpu_custom_call" | custom-call | tf_op jit(solution)/shard_map/score_gradient/pallas_call | solution.py:49
  29.9 3.4 %all-to-all-start.1 = ((bf16[8,96,128]{2,1,0:T(8,128)(2,1)}), bf16[8,96,128]{2,1,0:T(8,128)(2,1)S(1)}, u32[]{:S(2)}, u32[]{:S(2)}) async-start(bf16[8,96,128]{2,1,0:T(8,128)(2,1)} %score_gradient.1), calls=%async_computation.1 | async-start | bytes 393216 | tf_op jit(solution)/shard_map/all_to_all | solution.py:333
  33.3 0.7 select_reduce_fusion.1
  34.0 1.6 collective-permute-start.4
  35.5 0.2 collective-permute-start.5
  35.8 0.5 collective-permute-start.6
  36.3 3.0 %collective-permute-start.7 = (bf16[3,512,256]{2,1,0:T(8,128)(2,1)}, bf16[3,512,256]{2,1,0:T(8,128)(2,1)}, u32[]{:S(2)}, u32[]{:S(2)}) collective-permute-start(bf16[3,512,256]{2,1,0:T(8,128)(2,1)} %collective-permute-done.2.refs_8_), channel_id=1, source_target_pairs={{0,3},{1,0},{2,1},{3,2},{4,7},{5,4},{6,5},{7,6},{8,11},{9,8},{10,9... | collective-permute-start | bytes 2359304 | tf_op jit(solution)/shard_map/ppermute | solution.py:65
  39.3 0.8 all-to-all-done.1
  40.1 0.2 copy.35
  40.3 0.5 constant_dynamic-update-slice_fusion
  40.8 0.5 convolution_convert_fusion.1
  41.3 1.0 bitcast_reduce_fusion
  42.4 11.9 %collective-permute-done.4.refs_7_ = bf16[3,512,256]{2,1,0:T(8,128)(2,1)} collective-permute-done((bf16[3,512,256]{2,1,0:T(8,128)(2,1)}, bf16[3,512,256]{2,1,0:T(8,128)(2,1)}, u32[]{:S(2)}, u32[]{:S(2)}) %collective-permute-start.4) | collective-permute-done | bytes 786464 | tf_op jit(solution)/shard_map/ppermute | solution.py:65
  54.3 2.4 %collective-permute-done.5.refs_10_ = bf16[3,512,256]{2,1,0:T(8,128)(2,1)} collective-permute-done((bf16[3,512,256]{2,1,0:T(8,128)(2,1)}, bf16[3,512,256]{2,1,0:T(8,128)(2,1)}, u32[]{:S(2)}, u32[]{:S(2)}) %collective-permute-start.5) | collective-permute-done | bytes 786464 | tf_op jit(solution)/shard_map/ppermute | solution.py:65
  56.8 0.8 collective-permute-start.17
  57.5 0.6 select_reduce_fusion
  58.2 4.1 %collective-permute-start.16 = (bf16[128,512]{1,0:T(8,128)(2,1)S(1)}, bf16[128,512]{1,0:T(8,128)(2,1)S(1)}, u32[]{:S(2)}, u32[]{:S(2)}) collective-permute-start(bf16[128,512]{1,0:T(8,128)(2,1)S(1)} %get-tuple-element.99), channel_id=1, source_target_pairs={{0,2},{1,3},{2,0},{3,1},{4,6},{5,7},{6,4},{7,5},{8,10},{9,11},{10,... | collective-permute-start | bytes 393224 | tf_op jit(solution)/shard_map/ppermute | solution.py:65
  62.3 0.2 collective-permute-start.15
  62.5 1.4 collective-permute-start.14
  63.9 3.5 %collective-permute-start.13 = (bf16[128,512]{1,0:T(8,128)(2,1)S(1)}, bf16[128,512]{1,0:T(8,128)(2,1)S(1)}, u32[]{:S(2)}, u32[]{:S(2)}) collective-permute-start(bf16[128,512]{1,0:T(8,128)(2,1)S(1)} %get-tuple-element.100), channel_id=1, source_target_pairs={{0,8},{4,12},{8,0},{12,4},{1,9},{5,13},{9,1},{13,5},{2,10},{6,14},... | collective-permute-start | bytes 393224 | tf_op jit(solution)/shard_map/ppermute | solution.py:65
  67.4 0.9 collective-permute-start.12
  68.5 0.9 collective-permute-start.8
  69.4 2.1 %collective-permute-start.10 = (bf16[3,512,256]{2,1,0:T(8,128)(2,1)S(1)}, bf16[3,512,256]{2,1,0:T(8,128)(2,1)}, u32[]{:S(2)}, u32[]{:S(2)}) collective-permute-start(bf16[3,512,256]{2,1,0:T(8,128)(2,1)S(1)} %copy-done.15), channel_id=1, source_target_pairs={{0,3},{1,0},{2,1},{3,2},{4,7},{5,4},{6,5},{7,6},{8,11},{9,8},{10,9... | collective-permute-start | bytes 2359304 | tf_op jit(solution)/shard_map/ppermute | solution.py:65
  71.5 0.1 collective-permute-done.13.refs_12_
  71.6 1.9 collective-permute-start.11
  73.5 0.7 collective-permute-done.12.refs_11_
  74.2 0.6 copy-done.21
  74.9 28.6 %attention_tiles.3 = (bf16[4,3,512,256]{3,2,1,0:T(8,128)(2,1)}, f32[3,512,256]{2,1,0:T(8,128)}, bf16[3,512,256]{2,1,0:T(8,128)(2,1)}, bf16[3,512,256]{2,1,0:T(8,128)(2,1)}, bf16[3,512,256]{2,1,0:T(8,128)(2,1)}) custom-call(s32[3,16]{1,0:T(4,128)S(1)} %pad_add_fusion.table, bf16[2,512,512]{2,1,0:T(8,128)(2,1)} %refs_0_.3, bf16[2,512,512]{2,1,0:T(8,128)(2,1)} %refs_1_.3, ...), custom_call_target="tpu_custom_call" | custom-call | flops 21474836480 | bytes 20971520 | tf_op jit(solution)/shard_map/attention_tiles/pallas_call | solution.py:187
  103.5 7.1 %all-to-all-start.2 = ((bf16[4,3,512,256]{3,2,1,0:T(8,128)(2,1)}), bf16[4,3,512,256]{3,2,1,0:T(8,128)(2,1)}, u32[]{:S(2)}, u32[]{:S(2)}) async-start(bf16[4,3,512,256]{3,2,1,0:T(8,128)(2,1)} %get-tuple-element.79), calls=%async_computation.2 | async-start | bytes 6291456 | tf_op jit(solution)/shard_map/all_to_all | solution.py:418
  110.6 1.8 collective-permute-start.18
  112.5 2.6 %collective-permute-start.20 = (bf16[3,512,256]{2,1,0:T(8,128)(2,1)}, bf16[3,512,256]{2,1,0:T(8,128)(2,1)S(1)}, u32[]{:S(2)}, u32[]{:S(2)}) collective-permute-start(bf16[3,512,256]{2,1,0:T(8,128)(2,1)} %get-tuple-element.82), channel_id=1, source_target_pairs={{0,3},{1,0},{2,1},{3,2},{4,7},{5,4},{6,5},{7,6},{8,11},{9,8},{10,9... | collective-permute-start | bytes 2359304 | tf_op jit(solution)/shard_map/ppermute | solution.py:69
  115.1 28.7 %attention_tiles.2 = (bf16[4,3,512,256]{3,2,1,0:T(8,128)(2,1)}, f32[3,512,256]{2,1,0:T(8,128)}, bf16[3,512,256]{2,1,0:T(8,128)(2,1)}, bf16[3,512,256]{2,1,0:T(8,128)(2,1)}, bf16[3,512,256]{2,1,0:T(8,128)(2,1)}) custom-call(s32[3,16]{1,0:T(4,128)S(1)} %pad_add_fusion.table, bf16[2,512,512]{2,1,0:T(8,128)(2,1)} %refs_0_.3, bf16[2,512,512]{2,1,0:T(8,128)(2,1)} %refs_1_.3, ...), custom_call_target="tpu_custom_call" | custom-call | flops 21474836480 | bytes 20971520 | tf_op jit(solution)/shard_map/attention_tiles/pallas_call | solution.py:187
  143.9 0.8 copy-done.2
  144.7 0.2 copy-done.3
  145.0 0.3 copy-done.4
  145.3 4.8 %all-to-all-start.3 = ((bf16[4,3,512,256]{3,2,1,0:T(8,128)(2,1)}), bf16[4,3,512,256]{3,2,1,0:T(8,128)(2,1)}, u32[]{:S(2)}, u32[]{:S(2)}) async-start(bf16[4,3,512,256]{3,2,1,0:T(8,128)(2,1)} %get-tuple-element.83), calls=%async_computation.3 | async-start | bytes 6291456 | tf_op jit(solution)/shard_map/all_to_all | solution.py:418
  150.1 3.4 %collective-permute-start.22 = (bf16[3,512,256]{2,1,0:T(8,128)(2,1)}, bf16[3,512,256]{2,1,0:T(8,128)(2,1)S(1)}, u32[]{:S(2)}, u32[]{:S(2)}) collective-permute-start(bf16[3,512,256]{2,1,0:T(8,128)(2,1)} %get-tuple-element.86), channel_id=1, source_target_pairs={{0,2},{1,3},{2,0},{3,1},{4,6},{5,7},{6,4},{7,5},{8,10},{9,11},{10,... | collective-permute-start | bytes 2359304 | tf_op jit(solution)/shard_map/ppermute | solution.py:69
  153.5 0.8 collective-permute-start.23
  154.4 4.5 %summed.2 = (f32[2,512,512]{2,1,0:T(8,128)}, f32[2,512,512]{2,1,0:T(8,128)}, f32[2,512,512]{2,1,0:T(8,128)}) custom-call(bf16[4,3,512,256]{3,2,1,0:T(8,128)(2,1)} %all-to-all-done.2.got_x, f32[3,512,256]{2,1,0:T(8,128)} %get-tuple-element.89.own_z, bf16[3,512,256]{2,1,0:T(8,128)(2,1)} %copy-done.2, bf16[3,512,256]{2,1,0:T(8,128)(2,1)} %copy-done.3, ...), custom_call_target="tpu_custom_call" | custom-call | tf_op jit(solution)/shard_map/summed/pallas_call | solution.py:252
  158.8 11.0 %collective-permute-done.21.refs_0_ = bf16[3,512,256]{2,1,0:T(8,128)(2,1)S(1)} collective-permute-done((bf16[3,512,256]{2,1,0:T(8,128)(2,1)}, bf16[3,512,256]{2,1,0:T(8,128)(2,1)S(1)}, u32[]{:S(2)}, u32[]{:S(2)}) %collective-permute-start.21) | collective-permute-done | bytes 786464 | tf_op jit(solution)/shard_map/ppermute | solution.py:69
  169.8 18.0 %collective-permute-done.22.refs_1_ = bf16[3,512,256]{2,1,0:T(8,128)(2,1)S(1)} collective-permute-done((bf16[3,512,256]{2,1,0:T(8,128)(2,1)}, bf16[3,512,256]{2,1,0:T(8,128)(2,1)S(1)}, u32[]{:S(2)}, u32[]{:S(2)}) %collective-permute-start.22) | collective-permute-done | bytes 786464 | tf_op jit(solution)/shard_map/ppermute | solution.py:69
  187.8 0.9 copy-done.6
  188.7 0.3 copy-done.7
  189.0 4.5 %summed.3 = (f32[2,512,512]{2,1,0:T(8,128)}, f32[2,512,512]{2,1,0:T(8,128)}, f32[2,512,512]{2,1,0:T(8,128)}) custom-call(bf16[4,3,512,256]{3,2,1,0:T(8,128)(2,1)} %all-to-all-done.3.got_x, f32[3,512,256]{2,1,0:T(8,128)} %get-tuple-element.84.own_z, bf16[3,512,256]{2,1,0:T(8,128)(2,1)} %copy-done.5, ...), custom_call_target="tpu_custom_call", output_to_operand_aliasing={{0}: (5, {}), {1}: (6, {}), {2}: (7, {})} | custom-call | tf_op jit(solution)/shard_map/summed/pallas_call | solution.py:252
  (84 shorter events, 1.0 us)
Async XLA Ops:
  0.6 9.8 %copy-start = (bf16[2,512,512]{2,1,0:T(8,128)(2,1)S(1)}, bf16[2,512,512]{2,1,0:T(8,128)(2,1)}, u32[]{:S(2)}) copy-start(bf16[2,512,512]{2,1,0:T(8,128)(2,1)} %param.12) | copy-start | bytes 3145732
  0.6 9.8 %copy-start.8 = (bf16[512,96]{0,1:T(8,128)(2,1)S(1)}, bf16[512,96]{0,1:T(8,128)(2,1)}, u32[]{:S(2)}) copy-start(bf16[512,96]{0,1:T(8,128)(2,1)} %param.13) | copy-start | bytes 294916
  0.7 9.8 %copy-start.10 = (f32[96,512]{1,0:T(8,128)S(1)}, f32[96,512]{1,0:T(8,128)}, u32[]{:S(2)}) copy-start(f32[96,512]{1,0:T(8,128)} %param.14) | copy-start | bytes 589828
  4.4 25.4 %collective-permute-start.1 = (bf16[3,512,256]{2,1,0:T(8,128)(2,1)}, bf16[3,512,256]{2,1,0:T(8,128)(2,1)S(1)}, u32[]{:S(2)}, u32[]{:S(2)}) collective-permute-start(bf16[3,512,256]{2,1,0:T(8,128)(2,1)} %get-tuple-element.53), channel_id=1, source_target_pairs={{0,4},{4,8},{8,12},{12,0},{1,5},{5,9},{9,13},{13,1},{2,6},{6,10},{... | collective-permute-start | bytes 2359304 | tf_op jit(solution)/shard_map/ppermute | solution.py:65
  5.9 23.9 %collective-permute-start = (bf16[3,512,256]{2,1,0:T(8,128)(2,1)}, bf16[3,512,256]{2,1,0:T(8,128)(2,1)}, u32[]{:S(2)}, u32[]{:S(2)}) collective-permute-start(bf16[3,512,256]{2,1,0:T(8,128)(2,1)} %get-tuple-element.53), channel_id=1, source_target_pairs={{0,12},{4,0},{8,4},{12,8},{1,13},{5,1},{9,5},{13,9},{2,14},{6,2},{... | collective-permute-start | bytes 2359304 | tf_op jit(solution)/shard_map/ppermute | solution.py:65
  6.4 23.4 %collective-permute-start.3 = (bf16[3,512,256]{2,1,0:T(8,128)(2,1)}, bf16[3,512,256]{2,1,0:T(8,128)(2,1)}, u32[]{:S(2)}, u32[]{:S(2)}) collective-permute-start(bf16[3,512,256]{2,1,0:T(8,128)(2,1)} %get-tuple-element.54), channel_id=1, source_target_pairs={{0,1},{1,2},{2,3},{3,0},{4,5},{5,6},{6,7},{7,4},{8,9},{9,10},{10,1... | collective-permute-start | bytes 2359304 | tf_op jit(solution)/shard_map/ppermute | solution.py:65
  8.3 21.5 %collective-permute-start.2 = (bf16[3,512,256]{2,1,0:T(8,128)(2,1)}, bf16[3,512,256]{2,1,0:T(8,128)(2,1)}, u32[]{:S(2)}, u32[]{:S(2)}) collective-permute-start(bf16[3,512,256]{2,1,0:T(8,128)(2,1)} %get-tuple-element.54), channel_id=1, source_target_pairs={{0,3},{1,0},{2,1},{3,2},{4,7},{5,4},{6,5},{7,6},{8,11},{9,8},{10,9... | collective-permute-start | bytes 2359304 | tf_op jit(solution)/shard_map/ppermute | solution.py:65
  12.1 9.9 %copy-start.12 = (s32[16,16]{1,0:T(8,128)S(1)}, s32[16,16]{1,0:T(8,128)}, u32[]{:S(2)}) copy-start(s32[16,16]{1,0:T(8,128)} %param.23) | copy-start | bytes 3076
  12.1 9.9 %copy-start.13 = (s32[16,16]{1,0:T(8,128)S(1)}, s32[16,16]{1,0:T(8,128)}, u32[]{:S(2)}) copy-start(s32[16,16]{1,0:T(8,128)} %param.22) | copy-start | bytes 3076
  12.1 13.5 %all-to-all-start = ((f32[8,96,128]{2,1,0:T(8,128)}), f32[8,96,128]{2,1,0:T(8,128)S(1)}, u32[]{:S(2)}, u32[]{:S(2)}) async-start(f32[8,96,128]{2,1,0:T(8,128)} %copy.32), calls=%async_computation | async-start | bytes 786432 | tf_op jit(solution)/shard_map/all_to_all | solution.py:322
  20.4 19.9 %copy-start.22 = (s32[1,512]{1,0:T(1,128)S(1)}, s32[1,512]{1,0:T(1,128)}, u32[]{:S(2)}) copy-start(s32[1,512]{1,0:T(1,128)} %param.17) | copy-start | bytes 6148
  25.7 0.8 copy-start.1
  29.8 12.5 %copy-start.14 = (bf16[3,512,256]{2,1,0:T(8,128)(2,1)}, bf16[3,512,256]{2,1,0:T(8,128)(2,1)S(1)}, u32[]{:S(2)}) copy-start(bf16[3,512,256]{2,1,0:T(8,128)(2,1)S(1)} %collective-permute-done.1.refs_7_) | copy-start | bytes 2359300
  29.9 10.2 %all-to-all-start.1 = ((bf16[8,96,128]{2,1,0:T(8,128)(2,1)}), bf16[8,96,128]{2,1,0:T(8,128)(2,1)S(1)}, u32[]{:S(2)}, u32[]{:S(2)}) async-start(bf16[8,96,128]{2,1,0:T(8,128)(2,1)} %score_gradient.1), calls=%async_computation.1 | async-start | bytes 393216 | tf_op jit(solution)/shard_map/all_to_all | solution.py:333
  34.0 20.3 %collective-permute-start.4 = (bf16[3,512,256]{2,1,0:T(8,128)(2,1)}, bf16[3,512,256]{2,1,0:T(8,128)(2,1)}, u32[]{:S(2)}, u32[]{:S(2)}) collective-permute-start(bf16[3,512,256]{2,1,0:T(8,128)(2,1)} %get-tuple-element.67), channel_id=1, source_target_pairs={{0,4},{4,8},{8,12},{12,0},{1,5},{5,9},{9,13},{13,1},{2,6},{6,10},{... | collective-permute-start | bytes 2359304 | tf_op jit(solution)/shard_map/ppermute | solution.py:65
  35.5 21.2 %collective-permute-start.5 = (bf16[3,512,256]{2,1,0:T(8,128)(2,1)}, bf16[3,512,256]{2,1,0:T(8,128)(2,1)}, u32[]{:S(2)}, u32[]{:S(2)}) collective-permute-start(bf16[3,512,256]{2,1,0:T(8,128)(2,1)} %get-tuple-element.69), channel_id=1, source_target_pairs={{0,1},{1,2},{2,3},{3,0},{4,5},{5,6},{6,7},{7,4},{8,9},{9,10},{10,1... | collective-permute-start | bytes 2359304 | tf_op jit(solution)/shard_map/ppermute | solution.py:65
  35.8 21.0 %collective-permute-start.6 = (bf16[3,512,256]{2,1,0:T(8,128)(2,1)}, bf16[3,512,256]{2,1,0:T(8,128)(2,1)}, u32[]{:S(2)}, u32[]{:S(2)}) collective-permute-start(bf16[3,512,256]{2,1,0:T(8,128)(2,1)} %collective-permute-done.refs_5_), channel_id=1, source_target_pairs={{0,12},{4,0},{8,4},{12,8},{1,13},{5,1},{9,5},{13,9},{2,14},{6,2},{... | collective-permute-start | bytes 2359304 | tf_op jit(solution)/shard_map/ppermute | solution.py:65
  36.3 20.4 %collective-permute-start.7 = (bf16[3,512,256]{2,1,0:T(8,128)(2,1)}, bf16[3,512,256]{2,1,0:T(8,128)(2,1)}, u32[]{:S(2)}, u32[]{:S(2)}) collective-permute-start(bf16[3,512,256]{2,1,0:T(8,128)(2,1)} %collective-permute-done.2.refs_8_), channel_id=1, source_target_pairs={{0,3},{1,0},{2,1},{3,2},{4,7},{5,4},{6,5},{7,6},{8,11},{9,8},{10,9... | collective-permute-start | bytes 2359304 | tf_op jit(solution)/shard_map/ppermute | solution.py:65
  41.3 1.0 copy-start.11
  41.3 28.1 %copy-start.15 = (bf16[3,512,256]{2,1,0:T(8,128)(2,1)S(1)}, bf16[3,512,256]{2,1,0:T(8,128)(2,1)}, u32[]{:S(2)}) copy-start(bf16[3,512,256]{2,1,0:T(8,128)(2,1)} %get-tuple-element.69) | copy-start | bytes 2359300
  42.4 31.8 %copy-start.9 = (bf16[2,128,512]{2,1,0:T(8,128)(2,1)}, bf16[2,128,512]{2,1,0:T(8,128)(2,1)S(1)}, u32[]{:S(2)}) copy-start(bf16[2,128,512]{2,1,0:T(8,128)(2,1)S(1)} %fusion.12.refs_3_) | copy-start | bytes 786436
  56.8 10.7 %collective-permute-start.17 = (bf16[128,512]{1,0:T(8,128)(2,1)S(1)}, bf16[128,512]{1,0:T(8,128)(2,1)S(1)}, u32[]{:S(2)}, u32[]{:S(2)}) collective-permute-start(bf16[128,512]{1,0:T(8,128)(2,1)S(1)} %get-tuple-element.99), channel_id=1, source_target_pairs={{0,1},{1,2},{2,3},{3,0},{4,5},{5,6},{6,7},{7,4},{8,9},{9,10},{10,1... | collective-permute-start | bytes 393224 | tf_op jit(solution)/shard_map/ppermute | solution.py:65
  58.2 10.4 %collective-permute-start.16 = (bf16[128,512]{1,0:T(8,128)(2,1)S(1)}, bf16[128,512]{1,0:T(8,128)(2,1)S(1)}, u32[]{:S(2)}, u32[]{:S(2)}) collective-permute-start(bf16[128,512]{1,0:T(8,128)(2,1)S(1)} %get-tuple-element.99), channel_id=1, source_target_pairs={{0,2},{1,3},{2,0},{3,1},{4,6},{5,7},{6,4},{7,5},{8,10},{9,11},{10,... | collective-permute-start | bytes 393224 | tf_op jit(solution)/shard_map/ppermute | solution.py:65
  62.3 7.1 %collective-permute-start.15 = (bf16[128,512]{1,0:T(8,128)(2,1)S(1)}, bf16[128,512]{1,0:T(8,128)(2,1)S(1)}, u32[]{:S(2)}, u32[]{:S(2)}) collective-permute-start(bf16[128,512]{1,0:T(8,128)(2,1)S(1)} %get-tuple-element.99), channel_id=1, source_target_pairs={{0,3},{1,0},{2,1},{3,2},{4,7},{5,4},{6,5},{7,6},{8,11},{9,8},{10,9... | collective-permute-start | bytes 393224 | tf_op jit(solution)/shard_map/ppermute | solution.py:65
  62.5 9.0 %collective-permute-start.14 = (bf16[128,512]{1,0:T(8,128)(2,1)S(1)}, bf16[128,512]{1,0:T(8,128)(2,1)S(1)}, u32[]{:S(2)}, u32[]{:S(2)}) collective-permute-start(bf16[128,512]{1,0:T(8,128)(2,1)S(1)} %get-tuple-element.100), channel_id=1, source_target_pairs={{0,4},{4,8},{8,12},{12,0},{1,5},{5,9},{9,13},{13,1},{2,6},{6,10},{... | collective-permute-start | bytes 393224 | tf_op jit(solution)/shard_map/ppermute | solution.py:65
  63.9 7.7 %collective-permute-start.13 = (bf16[128,512]{1,0:T(8,128)(2,1)S(1)}, bf16[128,512]{1,0:T(8,128)(2,1)S(1)}, u32[]{:S(2)}, u32[]{:S(2)}) collective-permute-start(bf16[128,512]{1,0:T(8,128)(2,1)S(1)} %get-tuple-element.100), channel_id=1, source_target_pairs={{0,8},{4,12},{8,0},{12,4},{1,9},{5,13},{9,1},{13,5},{2,10},{6,14},... | collective-permute-start | bytes 393224 | tf_op jit(solution)/shard_map/ppermute | solution.py:65
  67.4 6.8 %copy-start.16 = (bf16[128,512]{1,0:T(8,128)(2,1)}, bf16[128,512]{1,0:T(8,128)(2,1)S(1)}, u32[]{:S(2)}) copy-start(bf16[128,512]{1,0:T(8,128)(2,1)S(1)} %collective-permute-done.17.refs_16_) | copy-start | bytes 393220
  67.4 6.8 %collective-permute-start.12 = (bf16[128,512]{1,0:T(8,128)(2,1)S(1)}, bf16[128,512]{1,0:T(8,128)(2,1)S(1)}, u32[]{:S(2)}, u32[]{:S(2)}) collective-permute-start(bf16[128,512]{1,0:T(8,128)(2,1)S(1)} %get-tuple-element.100), channel_id=1, source_target_pairs={{0,12},{4,0},{8,4},{12,8},{1,13},{5,1},{9,5},{13,9},{2,14},{6,2},{... | collective-permute-start | bytes 393224 | tf_op jit(solution)/shard_map/ppermute | solution.py:65
  68.5 5.7 %copy-start.17 = (bf16[128,512]{1,0:T(8,128)(2,1)}, bf16[128,512]{1,0:T(8,128)(2,1)S(1)}, u32[]{:S(2)}) copy-start(bf16[128,512]{1,0:T(8,128)(2,1)S(1)} %collective-permute-done.16.refs_15_) | copy-start | bytes 393220
  68.5 43.9 %collective-permute-start.8 = (bf16[3,512,256]{2,1,0:T(8,128)(2,1)}, bf16[3,512,256]{2,1,0:T(8,128)(2,1)}, u32[]{:S(2)}, u32[]{:S(2)}) collective-permute-start(bf16[3,512,256]{2,1,0:T(8,128)(2,1)} %get-tuple-element.67), channel_id=1, source_target_pairs={{0,12},{4,0},{8,4},{12,8},{1,13},{5,1},{9,5},{13,9},{2,14},{6,2},{... | collective-permute-start | bytes 2359304 | tf_op jit(solution)/shard_map/ppermute | solution.py:65
  69.4 4.8 %copy-start.18 = (bf16[128,512]{1,0:T(8,128)(2,1)}, bf16[128,512]{1,0:T(8,128)(2,1)S(1)}, u32[]{:S(2)}) copy-start(bf16[128,512]{1,0:T(8,128)(2,1)S(1)} %collective-permute-done.15.refs_14_) | copy-start | bytes 393220
  69.4 43.1 %collective-permute-start.10 = (bf16[3,512,256]{2,1,0:T(8,128)(2,1)S(1)}, bf16[3,512,256]{2,1,0:T(8,128)(2,1)}, u32[]{:S(2)}, u32[]{:S(2)}) collective-permute-start(bf16[3,512,256]{2,1,0:T(8,128)(2,1)S(1)} %copy-done.15), channel_id=1, source_target_pairs={{0,3},{1,0},{2,1},{3,2},{4,7},{5,4},{6,5},{7,6},{8,11},{9,8},{10,9... | collective-permute-start | bytes 2359304 | tf_op jit(solution)/shard_map/ppermute | solution.py:65
  71.5 2.7 %copy-start.19 = (bf16[128,512]{1,0:T(8,128)(2,1)}, bf16[128,512]{1,0:T(8,128)(2,1)S(1)}, u32[]{:S(2)}) copy-start(bf16[128,512]{1,0:T(8,128)(2,1)S(1)} %collective-permute-done.14.refs_13_) | copy-start | bytes 393220
  71.5 43.6 %collective-permute-start.9 = (bf16[3,512,256]{2,1,0:T(8,128)(2,1)}, bf16[3,512,256]{2,1,0:T(8,128)(2,1)}, u32[]{:S(2)}, u32[]{:S(2)}) collective-permute-start(bf16[3,512,256]{2,1,0:T(8,128)(2,1)} %collective-permute-done.4.refs_7_), channel_id=1, source_target_pairs={{0,4},{4,8},{8,12},{12,0},{1,5},{5,9},{9,13},{13,1},{2,6},{6,10},{... | collective-permute-start | bytes 2359304 | tf_op jit(solution)/shard_map/ppermute | solution.py:65
  71.6 2.6 %copy-start.20 = (bf16[128,512]{1,0:T(8,128)(2,1)}, bf16[128,512]{1,0:T(8,128)(2,1)S(1)}, u32[]{:S(2)}) copy-start(bf16[128,512]{1,0:T(8,128)(2,1)S(1)} %collective-permute-done.13.refs_12_) | copy-start | bytes 393220
  71.6 43.5 %collective-permute-start.11 = (bf16[3,512,256]{2,1,0:T(8,128)(2,1)}, bf16[3,512,256]{2,1,0:T(8,128)(2,1)}, u32[]{:S(2)}, u32[]{:S(2)}) collective-permute-start(bf16[3,512,256]{2,1,0:T(8,128)(2,1)} %collective-permute-done.5.refs_10_), channel_id=1, source_target_pairs={{0,1},{1,2},{2,3},{3,0},{4,5},{5,6},{6,7},{7,4},{8,9},{9,10},{10,1... | collective-permute-start | bytes 2359304 | tf_op jit(solution)/shard_map/ppermute | solution.py:65
  74.2 0.6 copy-start.21
  103.5 40.4 %all-to-all-start.2 = ((bf16[4,3,512,256]{3,2,1,0:T(8,128)(2,1)}), bf16[4,3,512,256]{3,2,1,0:T(8,128)(2,1)}, u32[]{:S(2)}, u32[]{:S(2)}) async-start(bf16[4,3,512,256]{3,2,1,0:T(8,128)(2,1)} %get-tuple-element.79), calls=%async_computation.2 | async-start | bytes 6291456 | tf_op jit(solution)/shard_map/all_to_all | solution.py:418
  110.6 33.2 %collective-permute-start.18 = (bf16[3,512,256]{2,1,0:T(8,128)(2,1)}, bf16[3,512,256]{2,1,0:T(8,128)(2,1)S(1)}, u32[]{:S(2)}, u32[]{:S(2)}) collective-permute-start(bf16[3,512,256]{2,1,0:T(8,128)(2,1)} %get-tuple-element.80), channel_id=1, source_target_pairs={{0,1},{1,2},{2,3},{3,0},{4,5},{5,6},{6,7},{7,4},{8,9},{9,10},{10,1... | collective-permute-start | bytes 2359304 | tf_op jit(solution)/shard_map/ppermute | solution.py:69
  112.5 31.4 %collective-permute-start.19 = (bf16[3,512,256]{2,1,0:T(8,128)(2,1)}, bf16[3,512,256]{2,1,0:T(8,128)(2,1)S(1)}, u32[]{:S(2)}, u32[]{:S(2)}) collective-permute-start(bf16[3,512,256]{2,1,0:T(8,128)(2,1)} %get-tuple-element.81), channel_id=1, source_target_pairs={{0,2},{1,3},{2,0},{3,1},{4,6},{5,7},{6,4},{7,5},{8,10},{9,11},{10,... | collective-permute-start | bytes 2359304 | tf_op jit(solution)/shard_map/ppermute | solution.py:69
  112.5 31.3 %collective-permute-start.20 = (bf16[3,512,256]{2,1,0:T(8,128)(2,1)}, bf16[3,512,256]{2,1,0:T(8,128)(2,1)S(1)}, u32[]{:S(2)}, u32[]{:S(2)}) collective-permute-start(bf16[3,512,256]{2,1,0:T(8,128)(2,1)} %get-tuple-element.82), channel_id=1, source_target_pairs={{0,3},{1,0},{2,1},{3,2},{4,7},{5,4},{6,5},{7,6},{8,11},{9,8},{10,9... | collective-permute-start | bytes 2359304 | tf_op jit(solution)/shard_map/ppermute | solution.py:69
  143.8 0.9 copy-start.2
  143.9 1.1 copy-start.3
  143.9 1.4 copy-start.4
  145.3 42.5 %all-to-all-start.3 = ((bf16[4,3,512,256]{3,2,1,0:T(8,128)(2,1)}), bf16[4,3,512,256]{3,2,1,0:T(8,128)(2,1)}, u32[]{:S(2)}, u32[]{:S(2)}) async-start(bf16[4,3,512,256]{3,2,1,0:T(8,128)(2,1)} %get-tuple-element.83), calls=%async_computation.3 | async-start | bytes 6291456 | tf_op jit(solution)/shard_map/all_to_all | solution.py:418
  150.1 19.7 %collective-permute-start.21 = (bf16[3,512,256]{2,1,0:T(8,128)(2,1)}, bf16[3,512,256]{2,1,0:T(8,128)(2,1)S(1)}, u32[]{:S(2)}, u32[]{:S(2)}) collective-permute-start(bf16[3,512,256]{2,1,0:T(8,128)(2,1)} %get-tuple-element.85), channel_id=1, source_target_pairs={{0,1},{1,2},{2,3},{3,0},{4,5},{5,6},{6,7},{7,4},{8,9},{9,10},{10,1... | collective-permute-start | bytes 2359304 | tf_op jit(solution)/shard_map/ppermute | solution.py:69
  150.1 37.6 %collective-permute-start.22 = (bf16[3,512,256]{2,1,0:T(8,128)(2,1)}, bf16[3,512,256]{2,1,0:T(8,128)(2,1)S(1)}, u32[]{:S(2)}, u32[]{:S(2)}) collective-permute-start(bf16[3,512,256]{2,1,0:T(8,128)(2,1)} %get-tuple-element.86), channel_id=1, source_target_pairs={{0,2},{1,3},{2,0},{3,1},{4,6},{5,7},{6,4},{7,5},{8,10},{9,11},{10,... | collective-permute-start | bytes 2359304 | tf_op jit(solution)/shard_map/ppermute | solution.py:69
  153.5 34.2 %collective-permute-start.23 = (bf16[3,512,256]{2,1,0:T(8,128)(2,1)}, bf16[3,512,256]{2,1,0:T(8,128)(2,1)S(1)}, u32[]{:S(2)}, u32[]{:S(2)}) collective-permute-start(bf16[3,512,256]{2,1,0:T(8,128)(2,1)} %get-tuple-element.87), channel_id=1, source_target_pairs={{0,3},{1,0},{2,1},{3,2},{4,7},{5,4},{6,5},{7,6},{8,11},{9,8},{10,9... | collective-permute-start | bytes 2359304 | tf_op jit(solution)/shard_map/ppermute | solution.py:69
  169.8 18.0 %copy-start.5 = (bf16[3,512,256]{2,1,0:T(8,128)(2,1)}, bf16[3,512,256]{2,1,0:T(8,128)(2,1)S(1)}, u32[]{:S(2)}) copy-start(bf16[3,512,256]{2,1,0:T(8,128)(2,1)S(1)} %collective-permute-done.21.refs_0_) | copy-start | bytes 2359300
  187.8 1.0 copy-start.6
  187.8 1.2 copy-start.7

commit v9 on v8

--- a/solution.py
+++ b/solution.py
@@ -322,17 +322,16 @@
     everyone = lax.all_to_all(
         by_node.reshape(groups, channels, members * span), MEMBER, 0, 0, tiled=True
     )
+    everyone, own_1, near = lax.optimization_barrier((everyone, own_1, near))
+    far = [fetched(near[0], "x", 1), fetched(near[2], "z", 1)]
+    before = [fetched(a, axis, 3) for a, axis in zip(own_1, ("x", "z"))]
     observed = lax.dynamic_slice_in_dim(truth_field, offset, span, 1)
     area = lax.dynamic_slice_in_dim(cell_surface_share, offset, span, 0)
     derivative = score_gradient(
         everyone, jnp.tile(observed, (1, members)), jnp.tile(area[None], (1, members))
     )
-    derivative, own_1, near, decoder_rows = lax.optimization_barrier(
-        (derivative, own_1, near, decoder_matrix.T)
-    )
     returned = lax.all_to_all(derivative, MEMBER, 0, 0, tiled=True)
-    far = [fetched(near[0], "x", 1), fetched(near[2], "z", 1)]
-    before = [fetched(a, axis, 3) for a, axis in zip(own_1, ("x", "z"))]
+    returned, own_1, before, far = lax.optimization_barrier((returned, own_1, before, far))
     grad_forecast = (
         returned.reshape(groups, channels, members, span)
         .transpose(2, 1, 0, 3)
@@ -407,7 +406,7 @@
             late_own,
             late_x,
             late_z,
-            decoder_rows,
+            decoder_matrix.T,
         )
         if parts:
             (first_x, first_own, first_z) = parts[0]

time: 194 us -> 189 us (0.974)
  waiting for transfers between devices: 46.3 us -> 41.7 us
    ppermute x18, waiting for transfers between devices: 15.2 us -> 4.67 us  [fetched(): lax.ppermute(x, axis, [(i, (i - distance) % SIDE) for i in range(SIDE)])]
    all_to_all x1, waiting for transfers between devices: 0.79 us -> 6.13 us  [shards(): returned = lax.all_to_all(derivative, MEMBER, 0, 0, tiled=True)]
    unnamed x46 -> x48, local copies, waits for them, and re-layouts: 4.02 us -> 3.28 us
  transfers between devices with their start and end apart: 28 -> 28, of which waited for: 8 -> 9; matrix products, arithmetic and copies ran while one was open for 5% -> 4% of each run, Pallas kernels for 36% -> 37%
where the time goes in v9:
time: 189 us; the launch traced here: 188 us
  Pallas kernels  77.1 us (41%)
  starting transfers between devices  55.9 us (30%)
  waiting for transfers between devices  41.7 us (22%)
  local copies, waits for them, and re-layouts  7.97 us (4%)
  matrix products  2.36 us (1%)
  other arithmetic  2.02 us (1%)
    pallas_call x2, Pallas kernels, attention_tiles(): pl.pallas_call(functools.partial(tile_kernel, base=2 * base), out_shape=[...  57.4 us
    ppermute x6, waiting for transfers between devices, delivered(): lax.ppermute(x, axis, [(i, (i + distance) % SIDE) for i in range(SIDE)])  29.2 us
    ppermute x18, starting transfers between devices, fetched(): lax.ppermute(x, axis, [(i, (i - distance) % SIDE) for i in range(SIDE)])  26.3 us
    all_to_all x2, starting transfers between devices, shards(): got_x = lax.all_to_all(send_x, 'x', 0, 0, tiled=True)  12 us
    pallas_call x2, Pallas kernels, summed(): pl.pallas_call(sum_kernel, out_shape=[shape] * 3, grid=(2,), in_specs=[pl...  8.93 us
    ppermute x6, starting transfers between devices, delivered(): lax.ppermute(x, axis, [(i, (i + distance) % SIDE) for i in range(SIDE)])  8.46 us
    pallas_call x2, Pallas kernels, outgoing(): pl.pallas_call(pack_kernel, out_shape=[pltpu.HBM((3, rows, lanes), BF16)]...  7.41 us
    all_to_all x1, waiting for transfers between devices, shards(): returned = lax.all_to_all(derivative, MEMBER, 0, 0, tiled=True)  6.13 us
  transfers between devices with their start and end apart: 28, of which 9 were waited for; matrix products, arithmetic and copies ran while one was open for 4% of the time, Pallas kernels for 37%

profile of v9, /device:TPU:2, one launch (start us, length us, event | category | flops | bytes accessed | tf_op | source)
XLA Modules:
  0.0 188.1 jit_solution(10633105538779974151)
XLA Ops:
  0.7 3.8 %outgoing.3 = (bf16[3,512,256]{2,1,0:T(8,128)(2,1)}, bf16[3,512,256]{2,1,0:T(8,128)(2,1)}) custom-call(bf16[2,512,512]{2,1,0:T(8,128)(2,1)} %refs_0_.3, bf16[2,512,512]{2,1,0:T(8,128)(2,1)} %refs_1_.3, bf16[2,512,512]{2,1,0:T(8,128)(2,1)} %refs_2_.3), custom_call_target="tpu_custom_call" | custom-call | tf_op jit(solution)/shard_map/outgoing/pallas_call | solution.py:277
  4.4 1.5 collective-permute-start.1
  5.9 0.5 collective-permute-start
  6.5 1.9 %collective-permute-start.3 = (bf16[3,512,256]{2,1,0:T(8,128)(2,1)}, bf16[3,512,256]{2,1,0:T(8,128)(2,1)}, u32[]{:S(2)}, u32[]{:S(2)}) collective-permute-start(bf16[3,512,256]{2,1,0:T(8,128)(2,1)} %get-tuple-element.60), channel_id=1, source_target_pairs={{0,1},{1,2},{2,3},{3,0},{4,5},{5,6},{6,7},{7,4},{8,9},{9,10},{10,1... | collective-permute-start | bytes 2359304 | tf_op jit(solution)/shard_map/ppermute | solution.py:65
  8.4 2.1 %collective-permute-start.2 = (bf16[3,512,256]{2,1,0:T(8,128)(2,1)}, bf16[3,512,256]{2,1,0:T(8,128)(2,1)}, u32[]{:S(2)}, u32[]{:S(2)}) collective-permute-start(bf16[3,512,256]{2,1,0:T(8,128)(2,1)} %get-tuple-element.60), channel_id=1, source_target_pairs={{0,3},{1,0},{2,1},{3,2},{4,7},{5,4},{6,5},{7,6},{8,11},{9,8},{10,9... | collective-permute-start | bytes 2359304 | tf_op jit(solution)/shard_map/ppermute | solution.py:65
  10.5 0.4 fusion
  11.0 0.2 copy.30
  11.2 0.9 copy.32
  12.2 4.6 %all-to-all-start = ((f32[8,96,128]{2,1,0:T(8,128)}), f32[8,96,128]{2,1,0:T(8,128)S(1)}, u32[]{:S(2)}, u32[]{:S(2)}) async-start(f32[8,96,128]{2,1,0:T(8,128)} %copy.32), calls=%async_computation | async-start | bytes 786432 | tf_op jit(solution)/shard_map/all_to_all | solution.py:322
  16.8 3.6 %outgoing.2 = (bf16[3,512,256]{2,1,0:T(8,128)(2,1)}, bf16[3,512,256]{2,1,0:T(8,128)(2,1)}) custom-call(bf16[2,512,512]{2,1,0:T(8,128)(2,1)} %refs_0_.3, bf16[2,512,512]{2,1,0:T(8,128)(2,1)} %refs_1_.3, bf16[2,512,512]{2,1,0:T(8,128)(2,1)} %refs_2_.3), custom_call_target="tpu_custom_call" | custom-call | tf_op jit(solution)/shard_map/outgoing/pallas_call | solution.py:277
  20.5 0.8 dynamic_slice.7
  21.3 0.6 tile.20.area_ref
  21.9 0.1 select_reduce_fusion.2
  22.1 0.9 constant_dynamic-slice_fusion
  23.1 0.7 copy.34.truth_ref
  24.0 1.8 all-to-all-done.forecast_ref
  25.7 2.1 %collective-permute-done.3.refs_10_ = bf16[3,512,256]{2,1,0:T(8,128)(2,1)} collective-permute-done((bf16[3,512,256]{2,1,0:T(8,128)(2,1)}, bf16[3,512,256]{2,1,0:T(8,128)(2,1)}, u32[]{:S(2)}, u32[]{:S(2)}) %collective-permute-start.3) | collective-permute-done | bytes 786464 | tf_op jit(solution)/shard_map/ppermute | solution.py:65
  27.8 1.5 collective-permute-start.4
  29.3 1.3 collective-permute-start.5
  30.6 0.5 collective-permute-start.6
  31.1 2.0 %collective-permute-start.7 = (bf16[3,512,256]{2,1,0:T(8,128)(2,1)}, bf16[3,512,256]{2,1,0:T(8,128)(2,1)}, u32[]{:S(2)}, u32[]{:S(2)}) collective-permute-start(bf16[3,512,256]{2,1,0:T(8,128)(2,1)} %collective-permute-done.2.refs_8_), channel_id=1, source_target_pairs={{0,3},{1,0},{2,1},{3,2},{4,7},{5,4},{6,5},{7,6},{8,11},{9,8},{10,9... | collective-permute-start | bytes 2359304 | tf_op jit(solution)/shard_map/ppermute | solution.py:65
  33.3 3.4 %score_gradient.1 = bf16[8,96,128]{2,1,0:T(8,128)(2,1)} custom-call(f32[8,96,128]{2,1,0:T(8,128)} %copy-done.1, f32[96,128]{1,0:T(8,128)} %copy.34.truth_ref, f32[1,128]{1,0:T(1,128)} %tile.20.area_ref), custom_call_target="tpu_custom_call" | custom-call | tf_op jit(solution)/shard_map/score_gradient/pallas_call | solution.py:49
  36.7 4.5 %all-to-all-start.1 = ((bf16[8,96,128]{2,1,0:T(8,128)(2,1)}), bf16[8,96,128]{2,1,0:T(8,128)(2,1)S(1)}, u32[]{:S(2)}, u32[]{:S(2)}) async-start(bf16[8,96,128]{2,1,0:T(8,128)(2,1)} %score_gradient.1), calls=%async_computation.1 | async-start | bytes 393216 | tf_op jit(solution)/shard_map/all_to_all | solution.py:333
  41.2 0.7 select_reduce_fusion.1
  41.9 6.1 %all-to-all-done.1 = bf16[8,96,128]{2,1,0:T(8,128)(2,1)S(1)} async-done(((bf16[8,96,128]{2,1,0:T(8,128)(2,1)}), bf16[8,96,128]{2,1,0:T(8,128)(2,1)S(1)}, u32[]{:S(2)}, u32[]{:S(2)}) %all-to-all-start.1) | async-done | bytes 196640 | tf_op jit(solution)/shard_map/all_to_all | solution.py:333
  48.0 0.6 collective-permute-done.5.refs_10_
  48.6 0.3 copy-done.16
  48.9 0.2 copy.35
  49.1 0.5 constant_dynamic-update-slice_fusion
  49.6 0.5 convolution_convert_fusion.1
  50.2 1.0 bitcast_reduce_fusion
  51.2 0.9 collective-permute-start.17
  52.1 0.6 select_reduce_fusion
  52.7 3.7 %collective-permute-start.16 = (bf16[128,512]{1,0:T(8,128)(2,1)S(1)}, bf16[128,512]{1,0:T(8,128)(2,1)S(1)}, u32[]{:S(2)}, u32[]{:S(2)}) collective-permute-start(bf16[128,512]{1,0:T(8,128)(2,1)S(1)} %get-tuple-element.111), channel_id=1, source_target_pairs={{0,2},{1,3},{2,0},{3,1},{4,6},{5,7},{6,4},{7,5},{8,10},{9,11},{10,... | collective-permute-start | bytes 393224 | tf_op jit(solution)/shard_map/ppermute | solution.py:65
  56.4 0.8 collective-permute-start.15
  57.2 1.5 collective-permute-start.14
  58.7 3.5 %collective-permute-start.13 = (bf16[128,512]{1,0:T(8,128)(2,1)S(1)}, bf16[128,512]{1,0:T(8,128)(2,1)S(1)}, u32[]{:S(2)}, u32[]{:S(2)}) collective-permute-start(bf16[128,512]{1,0:T(8,128)(2,1)S(1)} %get-tuple-element.112), channel_id=1, source_target_pairs={{0,8},{4,12},{8,0},{12,4},{1,9},{5,13},{9,1},{13,5},{2,10},{6,14},... | collective-permute-start | bytes 393224 | tf_op jit(solution)/shard_map/ppermute | solution.py:65
  62.3 0.9 collective-permute-start.12
  63.3 0.4 collective-permute-start.8
  63.8 2.1 %collective-permute-start.10 = (bf16[3,512,256]{2,1,0:T(8,128)(2,1)S(1)}, bf16[3,512,256]{2,1,0:T(8,128)(2,1)}, u32[]{:S(2)}, u32[]{:S(2)}) collective-permute-start(bf16[3,512,256]{2,1,0:T(8,128)(2,1)S(1)} %copy-done.15), channel_id=1, source_target_pairs={{0,3},{1,0},{2,1},{3,2},{4,7},{5,4},{6,5},{7,6},{8,11},{9,8},{10,9... | collective-permute-start | bytes 2359304 | tf_op jit(solution)/shard_map/ppermute | solution.py:65
  65.9 0.7 collective-permute-done.13.refs_12_
  66.6 1.2 collective-permute-start.11
  67.8 1.3 collective-permute-done.12.refs_11_
  69.1 0.6 copy-done.22
  69.7 28.7 %attention_tiles.3 = (bf16[4,3,512,256]{3,2,1,0:T(8,128)(2,1)}, f32[3,512,256]{2,1,0:T(8,128)}, bf16[3,512,256]{2,1,0:T(8,128)(2,1)}, bf16[3,512,256]{2,1,0:T(8,128)(2,1)}, bf16[3,512,256]{2,1,0:T(8,128)(2,1)}) custom-call(s32[3,16]{1,0:T(4,128)S(1)} %pad_add_fusion.table, bf16[2,512,512]{2,1,0:T(8,128)(2,1)} %refs_0_.3, bf16[2,512,512]{2,1,0:T(8,128)(2,1)} %refs_1_.3, ...), custom_call_target="tpu_custom_call" | custom-call | flops 21474836480 | bytes 20971520 | tf_op jit(solution)/shard_map/attention_tiles/pallas_call | solution.py:187
  98.4 7.0 %all-to-all-start.2 = ((bf16[4,3,512,256]{3,2,1,0:T(8,128)(2,1)}), bf16[4,3,512,256]{3,2,1,0:T(8,128)(2,1)}, u32[]{:S(2)}, u32[]{:S(2)}) async-start(bf16[4,3,512,256]{3,2,1,0:T(8,128)(2,1)} %get-tuple-element.91), calls=%async_computation.2 | async-start | bytes 6291456 | tf_op jit(solution)/shard_map/all_to_all | solution.py:417
  105.4 1.2 collective-permute-start.18
  106.6 0.2 collective-permute-start.19
  106.8 2.5 %collective-permute-start.20 = (bf16[3,512,256]{2,1,0:T(8,128)(2,1)}, bf16[3,512,256]{2,1,0:T(8,128)(2,1)S(1)}, u32[]{:S(2)}, u32[]{:S(2)}) collective-permute-start(bf16[3,512,256]{2,1,0:T(8,128)(2,1)} %get-tuple-element.94), channel_id=1, source_target_pairs={{0,3},{1,0},{2,1},{3,2},{4,7},{5,4},{6,5},{7,6},{8,11},{9,8},{10,9... | collective-permute-start | bytes 2359304 | tf_op jit(solution)/shard_map/ppermute | solution.py:69
  109.3 28.7 %attention_tiles.2 = (bf16[4,3,512,256]{3,2,1,0:T(8,128)(2,1)}, f32[3,512,256]{2,1,0:T(8,128)}, bf16[3,512,256]{2,1,0:T(8,128)(2,1)}, bf16[3,512,256]{2,1,0:T(8,128)(2,1)}, bf16[3,512,256]{2,1,0:T(8,128)(2,1)}) custom-call(s32[3,16]{1,0:T(4,128)S(1)} %pad_add_fusion.table, bf16[2,512,512]{2,1,0:T(8,128)(2,1)} %refs_0_.3, bf16[2,512,512]{2,1,0:T(8,128)(2,1)} %refs_1_.3, ...), custom_call_target="tpu_custom_call" | custom-call | flops 21474836480 | bytes 20971520 | tf_op jit(solution)/shard_map/attention_tiles/pallas_call | solution.py:187
  138.0 0.6 collective-permute-done.19.refs_1_
  138.6 0.3 copy-done.2
  138.9 0.6 copy-done.3
  139.5 0.2 copy-done.4
  139.8 5.0 %all-to-all-start.3 = ((bf16[4,3,512,256]{3,2,1,0:T(8,128)(2,1)}), bf16[4,3,512,256]{3,2,1,0:T(8,128)(2,1)}, u32[]{:S(2)}, u32[]{:S(2)}) async-start(bf16[4,3,512,256]{3,2,1,0:T(8,128)(2,1)} %get-tuple-element.95), calls=%async_computation.3 | async-start | bytes 6291456 | tf_op jit(solution)/shard_map/all_to_all | solution.py:417
  144.8 1.0 collective-permute-start.21
  145.8 2.4 %collective-permute-start.22 = (bf16[3,512,256]{2,1,0:T(8,128)(2,1)}, bf16[3,512,256]{2,1,0:T(8,128)(2,1)S(1)}, u32[]{:S(2)}, u32[]{:S(2)}) collective-permute-start(bf16[3,512,256]{2,1,0:T(8,128)(2,1)} %get-tuple-element.98), channel_id=1, source_target_pairs={{0,2},{1,3},{2,0},{3,1},{4,6},{5,7},{6,4},{7,5},{8,10},{9,11},{10,... | collective-permute-start | bytes 2359304 | tf_op jit(solution)/shard_map/ppermute | solution.py:69
  148.2 1.2 collective-permute-start.23
  149.3 4.5 %summed.2 = (f32[2,512,512]{2,1,0:T(8,128)}, f32[2,512,512]{2,1,0:T(8,128)}, f32[2,512,512]{2,1,0:T(8,128)}) custom-call(bf16[4,3,512,256]{3,2,1,0:T(8,128)(2,1)} %all-to-all-done.2.got_x, f32[3,512,256]{2,1,0:T(8,128)} %get-tuple-element.101.own_z, bf16[3,512,256]{2,1,0:T(8,128)(2,1)} %copy-done.2, bf16[3,512,256]{2,1,0:T(8,128)(2,1)} %copy-done.3, ...), custom_call_target="tpu_custom_call" | custom-call | tf_op jit(solution)/shard_map/summed/pallas_call | solution.py:252
  153.8 10.6 %collective-permute-done.21.refs_0_ = bf16[3,512,256]{2,1,0:T(8,128)(2,1)S(1)} collective-permute-done((bf16[3,512,256]{2,1,0:T(8,128)(2,1)}, bf16[3,512,256]{2,1,0:T(8,128)(2,1)S(1)}, u32[]{:S(2)}, u32[]{:S(2)}) %collective-permute-start.21) | collective-permute-done | bytes 786464 | tf_op jit(solution)/shard_map/ppermute | solution.py:69
  164.4 18.0 %collective-permute-done.22.refs_1_ = bf16[3,512,256]{2,1,0:T(8,128)(2,1)S(1)} collective-permute-done((bf16[3,512,256]{2,1,0:T(8,128)(2,1)}, bf16[3,512,256]{2,1,0:T(8,128)(2,1)S(1)}, u32[]{:S(2)}, u32[]{:S(2)}) %collective-permute-start.22) | collective-permute-done | bytes 786464 | tf_op jit(solution)/shard_map/ppermute | solution.py:69
  182.4 0.9 copy-done.6
  183.3 0.3 copy-done.7
  183.6 4.5 %summed.3 = (f32[2,512,512]{2,1,0:T(8,128)}, f32[2,512,512]{2,1,0:T(8,128)}, f32[2,512,512]{2,1,0:T(8,128)}) custom-call(bf16[4,3,512,256]{3,2,1,0:T(8,128)(2,1)} %all-to-all-done.3.got_x, f32[3,512,256]{2,1,0:T(8,128)} %get-tuple-element.96.own_z, bf16[3,512,256]{2,1,0:T(8,128)(2,1)} %copy-done.5, ...), custom_call_target="tpu_custom_call", output_to_operand_aliasing={{0}: (5, {}), {1}: (6, {}), {2}: (7, {})} | custom-call | tf_op jit(solution)/shard_map/summed/pallas_call | solution.py:252
  (86 shorter events, 1.1 us)
Async XLA Ops:
  0.6 9.9 %copy-start = (bf16[2,512,512]{2,1,0:T(8,128)(2,1)S(1)}, bf16[2,512,512]{2,1,0:T(8,128)(2,1)}, u32[]{:S(2)}) copy-start(bf16[2,512,512]{2,1,0:T(8,128)(2,1)} %param.12) | copy-start | bytes 3145732
  0.6 9.9 %copy-start.8 = (bf16[512,96]{0,1:T(8,128)(2,1)S(1)}, bf16[512,96]{0,1:T(8,128)(2,1)}, u32[]{:S(2)}) copy-start(bf16[512,96]{0,1:T(8,128)(2,1)} %param.13) | copy-start | bytes 294916
  0.7 9.9 %copy-start.10 = (f32[96,512]{1,0:T(8,128)S(1)}, f32[96,512]{1,0:T(8,128)}, u32[]{:S(2)}) copy-start(f32[96,512]{1,0:T(8,128)} %param.14) | copy-start | bytes 589828
  4.4 21.3 %collective-permute-start.1 = (bf16[3,512,256]{2,1,0:T(8,128)(2,1)}, bf16[3,512,256]{2,1,0:T(8,128)(2,1)S(1)}, u32[]{:S(2)}, u32[]{:S(2)}) collective-permute-start(bf16[3,512,256]{2,1,0:T(8,128)(2,1)} %get-tuple-element.59), channel_id=1, source_target_pairs={{0,4},{4,8},{8,12},{12,0},{1,5},{5,9},{9,13},{13,1},{2,6},{6,10},{... | collective-permute-start | bytes 2359304 | tf_op jit(solution)/shard_map/ppermute | solution.py:65
  5.9 19.8 %collective-permute-start = (bf16[3,512,256]{2,1,0:T(8,128)(2,1)}, bf16[3,512,256]{2,1,0:T(8,128)(2,1)}, u32[]{:S(2)}, u32[]{:S(2)}) collective-permute-start(bf16[3,512,256]{2,1,0:T(8,128)(2,1)} %get-tuple-element.59), channel_id=1, source_target_pairs={{0,12},{4,0},{8,4},{12,8},{1,13},{5,1},{9,5},{13,9},{2,14},{6,2},{... | collective-permute-start | bytes 2359304 | tf_op jit(solution)/shard_map/ppermute | solution.py:65
  6.5 21.3 %collective-permute-start.3 = (bf16[3,512,256]{2,1,0:T(8,128)(2,1)}, bf16[3,512,256]{2,1,0:T(8,128)(2,1)}, u32[]{:S(2)}, u32[]{:S(2)}) collective-permute-start(bf16[3,512,256]{2,1,0:T(8,128)(2,1)} %get-tuple-element.60), channel_id=1, source_target_pairs={{0,1},{1,2},{2,3},{3,0},{4,5},{5,6},{6,7},{7,4},{8,9},{9,10},{10,1... | collective-permute-start | bytes 2359304 | tf_op jit(solution)/shard_map/ppermute | solution.py:65
  8.4 19.4 %collective-permute-start.2 = (bf16[3,512,256]{2,1,0:T(8,128)(2,1)}, bf16[3,512,256]{2,1,0:T(8,128)(2,1)}, u32[]{:S(2)}, u32[]{:S(2)}) collective-permute-start(bf16[3,512,256]{2,1,0:T(8,128)(2,1)} %get-tuple-element.60), channel_id=1, source_target_pairs={{0,3},{1,0},{2,1},{3,2},{4,7},{5,4},{6,5},{7,6},{8,11},{9,8},{10,9... | collective-permute-start | bytes 2359304 | tf_op jit(solution)/shard_map/ppermute | solution.py:65
  12.2 9.7 %copy-start.12 = (s32[16,16]{1,0:T(8,128)S(1)}, s32[16,16]{1,0:T(8,128)}, u32[]{:S(2)}) copy-start(s32[16,16]{1,0:T(8,128)} %param.23) | copy-start | bytes 3076
  12.2 9.7 %copy-start.13 = (s32[16,16]{1,0:T(8,128)S(1)}, s32[16,16]{1,0:T(8,128)}, u32[]{:S(2)}) copy-start(s32[16,16]{1,0:T(8,128)} %param.22) | copy-start | bytes 3076
  12.2 13.5 %all-to-all-start = ((f32[8,96,128]{2,1,0:T(8,128)}), f32[8,96,128]{2,1,0:T(8,128)S(1)}, u32[]{:S(2)}, u32[]{:S(2)}) async-start(f32[8,96,128]{2,1,0:T(8,128)} %copy.32), calls=%async_computation | async-start | bytes 786432 | tf_op jit(solution)/shard_map/all_to_all | solution.py:322
  20.4 28.7 %copy-start.23 = (s32[1,512]{1,0:T(1,128)S(1)}, s32[1,512]{1,0:T(1,128)}, u32[]{:S(2)}) copy-start(s32[1,512]{1,0:T(1,128)} %param.17) | copy-start | bytes 6148
  25.7 7.6 %copy-start.1 = (f32[8,96,128]{2,1,0:T(8,128)}, f32[8,96,128]{2,1,0:T(8,128)S(1)}, u32[]{:S(2)}) copy-start(f32[8,96,128]{2,1,0:T(8,128)S(1)} %all-to-all-done.forecast_ref) | copy-start | bytes 1179652
  25.7 24.4 %copy-start.14 = (bf16[3,512,256]{2,1,0:T(8,128)(2,1)}, bf16[3,512,256]{2,1,0:T(8,128)(2,1)S(1)}, u32[]{:S(2)}) copy-start(bf16[3,512,256]{2,1,0:T(8,128)(2,1)S(1)} %collective-permute-done.1.refs_7_) | copy-start | bytes 2359300
  27.8 20.2 %collective-permute-start.4 = (bf16[3,512,256]{2,1,0:T(8,128)(2,1)}, bf16[3,512,256]{2,1,0:T(8,128)(2,1)S(1)}, u32[]{:S(2)}, u32[]{:S(2)}) collective-permute-start(bf16[3,512,256]{2,1,0:T(8,128)(2,1)} %get-tuple-element.79), channel_id=1, source_target_pairs={{0,4},{4,8},{8,12},{12,0},{1,5},{5,9},{9,13},{13,1},{2,6},{6,10},{... | collective-permute-start | bytes 2359304 | tf_op jit(solution)/shard_map/ppermute | solution.py:65
  29.3 19.3 %collective-permute-start.5 = (bf16[3,512,256]{2,1,0:T(8,128)(2,1)}, bf16[3,512,256]{2,1,0:T(8,128)(2,1)}, u32[]{:S(2)}, u32[]{:S(2)}) collective-permute-start(bf16[3,512,256]{2,1,0:T(8,128)(2,1)} %get-tuple-element.81), channel_id=1, source_target_pairs={{0,1},{1,2},{2,3},{3,0},{4,5},{5,6},{6,7},{7,4},{8,9},{9,10},{10,1... | collective-permute-start | bytes 2359304 | tf_op jit(solution)/shard_map/ppermute | solution.py:65
  30.6 18.1 %collective-permute-start.6 = (bf16[3,512,256]{2,1,0:T(8,128)(2,1)}, bf16[3,512,256]{2,1,0:T(8,128)(2,1)}, u32[]{:S(2)}, u32[]{:S(2)}) collective-permute-start(bf16[3,512,256]{2,1,0:T(8,128)(2,1)} %collective-permute-done.refs_5_), channel_id=1, source_target_pairs={{0,12},{4,0},{8,4},{12,8},{1,13},{5,1},{9,5},{13,9},{2,14},{6,2},{... | collective-permute-start | bytes 2359304 | tf_op jit(solution)/shard_map/ppermute | solution.py:65
  31.1 17.8 %collective-permute-start.7 = (bf16[3,512,256]{2,1,0:T(8,128)(2,1)}, bf16[3,512,256]{2,1,0:T(8,128)(2,1)}, u32[]{:S(2)}, u32[]{:S(2)}) collective-permute-start(bf16[3,512,256]{2,1,0:T(8,128)(2,1)} %collective-permute-done.2.refs_8_), channel_id=1, source_target_pairs={{0,3},{1,0},{2,1},{3,2},{4,7},{5,4},{6,5},{7,6},{8,11},{9,8},{10,9... | collective-permute-start | bytes 2359304 | tf_op jit(solution)/shard_map/ppermute | solution.py:65
  36.7 11.3 %all-to-all-start.1 = ((bf16[8,96,128]{2,1,0:T(8,128)(2,1)}), bf16[8,96,128]{2,1,0:T(8,128)(2,1)S(1)}, u32[]{:S(2)}, u32[]{:S(2)}) async-start(bf16[8,96,128]{2,1,0:T(8,128)(2,1)} %score_gradient.1), calls=%async_computation.1 | async-start | bytes 393216 | tf_op jit(solution)/shard_map/all_to_all | solution.py:333
  48.0 0.9 copy-start.16
  50.1 1.0 copy-start.11
  50.1 13.6 %copy-start.15 = (bf16[3,512,256]{2,1,0:T(8,128)(2,1)S(1)}, bf16[3,512,256]{2,1,0:T(8,128)(2,1)}, u32[]{:S(2)}) copy-start(bf16[3,512,256]{2,1,0:T(8,128)(2,1)} %get-tuple-element.81) | copy-start | bytes 2359300
  51.2 17.9 %copy-start.9 = (bf16[2,128,512]{2,1,0:T(8,128)(2,1)}, bf16[2,128,512]{2,1,0:T(8,128)(2,1)S(1)}, u32[]{:S(2)}) copy-start(bf16[2,128,512]{2,1,0:T(8,128)(2,1)S(1)} %fusion.12.refs_3_) | copy-start | bytes 786436
  51.2 11.0 %collective-permute-start.17 = (bf16[128,512]{1,0:T(8,128)(2,1)S(1)}, bf16[128,512]{1,0:T(8,128)(2,1)S(1)}, u32[]{:S(2)}, u32[]{:S(2)}) collective-permute-start(bf16[128,512]{1,0:T(8,128)(2,1)S(1)} %get-tuple-element.111), channel_id=1, source_target_pairs={{0,1},{1,2},{2,3},{3,0},{4,5},{5,6},{6,7},{7,4},{8,9},{9,10},{10,1... | collective-permute-start | bytes 393224 | tf_op jit(solution)/shard_map/ppermute | solution.py:65
  52.7 10.6 %collective-permute-start.16 = (bf16[128,512]{1,0:T(8,128)(2,1)S(1)}, bf16[128,512]{1,0:T(8,128)(2,1)S(1)}, u32[]{:S(2)}, u32[]{:S(2)}) collective-permute-start(bf16[128,512]{1,0:T(8,128)(2,1)S(1)} %get-tuple-element.111), channel_id=1, source_target_pairs={{0,2},{1,3},{2,0},{3,1},{4,6},{5,7},{6,4},{7,5},{8,10},{9,11},{10,... | collective-permute-start | bytes 393224 | tf_op jit(solution)/shard_map/ppermute | solution.py:65
  56.4 7.4 %collective-permute-start.15 = (bf16[128,512]{1,0:T(8,128)(2,1)S(1)}, bf16[128,512]{1,0:T(8,128)(2,1)S(1)}, u32[]{:S(2)}, u32[]{:S(2)}) collective-permute-start(bf16[128,512]{1,0:T(8,128)(2,1)S(1)} %get-tuple-element.111), channel_id=1, source_target_pairs={{0,3},{1,0},{2,1},{3,2},{4,7},{5,4},{6,5},{7,6},{8,11},{9,8},{10,9... | collective-permute-start | bytes 393224 | tf_op jit(solution)/shard_map/ppermute | solution.py:65
  57.2 8.7 %collective-permute-start.14 = (bf16[128,512]{1,0:T(8,128)(2,1)S(1)}, bf16[128,512]{1,0:T(8,128)(2,1)S(1)}, u32[]{:S(2)}, u32[]{:S(2)}) collective-permute-start(bf16[128,512]{1,0:T(8,128)(2,1)S(1)} %get-tuple-element.112), channel_id=1, source_target_pairs={{0,4},{4,8},{8,12},{12,0},{1,5},{5,9},{9,13},{13,1},{2,6},{6,10},{... | collective-permute-start | bytes 393224 | tf_op jit(solution)/shard_map/ppermute | solution.py:65
  58.7 7.9 %collective-permute-start.13 = (bf16[128,512]{1,0:T(8,128)(2,1)S(1)}, bf16[128,512]{1,0:T(8,128)(2,1)S(1)}, u32[]{:S(2)}, u32[]{:S(2)}) collective-permute-start(bf16[128,512]{1,0:T(8,128)(2,1)S(1)} %get-tuple-element.112), channel_id=1, source_target_pairs={{0,8},{4,12},{8,0},{12,4},{1,9},{5,13},{9,1},{13,5},{2,10},{6,14},... | collective-permute-start | bytes 393224 | tf_op jit(solution)/shard_map/ppermute | solution.py:65
  62.3 6.8 %copy-start.17 = (bf16[128,512]{1,0:T(8,128)(2,1)}, bf16[128,512]{1,0:T(8,128)(2,1)S(1)}, u32[]{:S(2)}) copy-start(bf16[128,512]{1,0:T(8,128)(2,1)S(1)} %collective-permute-done.17.refs_16_) | copy-start | bytes 393220
  62.3 6.8 %collective-permute-start.12 = (bf16[128,512]{1,0:T(8,128)(2,1)S(1)}, bf16[128,512]{1,0:T(8,128)(2,1)S(1)}, u32[]{:S(2)}, u32[]{:S(2)}) collective-permute-start(bf16[128,512]{1,0:T(8,128)(2,1)S(1)} %get-tuple-element.112), channel_id=1, source_target_pairs={{0,12},{4,0},{8,4},{12,8},{1,13},{5,1},{9,5},{13,9},{2,14},{6,2},{... | collective-permute-start | bytes 393224 | tf_op jit(solution)/shard_map/ppermute | solution.py:65
  63.3 5.8 %copy-start.18 = (bf16[128,512]{1,0:T(8,128)(2,1)}, bf16[128,512]{1,0:T(8,128)(2,1)S(1)}, u32[]{:S(2)}) copy-start(bf16[128,512]{1,0:T(8,128)(2,1)S(1)} %collective-permute-done.16.refs_15_) | copy-start | bytes 393220
  63.3 43.3 %collective-permute-start.8 = (bf16[3,512,256]{2,1,0:T(8,128)(2,1)}, bf16[3,512,256]{2,1,0:T(8,128)(2,1)}, u32[]{:S(2)}, u32[]{:S(2)}) collective-permute-start(bf16[3,512,256]{2,1,0:T(8,128)(2,1)} %get-tuple-element.79), channel_id=1, source_target_pairs={{0,12},{4,0},{8,4},{12,8},{1,13},{5,1},{9,5},{13,9},{2,14},{6,2},{... | collective-permute-start | bytes 2359304 | tf_op jit(solution)/shard_map/ppermute | solution.py:65
  63.8 5.3 %copy-start.19 = (bf16[128,512]{1,0:T(8,128)(2,1)}, bf16[128,512]{1,0:T(8,128)(2,1)S(1)}, u32[]{:S(2)}) copy-start(bf16[128,512]{1,0:T(8,128)(2,1)S(1)} %collective-permute-done.15.refs_14_) | copy-start | bytes 393220
  63.8 43.0 %collective-permute-start.10 = (bf16[3,512,256]{2,1,0:T(8,128)(2,1)S(1)}, bf16[3,512,256]{2,1,0:T(8,128)(2,1)}, u32[]{:S(2)}, u32[]{:S(2)}) collective-permute-start(bf16[3,512,256]{2,1,0:T(8,128)(2,1)S(1)} %copy-done.15), channel_id=1, source_target_pairs={{0,3},{1,0},{2,1},{3,2},{4,7},{5,4},{6,5},{7,6},{8,11},{9,8},{10,9... | collective-permute-start | bytes 2359304 | tf_op jit(solution)/shard_map/ppermute | solution.py:65
  65.9 3.2 %copy-start.20 = (bf16[128,512]{1,0:T(8,128)(2,1)}, bf16[128,512]{1,0:T(8,128)(2,1)S(1)}, u32[]{:S(2)}) copy-start(bf16[128,512]{1,0:T(8,128)(2,1)S(1)} %collective-permute-done.14.refs_13_) | copy-start | bytes 393220
  65.9 43.4 %collective-permute-start.9 = (bf16[3,512,256]{2,1,0:T(8,128)(2,1)}, bf16[3,512,256]{2,1,0:T(8,128)(2,1)}, u32[]{:S(2)}, u32[]{:S(2)}) collective-permute-start(bf16[3,512,256]{2,1,0:T(8,128)(2,1)} %copy-done.16), channel_id=1, source_target_pairs={{0,4},{4,8},{8,12},{12,0},{1,5},{5,9},{9,13},{13,1},{2,6},{6,10},{... | collective-permute-start | bytes 2359304 | tf_op jit(solution)/shard_map/ppermute | solution.py:65
  66.6 2.5 %copy-start.21 = (bf16[128,512]{1,0:T(8,128)(2,1)}, bf16[128,512]{1,0:T(8,128)(2,1)S(1)}, u32[]{:S(2)}) copy-start(bf16[128,512]{1,0:T(8,128)(2,1)S(1)} %collective-permute-done.13.refs_12_) | copy-start | bytes 393220
  66.6 42.7 %collective-permute-start.11 = (bf16[3,512,256]{2,1,0:T(8,128)(2,1)}, bf16[3,512,256]{2,1,0:T(8,128)(2,1)}, u32[]{:S(2)}, u32[]{:S(2)}) collective-permute-start(bf16[3,512,256]{2,1,0:T(8,128)(2,1)} %collective-permute-done.5.refs_10_), channel_id=1, source_target_pairs={{0,1},{1,2},{2,3},{3,0},{4,5},{5,6},{6,7},{7,4},{8,9},{9,10},{10,1... | collective-permute-start | bytes 2359304 | tf_op jit(solution)/shard_map/ppermute | solution.py:65
  69.1 0.6 copy-start.22
  98.4 40.2 %all-to-all-start.2 = ((bf16[4,3,512,256]{3,2,1,0:T(8,128)(2,1)}), bf16[4,3,512,256]{3,2,1,0:T(8,128)(2,1)}, u32[]{:S(2)}, u32[]{:S(2)}) async-start(bf16[4,3,512,256]{3,2,1,0:T(8,128)(2,1)} %get-tuple-element.91), calls=%async_computation.2 | async-start | bytes 6291456 | tf_op jit(solution)/shard_map/all_to_all | solution.py:417
  105.4 32.6 %collective-permute-start.18 = (bf16[3,512,256]{2,1,0:T(8,128)(2,1)}, bf16[3,512,256]{2,1,0:T(8,128)(2,1)S(1)}, u32[]{:S(2)}, u32[]{:S(2)}) collective-permute-start(bf16[3,512,256]{2,1,0:T(8,128)(2,1)} %get-tuple-element.92), channel_id=1, source_target_pairs={{0,1},{1,2},{2,3},{3,0},{4,5},{5,6},{6,7},{7,4},{8,9},{9,10},{10,1... | collective-permute-start | bytes 2359304 | tf_op jit(solution)/shard_map/ppermute | solution.py:69
  106.6 32.0 %collective-permute-start.19 = (bf16[3,512,256]{2,1,0:T(8,128)(2,1)}, bf16[3,512,256]{2,1,0:T(8,128)(2,1)S(1)}, u32[]{:S(2)}, u32[]{:S(2)}) collective-permute-start(bf16[3,512,256]{2,1,0:T(8,128)(2,1)} %get-tuple-element.93), channel_id=1, source_target_pairs={{0,2},{1,3},{2,0},{3,1},{4,6},{5,7},{6,4},{7,5},{8,10},{9,11},{10,... | collective-permute-start | bytes 2359304 | tf_op jit(solution)/shard_map/ppermute | solution.py:69
  106.8 31.8 %collective-permute-start.20 = (bf16[3,512,256]{2,1,0:T(8,128)(2,1)}, bf16[3,512,256]{2,1,0:T(8,128)(2,1)S(1)}, u32[]{:S(2)}, u32[]{:S(2)}) collective-permute-start(bf16[3,512,256]{2,1,0:T(8,128)(2,1)} %get-tuple-element.94), channel_id=1, source_target_pairs={{0,3},{1,0},{2,1},{3,2},{4,7},{5,4},{6,5},{7,6},{8,11},{9,8},{10,9... | collective-permute-start | bytes 2359304 | tf_op jit(solution)/shard_map/ppermute | solution.py:69
  138.0 0.9 copy-start.2
  138.6 0.9 copy-start.3
  138.6 1.1 copy-start.4
  139.8 42.6 %all-to-all-start.3 = ((bf16[4,3,512,256]{3,2,1,0:T(8,128)(2,1)}), bf16[4,3,512,256]{3,2,1,0:T(8,128)(2,1)}, u32[]{:S(2)}, u32[]{:S(2)}) async-start(bf16[4,3,512,256]{3,2,1,0:T(8,128)(2,1)} %get-tuple-element.95), calls=%async_computation.3 | async-start | bytes 6291456 | tf_op jit(solution)/shard_map/all_to_all | solution.py:417
  144.8 19.7 %collective-permute-start.21 = (bf16[3,512,256]{2,1,0:T(8,128)(2,1)}, bf16[3,512,256]{2,1,0:T(8,128)(2,1)S(1)}, u32[]{:S(2)}, u32[]{:S(2)}) collective-permute-start(bf16[3,512,256]{2,1,0:T(8,128)(2,1)} %get-tuple-element.97), channel_id=1, source_target_pairs={{0,1},{1,2},{2,3},{3,0},{4,5},{5,6},{6,7},{7,4},{8,9},{9,10},{10,1... | collective-permute-start | bytes 2359304 | tf_op jit(solution)/shard_map/ppermute | solution.py:69
  145.8 36.6 %collective-permute-start.22 = (bf16[3,512,256]{2,1,0:T(8,128)(2,1)}, bf16[3,512,256]{2,1,0:T(8,128)(2,1)S(1)}, u32[]{:S(2)}, u32[]{:S(2)}) collective-permute-start(bf16[3,512,256]{2,1,0:T(8,128)(2,1)} %get-tuple-element.98), channel_id=1, source_target_pairs={{0,2},{1,3},{2,0},{3,1},{4,6},{5,7},{6,4},{7,5},{8,10},{9,11},{10,... | collective-permute-start | bytes 2359304 | tf_op jit(solution)/shard_map/ppermute | solution.py:69
  148.2 34.2 %collective-permute-start.23 = (bf16[3,512,256]{2,1,0:T(8,128)(2,1)}, bf16[3,512,256]{2,1,0:T(8,128)(2,1)S(1)}, u32[]{:S(2)}, u32[]{:S(2)}) collective-permute-start(bf16[3,512,256]{2,1,0:T(8,128)(2,1)} %get-tuple-element.99), channel_id=1, source_target_pairs={{0,3},{1,0},{2,1},{3,2},{4,7},{5,4},{6,5},{7,6},{8,11},{9,8},{10,9... | collective-permute-start | bytes 2359304 | tf_op jit(solution)/shard_map/ppermute | solution.py:69
  164.4 18.0 %copy-start.5 = (bf16[3,512,256]{2,1,0:T(8,128)(2,1)}, bf16[3,512,256]{2,1,0:T(8,128)(2,1)S(1)}, u32[]{:S(2)}) copy-start(bf16[3,512,256]{2,1,0:T(8,128)(2,1)S(1)} %collective-permute-done.21.refs_0_) | copy-start | bytes 2359300
  182.4 0.9 copy-start.6
  182.4 1.2 copy-start.7
